TPU v7x, 32 devices: a whole 2x2x4 slice. The times are simulated.
32 devices in a mesh: lat: 8 (over z, x), lon: 4 (over y, core).
Axes of the slice: x: 2, y: 2, z: 4, core: 2. Of those that a mesh axis runs over, the one named last changes fastest.
Arguments:
- wind_u: float32 [4, 1536, 2560], P(None, 'lat', 'lon'), may hold values from -6 to 6
- wind_v: float32 [4, 1536, 2560], P(None, 'lat', 'lon'), may hold values from -6 to 6
- basis: bfloat16 [800, 640, 768], P('lat'), may hold values from -6 to 6
- wave_slots: int32 [640], replicated, may hold values from 0 to 799, as said below
- degree_count: int32 [640], replicated, may hold values from 1 to 640, as said below
- viscosity: float32 [4], replicated, may hold values from 0.5 to 50
Outputs:
- spectral: float32 [800, 4, 2, 2, 640], P('lat', 'lon')
- tendency: float32 [4, 2, 1536, 2560], P(None, None, 'lat', 'lon')
Inputs may be any that keep to these rules, and one draw needn't show every extreme that they name: `wave_slots`: all values differ; slot s belongs to owner s // 100, so an owner holds at most 100 wavenumbers, and one owner holds exactly 100. degree_count[0] = 640, and degree_count[m] <= 640 - m.
All inputs are finite; a program needn't handle non-finite values.
Results may differ from a plain program's by a relative error of at most 0.0048.
Values may be sent and summed in bfloat16 or wider, within the bound.
No kernel may reach another device: no remote copies, remote signals or barrier semaphores. Data moves between devices by JAX's collectives and lax.ppermute only.
A program may use at most 256 MiB of HBM per device.

v0:
```python
import functools
import math

import jax
import jax.numpy as jnp
from jax import lax
from jax.experimental import pallas as pl
from jax.experimental.pallas import tpu as pltpu
from jax.sharding import PartitionSpec as P

BF16 = jnp.bfloat16
F32 = jnp.float32
VMEM_LIMIT = 60 * 1024 * 1024
STEP = 128
LANES = 128
DEPTH = 3
NT = (((1,), (1,)), ((), ()))
NN = (((1,), (0,)), ((), ()))


def dot(a, b, dims=NN):
    return lax.dot_general(a, b, dims, preferred_element_type=F32)


def split_high_low(value):
    high = lax.reduce_precision(value, 8, 7)
    return high.astype(BF16), (value - high).astype(BF16)


def wave_tables(sectors, columns, waves):
    length = sectors * columns
    wave_ids = jnp.arange(waves, dtype=jnp.int32)
    unit = 2.0 * math.pi / length

    def angle(places):
        return (wave_ids[:, None] * places[None, :] % length).astype(F32) * unit

    inner = angle(jnp.arange(columns, dtype=jnp.int32))
    outer = angle(jnp.arange(sectors, dtype=jnp.int32) * columns)
    scaling = 1.0 / math.sqrt(length)
    near_cos, near_sin = lax.optimization_barrier((jnp.cos(inner) * scaling, jnp.sin(inner) * scaling))
    far_cos, far_sin = jnp.cos(outer).T[:, :, None], jnp.sin(outer).T[:, :, None]
    real = far_cos * near_cos - far_sin * near_sin
    imag = -(far_sin * near_cos + far_cos * near_sin)
    return split_high_low(real) + split_high_low(imag)


def forward_kernel(lines, real_hi, real_lo, imag_hi, imag_lo, one_hot, mirror, out, by_wave):
    step = pl.program_id(0)
    sectors, rows, _ = lines.shape
    owners = one_hot.shape[0]
    size = real_hi.shape[1]
    place = pl.ds(pl.multiple_of(step * size, size), size)
    for part, (high, low) in enumerate(((real_hi, real_lo), (imag_hi, imag_lo))):
        total = None
        for sector in range(sectors):
            line = lines[sector]
            term = dot(high[sector], line, NT) + dot(low[sector], line, NT)
            total = term if total is None else total + term
        by_wave[part, place, :] = total.astype(BF16)

    @pl.when(step == pl.num_programs(0) - 1)
    def _():
        for part in range(2):
            turned = dot(by_wave[part], mirror[...]).astype(BF16)
            for owner in range(owners):
                out[owner, :, part * rows : (part + 1) * rows] = dot(one_hot[owner], turned).astype(BF16)


def to_owners(lines, tables, one_hot, mirror):
    sectors, rows, columns = lines.shape
    owners, capacity, waves = one_hot.shape
    size = 128
    table_spec = pl.BlockSpec((sectors, size, columns), lambda i: (0, i, 0))
    return pl.pallas_call(
        forward_kernel,
        grid=(waves // size,),
        in_specs=[pl.BlockSpec((sectors, rows, columns), lambda i: (0, 0, 0))]
        + [table_spec] * 4
        + [
            pl.BlockSpec((owners, capacity, waves), lambda i: (0, 0, 0)),
            pl.BlockSpec((rows, rows), lambda i: (0, 0)),
        ],
        out_specs=pl.BlockSpec((owners, capacity, 2 * rows), lambda i: (0, 0, 0)),
        out_shape=jax.ShapeDtypeStruct((owners, capacity, 2 * rows), BF16),
        scratch_shapes=[pltpu.VMEM((2, waves, rows), BF16)],
        compiler_params=pltpu.CompilerParams(vmem_limit_bytes=VMEM_LIMIT),
        name="to_owners",
    )(lines, *tables, one_hot, mirror)


def backward_kernel(slot_rows, real_hi, real_lo, imag_hi, imag_lo, one_hot, mirror, out, by_wave):
    owners, capacity, waves = one_hot.shape
    rows = mirror.shape[0]

    @pl.when(pl.program_id(0) == 0)
    def _():
        wave_ids = lax.broadcasted_iota(jnp.int32, (1, waves), 1)
        weight = jnp.where(wave_ids == 0, 1.0, 2.0).astype(F32)
        for part in range(2):
            total = None
            for owner in range(owners):
                piece = slot_rows[owner, :, part * rows : (part + 1) * rows]
                turned = dot(mirror[...], piece, NT).astype(BF16)
                term = dot(turned, one_hot[owner])
                total = term if total is None else total + term
            by_wave[part] = (total * weight).astype(BF16)

    real, imag = by_wave[0], by_wave[1]
    total = dot(real, real_hi[0]) + dot(real, real_lo[0]) + dot(imag, imag_hi[0]) + dot(imag, imag_lo[0])
    out[0] = total.astype(BF16)


def to_sectors(slot_rows, tables, one_hot, mirror):
    owners, capacity, waves = one_hot.shape
    sectors, _, columns = tables[0].shape
    rows = mirror.shape[0]
    table_spec = pl.BlockSpec((1, waves, columns), lambda i: (i, 0, 0))
    return pl.pallas_call(
        backward_kernel,
        grid=(sectors,),
        in_specs=[pl.BlockSpec((owners, capacity, 2 * rows), lambda i: (0, 0, 0))]
        + [table_spec] * 4
        + [
            pl.BlockSpec((owners, capacity, waves), lambda i: (0, 0, 0)),
            pl.BlockSpec((rows, rows), lambda i: (0, 0)),
        ],
        out_specs=pl.BlockSpec((1, rows, columns), lambda i: (i, 0, 0)),
        out_shape=jax.ShapeDtypeStruct((sectors, rows, columns), BF16),
        scratch_shapes=[pltpu.VMEM((2, rows, waves), BF16)],
        compiler_params=pltpu.CompilerParams(vmem_limit_bytes=VMEM_LIMIT),
        name="to_sectors",
    )(slot_rows, *tables, one_hot, mirror)


def legendre_kernel(fields, lat_rows, group, order, blocks, received, damping, basis, spectral, returned, held, buffer, sems):
    sources, capacity, _ = received.shape
    degrees, half_lat = basis.shape[1:]
    half_sources = sources // 2
    combos = 2 * fields
    lane_blocks = held.shape[0]
    stride = held.shape[1] // (2 * combos)
    groups = capacity // group
    most = degrees // STEP
    scale = 1.0 / math.sqrt(degrees)

    def copies(index, count):
        ring = lax.rem(index, DEPTH)
        rows = pl.ds(0, count * STEP)
        return [
            pltpu.make_async_copy(
                basis.at[order[index * group + i], rows, :], buffer.at[ring, i, rows, :], sems.at[ring, i]
            )
            for i in range(group)
        ]

    def fetch(index):
        for count in range(1, most + 1):

            @pl.when(blocks[index] == count)
            def _():
                for copy in copies(index, count):
                    copy.start()

    for index in range(min(DEPTH - 1, groups)):
        fetch(index)

    def place_of(source):
        side, near = (0, source) if source < half_sources else (1, sources - 1 - source)
        return side, near * lat_rows

    def pieces(source, part, field):
        side, lane = place_of(source)
        row = (side * combos + field * 2 + part) * stride
        column = (part * fields + field) * lat_rows
        end = lane + lat_rows
        while lane < end:
            width = min(LANES - lane % LANES, end - lane)
            yield row, lane // LANES, lane % LANES, column, width
            lane, column = lane + width, column + width

    def load_slot(slot):
        rows = pl.ds(slot, 2 * combos, stride=stride)
        return jnp.concatenate([held[block, rows, :] for block in range(lane_blocks)], axis=1)

    def store_slot(slot, value):
        rows = pl.ds(slot, 2 * combos, stride=stride)
        for block in range(lane_blocks):
            held[block, rows, :] = value[:, block * LANES : (block + 1) * LANES]

    for source in range(sources):
        for part in range(2):
            for field in range(fields):
                for row, block, lane, column, width in pieces(source, part, field):
                    held[block, row : row + capacity, lane : lane + width] = received[
                        source, :, column : column + width
                    ].astype(F32)

    def one_group(index, count):
        ring = lax.rem(index, DEPTH)
        slots = [order[index * group + i] for i in range(group)]
        if count == 0:
            for slot in slots:
                spectral[slot] = jnp.zeros(spectral.shape[1:], F32)
                store_slot(slot, jnp.zeros((2 * combos, half_lat), F32))
            return
        width = count * STEP
        for copy in copies(index, count):
            copy.wait()
        parity = 1.0 - 2.0 * (lax.broadcasted_iota(jnp.int32, (1, width), 1) % 2).astype(F32)
        left = [load_slot(slot).astype(BF16) for slot in slots]
        sums = [dot(left[i], buffer[ring, i, :width, :], NT) for i in range(group)]
        damped = []
        for i, slot in enumerate(slots):
            swapped = jnp.concatenate([sums[i][combos:], sums[i][:combos]], axis=0)
            damped.append((sums[i] + parity * swapped) * damping[slot, :, :width])
        backs = [dot(damped[i].astype(BF16), buffer[ring, i, :width, :]) * scale for i in range(group)]
        for i, slot in enumerate(slots):
            for field in range(fields):
                spectral[slot, field // 2, field % 2, :, :width] = damped[i][2 * field : 2 * field + 2]
                if width < degrees:
                    spectral[slot, field // 2, field % 2, :, width:] = jnp.zeros((2, degrees - width), F32)
        for i, slot in enumerate(slots):
            store_slot(slot, backs[i])

    def loop_body(index, carry):
        @pl.when(index + DEPTH - 1 < groups)
        def _():
            fetch(index + DEPTH - 1)

        for count in range(most + 1):
            pl.when(blocks[index] == count)(functools.partial(one_group, index, count))
        return carry

    lax.fori_loop(0, groups, loop_body, 0)

    for source in range(sources):
        for part in range(2):
            for field in range(fields):
                for row, block, lane, column, width in pieces(source, part, field):
                    returned[source, :, column : column + width] = held[
                        block, row : row + capacity, lane : lane + width
                    ].astype(BF16)


def legendre(received, basis, damping, order, blocks, level_dev, lat_rows, group):
    sources, capacity, lanes = received.shape
    degrees, half_lat = basis.shape[1:]
    fields = 2 * level_dev
    stride = -(-capacity // 8) * 8
    smem, vmem, hbm = (pl.BlockSpec(memory_space=space) for space in (pltpu.SMEM, pltpu.VMEM, pl.ANY))
    return pl.pallas_call(
        functools.partial(legendre_kernel, fields, lat_rows, group),
        in_specs=[smem, smem, vmem, vmem, hbm],
        out_specs=[vmem, vmem],
        out_shape=[
            jax.ShapeDtypeStruct((capacity, level_dev, 2, 2, degrees), F32),
            jax.ShapeDtypeStruct((sources, capacity, lanes), BF16),
        ],
        scratch_shapes=[
            pltpu.VMEM((half_lat // LANES, 4 * fields * stride, LANES), F32),
            pltpu.VMEM((DEPTH, group, degrees, half_lat), BF16),
            pltpu.SemaphoreType.DMA((DEPTH, group)),
        ],
        compiler_params=pltpu.CompilerParams(vmem_limit_bytes=VMEM_LIMIT),
        name="legendre",
    )(order, blocks, received, damping, basis)


def body(wind_u, wind_v, basis, wave_slots, degree_count, viscosity):
    sectors = lax.axis_size("lon")
    owners = lax.axis_size("lat")
    sector_index = lax.axis_index("lon")
    owner_index = lax.axis_index("lat")
    levels, lat_rows, lon_cols = wind_u.shape
    level_dev = levels // sectors
    assert level_dev == 1
    capacity, degrees, half_lat = basis.shape
    latitudes = 2 * half_lat
    waves = wave_slots.shape[0]
    slot_total = capacity * owners
    rows = level_dev * 2 * lat_rows
    products = jnp.stack([wind_u * wind_v, wind_u * wind_u - wind_v * wind_v], axis=1)
    products = products.astype(BF16).reshape(sectors, rows, lon_cols)
    lines = lax.all_to_all(products, "lon", split_axis=0, concat_axis=0, tiled=True)

    slot_ids = jnp.arange(slot_total, dtype=jnp.int32)
    matches = wave_slots[:, None] == slot_ids[None, :]
    wave_ids = jnp.arange(waves, dtype=jnp.int32)
    wave_of_slot = jnp.sum(jnp.where(matches, wave_ids[:, None] + 1, 0), axis=0) - 1
    count_of_slot = jnp.sum(jnp.where(matches, degree_count[:, None], 0), axis=0)
    one_hot = (wave_of_slot.reshape(owners, capacity, 1) == wave_ids).astype(BF16)
    row_ids = jnp.arange(rows, dtype=jnp.int32)
    mirrored = row_ids // lat_rows * lat_rows + (lat_rows - 1 - row_ids % lat_rows)
    south = owner_index >= owners // 2
    mirror = (row_ids[:, None] == jnp.where(south, mirrored, row_ids)[None, :]).astype(BF16)
    tables = wave_tables(sectors, lon_cols, waves)

    wave_here = lax.dynamic_slice_in_dim(wave_of_slot, owner_index * capacity, capacity)
    count_here = lax.dynamic_slice_in_dim(count_of_slot, owner_index * capacity, capacity)
    rates = lax.dynamic_slice_in_dim(viscosity, sector_index * level_dev, level_dev)
    degree_ids = jnp.arange(degrees, dtype=jnp.int32)
    total_degree = wave_here[:, None] + degree_ids[None, :]
    scaled = (total_degree * (total_degree + 1)).astype(F32) / float(degrees * (degrees + 1))
    damping = 1.0 / (1.0 + rates[0] * (scaled * scaled))
    kept = degree_ids[None, :] < count_here[:, None]
    damping = jnp.where(kept, damping * (1.0 / math.sqrt(latitudes)), 0.0)[:, None, :]
    here_ids = jnp.arange(capacity, dtype=jnp.int32)
    ahead = (count_here[None, :] > count_here[:, None]) | (
        (count_here[None, :] == count_here[:, None]) & (here_ids[None, :] < here_ids[:, None])
    )
    rank = jnp.sum(ahead.astype(jnp.int32), axis=1)
    sorted_here = rank[:, None] == here_ids[None, :]
    order = jnp.sum(jnp.where(sorted_here, here_ids[:, None], 0), axis=0)
    sorted_count = jnp.sum(jnp.where(sorted_here, count_here[:, None], 0), axis=0)
    group = max(size for size in range(1, 6) if capacity % size == 0)
    blocks = (sorted_count[::group] + (STEP - 1)) // STEP

    fourier = to_owners(lines, tables, one_hot, mirror)
    received = lax.all_to_all(fourier, "lat", split_axis=0, concat_axis=0, tiled=True)
    spectral, returned = legendre(received, basis, damping, order, blocks, level_dev, lat_rows, group)
    regrouped = lax.all_to_all(returned, "lat", split_axis=0, concat_axis=0, tiled=True)
    grid_lines = to_sectors(regrouped, tables, one_hot, mirror)
    tendency = lax.all_to_all(grid_lines, "lon", split_axis=0, concat_axis=0, tiled=True)
    return spectral, tendency.astype(F32).reshape(levels, 2, lat_rows, lon_cols)


def solution(mesh):
    return jax.shard_map(
        body,
        mesh=mesh,
        in_specs=(
            P(None, "lat", "lon"),
            P(None, "lat", "lon"),
            P("lat", None, None),
            P(),
            P(),
            P(),
        ),
        out_specs=(P("lat", "lon", None, None, None), P(None, None, "lat", "lon")),
        check_vma=False,
    )
```

profile of v0, /device:TPU:0, one launch (start us, length us, event | category | flops | bytes accessed | tf_op | source)
XLA Modules:
  0.0 220.3 jit_solution(13221376808942157081)
XLA Ops:
  0.6 2.5 %fusion.8 = (bf16[4,1,192,640]{3,2,0,1:T(8,128)(2,1)S(1)}, bf16[4,1,192,640]{3,2,0,1:T(8,128)(2,1)S(1)}) fusion(f32[4,192,640]{2,1,0:T(8,128)} %param.6, f32[4,192,640]{2,1,0:T(8,128)} %param.7), kind=kLoop, calls=%fused_computation.26 | loop fusion | flops 2949120 | bytes 5898240 | tf_op jit(solution)/shard_map/stack | solution.py:283
  3.2 0.2 pad_maximum_fusion
  3.4 1.5 copy.9
  4.8 4.3 %all-to-all-start = ((bf16[4,384,640]{2,1,0:T(8,128)(2,1)}), bf16[4,384,640]{2,1,0:T(8,128)(2,1)S(1)}, u32[]{:S(2)}, u32[]{:S(2)}) async-start(bf16[4,384,640]{2,1,0:T(8,128)(2,1)} %bitcast.8), calls=%async_computation | async-start | bytes 3932160 | tf_op jit(solution)/shard_map/all_to_all | solution.py:285
  9.1 0.0 copy-start.2
  9.1 0.0 copy-start.3
  9.1 7.7 %sine_multiply_fusion = (f32[640,640]{1,0:T(8,128)}, f32[640,640]{1,0:T(8,128)}) fusion(), kind=kLoop, calls=%fused_computation.19 | loop fusion | flops 4505600 | bytes 3276800 | tf_op jit(solution)/shard_map/mul | solution.py:41
  16.8 0.0 copy-done.2
  16.8 0.0 copy-done.3
  16.8 0.7 select_reduce_fusion
  17.5 0.1 sub.44
  17.6 0.2 fusion.26
  17.7 0.8 fusion.10.mirror
  18.6 1.3 fusion.2.one_hot
  19.8 7.7 %fusion.1 = (bf16[4,640,640]{2,1,0:T(8,128)(2,1)}, bf16[4,640,640]{2,1,0:T(8,128)(2,1)}, bf16[4,640,640]{2,1,0:T(8,128)(2,1)}, bf16[4,640,640]{2,1,0:T(8,128)(2,1)}) fusion(f32[640,640]{1,0:T(8,128)} %get-tuple-element.7, f32[4,640]{1,0:T(4,128)S(1)} %get-tuple-element.21, f32[640,640]{1,0:T(8,128)} %get-tuple-element.6, f32[4,640]{1,0:T(4,128)S(1)} %get-tuple-element.20), kind=kLoop, calls=%fused_computation.5 | loop fusion | flops 24576000 | bytes 16404480 | tf_op jit(solution)/shard_map/convert_element_type | solution.py:27
  27.5 5.8 %all-to-all-done.lines = bf16[4,384,640]{2,1,0:T(8,128)(2,1)S(1)} async-done(((bf16[4,384,640]{2,1,0:T(8,128)(2,1)}), bf16[4,384,640]{2,1,0:T(8,128)(2,1)S(1)}, u32[]{:S(2)}, u32[]{:S(2)}) %all-to-all-start) | async-done | bytes 1966112 | tf_op jit(solution)/shard_map/all_to_all | solution.py:285
  33.4 0.0 copy-start
  33.4 1.3 copy-done
  34.7 19.0 %to_owners.1 = bf16[8,100,768]{2,1,0:T(8,128)(2,1)} custom-call(bf16[4,384,640]{2,1,0:T(8,128)(2,1)} %copy-done, bf16[4,640,640]{2,1,0:T(8,128)(2,1)} %get-tuple-element.19.real_hi, bf16[4,640,640]{2,1,0:T(8,128)(2,1)} %get-tuple-element.18.real_lo, bf16[4,640,640]{2,1,0:T(8,128)(2,1)} %get-tuple-element.17.imag_hi, ...), custom_call_target="tpu_custom_call" | custom-call | tf_op jit(solution)/shard_map/to_owners/pallas_call | solution.py:75
  53.7 0.0 copy-start.4
  53.7 6.7 %all-to-all-start.1 = ((bf16[8,100,768]{2,1,0:T(8,128)(2,1)}), bf16[8,100,768]{2,1,0:T(8,128)(2,1)S(1)}, u32[]{:S(2)}, u32[]{:S(2)}) async-start(bf16[8,100,768]{2,1,0:T(8,128)(2,1)} %to_owners.1), calls=%async_computation.1 | async-start | bytes 2555904 | tf_op jit(solution)/shard_map/all_to_all | solution.py:320
  60.4 0.1 dynamic_slice.11
  60.5 0.1 dynamic_slice.9
  60.6 0.2 convert_reduce_fusion
  60.7 0.7 select_reduce_fusion.2
  61.4 0.1 slice.3
  61.5 0.0 copy-done.4
  61.5 0.6 dynamic_slice.10
  62.1 0.5 and_select_fusion.blocks
  62.6 2.5 %compare_select_fusion.damping = f32[100,1,640]{2,1,0:T(1,128)} fusion(s32[100]{0:T(128)S(1)} %dynamic_slice.11, s32[100]{0:T(128)S(1)} %dynamic_slice.9, f32[]{:T(128)} %bitcast.3), kind=kLoop, calls=%fused_computation.25 | loop fusion | flops 768000 | bytes 256804 | tf_op jit(solution)/shard_map/jit(_where)/select_n | solution.py:307
  65.1 25.7 %all-to-all-done.1.received = bf16[8,100,768]{2,1,0:T(8,128)(2,1)S(1)} async-done(((bf16[8,100,768]{2,1,0:T(8,128)(2,1)}), bf16[8,100,768]{2,1,0:T(8,128)(2,1)S(1)}, u32[]{:S(2)}, u32[]{:S(2)}) %all-to-all-start.1) | async-done | bytes 1228832 | tf_op jit(solution)/shard_map/all_to_all | solution.py:320
  90.8 0.0 copy-start.1
  90.8 1.0 copy-done.1
  91.8 25.5 %legendre.1 = (f32[100,1,2,2,640]{4,3,2,1,0:T(2,128)}, bf16[8,100,768]{2,1,0:T(8,128)(2,1)}) custom-call(s32[100]{0:T(128)} %get-tuple-element.13.order, s32[20]{0:T(128)} %and_select_fusion.blocks, bf16[8,100,768]{2,1,0:T(8,128)(2,1)} %copy-done.1, f32[100,1,640]{2,1,0:T(1,128)} %compare_select_fusion.damping, bf16[100,640,768]{2,1,0:T(8,128)(2,1)} %basis.1), custom_call_target="tpu_custom_call" | custom-call | tf_op jit(solution)/shard_map/legendre/pallas_call | solution.py:252
  117.4 56.7 %all_to_all.20.slot_rows = bf16[8,100,768]{2,1,0:T(8,128)(2,1)} all-to-all(bf16[8,100,768]{2,1,0:T(8,128)(2,1)} %get-tuple-element.9), channel_id=1, replica_groups=mesh['lat'=8,'lon'=4] {'lat'}, dimensions={0} | all-to-all | bytes 2457600 | tf_op jit(solution)/shard_map/all_to_all | solution.py:322
  174.1 16.2 %to_sectors.1 = bf16[4,384,640]{2,1,0:T(8,128)(2,1)} custom-call(bf16[8,100,768]{2,1,0:T(8,128)(2,1)} %all_to_all.20.slot_rows, bf16[4,640,640]{2,1,0:T(8,128)(2,1)} %get-tuple-element.19.real_hi, bf16[4,640,640]{2,1,0:T(8,128)(2,1)} %get-tuple-element.18.real_lo, bf16[4,640,640]{2,1,0:T(8,128)(2,1)} %get-tuple-element.17.imag_hi, ...), custom_call_target="tpu_custom_call" | custom-call | tf_op jit(solution)/shard_map/to_sectors/pallas_call | solution.py:119
  190.3 27.8 %all_to_all.21 = bf16[4,384,640]{2,1,0:T(8,128)(2,1)S(1)} all-to-all(bf16[4,384,640]{2,1,0:T(8,128)(2,1)} %to_sectors.1), channel_id=1, replica_groups=mesh['lat'=8,'lon'=4] {'lon'}, dimensions={0} | all-to-all | bytes 3932160 | tf_op jit(solution)/shard_map/all_to_all | solution.py:324
  218.1 2.2 convert.11
  (4 shorter events, 0.0 us)
Async XLA Ops:
  4.8 28.5 %all-to-all-start = ((bf16[4,384,640]{2,1,0:T(8,128)(2,1)}), bf16[4,384,640]{2,1,0:T(8,128)(2,1)S(1)}, u32[]{:S(2)}, u32[]{:S(2)}) async-start(bf16[4,384,640]{2,1,0:T(8,128)(2,1)} %bitcast.8), calls=%async_computation | async-start | bytes 3932160 | tf_op jit(solution)/shard_map/all_to_all | solution.py:285
  9.1 7.7 %copy-start.2 = (s32[640]{0:T(1024)S(1)}, s32[640]{0:T(1024)}, u32[]{:S(2)}) copy-start(s32[640]{0:T(1024)} %param.9) | copy-start | bytes 7684
  9.1 7.7 %copy-start.3 = (s32[640]{0:T(1024)S(1)}, s32[640]{0:T(1024)}, u32[]{:S(2)}) copy-start(s32[640]{0:T(1024)} %param.10) | copy-start | bytes 7684
  33.4 1.3 copy-start
  53.7 7.9 %copy-start.4 = (f32[4]{0:T(128)S(1)}, f32[4]{0:T(128)}, u32[]{:S(2)}) copy-start(f32[4]{0:T(128)} %param.11) | copy-start | bytes 52
  53.7 37.1 %all-to-all-start.1 = ((bf16[8,100,768]{2,1,0:T(8,128)(2,1)}), bf16[8,100,768]{2,1,0:T(8,128)(2,1)S(1)}, u32[]{:S(2)}, u32[]{:S(2)}) async-start(bf16[8,100,768]{2,1,0:T(8,128)(2,1)} %to_owners.1), calls=%async_computation.1 | async-start | bytes 2555904 | tf_op jit(solution)/shard_map/all_to_all | solution.py:320
  90.8 1.0 copy-start.1
where the time goes:
time: 221 us; the launch traced here: 220 us
  blocking collectives  84.5 us (38%)
  Pallas kernels  60.8 us (28%)
  waiting for transfers between devices  31.5 us (14%)
  other arithmetic  27.1 us (12%)
  starting transfers between devices  11 us (5%)
  local copies, waits for them, and re-layouts  4.7 us (2%)
    all_to_all x1, blocking collectives, body(): lax.all_to_all(returned, 'lat', split_axis=0, concat_axis=0, tiled=True)  56.7 us
    all_to_all x1, blocking collectives, body(): lax.all_to_all(grid_lines, 'lon', split_axis=0, concat_axis=0, tiled=True)  27.8 us
    all_to_all x1, waiting for transfers between devices, body(): lax.all_to_all(fourier, 'lat', split_axis=0, concat_axis=0, tiled=True)  25.7 us
    pallas_call x1, Pallas kernels, legendre(): pl.pallas_call(functools.partial(legendre_kernel, fields, lat_rows, group...  25.5 us
    pallas_call x1, Pallas kernels, to_owners(): pl.pallas_call(forward_kernel, grid=(waves // size,), in_specs=[pl.BlockS...  19 us
    pallas_call x1, Pallas kernels, to_sectors(): pl.pallas_call(backward_kernel, grid=(sectors,), in_specs=[pl.BlockSpec((...  16.2 us
    convert_element_type x1, other arithmetic, split_high_low(): return (high.astype(BF16), (value - high).astype(BF16))  7.71 us
    mul x1, other arithmetic, wave_tables(): jnp.sin(inner) * scaling  7.67 us
  transfers between devices with their start and end apart: 2, of which 2 were waited for; matrix products, arithmetic and copies ran while one was open for 10% of the time, Pallas kernels for 0%

commit v1 on v0

--- a/solution.py
+++ b/solution.py
@@ -45,7 +45,8 @@
     return split_high_low(real) + split_high_low(imag)
 
 
-def forward_kernel(lines, real_hi, real_lo, imag_hi, imag_lo, one_hot, mirror, out, by_wave):
+def forward_kernel(lines, real_hi, real_lo, imag_hi, imag_lo, one_hot, mirror, *rest):
+    outs, by_wave = rest[:-1], rest[-1]
     step = pl.program_id(0)
     sectors, rows, _ = lines.shape
     owners = one_hot.shape[0]
@@ -64,10 +65,16 @@
         for part in range(2):
             turned = dot(by_wave[part], mirror[...]).astype(BF16)
             for owner in range(owners):
-                out[owner, :, part * rows : (part + 1) * rows] = dot(one_hot[owner], turned).astype(BF16)
-
-
-def to_owners(lines, tables, one_hot, mirror):
+                first = 0
+                for out in outs:
+                    last = first + out.shape[1]
+                    out[owner, :, part * rows : (part + 1) * rows] = dot(
+                        one_hot[owner, first:last, :], turned
+                    ).astype(BF16)
+                    first = last
+
+
+def to_owners(lines, tables, one_hot, mirror, chunks):
     sectors, rows, columns = lines.shape
     owners, capacity, waves = one_hot.shape
     size = 128
@@ -81,15 +88,16 @@
             pl.BlockSpec((owners, capacity, waves), lambda i: (0, 0, 0)),
             pl.BlockSpec((rows, rows), lambda i: (0, 0)),
         ],
-        out_specs=pl.BlockSpec((owners, capacity, 2 * rows), lambda i: (0, 0, 0)),
-        out_shape=jax.ShapeDtypeStruct((owners, capacity, 2 * rows), BF16),
+        out_specs=[pl.BlockSpec((owners, chunk, 2 * rows), lambda i: (0, 0, 0)) for chunk in chunks],
+        out_shape=[jax.ShapeDtypeStruct((owners, chunk, 2 * rows), BF16) for chunk in chunks],
         scratch_shapes=[pltpu.VMEM((2, waves, rows), BF16)],
         compiler_params=pltpu.CompilerParams(vmem_limit_bytes=VMEM_LIMIT),
         name="to_owners",
     )(lines, *tables, one_hot, mirror)
 
 
-def backward_kernel(slot_rows, real_hi, real_lo, imag_hi, imag_lo, one_hot, mirror, out, by_wave):
+def backward_kernel(count, *refs):
+    pieces, (real_hi, real_lo, imag_hi, imag_lo, one_hot, mirror, out, by_wave) = refs[:count], refs[count:]
     owners, capacity, waves = one_hot.shape
     rows = mirror.shape[0]
 
@@ -100,10 +108,13 @@
         for part in range(2):
             total = None
             for owner in range(owners):
-                piece = slot_rows[owner, :, part * rows : (part + 1) * rows]
-                turned = dot(mirror[...], piece, NT).astype(BF16)
-                term = dot(turned, one_hot[owner])
-                total = term if total is None else total + term
+                first = 0
+                for piece in pieces:
+                    last = first + piece.shape[1]
+                    turned = dot(mirror[...], piece[owner, :, part * rows : (part + 1) * rows], NT).astype(BF16)
+                    term = dot(turned, one_hot[owner, first:last, :])
+                    total = term if total is None else total + term
+                    first = last
             by_wave[part] = (total * weight).astype(BF16)
 
     real, imag = by_wave[0], by_wave[1]
@@ -111,15 +122,15 @@
     out[0] = total.astype(BF16)
 
 
-def to_sectors(slot_rows, tables, one_hot, mirror):
+def to_sectors(pieces, tables, one_hot, mirror):
     owners, capacity, waves = one_hot.shape
     sectors, _, columns = tables[0].shape
     rows = mirror.shape[0]
     table_spec = pl.BlockSpec((1, waves, columns), lambda i: (i, 0, 0))
     return pl.pallas_call(
-        backward_kernel,
+        functools.partial(backward_kernel, len(pieces)),
         grid=(sectors,),
-        in_specs=[pl.BlockSpec((owners, capacity, 2 * rows), lambda i: (0, 0, 0))]
+        in_specs=[pl.BlockSpec(piece.shape, lambda i: (0, 0, 0)) for piece in pieces]
         + [table_spec] * 4
         + [
             pl.BlockSpec((owners, capacity, waves), lambda i: (0, 0, 0)),
@@ -130,10 +141,11 @@
         scratch_shapes=[pltpu.VMEM((2, rows, waves), BF16)],
         compiler_params=pltpu.CompilerParams(vmem_limit_bytes=VMEM_LIMIT),
         name="to_sectors",
-    )(slot_rows, *tables, one_hot, mirror)
-
-
-def legendre_kernel(fields, lat_rows, group, order, blocks, received, damping, basis, spectral, returned, held, buffer, sems):
+    )(*pieces, *tables, one_hot, mirror)
+
+
+def legendre_kernel(fields, lat_rows, group, start, aliased, order, blocks, received, damping, basis, *rest):
+    spectral_out, returned, spectral, held, buffer, sems, out_sem = rest[aliased:]
     sources, capacity, _ = received.shape
     degrees, half_lat = basis.shape[1:]
     half_sources = sources // 2
@@ -149,7 +161,7 @@
         rows = pl.ds(0, count * STEP)
         return [
             pltpu.make_async_copy(
-                basis.at[order[index * group + i], rows, :], buffer.at[ring, i, rows, :], sems.at[ring, i]
+                basis.at[start + order[index * group + i], rows, :], buffer.at[ring, i, rows, :], sems.at[ring, i]
             )
             for i in range(group)
         ]
@@ -233,6 +245,8 @@
         return carry
 
     lax.fori_loop(0, groups, loop_body, 0)
+    spectral_copy = pltpu.make_async_copy(spectral, spectral_out.at[pl.ds(start, capacity)], out_sem)
+    spectral_copy.start()
 
     for source in range(sources):
         for part in range(2):
@@ -241,30 +255,53 @@
                     returned[source, :, column : column + width] = held[
                         block, row : row + capacity, lane : lane + width
                     ].astype(BF16)
-
-
-def legendre(received, basis, damping, order, blocks, level_dev, lat_rows, group):
+    spectral_copy.wait()
+
+
+def legendre(received, basis, damping, order, blocks, level_dev, lat_rows, group, start, spectral=None):
     sources, capacity, lanes = received.shape
-    degrees, half_lat = basis.shape[1:]
+    slots, degrees, half_lat = basis.shape
     fields = 2 * level_dev
     stride = -(-capacity // 8) * 8
     smem, vmem, hbm = (pl.BlockSpec(memory_space=space) for space in (pltpu.SMEM, pltpu.VMEM, pl.ANY))
+    earlier = () if spectral is None else (spectral,)
+    spectral_shape = (level_dev, 2, 2, degrees)
     return pl.pallas_call(
-        functools.partial(legendre_kernel, fields, lat_rows, group),
-        in_specs=[smem, smem, vmem, vmem, hbm],
-        out_specs=[vmem, vmem],
+        functools.partial(legendre_kernel, fields, lat_rows, group, start, len(earlier)),
+        in_specs=[smem, smem, vmem, vmem, hbm] + [hbm] * len(earlier),
+        out_specs=[hbm, vmem],
         out_shape=[
-            jax.ShapeDtypeStruct((capacity, level_dev, 2, 2, degrees), F32),
+            jax.ShapeDtypeStruct((slots,) + spectral_shape, F32),
             jax.ShapeDtypeStruct((sources, capacity, lanes), BF16),
         ],
         scratch_shapes=[
+            pltpu.VMEM((capacity,) + spectral_shape, F32),
             pltpu.VMEM((half_lat // LANES, 4 * fields * stride, LANES), F32),
             pltpu.VMEM((DEPTH, group, degrees, half_lat), BF16),
             pltpu.SemaphoreType.DMA((DEPTH, group)),
+            pltpu.SemaphoreType.DMA,
         ],
+        input_output_aliases={5: 0} if earlier else {},
+        cost_estimate=pl.CostEstimate(
+            flops=4 * capacity * degrees * half_lat * 4 * fields,
+            bytes_accessed=2 * capacity * degrees * half_lat,
+            transcendentals=0,
+        ),
         compiler_params=pltpu.CompilerParams(vmem_limit_bytes=VMEM_LIMIT),
         name="legendre",
-    )(order, blocks, received, damping, basis)
+    )(order, blocks, received, damping, basis, *earlier)
+
+
+def degree_order(counts):
+    size = counts.shape[0]
+    ids = jnp.arange(size, dtype=jnp.int32)
+    ahead = (counts[None, :] > counts[:, None]) | ((counts[None, :] == counts[:, None]) & (ids[None, :] < ids[:, None]))
+    rank = jnp.sum(ahead.astype(jnp.int32), axis=1)
+    placed = rank[:, None] == ids[None, :]
+    order = jnp.sum(jnp.where(placed, ids[:, None], 0), axis=0)
+    sorted_counts = jnp.sum(jnp.where(placed, counts[:, None], 0), axis=0)
+    group = max(g for g in range(1, 6) if size % g == 0)
+    return order, (sorted_counts[::group] + (STEP - 1)) // STEP, group
 
 
 def body(wind_u, wind_v, basis, wave_slots, degree_count, viscosity):
@@ -305,21 +342,20 @@
     damping = 1.0 / (1.0 + rates[0] * (scaled * scaled))
     kept = degree_ids[None, :] < count_here[:, None]
     damping = jnp.where(kept, damping * (1.0 / math.sqrt(latitudes)), 0.0)[:, None, :]
-    here_ids = jnp.arange(capacity, dtype=jnp.int32)
-    ahead = (count_here[None, :] > count_here[:, None]) | (
-        (count_here[None, :] == count_here[:, None]) & (here_ids[None, :] < here_ids[:, None])
-    )
-    rank = jnp.sum(ahead.astype(jnp.int32), axis=1)
-    sorted_here = rank[:, None] == here_ids[None, :]
-    order = jnp.sum(jnp.where(sorted_here, here_ids[:, None], 0), axis=0)
-    sorted_count = jnp.sum(jnp.where(sorted_here, count_here[:, None], 0), axis=0)
-    group = max(size for size in range(1, 6) if capacity % size == 0)
-    blocks = (sorted_count[::group] + (STEP - 1)) // STEP
-
-    fourier = to_owners(lines, tables, one_hot, mirror)
-    received = lax.all_to_all(fourier, "lat", split_axis=0, concat_axis=0, tiled=True)
-    spectral, returned = legendre(received, basis, damping, order, blocks, level_dev, lat_rows, group)
-    regrouped = lax.all_to_all(returned, "lat", split_axis=0, concat_axis=0, tiled=True)
+    head = capacity // 32 * 16 or capacity
+    chunks = (head, capacity - head) if head < capacity else (capacity,)
+
+    fourier = to_owners(lines, tables, one_hot, mirror, chunks)
+    spectral, start, regrouped = None, 0, []
+    for piece in fourier:
+        end = start + piece.shape[1]
+        received = lax.all_to_all(piece, "lat", split_axis=0, concat_axis=0, tiled=True)
+        order, blocks, group = degree_order(count_here[start:end])
+        spectral, returned = legendre(
+            received, basis, damping[start:end], order, blocks, level_dev, lat_rows, group, start, spectral
+        )
+        regrouped.append(lax.all_to_all(returned, "lat", split_axis=0, concat_axis=0, tiled=True))
+        start = end
     grid_lines = to_sectors(regrouped, tables, one_hot, mirror)
     tendency = lax.all_to_all(grid_lines, "lon", split_axis=0, concat_axis=0, tiled=True)
     return spectral, tendency.astype(F32).reshape(levels, 2, lat_rows, lon_cols)

time: 221 us -> 217 us (0.982); the launches traced: 220 us -> 219 us
  waiting for transfers between devices: 31.5 us -> 5.88 us
  starting transfers between devices: 11 us -> 24 us
  Pallas kernels: 60.8 us -> 70.3 us
    all_to_all x1 -> x2, waiting for transfers between devices: 25.7 us -> 0.01 us  [the longest x1 0.01 us: body(): lax.all_to_all(piece, 'lat', split_axis=0, concat_axis=0, tiled=True)]
    all_to_all x0 -> x1, blocking collectives: none -> 23.1 us  [body(): lax.all_to_all(piece, 'lat', split_axis=0, concat_axis=0, tiled=True)]
    all_to_all x1, blocking collectives: 56.7 us -> 34.9 us  [body(): lax.all_to_all(returned, 'lat', split_axis=0, concat_axis=0, tiled=True)]
    all_to_all x1 -> x2, starting transfers between devices: 6.72 us -> 19.7 us  [the longest x1 16 us: body(): lax.all_to_all(returned, 'lat', split_axis=0, concat_axis=0, tiled=True)]
    pallas_call x1, Pallas kernels: 16.2 us -> 20.9 us  [to_sectors(): pl.pallas_call(functools.partial(backward_kernel, len(pieces)), grid=(sec...]
    pallas_call x1 -> x2, Pallas kernels: 25.5 us -> 29.4 us  [legendre(): pl.pallas_call(functools.partial(legendre_kernel, fields, lat_rows, group...]
  transfers between devices with their start and end apart: 2 -> 3, of which waited for: 2 -> 1; matrix products, arithmetic and copies ran while one was open for 10% -> 11% of each run, Pallas kernels for 0% -> 13%
where the time goes in v1:
time: 217 us; the launch traced here: 219 us
  blocking collectives  85.8 us (40%)
  Pallas kernels  70.3 us (32%)
  other arithmetic  26.7 us (12%)
  starting transfers between devices  24 us (11%)
  waiting for transfers between devices  5.88 us (3%)
  local copies, waits for them, and re-layouts  5.36 us (2%)
    all_to_all x1, blocking collectives, body(): lax.all_to_all(returned, 'lat', split_axis=0, concat_axis=0, tiled=True)  34.9 us
    pallas_call x2, Pallas kernels, legendre(): pl.pallas_call(functools.partial(legendre_kernel, fields, lat_rows, group...  29.4 us
    all_to_all x1, blocking collectives, body(): lax.all_to_all(grid_lines, 'lon', split_axis=0, concat_axis=0, tiled=True)  27.8 us
    all_to_all x1, blocking collectives, body(): lax.all_to_all(piece, 'lat', split_axis=0, concat_axis=0, tiled=True)  23.1 us
    pallas_call x1, Pallas kernels, to_sectors(): pl.pallas_call(functools.partial(backward_kernel, len(pieces)), grid=(sec...  20.9 us
    pallas_call x1, Pallas kernels, to_owners(): pl.pallas_call(forward_kernel, grid=(waves // size,), in_specs=[pl.BlockS...  20 us
    all_to_all x1, starting transfers between devices, body(): lax.all_to_all(returned, 'lat', split_axis=0, concat_axis=0, tiled=True)  16 us
    convert_element_type x1, other arithmetic, split_high_low(): return (high.astype(BF16), (value - high).astype(BF16))  7.7 us
  transfers between devices with their start and end apart: 3, of which 1 were waited for; matrix products, arithmetic and copies ran while one was open for 11% of the time, Pallas kernels for 13%

profile of v1, /device:TPU:0, one launch (start us, length us, event | category | flops | bytes accessed | tf_op | source)
XLA Modules:
  0.0 218.8 jit_solution(1032220906095400445)
XLA Ops:
  0.6 2.5 %fusion.8 = (bf16[4,1,192,640]{3,2,0,1:T(8,128)(2,1)S(1)}, bf16[4,1,192,640]{3,2,0,1:T(8,128)(2,1)S(1)}) fusion(f32[4,192,640]{2,1,0:T(8,128)} %param.6, f32[4,192,640]{2,1,0:T(8,128)} %param.7), kind=kLoop, calls=%fused_computation.25 | loop fusion | flops 2949120 | bytes 5898240 | tf_op jit(solution)/shard_map/stack | solution.py:320
  3.2 0.2 pad_maximum_fusion
  3.4 1.5 copy.11
  4.8 4.3 %all-to-all-start = ((bf16[4,384,640]{2,1,0:T(8,128)(2,1)}), bf16[4,384,640]{2,1,0:T(8,128)(2,1)S(1)}, u32[]{:S(2)}, u32[]{:S(2)}) async-start(bf16[4,384,640]{2,1,0:T(8,128)(2,1)} %bitcast.11), calls=%async_computation | async-start | bytes 3932160 | tf_op jit(solution)/shard_map/all_to_all | solution.py:322
  9.1 0.0 copy-start.3
  9.1 0.0 copy-start.4
  9.1 7.7 %sine_multiply_fusion = (f32[640,640]{1,0:T(8,128)}, f32[640,640]{1,0:T(8,128)}) fusion(), kind=kLoop, calls=%fused_computation.19 | loop fusion | flops 4505600 | bytes 3276800 | tf_op jit(solution)/shard_map/mul | solution.py:41
  16.8 0.0 copy-done.3
  16.8 0.0 copy-done.4
  16.8 0.7 select_reduce_fusion
  17.5 0.1 sub.48
  17.6 0.2 fusion.29
  17.8 0.8 fusion.10.mirror.refs_7_
  18.5 1.2 fusion.2.one_hot.refs_6_
  19.8 7.7 %fusion.1 = (bf16[4,640,640]{2,1,0:T(8,128)(2,1)}, bf16[4,640,640]{2,1,0:T(8,128)(2,1)}, bf16[4,640,640]{2,1,0:T(8,128)(2,1)}, bf16[4,640,640]{2,1,0:T(8,128)(2,1)}) fusion(f32[640,640]{1,0:T(8,128)} %get-tuple-element.11, f32[4,640]{1,0:T(4,128)S(1)} %get-tuple-element.31, f32[640,640]{1,0:T(8,128)} %get-tuple-element.10, f32[4,640]{1,0:T(4,128)S(1)} %get-tuple-element.30), kind=kLoop, calls=%fused_computation.5 | loop fusion | flops 24576000 | bytes 16404480 | tf_op jit(solution)/shard_map/convert_element_type | solution.py:27
  27.5 5.9 %all-to-all-done.lines = bf16[4,384,640]{2,1,0:T(8,128)(2,1)S(1)} async-done(((bf16[4,384,640]{2,1,0:T(8,128)(2,1)}), bf16[4,384,640]{2,1,0:T(8,128)(2,1)S(1)}, u32[]{:S(2)}, u32[]{:S(2)}) %all-to-all-start) | async-done | bytes 1966112 | tf_op jit(solution)/shard_map/all_to_all | solution.py:322
  33.4 0.0 copy-start
  33.4 1.3 copy-done
  34.6 20.0 %to_owners.1 = (bf16[8,48,768]{2,1,0:T(8,128)(2,1)}, bf16[8,52,768]{2,1,0:T(8,128)(2,1)}) custom-call(bf16[4,384,640]{2,1,0:T(8,128)(2,1)} %copy-done, bf16[4,640,640]{2,1,0:T(8,128)(2,1)} %get-tuple-element.29.real_hi.refs_2_, bf16[4,640,640]{2,1,0:T(8,128)(2,1)} %get-tuple-element.28.real_lo.refs_3_, ...), custom_call_target="tpu_custom_call" | custom-call | tf_op jit(solution)/shard_map/to_owners/pallas_call | solution.py:82
  54.7 0.0 copy-start.5
  54.7 23.1 %all_to_all.30.received = bf16[8,48,768]{2,1,0:T(8,128)(2,1)} all-to-all(bf16[8,48,768]{2,1,0:T(8,128)(2,1)} %get-tuple-element.13), channel_id=1, replica_groups=mesh['lat'=8,'lon'=4] {'lat'}, dimensions={0} | all-to-all | bytes 1179648 | tf_op jit(solution)/shard_map/all_to_all | solution.py:352
  77.8 3.7 %all-to-all-start.1 = ((bf16[8,52,768]{2,1,0:T(8,128)(2,1)}), bf16[8,52,768]{2,1,0:T(8,128)(2,1)S(1)}, u32[]{:S(2)}, u32[]{:S(2)}) async-start(bf16[8,52,768]{2,1,0:T(8,128)(2,1)} %get-tuple-element.12), calls=%async_computation.1 | async-start | bytes 1376256 | tf_op jit(solution)/shard_map/all_to_all | solution.py:352
  81.5 0.1 dynamic_slice.11
  81.6 0.1 dynamic_slice.9
  81.7 0.2 convert_reduce_fusion.1
  81.8 0.6 select_reduce_fusion.4
  82.5 0.1 slice.29
  82.6 0.0 copy-done.5
  82.6 0.6 dynamic_slice.10
  83.2 0.8 fusion.18
  84.0 0.8 copy.12.damping
  84.8 0.5 and_select_fusion.blocks
  85.3 15.3 %legendre.2 = (f32[100,1,2,2,640]{4,3,2,1,0:T(2,128)}, bf16[8,48,768]{2,1,0:T(8,128)(2,1)}) custom-call(s32[48]{0:T(128)} %get-tuple-element.21.order, s32[12]{0:T(128)} %and_select_fusion.blocks, bf16[8,48,768]{2,1,0:T(8,128)(2,1)} %all_to_all.30.received, f32[48,1,640]{2,1,0:T(1,128)} %copy.12.damping, bf16[100,640,768]{2,1,0:T(8,128)(2,1)} %basis.3), custom_call_target="tpu_custom_call" | custom-call | flops 754974720 | bytes 47185920 | tf_op jit(solution)/shard_map/legendre/pallas_call | solution.py:269
  100.6 0.0 all-to-all-done.1.received
  100.6 0.0 copy-start.1
  100.6 16.0 %all-to-all-start.3 = ((bf16[8,48,768]{2,1,0:T(8,128)(2,1)}), bf16[8,48,768]{2,1,0:T(8,128)(2,1)S(1)}, u32[]{:S(2)}, u32[]{:S(2)}) async-start(bf16[8,48,768]{2,1,0:T(8,128)(2,1)} %get-tuple-element.16), calls=%async_computation.3 | async-start | bytes 1179648 | tf_op jit(solution)/shard_map/all_to_all | solution.py:357
  116.6 0.1 slice.24
  116.7 0.2 convert_reduce_fusion
  116.8 0.6 select_reduce_fusion.2
  117.5 0.1 slice.25
  117.6 0.8 slice.27.damping
  118.3 0.5 and_select_fusion.1.blocks
  118.9 0.0 copy-done.1
  118.9 14.1 %legendre.3 = (f32[100,1,2,2,640]{4,3,2,1,0:T(2,128)}, bf16[8,52,768]{2,1,0:T(8,128)(2,1)}) custom-call(s32[52]{0:T(128)} %get-tuple-element.23.order, s32[13]{0:T(128)} %and_select_fusion.1.blocks, bf16[8,52,768]{2,1,0:T(8,128)(2,1)} %copy-done.1, f32[52,1,640]{2,1,0:T(1,128)} %slice.27.damping, ...), custom_call_target="tpu_custom_call", output_to_operand_aliasing={{0}: (5, {})} | custom-call | flops 817889280 | bytes 51118080 | tf_op jit(solution)/shard_map/legendre/pallas_call | solution.py:269
  133.0 0.0 all-to-all-done.3.refs_0_
  133.0 0.0 copy-start.2
  133.0 34.9 %all_to_all.31.refs_1_ = bf16[8,52,768]{2,1,0:T(8,128)(2,1)} all-to-all(bf16[8,52,768]{2,1,0:T(8,128)(2,1)} %get-tuple-element.17), channel_id=1, replica_groups=mesh['lat'=8,'lon'=4] {'lat'}, dimensions={0} | all-to-all | bytes 1277952 | tf_op jit(solution)/shard_map/all_to_all | solution.py:357
  167.9 0.0 copy-done.2
  167.9 20.9 %to_sectors.1 = bf16[4,384,640]{2,1,0:T(8,128)(2,1)} custom-call(bf16[8,48,768]{2,1,0:T(8,128)(2,1)} %copy-done.2, bf16[8,52,768]{2,1,0:T(8,128)(2,1)} %all_to_all.31.refs_1_, bf16[4,640,640]{2,1,0:T(8,128)(2,1)} %get-tuple-element.29.real_hi.refs_2_, bf16[4,640,640]{2,1,0:T(8,128)(2,1)} %get-tuple-element.28.real_lo.refs_3_, ...), custom_call_target="tpu_custom_call" | custom-call | tf_op jit(solution)/shard_map/to_sectors/pallas_call | solution.py:130
  188.8 27.8 %all_to_all.32 = bf16[4,384,640]{2,1,0:T(8,128)(2,1)S(1)} all-to-all(bf16[4,384,640]{2,1,0:T(8,128)(2,1)} %to_sectors.1), channel_id=1, replica_groups=mesh['lat'=8,'lon'=4] {'lon'}, dimensions={0} | all-to-all | bytes 3932160 | tf_op jit(solution)/shard_map/all_to_all | solution.py:360
  216.6 2.2 convert.11
  (6 shorter events, 0.0 us)
Async XLA Ops:
  4.8 28.5 %all-to-all-start = ((bf16[4,384,640]{2,1,0:T(8,128)(2,1)}), bf16[4,384,640]{2,1,0:T(8,128)(2,1)S(1)}, u32[]{:S(2)}, u32[]{:S(2)}) async-start(bf16[4,384,640]{2,1,0:T(8,128)(2,1)} %bitcast.11), calls=%async_computation | async-start | bytes 3932160 | tf_op jit(solution)/shard_map/all_to_all | solution.py:322
  9.1 7.7 %copy-start.3 = (s32[640]{0:T(1024)S(1)}, s32[640]{0:T(1024)}, u32[]{:S(2)}) copy-start(s32[640]{0:T(1024)} %param.9) | copy-start | bytes 7684
  9.1 7.7 %copy-start.4 = (s32[640]{0:T(1024)S(1)}, s32[640]{0:T(1024)}, u32[]{:S(2)}) copy-start(s32[640]{0:T(1024)} %param.10) | copy-start | bytes 7684
  33.4 1.3 copy-start
  54.7 27.9 %copy-start.5 = (f32[4]{0:T(128)S(1)}, f32[4]{0:T(128)}, u32[]{:S(2)}) copy-start(f32[4]{0:T(128)} %param.11) | copy-start | bytes 52
  77.8 22.8 %all-to-all-start.1 = ((bf16[8,52,768]{2,1,0:T(8,128)(2,1)}), bf16[8,52,768]{2,1,0:T(8,128)(2,1)S(1)}, u32[]{:S(2)}, u32[]{:S(2)}) async-start(bf16[8,52,768]{2,1,0:T(8,128)(2,1)} %get-tuple-element.12), calls=%async_computation.1 | async-start | bytes 1376256 | tf_op jit(solution)/shard_map/all_to_all | solution.py:352
  100.6 18.3 %copy-start.1 = (bf16[8,52,768]{2,1,0:T(8,128)(2,1)}, bf16[8,52,768]{2,1,0:T(8,128)(2,1)S(1)}, u32[]{:S(2)}) copy-start(bf16[8,52,768]{2,1,0:T(8,128)(2,1)S(1)} %all-to-all-done.1.received) | copy-start | bytes 1916932
  100.6 32.4 %all-to-all-start.3 = ((bf16[8,48,768]{2,1,0:T(8,128)(2,1)}), bf16[8,48,768]{2,1,0:T(8,128)(2,1)S(1)}, u32[]{:S(2)}, u32[]{:S(2)}) async-start(bf16[8,48,768]{2,1,0:T(8,128)(2,1)} %get-tuple-element.16), calls=%async_computation.3 | async-start | bytes 1179648 | tf_op jit(solution)/shard_map/all_to_all | solution.py:357
  133.0 34.9 %copy-start.2 = (bf16[8,48,768]{2,1,0:T(8,128)(2,1)}, bf16[8,48,768]{2,1,0:T(8,128)(2,1)S(1)}, u32[]{:S(2)}) copy-start(bf16[8,48,768]{2,1,0:T(8,128)(2,1)S(1)} %all-to-all-done.3.refs_0_) | copy-start | bytes 1769476

commit v2 on v0

v2 whole, which is shorter than its diff:
```python
import functools
import math

import jax
import jax.numpy as jnp
import numpy as np
from jax import lax
from jax.experimental import pallas as pl
from jax.experimental.pallas import tpu as pltpu
from jax.sharding import PartitionSpec as P

BF16 = jnp.bfloat16
F32 = jnp.float32
VMEM_LIMIT = 60 * 1024 * 1024
STEP = 128
LANES = 128
DEPTH = 3
NT = (((1,), (1,)), ((), ()))
NN = (((1,), (0,)), ((), ()))


def dot(a, b, dims=NN):
    return lax.dot_general(a, b, dims, preferred_element_type=F32)


def split_high_low(value):
    high = lax.reduce_precision(value, 8, 7)
    return high.astype(BF16), (value - high).astype(BF16)


def wave_tables(sectors, columns, waves):
    length = sectors * columns
    places = jnp.arange(columns, dtype=jnp.int32)
    wave_ids = jnp.arange(waves, dtype=jnp.int32)
    angles = (places[:, None] * wave_ids[None, :] % length).astype(F32) * (2.0 * math.pi / length)
    scaling = 1.0 / math.sqrt(length)
    cos_hi, cos_lo = split_high_low(jnp.cos(angles) * scaling)
    sin_hi, sin_lo = split_high_low(jnp.sin(angles) * scaling)
    size = min(LANES, waves)

    def side_by_side(a, b):
        shape = (columns, waves // size, size)
        return jnp.concatenate([a.reshape(shape), b.reshape(shape)], axis=2).reshape(columns, 2 * waves)

    forward = jnp.concatenate([side_by_side(cos_hi, sin_hi), side_by_side(cos_lo, sin_lo)], axis=0)
    quarters = (cos_hi, sin_hi, cos_lo, sin_lo)
    if columns != waves:
        quarters = tuple(quarter.T for quarter in quarters)
    return forward, jnp.concatenate(quarters, axis=0)


def sector_turns(sectors, waves):
    turns = 2.0 * np.pi * (np.arange(sectors)[:, None] * np.arange(waves)[None, :] % sectors) / sectors
    return tuple(np.round(f(turns), 12).astype(np.float32)[:, None, :] for f in (np.cos, np.sin))


def forward_kernel(lines, table, turn_cos, turn_sin, one_hot, mirror, out, by_wave, by_slot):
    step = pl.program_id(0)
    sectors, rows, columns = lines.shape
    size = table.shape[1] // 2
    devices, wire_rows, lanes = out.shape
    padded = one_hot.shape[0] // devices
    blocks = 2 * rows // lanes
    share = wire_rows // blocks
    both = jnp.concatenate([lines[...].reshape(sectors * rows, columns)] * 2, axis=1)
    sums = dot(both, table[...])
    real = imag = None
    for sector in range(sectors):
        own = sums[sector * rows : (sector + 1) * rows]
        own_cos, own_sin = own[:, :size], own[:, size:]
        cos, sin = turn_cos[sector], turn_sin[sector]
        own_real, own_imag = own_cos * cos - own_sin * sin, own_cos * sin + own_sin * cos
        real, imag = (own_real, own_imag) if real is None else (real + own_real, imag + own_imag)
    place = pl.ds(pl.multiple_of(step * size, size), size)
    by_wave[0, :, place] = real.astype(BF16)
    by_wave[1, :, place] = (-imag).astype(BF16)

    @pl.when(step == pl.num_programs(0) - 1)
    def _():
        for part in range(2):
            turned = dot(mirror[...], by_wave[part]).astype(BF16)
            by_slot[:, part * rows : (part + 1) * rows] = dot(one_hot[...], turned, NT)
        for device in range(devices):
            own = by_slot[device * padded : (device + 1) * padded, :]
            out[device] = jnp.concatenate(
                [own[:share, block * lanes : (block + 1) * lanes] for block in range(blocks)], axis=0
            ).astype(BF16)


def to_owners(lines, table, turns, one_hot, mirror, share):
    sectors, rows, columns = lines.shape
    slots, waves = one_hot.shape
    devices = slots // round_up(share, 8)
    size = min(LANES, waves)
    lanes = wire_lanes(rows)
    out = (devices, share * (2 * rows // lanes), lanes)
    turn_spec = pl.BlockSpec((sectors, 1, size), lambda i: (0, 0, i))
    return pl.pallas_call(
        forward_kernel,
        grid=(waves // size,),
        in_specs=[
            pl.BlockSpec((sectors, rows, columns), lambda i: (0, 0, 0)),
            pl.BlockSpec((2 * columns, 2 * size), lambda i: (0, i)),
            turn_spec,
            turn_spec,
            pl.BlockSpec((slots, waves), lambda i: (0, 0)),
            pl.BlockSpec((rows, rows), lambda i: (0, 0)),
        ],
        out_specs=pl.BlockSpec(out, lambda i: (0, 0, 0)),
        out_shape=jax.ShapeDtypeStruct(out, BF16),
        scratch_shapes=[pltpu.VMEM((2, rows, waves), BF16), pltpu.VMEM((slots, 2 * rows), F32)],
        cost_estimate=pl.CostEstimate(flops=8 * sectors * rows * columns * waves, bytes_accessed=10**7, transcendentals=0),
        compiler_params=pltpu.CompilerParams(vmem_limit_bytes=VMEM_LIMIT),
        name="to_owners",
    )(lines, table, *turns, one_hot, mirror)


def backward_kernel(exact, wire, table, turn_cos, turn_sin, one_hot, mirror, out, by_slot, by_wave):
    devices, wire_rows, lanes = wire.shape
    sectors, rows, columns = out.shape
    waves = table.shape[0] // 4
    padded = by_slot.shape[0] // devices
    blocks = 2 * rows // lanes
    share = wire_rows // blocks

    @pl.when(pl.program_id(0) == 0)
    def _():
        for device in range(devices):
            own = wire[device].astype(F32)
            for block in range(blocks):
                piece = own[block * share : (block + 1) * share]
                if padded > share:
                    piece = jnp.concatenate([piece, jnp.zeros((padded - share, lanes), F32)], axis=0)
                by_slot[device * padded : (device + 1) * padded, block * lanes : (block + 1) * lanes] = piece.astype(BF16)
        wave_ids = lax.broadcasted_iota(jnp.int32, (1, waves), 1)
        weight = jnp.where(wave_ids == 0, 1.0, 2.0).astype(F32)
        for part in range(2):
            ordered = dot(one_hot[...], by_slot[:, part * rows : (part + 1) * rows]).astype(BF16)
            by_wave[part] = dot(mirror[...], ordered, NT) * weight

    left = []
    for sector in range(sectors):
        cos, sin = turn_cos[sector], turn_sin[sector]
        real = by_wave[0] * cos - by_wave[1] * sin
        minus = -(by_wave[0] * sin) - by_wave[1] * cos
        left.append(jnp.concatenate([real, minus], axis=1))
    left = jnp.concatenate(left, axis=0)
    high = left.astype(BF16)
    total = dot(jnp.concatenate([high, high], axis=1), table[...])
    if not exact:
        low = (left - high.astype(F32)).astype(BF16)
        total += dot(low, table[: 2 * waves])
    out[...] = total.reshape(sectors, rows, columns).astype(BF16)


def to_sectors(wire, table, turns, one_hot, mirror, share):
    devices, wire_rows, lanes = wire.shape
    rows = mirror.shape[0]
    waves, slots = one_hot.shape
    columns = table.shape[1]
    sectors = turns[0].shape[0]
    together = 2 if sectors % 2 == 0 else 1
    turn_spec = pl.BlockSpec((together, 1, waves), lambda i: (i, 0, 0))
    return pl.pallas_call(
        functools.partial(backward_kernel, sectors in (1, 2, 4)),
        grid=(sectors // together,),
        in_specs=[
            pl.BlockSpec(wire.shape, lambda i: (0, 0, 0)),
            pl.BlockSpec(table.shape, lambda i: (0, 0)),
            turn_spec,
            turn_spec,
            pl.BlockSpec((waves, slots), lambda i: (0, 0)),
            pl.BlockSpec((rows, rows), lambda i: (0, 0)),
        ],
        out_specs=pl.BlockSpec((together, rows, columns), lambda i: (i, 0, 0)),
        out_shape=jax.ShapeDtypeStruct((sectors, rows, columns), BF16),
        scratch_shapes=[pltpu.VMEM((slots, 2 * rows), BF16), pltpu.VMEM((2, rows, waves), F32)],
        cost_estimate=pl.CostEstimate(flops=8 * sectors * rows * columns * waves, bytes_accessed=10**7, transcendentals=0),
        compiler_params=pltpu.CompilerParams(vmem_limit_bytes=VMEM_LIMIT),
        name="to_sectors",
    )(wire, table, *turns, one_hot, mirror)


def round_up(value, unit):
    return -(-value // unit) * unit


def wire_lanes(rows):
    return LANES if 2 * rows % LANES == 0 else 2 * rows


def legendre_kernel(sides, lat_rows, group, first, order, blocks, received, damping, basis, spectral, returned, held, buffer, sems):
    devices, wire_rows, lanes = received.shape
    sectors, share = spectral.shape[:2]
    slots, degrees, half_lat = basis.shape
    sources = devices // sectors
    fields = sides // 2
    combos = sectors * sides
    lane_blocks = held.shape[0]
    stride = held.shape[1] // (2 * combos)
    wire_blocks = wire_rows // share
    groups = share // group
    most = degrees // STEP
    scale = 1.0 / math.sqrt(degrees)

    def copies(index, count):
        ring = lax.rem(index, DEPTH)
        rows = pl.ds(0, count * STEP)
        return [
            pltpu.make_async_copy(
                basis.at[jnp.minimum(first[0] + order[index * group + i], slots - 1), rows, :],
                buffer.at[ring, i, rows, :],
                sems.at[ring, i],
            )
            for i in range(group)
        ]

    def fetch(index):
        for count in range(1, most + 1):

            @pl.when(blocks[index] == count)
            def _():
                for copy in copies(index, count):
                    copy.start()

    for index in range(min(DEPTH - 1, groups)):
        fetch(index)

    def wire_pieces(device, wire_block):
        source, sector = divmod(device, sectors)
        side, near = (0, source) if source < sources // 2 else (1, sources - 1 - source)
        column, end = wire_block * lanes, (wire_block + 1) * lanes
        while column < end:
            part_field, lat = divmod(column, lat_rows)
            part, field = divmod(part_field, fields)
            row = (side * combos + sector * sides + field * 2 + part) * stride
            place = near * lat_rows + lat
            width = min(end - column, lat_rows - lat, LANES - place % LANES)
            yield column - wire_block * lanes, width, row, place // LANES, place % LANES
            column += width

    for device in range(devices):
        own = received[device].astype(F32)
        for wire_block in range(wire_blocks):
            piece = own[wire_block * share : (wire_block + 1) * share]
            for at, width, row, block, lane in wire_pieces(device, wire_block):
                held[block, row : row + share, lane : lane + width] = piece[:, at : at + width]

    def load_slot(slot):
        rows = pl.ds(slot, 2 * combos, stride=stride)
        return jnp.concatenate([held[block, rows, :] for block in range(lane_blocks)], axis=1)

    def store_slot(slot, value):
        rows = pl.ds(slot, 2 * combos, stride=stride)
        for block in range(lane_blocks):
            held[block, rows, :] = value[:, block * LANES : (block + 1) * LANES]

    def one_group(index, count):
        ring = lax.rem(index, DEPTH)
        here = [order[index * group + i] for i in range(group)]
        if count == 0:
            for slot in here:
                for sector in range(sectors):
                    spectral[sector, slot] = jnp.zeros(spectral.shape[2:], F32)
                store_slot(slot, jnp.zeros((2 * combos, half_lat), F32))
            return
        width = count * STEP
        for copy in copies(index, count):
            copy.wait()
        parity = 1.0 - 2.0 * (lax.broadcasted_iota(jnp.int32, (1, width), 1) % 2).astype(F32)
        left = [load_slot(slot).astype(BF16) for slot in here]
        sums = [dot(left[i], buffer[ring, i, :width, :], NT) for i in range(group)]
        damped = [
            (sums[i][:combos] + parity * sums[i][combos:]) * damping[slot, :, :width] for i, slot in enumerate(here)
        ]
        turned = [jnp.concatenate([value, parity * value], axis=0).astype(BF16) for value in damped]
        backs = [dot(turned[i], buffer[ring, i, :width, :]) * scale for i in range(group)]
        for i, slot in enumerate(here):
            for sector in range(sectors):
                spectral[sector, slot, :, :width] = damped[i][sector * sides : (sector + 1) * sides]
                if width < degrees:
                    spectral[sector, slot, :, width:] = jnp.zeros((sides, degrees - width), F32)
        for i, slot in enumerate(here):
            store_slot(slot, backs[i])

    def loop_body(index, carry):
        @pl.when(index + DEPTH - 1 < groups)
        def _():
            fetch(index + DEPTH - 1)

        for count in range(most + 1):
            pl.when(blocks[index] == count)(functools.partial(one_group, index, count))
        return carry

    lax.fori_loop(0, groups, loop_body, 0)

    for device in range(devices):
        pieces = []
        for wire_block in range(wire_blocks):
            parts = [
                held[block, row : row + share, lane : lane + width]
                for _, width, row, block, lane in wire_pieces(device, wire_block)
            ]
            pieces.append(jnp.concatenate(parts, axis=1) if len(parts) > 1 else parts[0])
        returned[device] = jnp.concatenate(pieces, axis=0).astype(BF16)


def legendre(received, basis, damping, first, order, blocks, sectors, sides, lat_rows, group):
    share = order.shape[0]
    degrees, half_lat = basis.shape[1:]
    combos = sectors * sides
    smem, vmem, hbm = (pl.BlockSpec(memory_space=space) for space in (pltpu.SMEM, pltpu.VMEM, pl.ANY))
    return pl.pallas_call(
        functools.partial(legendre_kernel, sides, lat_rows, group),
        in_specs=[smem, smem, smem, vmem, vmem, hbm],
        out_specs=[vmem, vmem],
        out_shape=[
            jax.ShapeDtypeStruct((sectors, share, sides, degrees), F32),
            jax.ShapeDtypeStruct(received.shape, BF16),
        ],
        scratch_shapes=[
            pltpu.VMEM((half_lat // LANES, 2 * combos * round_up(share, 8), LANES), F32),
            pltpu.VMEM((DEPTH, group, degrees, half_lat), BF16),
            pltpu.SemaphoreType.DMA((DEPTH, group)),
        ],
        cost_estimate=pl.CostEstimate(
            flops=4 * share * degrees * half_lat * 2 * combos,
            bytes_accessed=2 * share * degrees * half_lat,
            transcendentals=0,
        ),
        compiler_params=pltpu.CompilerParams(vmem_limit_bytes=VMEM_LIMIT),
        name="legendre",
    )(first, order, blocks, received, damping, basis)


def degree_order(counts):
    size = counts.shape[0]
    ids = jnp.arange(size, dtype=jnp.int32)
    ahead = (counts[None, :] > counts[:, None]) | ((counts[None, :] == counts[:, None]) & (ids[None, :] < ids[:, None]))
    rank = jnp.sum(ahead.astype(jnp.int32), axis=1)
    placed = rank[:, None] == ids[None, :]
    order = jnp.sum(jnp.where(placed, ids[:, None], 0), axis=0)
    sorted_counts = jnp.sum(jnp.where(placed, counts[:, None], 0), axis=0)
    group = max(g for g in range(1, 6) if size % g == 0)
    return order, (sorted_counts[::group] + (STEP - 1)) // STEP, group


def body(wind_u, wind_v, basis, wave_slots, degree_count, viscosity):
    sectors = lax.axis_size("lon")
    owners = lax.axis_size("lat")
    sector_index = lax.axis_index("lon")
    owner_index = lax.axis_index("lat")
    levels, lat_rows, lon_cols = wind_u.shape
    capacity, degrees, half_lat = basis.shape
    waves = wave_slots.shape[0]
    slot_total = capacity * owners
    level_dev = levels // sectors
    fields = 2 * level_dev
    rows = fields * lat_rows
    share = -(-capacity // sectors)
    padded = round_up(share, 8)
    products = jnp.stack([wind_u * wind_v, wind_u * wind_u - wind_v * wind_v], axis=1)
    products = products.astype(BF16).reshape(sectors, rows, lon_cols)
    lines = lax.all_to_all(products, "lon", split_axis=0, concat_axis=0, tiled=True)

    slot_ids = jnp.arange(slot_total, dtype=jnp.int32)
    matches = wave_slots[:, None] == slot_ids[None, :]
    wave_ids = jnp.arange(waves, dtype=jnp.int32)
    wave_of_slot = jnp.sum(jnp.where(matches, wave_ids[:, None] + 1, 0), axis=0) - 1
    count_of_slot = jnp.sum(jnp.where(matches, degree_count[:, None], 0), axis=0)
    places = jnp.arange(owners * sectors * padded, dtype=jnp.int32)
    place_owner, place_sector, place_slot = places // (sectors * padded), places // padded % sectors, places % padded
    in_owner = place_sector * share + place_slot
    named = jnp.where((place_slot < share) & (in_owner < capacity), place_owner * capacity + in_owner, -1)
    one_hot = (named[:, None] == wave_slots[None, :]).astype(BF16)
    one_hot_turned = (wave_slots[:, None] == named[None, :]).astype(BF16)
    row_ids = jnp.arange(rows, dtype=jnp.int32)
    mirrored = row_ids // lat_rows * lat_rows + (lat_rows - 1 - row_ids % lat_rows)
    south = owner_index >= owners // 2
    mirror = (row_ids[:, None] == jnp.where(south, mirrored, row_ids)[None, :]).astype(BF16)
    forward_table, backward_table = wave_tables(sectors, lon_cols, waves)
    turns = tuple(jnp.asarray(turn) for turn in sector_turns(sectors, waves))

    first = sector_index * share
    local_ids = jnp.arange(share, dtype=jnp.int32)
    inside = first + local_ids < capacity
    at = owner_index * capacity + jnp.minimum(first + local_ids, capacity - 1)
    here = at[:, None] == slot_ids[None, :]
    wave_here = jnp.sum(jnp.where(here, wave_of_slot[None, :], 0), axis=1)
    count_here = jnp.where(inside, jnp.sum(jnp.where(here, count_of_slot[None, :], 0), axis=1), 0)
    degree_ids = jnp.arange(degrees, dtype=jnp.int32)
    total_degree = wave_here[:, None] + degree_ids[None, :]
    scaled = (total_degree * (total_degree + 1)).astype(F32) / float(degrees * (degrees + 1))
    kept = degree_ids[None, :] < count_here[:, None]
    sides = 2 * fields
    rates = jnp.repeat(viscosity, 4)
    damping = 1.0 / (1.0 + rates[None, :, None] * (scaled * scaled)[:, None, :])
    damping = jnp.where(kept[:, None, :], damping * (1.0 / math.sqrt(2 * half_lat)), 0.0)
    order, blocks, group = degree_order(count_here)
    lines, forward_table, backward_table, one_hot, one_hot_turned, mirror, damping, order, blocks = lax.optimization_barrier(
        (lines, forward_table, backward_table, one_hot, one_hot_turned, mirror, damping, order, blocks)
    )

    fourier = to_owners(lines, forward_table, turns, one_hot, mirror, share)
    received = lax.all_to_all(fourier, ("lat", "lon"), split_axis=0, concat_axis=0, tiled=True)
    spectral, returned = legendre(
        received, basis, damping, first[None], order, blocks, sectors, sides, lat_rows, group
    )
    regrouped = lax.all_to_all(returned, ("lat", "lon"), split_axis=0, concat_axis=0, tiled=True)
    spectral = lax.all_to_all(spectral.astype(BF16), "lon", split_axis=0, concat_axis=0, tiled=True)
    spectral = spectral.reshape(sectors * share, level_dev, 2, 2, degrees)[:capacity].astype(F32)
    grid_lines = to_sectors(regrouped, backward_table, turns, one_hot_turned, mirror, share)
    tendency = lax.all_to_all(grid_lines, "lon", split_axis=0, concat_axis=0, tiled=True)
    return spectral, tendency.astype(F32).reshape(levels, 2, lat_rows, lon_cols)


def solution(mesh):
    return jax.shard_map(
        body,
        mesh=mesh,
        in_specs=(
            P(None, "lat", "lon"),
            P(None, "lat", "lon"),
            P("lat", None, None),
            P(),
            P(),
            P(),
        ),
        out_specs=(P("lat", "lon", None, None, None), P(None, None, "lat", "lon")),
        check_vma=False,
    )
```

time: 221 us -> 206 us (0.932)
  blocking collectives: 84.5 us -> 39.8 us
  other arithmetic: 27.1 us -> 48.3 us
  waiting for transfers between devices: 31.5 us -> 52.2 us
  Pallas kernels: 60.8 us -> 43 us
  starting transfers between devices: 11 us -> 14.7 us
  local copies, waits for them, and re-layouts: 4.7 us -> 7.13 us
    all_to_all x2 -> x1, blocking collectives: 84.5 us -> 39.8 us  [body(): lax.all_to_all(fourier, ('lat', 'lon'), split_axis=0, concat_axis=0, tile...]
    all_to_all x1 -> x3, waiting for transfers between devices: 25.7 us -> 52.2 us  [the longest x1 29.4 us: body(): lax.all_to_all(returned, ('lat', 'lon'), split_axis=0, concat_axis=0, til...]
    convert_element_type x1 -> x3, other arithmetic: 7.71 us -> 22.8 us  [split_high_low(): return (high.astype(BF16), (value - high).astype(BF16))]
    concatenate x0 -> x3, other arithmetic: none -> 12.2 us  [the longest x1 8.75 us: wave_tables(): return (forward, jnp.concatenate(quarters, axis=0))]
    pallas_call x2, Pallas kernels: 41.8 us -> 31.3 us  [the longest x1 18.7 us: legendre(): pl.pallas_call(functools.partial(legendre_kernel, sides, lat_rows, group)...]
    mul x2, other arithmetic: 7.68 us -> 0.09 us  [the longest x1 0.09 us: body(): damping = 1.0 / (1.0 + rates[None, :, None] * (scaled * scaled)[:, None, :])]
    pallas_call x1, Pallas kernels: 19 us -> 11.8 us  [to_owners(): pl.pallas_call(forward_kernel, grid=(waves // size,), in_specs=[pl.BlockS...]
    all_to_all x1, waiting for transfers between devices: 5.83 us -> 0.01 us  [body(): lax.all_to_all(products, 'lon', split_axis=0, concat_axis=0, tiled=True)]
  transfers between devices with their start and end apart: 2 -> 4, of which waited for: 2 -> 2; matrix products, arithmetic and copies ran while one was open for 10% -> 24% of each run, Pallas kernels for 0% -> 6%
where the time goes in v2:
time: 206 us
  waiting for transfers between devices  52.2 us (25%)
  other arithmetic  48.3 us (23%)
  Pallas kernels  43 us (21%)
  blocking collectives  39.8 us (19%)
  starting transfers between devices  14.7 us (7%)
  local copies, waits for them, and re-layouts  7.13 us (3%)
    all_to_all x1, blocking collectives, body(): lax.all_to_all(fourier, ('lat', 'lon'), split_axis=0, concat_axis=0, tile...  39.8 us
    all_to_all x1, waiting for transfers between devices, body(): lax.all_to_all(returned, ('lat', 'lon'), split_axis=0, concat_axis=0, til...  29.4 us
    convert_element_type x3, other arithmetic, split_high_low(): return (high.astype(BF16), (value - high).astype(BF16))  22.8 us
    all_to_all x1, waiting for transfers between devices, body(): lax.all_to_all(grid_lines, 'lon', split_axis=0, concat_axis=0, tiled=True)  22.7 us
    pallas_call x1, Pallas kernels, legendre(): pl.pallas_call(functools.partial(legendre_kernel, sides, lat_rows, group)...  18.7 us
    pallas_call x1, Pallas kernels, to_sectors(): pl.pallas_call(functools.partial(backward_kernel, sectors in (1, 2, 4)),...  12.5 us
    pallas_call x1, Pallas kernels, to_owners(): pl.pallas_call(forward_kernel, grid=(waves // size,), in_specs=[pl.BlockS...  11.8 us
    concatenate x1, other arithmetic, wave_tables(): return (forward, jnp.concatenate(quarters, axis=0))  8.75 us
  transfers between devices with their start and end apart: 4, of which 2 were waited for; matrix products, arithmetic and copies ran while one was open for 24% of the time, Pallas kernels for 6%

profile of v2, /device:TPU:0, one launch (start us, length us, event | category | flops | bytes accessed | tf_op | source)
XLA Modules:
  0.0 205.9 jit_solution(70735881403645127)
XLA Ops:
  0.6 2.5 %fusion.14 = (bf16[4,1,192,640]{3,2,0,1:T(8,128)(2,1)S(1)}, bf16[4,1,192,640]{3,2,0,1:T(8,128)(2,1)S(1)}) fusion(f32[4,192,640]{2,1,0:T(8,128)} %param.8, f32[4,192,640]{2,1,0:T(8,128)} %param.9), kind=kLoop, calls=%fused_computation.43 | loop fusion | flops 2949120 | bytes 5898240 | tf_op jit(solution)/shard_map/stack | solution.py:362
  3.2 0.2 pad_maximum_fusion.2
  3.4 1.5 copy.16
  4.9 0.0 copy-start.4
  4.9 0.0 copy-start.5
  4.9 4.6 %all-to-all-start = ((bf16[4,384,640]{2,1,0:T(8,128)(2,1)}), bf16[4,384,640]{2,1,0:T(8,128)(2,1)}, u32[]{:S(2)}, u32[]{:S(2)}) async-start(bf16[4,384,640]{2,1,0:T(8,128)(2,1)} %bitcast.3), calls=%async_computation | async-start | bytes 3932160 | tf_op jit(solution)/shard_map/all_to_all | solution.py:364
  9.5 0.0 copy-done.4
  9.5 0.0 copy-done.5
  9.5 0.7 select_reduce_fusion.1
  10.2 0.2 select_reduce_fusion.3
  10.4 0.2 convert_reduce_fusion
  10.6 0.1 iota_compare_fusion.3
  10.7 7.9 %fusion.2 = (bf16[640,640]{1,0:T(8,128)(2,1)}, bf16[640,640]{1,0:T(8,128)(2,1)}) fusion(), kind=kLoop, calls=%fused_computation.22 | loop fusion | flops 6963200 | bytes 1638400 | tf_op jit(solution)/shard_map/convert_element_type | solution.py:28
  18.6 0.7 select_reduce_fusion.4
  19.3 0.1 slice.3
  19.4 0.6 and_select_fusion.blocks
  20.0 7.9 %reduce-precision_convert_fusion.3 = (bf16[640,5,128]{0,2,1:T(8,128)(2,1)S(1)}, bf16[640,5,128]{0,2,1:T(8,128)(2,1)S(1)}, bf16[640,5,128]{0,2,1:T(8,128)(2,1)S(1)}, bf16[640,5,128]{0,2,1:T(8,128)(2,1)S(1)}) fusion(s32[5,128]{1,0:T(8,128)S(1)} %multiply_add_fusion), kind=kLoop, calls=%fused_computation.13 | loop fusion | flops 7782400 | bytes 3279360 | tf_op jit(solution)/shard_map/convert_element_type | solution.py:28
  27.9 1.5 pad_maximum_fusion.3
  29.4 1.2 copy.17
  30.6 0.0 copy-start.6
  30.6 2.7 %copy.18 = bf16[640,1280]{1,0:T(8,128)(2,1)S(1)} copy(bf16[640,1280]{0,1:T(8,128)(2,1)} %bitcast.12) | data formatting | bytes 3276800 | tf_op jit(solution)/shard_map/reshape | solution.py:43
  33.3 0.1 fusion.19
  33.4 0.0 copy-done.6
  33.4 0.1 broadcast_in_dim.113
  33.5 0.1 mul.234
  33.6 0.8 fusion.16.mirror
  34.4 1.4 compare_convert_fusion.one_hot
  35.7 1.2 multiply_select_fusion.damping
  37.0 0.0 copy-start
  37.0 0.0 copy-start.1
  37.0 7.0 %reduce-precision_convert_fusion = (bf16[640,640]{1,0:T(8,128)(2,1)S(1)}, bf16[640,640]{1,0:T(8,128)(2,1)S(1)}) fusion(), kind=kLoop, calls=%fused_computation.7 | loop fusion | flops 6144000 | bytes 1638400 | tf_op jit(solution)/shard_map/convert_element_type | solution.py:28
  44.0 1.4 compare_convert_fusion.1.one_hot
  45.4 0.0 copy-done
  45.4 0.0 copy-done.1
  45.4 8.7 %pad_maximum_fusion.1.table = bf16[2560,640]{1,0:T(8,128)(2,1)} fusion(bf16[640,640]{1,0:T(8,128)(2,1)S(1)} %copy-done.1, bf16[640,640]{1,0:T(8,128)(2,1)S(1)} %copy-done, bf16[640,640]{1,0:T(8,128)(2,1)S(1)} %get-tuple-element.44, bf16[640,640]{1,0:T(8,128)(2,1)S(1)} %get-tuple-element.45), kind=kLoop, calls=%fused_computation.1 | loop fusion | flops 13107200 | bytes 6553600 | tf_op jit(solution)/shard_map/concatenate | solution.py:49
  54.2 1.9 pad_maximum_fusion.table
  56.1 0.0 all-to-all-done.lines
  56.1 11.8 %to_owners.1 = bf16[32,150,128]{2,1,0:T(8,128)(2,1)} custom-call(bf16[4,384,640]{2,1,0:T(8,128)(2,1)} %all-to-all-done.lines, bf16[1280,1280]{1,0:T(8,128)(2,1)} %pad_maximum_fusion.table, f32[4,1,640]{2,1,0:T(1,128)} %constant.151.clone.turn_cos, f32[4,1,640]{2,1,0:T(1,128)} %constant.152.clone.turn_sin, bf16[1024,640]{1,0:T(8,128)(2,1)} %compare_convert_fusion.1.one_hot, ...), custom_call_target="tpu_custom_call" | custom-call | flops 5033164800 | bytes 10000000 | tf_op jit(solution)/shard_map/to_owners/pallas_call | solution.py:98
  67.9 39.8 %all_to_all.25.received = bf16[32,150,128]{2,1,0:T(8,128)(2,1)} all-to-all(bf16[32,150,128]{2,1,0:T(8,128)(2,1)} %to_owners.1), channel_id=1, replica_groups=mesh['lat'=8,'lon'=4] {'lat','lon'}, dimensions={0} | all-to-all | bytes 2457600 | tf_op jit(solution)/shard_map/all_to_all | solution.py:405
  107.7 18.7 %legendre.1 = (f32[4,25,4,640]{3,2,1,0:T(4,128)}, bf16[32,150,128]{2,1,0:T(8,128)(2,1)}) custom-call(s32[1]{0:T(128)} %bitcast.first, s32[25]{0:T(128)} %get-tuple-element.13.order, s32[5]{0:T(128)} %and_select_fusion.blocks, bf16[32,150,128]{2,1,0:T(8,128)(2,1)} %all_to_all.25.received, f32[25,16,640]{2,1,0:T(8,128)} %multiply_select_fusion.damping, ...), custom_call_target="tpu_custom_call" | custom-call | flops 1572864000 | bytes 24576000 | tf_op jit(solution)/shard_map/legendre/pallas_call | solution.py:313
  126.4 0.0 copy-start.3
  126.4 2.8 %all-to-all-start.3 = ((bf16[32,150,128]{2,1,0:T(8,128)(2,1)}), bf16[32,150,128]{2,1,0:T(8,128)(2,1)S(1)}, u32[]{:S(2)}, u32[]{:S(2)}) async-start(bf16[32,150,128]{2,1,0:T(8,128)(2,1)} %get-tuple-element.21), calls=%async_computation.3 | async-start | bytes 2490368 | tf_op jit(solution)/shard_map/all_to_all | solution.py:409
  129.2 0.0 copy-done.3
  129.3 1.0 convert_element_type.103
  130.2 29.4 %all-to-all-done.3.wire = bf16[32,150,128]{2,1,0:T(8,128)(2,1)S(1)} async-done(((bf16[32,150,128]{2,1,0:T(8,128)(2,1)}), bf16[32,150,128]{2,1,0:T(8,128)(2,1)S(1)}, u32[]{:S(2)}, u32[]{:S(2)}) %all-to-all-start.3) | async-done | bytes 1228832 | tf_op jit(solution)/shard_map/all_to_all | solution.py:409
  159.7 0.0 copy-start.2
  159.7 3.7 %all-to-all-start.2 = ((bf16[4,25,4,640]{3,2,1,0:T(4,128)(2,1)}), bf16[4,25,4,640]{3,2,1,0:T(4,128)(2,1)S(1)}, u32[]{:S(2)}, u32[]{:S(2)}) async-start(bf16[4,25,4,640]{3,2,1,0:T(4,128)(2,1)} %convert_element_type.103), calls=%async_computation.2 | async-start | bytes 1024000 | tf_op jit(solution)/shard_map/all_to_all | solution.py:410
  163.4 0.0 copy-done.2
  163.4 12.5 %to_sectors.1 = bf16[4,384,640]{2,1,0:T(8,128)(2,1)} custom-call(bf16[32,150,128]{2,1,0:T(8,128)(2,1)} %copy-done.2, bf16[2560,640]{1,0:T(8,128)(2,1)} %pad_maximum_fusion.1.table, f32[4,1,640]{2,1,0:T(1,128)} %constant.151.clone.turn_cos, f32[4,1,640]{2,1,0:T(1,128)} %constant.152.clone.turn_sin, bf16[640,1024]{1,0:T(8,128)(2,1)} %compare_convert_fusion.one_hot, ...), custom_call_target="tpu_custom_call" | custom-call | flops 5033164800 | bytes 10000000 | tf_op jit(solution)/shard_map/to_sectors/pallas_call | solution.py:164
  175.9 0.0 all-to-all-done.2
  175.9 3.6 %all-to-all-start.4 = ((bf16[4,384,640]{2,1,0:T(8,128)(2,1)}), bf16[4,384,640]{2,1,0:T(8,128)(2,1)S(1)}, u32[]{:S(2)}, u32[]{:S(2)}) async-start(bf16[4,384,640]{2,1,0:T(8,128)(2,1)} %to_sectors.1), calls=%async_computation.4 | async-start | bytes 3932160 | tf_op jit(solution)/shard_map/all_to_all | solution.py:413
  179.5 1.5 reshape.261
  181.0 22.7 %all-to-all-done.4 = bf16[4,384,640]{2,1,0:T(8,128)(2,1)S(1)} async-done(((bf16[4,384,640]{2,1,0:T(8,128)(2,1)}), bf16[4,384,640]{2,1,0:T(8,128)(2,1)S(1)}, u32[]{:S(2)}, u32[]{:S(2)}) %all-to-all-start.4) | async-done | bytes 1966112 | tf_op jit(solution)/shard_map/all_to_all | solution.py:413
  203.7 2.2 %convert.12 = f32[4,2,192,640]{3,2,1,0:T(8,128)} convert(bf16[4,2,192,640]{3,2,1,0:T(8,128)(2,1)S(1)} %bitcast.11) | non-fusion elementwise | flops 983040 | bytes 5898240 | tf_op jit(solution)/shard_map/reshape | solution.py:414
  (7 shorter events, 0.0 us)
Async XLA Ops:
  4.9 4.6 %copy-start.4 = (s32[640]{0:T(1024)S(1)}, s32[640]{0:T(1024)}, u32[]{:S(2)}) copy-start(s32[640]{0:T(1024)} %param.11) | copy-start | bytes 7684
  4.9 4.6 %copy-start.5 = (s32[640]{0:T(1024)S(1)}, s32[640]{0:T(1024)}, u32[]{:S(2)}) copy-start(s32[640]{0:T(1024)} %param.12) | copy-start | bytes 7684
  4.9 51.2 %all-to-all-start = ((bf16[4,384,640]{2,1,0:T(8,128)(2,1)}), bf16[4,384,640]{2,1,0:T(8,128)(2,1)}, u32[]{:S(2)}, u32[]{:S(2)}) async-start(bf16[4,384,640]{2,1,0:T(8,128)(2,1)} %bitcast.3), calls=%async_computation | async-start | bytes 3932160 | tf_op jit(solution)/shard_map/all_to_all | solution.py:364
  30.6 2.8 %copy-start.6 = (f32[4]{0:T(128)S(1)}, f32[4]{0:T(128)}, u32[]{:S(2)}) copy-start(f32[4]{0:T(128)} %param.13) | copy-start | bytes 52
  37.0 8.5 %copy-start = (bf16[640,640]{1,0:T(8,128)(2,1)S(1)}, bf16[640,640]{1,0:T(8,128)(2,1)}, u32[]{:S(2)}) copy-start(bf16[640,640]{1,0:T(8,128)(2,1)} %get-tuple-element.46) | copy-start | bytes 2457604
  37.0 8.5 %copy-start.1 = (bf16[640,640]{1,0:T(8,128)(2,1)S(1)}, bf16[640,640]{1,0:T(8,128)(2,1)}, u32[]{:S(2)}) copy-start(bf16[640,640]{1,0:T(8,128)(2,1)} %get-tuple-element.47) | copy-start | bytes 2457604
  126.4 2.8 %copy-start.3 = (f32[4,25,4,640]{3,2,1,0:T(4,128)S(1)}, f32[4,25,4,640]{3,2,1,0:T(4,128)}, u32[]{:S(2)}) copy-start(f32[4,25,4,640]{3,2,1,0:T(4,128)} %get-tuple-element.20) | copy-start | bytes 3072004
  126.4 33.2 %all-to-all-start.3 = ((bf16[32,150,128]{2,1,0:T(8,128)(2,1)}), bf16[32,150,128]{2,1,0:T(8,128)(2,1)S(1)}, u32[]{:S(2)}, u32[]{:S(2)}) async-start(bf16[32,150,128]{2,1,0:T(8,128)(2,1)} %get-tuple-element.21), calls=%async_computation.3 | async-start | bytes 2490368 | tf_op jit(solution)/shard_map/all_to_all | solution.py:409
  159.7 3.7 %copy-start.2 = (bf16[32,150,128]{2,1,0:T(8,128)(2,1)}, bf16[32,150,128]{2,1,0:T(8,128)(2,1)S(1)}, u32[]{:S(2)}) copy-start(bf16[32,150,128]{2,1,0:T(8,128)(2,1)S(1)} %all-to-all-done.3.wire) | copy-start | bytes 3686404
  159.7 16.2 %all-to-all-start.2 = ((bf16[4,25,4,640]{3,2,1,0:T(4,128)(2,1)}), bf16[4,25,4,640]{3,2,1,0:T(4,128)(2,1)S(1)}, u32[]{:S(2)}, u32[]{:S(2)}) async-start(bf16[4,25,4,640]{3,2,1,0:T(4,128)(2,1)} %convert_element_type.103), calls=%async_computation.2 | async-start | bytes 1024000 | tf_op jit(solution)/shard_map/all_to_all | solution.py:410
  175.9 27.8 %all-to-all-start.4 = ((bf16[4,384,640]{2,1,0:T(8,128)(2,1)}), bf16[4,384,640]{2,1,0:T(8,128)(2,1)S(1)}, u32[]{:S(2)}, u32[]{:S(2)}) async-start(bf16[4,384,640]{2,1,0:T(8,128)(2,1)} %to_sectors.1), calls=%async_computation.4 | async-start | bytes 3932160 | tf_op jit(solution)/shard_map/all_to_all | solution.py:413

commit v3 on v2

v3 whole, which is shorter than its diff:
```python
import functools
import math

import jax
import jax.numpy as jnp
import numpy as np
from jax import lax
from jax.experimental import pallas as pl
from jax.experimental.pallas import tpu as pltpu
from jax.sharding import PartitionSpec as P

BF16 = jnp.bfloat16
F32 = jnp.float32
VMEM_LIMIT = 60 * 1024 * 1024
STEP = 128
LANES = 128
DEPTH = 3
NT = (((1,), (1,)), ((), ()))
NN = (((1,), (0,)), ((), ()))


def dot(a, b, dims=NN):
    return lax.dot_general(a, b, dims, preferred_element_type=F32)


def phases(rows, columns, length):
    turns = 2.0 * np.pi * (rows[:, None] * columns[None, :] % length) / length
    return np.cos(turns), np.sin(turns)


def table_kernel(interleaved, near_cos, near_sin, far_cos, far_sin, out):
    near, lanes = near_cos.shape
    count = far_cos.shape[0] * near
    size = min(LANES, lanes)
    for step in range(far_cos.shape[0]):
        cos = far_cos[step] * near_cos[...] - far_sin[step] * near_sin[...]
        sin = far_sin[step] * near_cos[...] + far_cos[step] * near_sin[...]
        high = (cos.astype(BF16), sin.astype(BF16))
        low = tuple((value - top.astype(F32)).astype(BF16) for value, top in zip((cos, sin), high))
        for term, pair in enumerate((high, low)):
            for which, value in enumerate(pair):
                if interleaved:
                    row = term * count + step * near
                    for block in range(lanes // size):
                        lane = (2 * block + which) * size
                        out[row : row + near, lane : lane + size] = value[:, block * size : (block + 1) * size]
                else:
                    row = (2 * term + which) * count + step * near
                    out[row : row + near, :] = value


def wave_table(rows, columns, length, interleaved):
    near = 32
    near_cos, near_sin = phases(np.arange(near), np.arange(columns), length)
    far_cos, far_sin = phases(np.arange(rows // near) * near, np.arange(columns), length)
    scaling = 1.0 / math.sqrt(length)
    shape = (2 * rows, 2 * columns) if interleaved else (4 * rows, columns)
    return pl.pallas_call(
        functools.partial(table_kernel, interleaved),
        out_shape=jax.ShapeDtypeStruct(shape, BF16),
        compiler_params=pltpu.CompilerParams(vmem_limit_bytes=VMEM_LIMIT),
        name="wave_table",
    )(
        jnp.asarray(near_cos * scaling, F32),
        jnp.asarray(near_sin * scaling, F32),
        jnp.asarray(far_cos[:, None, :], F32),
        jnp.asarray(far_sin[:, None, :], F32),
    )


def sector_turns(sectors, waves):
    both = phases(np.arange(sectors), np.arange(waves), sectors)
    return tuple(jnp.asarray(np.round(turn, 12)[:, None, :], F32) for turn in both)


def product_kernel(count, chosen, *refs):
    winds, outs = refs[: 2 * count], refs[2 * count :]
    for i in range(count):
        u, v = winds[2 * i][0], winds[2 * i + 1][0]
        lat_rows = u.shape[0]
        outs[i][:lat_rows] = (u * v).astype(BF16)
        outs[i][lat_rows:] = (u * u - v * v).astype(BF16)


def wind_products(wind_u, wind_v, chosen):
    _, lat_rows, columns = wind_u.shape
    count = chosen.shape[0]
    specs = [
        pl.BlockSpec((1, lat_rows, columns), functools.partial(lambda i, step, chosen: (chosen[i], 0, 0), i))
        for i in range(count)
        for _ in range(2)
    ]
    return pl.pallas_call(
        functools.partial(product_kernel, count),
        grid_spec=pltpu.PrefetchScalarGridSpec(
            num_scalar_prefetch=1,
            grid=(1,),
            in_specs=specs,
            out_specs=[pl.BlockSpec((2 * lat_rows, columns), lambda step, chosen: (0, 0))] * count,
        ),
        out_shape=[jax.ShapeDtypeStruct((2 * lat_rows, columns), BF16)] * count,
        compiler_params=pltpu.CompilerParams(vmem_limit_bytes=VMEM_LIMIT),
        name="wind_products",
    )(chosen, *[wind_u, wind_v] * count)


def forward_kernel(count, begun, ends, *refs):
    lines, refs = refs[:count], refs[count:]
    table, turn_cos, turn_sin = refs[:3]
    earlier, refs = (refs[3], refs[4:]) if begun else (None, refs[3:])
    step = pl.program_id(0)
    size = table.shape[1] // 2
    rows = lines[0].shape[0]
    both = jnp.concatenate([jnp.concatenate([line[...]] * 2, axis=1) for line in lines], axis=0)
    sums = dot(both, table[...])
    real, imag = (earlier[0], earlier[1]) if begun else (None, None)
    for i in range(count):
        own = sums[i * rows : (i + 1) * rows]
        own_cos, own_sin = own[:, :size], own[:, size:]
        cos, sin = turn_cos[i], turn_sin[i]
        own_real, own_imag = own_cos * cos - own_sin * sin, own_cos * sin + own_sin * cos
        real, imag = (own_real, own_imag) if real is None else (real + own_real, imag + own_imag)
    if not ends:
        refs[0][0], refs[0][1] = real, imag
        return
    one_hot, mirror, out, by_wave, by_slot = refs
    devices, wire_rows, lanes = out.shape
    padded = one_hot.shape[0] // devices
    blocks = 2 * rows // lanes
    share = wire_rows // blocks
    place = pl.ds(pl.multiple_of(step * size, size), size)
    by_wave[0, :, place] = real.astype(BF16)
    by_wave[1, :, place] = (-imag).astype(BF16)

    @pl.when(step == pl.num_programs(0) - 1)
    def _():
        for part in range(2):
            turned = dot(mirror[...], by_wave[part]).astype(BF16)
            by_slot[:, part * rows : (part + 1) * rows] = dot(one_hot[...], turned, NT)
        for device in range(devices):
            own = by_slot[device * padded : (device + 1) * padded, :]
            out[device] = jnp.concatenate(
                [own[:share, block * lanes : (block + 1) * lanes] for block in range(blocks)], axis=0
            ).astype(BF16)


def forward(lines, table, turns, earlier=None, end=None):
    rows, columns = lines[0].shape
    waves = table.shape[1] // 2
    size = min(LANES, waves)
    turn_spec = pl.BlockSpec((len(lines), 1, size), lambda i: (0, 0, i))
    sum_spec = pl.BlockSpec((2, rows, size), lambda i: (0, 0, i))
    args = list(lines) + [table, *turns]
    in_specs = [pl.BlockSpec((rows, columns), lambda i: (0, 0))] * len(lines)
    in_specs += [pl.BlockSpec((2 * columns, 2 * size), lambda i: (0, i)), turn_spec, turn_spec]
    if earlier is not None:
        args.append(earlier)
        in_specs.append(sum_spec)
    if end is None:
        out_shape, out_spec, scratch = jax.ShapeDtypeStruct((2, rows, waves), F32), sum_spec, []
    else:
        one_hot, mirror, share = end
        slots = one_hot.shape[0]
        lanes = wire_lanes(rows)
        out = (slots // round_up(share, 8), share * (2 * rows // lanes), lanes)
        args += [one_hot, mirror]
        in_specs += [pl.BlockSpec((slots, waves), lambda i: (0, 0)), pl.BlockSpec((rows, rows), lambda i: (0, 0))]
        out_shape, out_spec = jax.ShapeDtypeStruct(out, BF16), pl.BlockSpec(out, lambda i: (0, 0, 0))
        scratch = [pltpu.VMEM((2, rows, waves), BF16), pltpu.VMEM((slots, 2 * rows), F32)]
    return pl.pallas_call(
        functools.partial(forward_kernel, len(lines), earlier is not None, end is not None),
        grid=(waves // size,),
        in_specs=in_specs,
        out_specs=out_spec,
        out_shape=out_shape,
        scratch_shapes=scratch,
        cost_estimate=pl.CostEstimate(
            flops=8 * len(lines) * rows * columns * waves, bytes_accessed=10**7, transcendentals=0
        ),
        compiler_params=pltpu.CompilerParams(vmem_limit_bytes=VMEM_LIMIT),
        name="forward",
    )(*args)


def sector_lines(exact, by_wave, table, turn_cos, turn_sin):
    count = turn_cos.shape[0]
    left = []
    for i in range(count):
        cos, sin = turn_cos[i], turn_sin[i]
        real = by_wave[0] * cos - by_wave[1] * sin
        minus = -(by_wave[0] * sin) - by_wave[1] * cos
        left.append(jnp.concatenate([real, minus], axis=1))
    left = jnp.concatenate(left, axis=0) if count > 1 else left[0]
    high = left.astype(BF16)
    total = dot(jnp.concatenate([high, high], axis=1), table[...])
    if not exact:
        low = (left - high.astype(F32)).astype(BF16)
        total += dot(low, table[: low.shape[1]])
    return total.astype(BF16)


def backward_first_kernel(exact, wire, table_hbm, turn_cos, turn_sin, one_hot, mirror, out, by_wave, by_slot, table, sem):
    table_copy = pltpu.make_async_copy(table_hbm, table, sem)
    table_copy.start()
    devices, wire_rows, lanes = wire.shape
    rows = out.shape[0]
    waves = one_hot.shape[0]
    padded = by_slot.shape[0] // devices
    blocks = 2 * rows // lanes
    share = wire_rows // blocks
    for device in range(devices):
        own = wire[device].astype(F32)
        for block in range(blocks):
            piece = own[block * share : (block + 1) * share]
            if padded > share:
                piece = jnp.concatenate([piece, jnp.zeros((padded - share, lanes), F32)], axis=0)
            by_slot[device * padded : (device + 1) * padded, block * lanes : (block + 1) * lanes] = piece.astype(BF16)
    wave_ids = lax.broadcasted_iota(jnp.int32, (1, waves), 1)
    weight = jnp.where(wave_ids == 0, 1.0, 2.0).astype(F32)
    for part in range(2):
        ordered = dot(one_hot[...], by_slot[:, part * rows : (part + 1) * rows]).astype(BF16)
        by_wave[part] = dot(mirror[...], ordered, NT) * weight
    table_copy.wait()
    out[...] = sector_lines(exact, by_wave, table, turn_cos, turn_sin)


def backward_first(wire, table, turns, one_hot, mirror, exact):
    rows = mirror.shape[0]
    waves, slots = one_hot.shape
    vmem, hbm = pl.BlockSpec(memory_space=pltpu.VMEM), pl.BlockSpec(memory_space=pl.ANY)
    return pl.pallas_call(
        functools.partial(backward_first_kernel, exact),
        in_specs=[vmem, hbm, vmem, vmem, vmem, vmem],
        out_specs=[vmem, vmem],
        out_shape=[
            jax.ShapeDtypeStruct((rows, table.shape[1]), BF16),
            jax.ShapeDtypeStruct((2, rows, waves), F32),
        ],
        scratch_shapes=[
            pltpu.VMEM((slots, 2 * rows), BF16),
            pltpu.VMEM(table.shape, BF16),
            pltpu.SemaphoreType.DMA,
        ],
        cost_estimate=pl.CostEstimate(flops=10**9, bytes_accessed=10**7, transcendentals=0),
        compiler_params=pltpu.CompilerParams(vmem_limit_bytes=VMEM_LIMIT),
        name="backward_first",
    )(wire, table, *turns, one_hot, mirror)


def backward_rest_kernel(exact, by_wave, table, turn_cos, turn_sin, *outs):
    rows = outs[0].shape[0]
    total = sector_lines(exact, by_wave, table, turn_cos, turn_sin)
    for i, out in enumerate(outs):
        out[...] = total[i * rows : (i + 1) * rows]


def backward_rest(by_wave, table, turns, exact):
    _, rows, _ = by_wave.shape
    count = turns[0].shape[0]
    vmem = pl.BlockSpec(memory_space=pltpu.VMEM)
    return pl.pallas_call(
        functools.partial(backward_rest_kernel, exact),
        in_specs=[vmem] * 4,
        out_specs=[vmem] * count,
        out_shape=[jax.ShapeDtypeStruct((rows, table.shape[1]), BF16)] * count,
        cost_estimate=pl.CostEstimate(flops=3 * 10**9, bytes_accessed=10**7, transcendentals=0),
        compiler_params=pltpu.CompilerParams(vmem_limit_bytes=VMEM_LIMIT),
        name="backward_rest",
    )(by_wave, table, *turns)


def placing_kernel(count, chosen, *refs):
    blocks, (out, wide, sems) = refs[:count], refs[-3:]
    copies = []
    for i in range(count):
        wide[i] = blocks[i][...].astype(F32)
        copies.append(pltpu.make_async_copy(wide.at[i], out.at[chosen[i]], sems.at[i]))
        copies[-1].start()
    for copy in copies:
        copy.wait()


def placed(blocks, chosen, total, earlier=None):
    count = len(blocks)
    shape = blocks[0].shape
    smem, vmem, hbm = (pl.BlockSpec(memory_space=space) for space in (pltpu.SMEM, pltpu.VMEM, pl.ANY))
    more = () if earlier is None else (earlier,)
    return pl.pallas_call(
        functools.partial(placing_kernel, count),
        in_specs=[smem] + [vmem] * count + [hbm] * len(more),
        out_specs=hbm,
        out_shape=jax.ShapeDtypeStruct((total,) + shape, F32),
        scratch_shapes=[pltpu.VMEM((count,) + shape, F32), pltpu.SemaphoreType.DMA((count,))],
        input_output_aliases={1 + count: 0} if more else {},
        compiler_params=pltpu.CompilerParams(vmem_limit_bytes=VMEM_LIMIT),
        name="placed",
    )(chosen, *blocks, *more)


def round_up(value, unit):
    return -(-value // unit) * unit


def wire_lanes(rows):
    return LANES if 2 * rows % LANES == 0 else 2 * rows


def legendre_kernel(sides, lat_rows, group, place, order, blocks, received, damping, basis, spectral, returned, held, buffer, sems):
    devices, wire_rows, lanes = received.shape
    sectors, share = spectral.shape[:2]
    slots, degrees, half_lat = basis.shape
    sources = devices // sectors
    fields = sides // 2
    combos = sectors * sides
    lane_blocks = held.shape[0]
    stride = held.shape[1] // (2 * combos)
    wire_blocks = wire_rows // share
    groups = share // group
    most = degrees // STEP
    scale = 1.0 / math.sqrt(degrees)

    def copies(index, count):
        ring = lax.rem(index, DEPTH)
        rows = pl.ds(0, count * STEP)
        return [
            pltpu.make_async_copy(
                basis.at[jnp.minimum(place[0] + order[index * group + i], slots - 1), rows, :],
                buffer.at[ring, i, rows, :],
                sems.at[ring, i],
            )
            for i in range(group)
        ]

    def fetch(index):
        for count in range(1, most + 1):

            @pl.when(blocks[index] == count)
            def _():
                for copy in copies(index, count):
                    copy.start()

    for index in range(min(DEPTH - 1, groups)):
        fetch(index)

    def wire_pieces(device, wire_block):
        source, sector = divmod(device, sectors)
        side, near = (0, source) if source < sources // 2 else (1, sources - 1 - source)
        column, end = wire_block * lanes, (wire_block + 1) * lanes
        while column < end:
            part_field, lat = divmod(column, lat_rows)
            part, field = divmod(part_field, fields)
            row = (side * combos + sector * sides + field * 2 + part) * stride
            place = near * lat_rows + lat
            width = min(end - column, lat_rows - lat, LANES - place % LANES)
            yield column - wire_block * lanes, width, row, place // LANES, place % LANES
            column += width

    for device in range(devices):
        own = received[device].astype(F32)
        for wire_block in range(wire_blocks):
            piece = own[wire_block * share : (wire_block + 1) * share]
            for at, width, row, block, lane in wire_pieces(device, wire_block):
                held[block, row : row + share, lane : lane + width] = piece[:, at : at + width]

    def load_slot(slot):
        rows = pl.ds(slot, 2 * combos, stride=stride)
        return jnp.concatenate([held[block, rows, :] for block in range(lane_blocks)], axis=1)

    def store_slot(slot, value):
        rows = pl.ds(slot, 2 * combos, stride=stride)
        for block in range(lane_blocks):
            held[block, rows, :] = value[:, block * LANES : (block + 1) * LANES]

    def one_group(index, count):
        ring = lax.rem(index, DEPTH)
        here = [order[index * group + i] for i in range(group)]
        if count == 0:
            for slot in here:
                for sector in range(sectors):
                    spectral[place[1] ^ sector, slot] = jnp.zeros(spectral.shape[2:], F32)
                store_slot(slot, jnp.zeros((2 * combos, half_lat), F32))
            return
        width = count * STEP
        for copy in copies(index, count):
            copy.wait()
        parity = 1.0 - 2.0 * (lax.broadcasted_iota(jnp.int32, (1, width), 1) % 2).astype(F32)
        left = [load_slot(slot).astype(BF16) for slot in here]
        sums = [dot(left[i], buffer[ring, i, :width, :], NT) for i in range(group)]
        damped = [
            (sums[i][:combos] + parity * sums[i][combos:]) * damping[slot, :, :width] for i, slot in enumerate(here)
        ]
        turned = [jnp.concatenate([value, parity * value], axis=0).astype(BF16) for value in damped]
        backs = [dot(turned[i], buffer[ring, i, :width, :]) * scale for i in range(group)]
        for i, slot in enumerate(here):
            for sector in range(sectors):
                spectral[place[1] ^ sector, slot, :, :width] = damped[i][sector * sides : (sector + 1) * sides]
                if width < degrees:
                    spectral[place[1] ^ sector, slot, :, width:] = jnp.zeros((sides, degrees - width), F32)
        for i, slot in enumerate(here):
            store_slot(slot, backs[i])

    def loop_body(index, carry):
        @pl.when(index + DEPTH - 1 < groups)
        def _():
            fetch(index + DEPTH - 1)

        for count in range(most + 1):
            pl.when(blocks[index] == count)(functools.partial(one_group, index, count))
        return carry

    lax.fori_loop(0, groups, loop_body, 0)

    for device in range(devices):
        pieces = []
        for wire_block in range(wire_blocks):
            parts = [
                held[block, row : row + share, lane : lane + width]
                for _, width, row, block, lane in wire_pieces(device, wire_block)
            ]
            pieces.append(jnp.concatenate(parts, axis=1) if len(parts) > 1 else parts[0])
        returned[device] = jnp.concatenate(pieces, axis=0).astype(BF16)


def legendre(received, basis, damping, place, order, blocks, sectors, sides, lat_rows, group):
    share = order.shape[0]
    degrees, half_lat = basis.shape[1:]
    combos = sectors * sides
    smem, vmem, hbm = (pl.BlockSpec(memory_space=space) for space in (pltpu.SMEM, pltpu.VMEM, pl.ANY))
    return pl.pallas_call(
        functools.partial(legendre_kernel, sides, lat_rows, group),
        in_specs=[smem, smem, smem, vmem, vmem, hbm],
        out_specs=[vmem, vmem],
        out_shape=[
            jax.ShapeDtypeStruct((sectors, share, sides, degrees), F32),
            jax.ShapeDtypeStruct(received.shape, BF16),
        ],
        scratch_shapes=[
            pltpu.VMEM((half_lat // LANES, 2 * combos * round_up(share, 8), LANES), F32),
            pltpu.VMEM((DEPTH, group, degrees, half_lat), BF16),
            pltpu.SemaphoreType.DMA((DEPTH, group)),
        ],
        cost_estimate=pl.CostEstimate(
            flops=4 * share * degrees * half_lat * 2 * combos,
            bytes_accessed=2 * share * degrees * half_lat,
            transcendentals=0,
        ),
        compiler_params=pltpu.CompilerParams(vmem_limit_bytes=VMEM_LIMIT),
        name="legendre",
    )(place, order, blocks, received, damping, basis)


def degree_order(counts):
    size = counts.shape[0]
    ids = jnp.arange(size, dtype=jnp.int32)
    ahead = (counts[None, :] > counts[:, None]) | ((counts[None, :] == counts[:, None]) & (ids[None, :] < ids[:, None]))
    rank = jnp.sum(ahead.astype(jnp.int32), axis=1)
    placed = rank[:, None] == ids[None, :]
    order = jnp.sum(jnp.where(placed, ids[:, None], 0), axis=0)
    sorted_counts = jnp.sum(jnp.where(placed, counts[:, None], 0), axis=0)
    group = max(g for g in range(1, 6) if size % g == 0)
    return order, (sorted_counts[::group] + (STEP - 1)) // STEP, group


def body(wind_u, wind_v, basis, wave_slots, degree_count, viscosity):
    sectors = lax.axis_size("lon")
    owners = lax.axis_size("lat")
    sector_index = lax.axis_index("lon")
    owner_index = lax.axis_index("lat")
    levels, lat_rows, lon_cols = wind_u.shape
    capacity, degrees, half_lat = basis.shape
    waves = wave_slots.shape[0]
    slot_total = capacity * owners
    assert levels == sectors and sectors & (sectors - 1) == 0
    rows = 2 * lat_rows
    share = -(-capacity // sectors)
    padded = round_up(share, 8)
    length = sectors * lon_cols
    masks = [sectors // 2] + [mask for mask in range(sectors - 1, 0, -1) if mask != sectors // 2] + [0]

    def across(value, mask):
        return lax.ppermute(value, "lon", [(i, i ^ mask) for i in range(sectors)]) if mask else value

    def partners(some):
        return jnp.stack([sector_index ^ mask for mask in some]).astype(jnp.int32)

    far, rest = masks[:1], masks[1:]
    sent = list(wind_products(wind_u, wind_v, partners(far))) + list(wind_products(wind_u, wind_v, partners(rest)))
    lines = {mask: across(value, mask) for mask, value in zip(masks, sent)}

    slot_ids = jnp.arange(slot_total, dtype=jnp.int32)
    wave_ids = jnp.arange(waves, dtype=jnp.int32)
    places = jnp.arange(owners * sectors * padded, dtype=jnp.int32)
    place_owner, place_sector, place_slot = places // (sectors * padded), places // padded % sectors, places % padded
    in_owner = place_sector * share + place_slot
    named = jnp.where((place_slot < share) & (in_owner < capacity), place_owner * capacity + in_owner, -1)
    one_hot = (named[:, None] == wave_slots[None, :]).astype(BF16)
    one_hot_turned = (wave_slots[:, None] == named[None, :]).astype(BF16)
    row_ids = jnp.arange(rows, dtype=jnp.int32)
    mirrored = row_ids // lat_rows * lat_rows + (lat_rows - 1 - row_ids % lat_rows)
    south = owner_index >= owners // 2
    mirror = (row_ids[:, None] == jnp.where(south, mirrored, row_ids)[None, :]).astype(BF16)
    forward_table = wave_table(lon_cols, waves, length, True)
    backward_table = wave_table(waves, lon_cols, length, False)
    turns = sector_turns(sectors, waves)

    def turns_of(some):
        at = partners(some)
        return tuple(jnp.take(turn, at, axis=0) for turn in turns)

    first = sector_index * share
    local_ids = jnp.arange(share, dtype=jnp.int32)
    inside = first + local_ids < capacity
    at = owner_index * capacity + jnp.minimum(first + local_ids, capacity - 1)
    here = at[:, None] == wave_slots[None, :]
    wave_here = jnp.sum(jnp.where(here, wave_ids[None, :], 0), axis=1)
    count_here = jnp.where(inside, jnp.sum(jnp.where(here, degree_count[None, :], 0), axis=1), 0)
    degree_ids = jnp.arange(degrees, dtype=jnp.int32)
    total_degree = wave_here[:, None] + degree_ids[None, :]
    scaled = (total_degree * (total_degree + 1)).astype(F32) / float(degrees * (degrees + 1))
    kept = degree_ids[None, :] < count_here[:, None]
    sides = 4
    rates = jnp.repeat(viscosity, sides)
    damping = 1.0 / (1.0 + rates[None, :, None] * (scaled * scaled)[:, None, :])
    damping = jnp.where(kept[:, None, :], damping * (1.0 / math.sqrt(2 * half_lat)), 0.0)
    order, blocks, group = degree_order(count_here)

    by_arrival = [0, *[mask for mask in reversed(masks) if mask and mask < sectors // 2], *masks]
    by_arrival = list(dict.fromkeys(by_arrival))
    early, late = by_arrival[:-1], by_arrival[-1:]
    sums = forward([lines[mask] for mask in early], forward_table, turns_of(early))
    fourier = forward([lines[mask] for mask in late], forward_table, turns_of(late), sums, (one_hot, mirror, share))
    received = lax.all_to_all(fourier, ("lat", "lon"), split_axis=0, concat_axis=0, tiled=True)
    place = jnp.stack([first, sector_index]).astype(jnp.int32)
    spectral, returned = legendre(
        received, basis, damping, place, order, blocks, sectors, sides, lat_rows, group
    )
    regrouped = lax.all_to_all(returned, ("lat", "lon"), split_axis=0, concat_axis=0, tiled=True)

    coefficients = jnp.zeros((sectors * share, 1, 2, 2, degrees), F32)
    for mask in masks:
        own = across(spectral[mask].astype(BF16), mask).astype(F32).reshape(share, 1, 2, 2, degrees)
        coefficients = lax.dynamic_update_slice_in_dim(coefficients, own, (sector_index ^ mask) * share, 0)

    exact = sectors in (1, 2, 4)
    far_lines, by_wave = backward_first(regrouped, backward_table, turns_of(far), one_hot_turned, mirror, exact)
    made = [far_lines, *backward_rest(by_wave, backward_table, turns_of(rest), exact)]
    back = {mask: across(value, mask) for mask, value in zip(masks, made)}
    tendency = placed([back[mask] for mask in early], partners(early), sectors)
    tendency = placed([back[mask] for mask in late], partners(late), sectors, tendency)
    return coefficients[:capacity], tendency.reshape(levels, 2, lat_rows, lon_cols)


def solution(mesh):
    return jax.shard_map(
        body,
        mesh=mesh,
        in_specs=(
            P(None, "lat", "lon"),
            P(None, "lat", "lon"),
            P("lat", None, None),
            P(),
            P(),
            P(),
        ),
        out_specs=(P("lat", "lon", None, None, None), P(None, None, "lat", "lon")),
        check_vma=False,
    )
```

time: 206 us -> 176 us (0.85)
  blocking collectives: 39.8 us -> 0 us
  other arithmetic: 48.3 us -> 10.1 us
  Pallas kernels: 43 us -> 64.3 us
  waiting for transfers between devices: 52.2 us -> 68.8 us
  starting transfers between devices: 14.7 us -> 21.7 us
  local copies, waits for them, and re-layouts: 7.13 us -> 9.93 us
    all_to_all x1 -> x0, blocking collectives: 39.8 us -> none  [body(): lax.all_to_all(fourier, ('lat', 'lon'), split_axis=0, concat_axis=0, tile...]
    ppermute x0 -> x9, waiting for transfers between devices: none -> 33 us  [across(): lax.ppermute(value, 'lon', [(i, i ^ mask) for i in range(sectors)])]
    pallas_call x2 -> x10, Pallas kernels: 24.3 us -> 50.2 us  [the longest x2 16.7 us: forward(): pl.pallas_call(functools.partial(forward_kernel, len(lines), earlier is n...]
    convert_element_type x4 -> x1, other arithmetic: 23.8 us -> 0.17 us  [body(): across(spectral[mask].astype(BF16), mask).astype(F32)]
    all_to_all x1, waiting for transfers between devices: 29.4 us -> 9.42 us  [body(): lax.all_to_all(returned, ('lat', 'lon'), split_axis=0, concat_axis=0, til...]
    concatenate x3 -> x0, other arithmetic: 12.2 us -> none  [the longest x1 8.75 us: wave_tables(): return (forward, jnp.concatenate(quarters, axis=0))]
    ppermute x0 -> x9, starting transfers between devices: none -> 7.24 us  [across(): lax.ppermute(value, 'lon', [(i, i ^ mask) for i in range(sectors)])]
    all_to_all x3 -> x1, starting transfers between devices: 11.8 us -> 5.98 us  [body(): lax.all_to_all(fourier, ('lat', 'lon'), split_axis=0, concat_axis=0, tile...]
  transfers between devices with their start and end apart: 4 -> 11, of which waited for: 2 -> 8; matrix products, arithmetic and copies ran while one was open for 24% -> 8% of each run, Pallas kernels for 6% -> 20%
where the time goes in v3:
time: 176 us
  waiting for transfers between devices  68.8 us (39%)
  Pallas kernels  64.3 us (37%)
  starting transfers between devices  21.7 us (12%)
  other arithmetic  10.1 us (6%)
  local copies, waits for them, and re-layouts  9.93 us (6%)
    ppermute x9, waiting for transfers between devices, across(): lax.ppermute(value, 'lon', [(i, i ^ mask) for i in range(sectors)])  33 us
    all_to_all x1, waiting for transfers between devices, body(): lax.all_to_all(fourier, ('lat', 'lon'), split_axis=0, concat_axis=0, tile...  26.4 us
    pallas_call x2, Pallas kernels, forward(): pl.pallas_call(functools.partial(forward_kernel, len(lines), earlier is n...  16.7 us
    pallas_call x1, Pallas kernels, legendre(): pl.pallas_call(functools.partial(legendre_kernel, sides, lat_rows, group)...  14.1 us
    all_to_all x1, waiting for transfers between devices, body(): lax.all_to_all(returned, ('lat', 'lon'), split_axis=0, concat_axis=0, til...  9.42 us
    all_to_all x1, starting transfers between devices, body(): lax.all_to_all(returned, ('lat', 'lon'), split_axis=0, concat_axis=0, til...  8.53 us
    pallas_call x1, Pallas kernels, backward_rest(): pl.pallas_call(functools.partial(backward_rest_kernel, exact), in_specs=[...  8.23 us
    pallas_call x1, Pallas kernels, backward_first(): pl.pallas_call(functools.partial(backward_first_kernel, exact), in_specs=...  7.52 us
  transfers between devices with their start and end apart: 11, of which 8 were waited for; matrix products, arithmetic and copies ran while one was open for 8% of the time, Pallas kernels for 20%

profile of v3, /device:TPU:0, one launch (start us, length us, event | category | flops | bytes accessed | tf_op | source)
XLA Modules:
  0.0 176.1 jit_solution(1861221953191092461)
XLA Ops:
  0.6 0.7 compare_select_fusion.2
  1.3 3.6 %wind_products.2 = (bf16[384,640]{1,0:T(8,128)(2,1)}, bf16[384,640]{1,0:T(8,128)(2,1)}, bf16[384,640]{1,0:T(8,128)(2,1)}) custom-call(s32[3]{0:T(128)} %get-tuple-element.40.chosen, f32[4,192,640]{2,1,0:T(8,128)} %refs_0_.3, f32[4,192,640]{2,1,0:T(8,128)} %refs_1_.3, f32[4,192,640]{2,1,0:T(8,128)} %refs_0_.3, f32[4,192,640]{2,1,0:T(8,128)} %refs_1_.3, ...), custom_call_target="tpu_custom_call" | custom-call | tf_op jit(solution)/shard_map/wind_products/pallas_call | solution.py:93
  5.0 0.6 collective-permute-start.1
  5.5 2.1 %wind_products.3 = bf16[384,640]{1,0:T(8,128)(2,1)} custom-call(s32[1]{0:T(128)} %bitcast.6.chosen, f32[4,192,640]{2,1,0:T(8,128)} %refs_0_.3, f32[4,192,640]{2,1,0:T(8,128)} %refs_1_.3), custom_call_target="tpu_custom_call" | custom-call | tf_op jit(solution)/shard_map/wind_products/pallas_call | solution.py:93
  7.6 2.6 %collective-permute-start.2 = (bf16[384,640]{1,0:T(8,128)(2,1)}, bf16[384,640]{1,0:T(8,128)(2,1)S(1)}, u32[]{:S(2)}, u32[]{:S(2)}) collective-permute-start(bf16[384,640]{1,0:T(8,128)(2,1)} %wind_products.3), channel_id=1, source_target_pairs={{0,2},{1,3},{2,0},{3,1},{4,6},{5,7},{6,4},{7,5},{8,10},{9,11},{10,... | collective-permute-start | bytes 1474568 | tf_op jit(solution)/shard_map/ppermute | solution.py:481
  10.2 0.6 gather_fusion
  10.8 0.6 gather_fusion.1
  11.4 0.8 fusion.refs_6_.mirror
  12.2 1.4 compare_convert_fusion.1.refs_5_
  13.6 0.7 broadcast_select_fusion.2
  14.3 3.5 %wave_table.2.refs_3_.refs_1_ = bf16[1280,1280]{1,0:T(8,128)(2,1)} custom-call(f32[32,640]{1,0:T(8,128)} %constant.162.clone.near_cos, f32[32,640]{1,0:T(8,128)} %constant.163.clone.near_sin, f32[20,1,640]{2,1,0:T(1,128)} %constant.164.clone.far_cos, f32[20,1,640]{2,1,0:T(1,128)} %constant.165.clone.far_sin), custom_call_target="tpu_custom_call" | custom-call | tf_op jit(solution)/shard_map/wave_table/pallas_call | solution.py:58
  17.8 0.6 broadcast_select_fusion.4
  18.4 4.1 %collective-permute-done.2.refs_2_ = bf16[384,640]{1,0:T(8,128)(2,1)S(1)} collective-permute-done((bf16[384,640]{1,0:T(8,128)(2,1)}, bf16[384,640]{1,0:T(8,128)(2,1)S(1)}, u32[]{:S(2)}, u32[]{:S(2)}) %collective-permute-start.2) | collective-permute-done | bytes 491552 | tf_op jit(solution)/shard_map/ppermute | solution.py:481
  22.5 0.8 copy-done.19
  23.3 7.7 %forward.2.refs_4_ = f32[2,384,640]{2,1,0:T(8,128)} custom-call(bf16[384,640]{1,0:T(8,128)(2,1)} %get-tuple-element.15.refs_0_, bf16[384,640]{1,0:T(8,128)(2,1)} %copy-done.18, bf16[384,640]{1,0:T(8,128)(2,1)} %copy-done.19, bf16[1280,1280]{1,0:T(8,128)(2,1)} %wave_table.2.refs_3_.refs_1_, f32[3,1,640]{2,1,0:T(1,128)} %get-tuple-element.54.refs_4_, ...), custom_call_target="tpu_custom_call" | custom-call | flops 3774873600 | bytes 10000000 | tf_op jit(solution)/shard_map/forward/pallas_call | solution.py:170
  31.0 1.5 collective-permute-done.refs_0_
  32.4 0.8 copy-done.6
  33.2 9.0 %forward.3 = bf16[32,150,128]{2,1,0:T(8,128)(2,1)} custom-call(bf16[384,640]{1,0:T(8,128)(2,1)} %copy-done.6, bf16[1280,1280]{1,0:T(8,128)(2,1)} %wave_table.2.refs_3_.refs_1_, f32[1,1,640]{2,1,0:T(1,128)} %get-tuple-element.57.refs_2_, f32[1,1,640]{2,1,0:T(1,128)} %get-tuple-element.48.refs_3_, f32[2,384,640]{2,1,0:T(8,128)} %forward.2.refs_4_, ...), custom_call_target="tpu_custom_call" | custom-call | flops 1258291200 | bytes 10000000 | tf_op jit(solution)/shard_map/forward/pallas_call | solution.py:170
  42.2 6.0 %all-to-all-start = ((bf16[32,150,128]{2,1,0:T(8,128)(2,1)}), bf16[32,150,128]{2,1,0:T(8,128)(2,1)S(1)}, u32[]{:S(2)}, u32[]{:S(2)}) async-start(bf16[32,150,128]{2,1,0:T(8,128)(2,1)} %forward.3), calls=%async_computation | async-start | bytes 2490368 | tf_op jit(solution)/shard_map/all_to_all | solution.py:532
  48.2 0.2 fusion.2
  48.4 0.2 convert_reduce_fusion
  48.6 0.7 select_reduce_fusion
  49.3 0.1 slice.19
  49.4 0.1 broadcast_in_dim.104
  49.5 0.1 mul.90
  49.6 0.6 pad_add_fusion.place
  50.1 0.5 and_select_fusion.blocks
  50.6 0.1 iota_compare_fusion.1
  50.7 0.1 fusion.5
  50.8 1.2 multiply_select_fusion.damping
  52.1 26.4 %all-to-all-done.received = bf16[32,150,128]{2,1,0:T(8,128)(2,1)S(1)} async-done(((bf16[32,150,128]{2,1,0:T(8,128)(2,1)}), bf16[32,150,128]{2,1,0:T(8,128)(2,1)S(1)}, u32[]{:S(2)}, u32[]{:S(2)}) %all-to-all-start) | async-done | bytes 1228832 | tf_op jit(solution)/shard_map/all_to_all | solution.py:532
  78.4 1.0 copy-done.1
  79.5 14.1 %legendre.1 = (f32[4,25,4,640]{3,2,1,0:T(4,128)}, bf16[32,150,128]{2,1,0:T(8,128)(2,1)}) custom-call(s32[2]{0:T(128)} %pad_add_fusion.place, s32[25]{0:T(128)} %get-tuple-element.38.order, s32[5]{0:T(128)} %and_select_fusion.blocks, bf16[32,150,128]{2,1,0:T(8,128)(2,1)} %copy-done.1, f32[25,16,640]{2,1,0:T(8,128)} %multiply_select_fusion.damping, ...), custom_call_target="tpu_custom_call" | custom-call | flops 1572864000 | bytes 24576000 | tf_op jit(solution)/shard_map/legendre/pallas_call | solution.py:429
  93.6 8.5 %all-to-all-start.1 = ((bf16[32,150,128]{2,1,0:T(8,128)(2,1)}), bf16[32,150,128]{2,1,0:T(8,128)(2,1)S(1)}, u32[]{:S(2)}, u32[]{:S(2)}) async-start(bf16[32,150,128]{2,1,0:T(8,128)(2,1)} %get-tuple-element.18), calls=%async_computation.1 | async-start | bytes 2490368 | tf_op jit(solution)/shard_map/all_to_all | solution.py:537
  102.2 3.5 %wave_table.3.table_hbm.table = bf16[2560,640]{1,0:T(8,128)(2,1)} custom-call(f32[32,640]{1,0:T(8,128)} %constant.162.clone.near_cos, f32[32,640]{1,0:T(8,128)} %constant.163.clone.near_sin, f32[20,1,640]{2,1,0:T(1,128)} %constant.164.clone.far_cos, f32[20,1,640]{2,1,0:T(1,128)} %constant.165.clone.far_sin), custom_call_target="tpu_custom_call" | custom-call | tf_op jit(solution)/shard_map/wave_table/pallas_call | solution.py:58
  105.7 0.6 gather_fusion.2
  106.2 0.6 gather_fusion.3
  106.8 1.4 compare_convert_fusion.one_hot
  108.2 0.2 convert.10
  108.4 0.2 slice_convert_fusion
  108.6 1.6 collective-permute-start.3
  110.2 0.7 broadcast_select_fusion
  110.9 0.6 collective-permute-start.5
  111.5 0.2 reshape.306
  111.7 6.3 %collective-permute-done.3 = bf16[25,4,640]{2,1,0:T(4,128)(2,1)S(1)} collective-permute-done((bf16[25,4,640]{2,1,0:T(4,128)(2,1)S(1)}, bf16[25,4,640]{2,1,0:T(4,128)(2,1)S(1)}, u32[]{:S(2)}, u32[]{:S(2)}) %collective-permute-start.3) | collective-permute-done | bytes 128032 | tf_op jit(solution)/shard_map/ppermute | solution.py:481
  118.0 0.2 reshape.301
  118.1 4.2 %collective-permute-done.4 = bf16[25,4,640]{2,1,0:T(4,128)(2,1)S(1)} collective-permute-done((bf16[25,4,640]{2,1,0:T(4,128)(2,1)S(1)}, bf16[25,4,640]{2,1,0:T(4,128)(2,1)S(1)}, u32[]{:S(2)}, u32[]{:S(2)}) %collective-permute-start.4) | collective-permute-done | bytes 128032 | tf_op jit(solution)/shard_map/ppermute | solution.py:481
  122.4 0.2 reshape.303
  122.6 0.3 broadcast_in_dim.98
  122.8 0.1 bitcast_dynamic-update-slice_fusion.3
  122.9 9.4 %all-to-all-done.1.wire = bf16[32,150,128]{2,1,0:T(8,128)(2,1)S(1)} async-done(((bf16[32,150,128]{2,1,0:T(8,128)(2,1)}), bf16[32,150,128]{2,1,0:T(8,128)(2,1)S(1)}, u32[]{:S(2)}, u32[]{:S(2)}) %all-to-all-start.1) | async-done | bytes 1228832 | tf_op jit(solution)/shard_map/all_to_all | solution.py:537
  132.3 1.0 copy-done
  133.4 7.5 %backward_first.1 = (bf16[384,640]{1,0:T(8,128)(2,1)}, f32[2,384,640]{2,1,0:T(8,128)}) custom-call(bf16[32,150,128]{2,1,0:T(8,128)(2,1)} %copy-done, bf16[2560,640]{1,0:T(8,128)(2,1)} %wave_table.3.table_hbm.table, f32[1,1,640]{2,1,0:T(1,128)} %get-tuple-element.58.turn_cos, f32[1,1,640]{2,1,0:T(1,128)} %get-tuple-element.47.turn_sin, ...), custom_call_target="tpu_custom_call" | custom-call | flops 1000000000 | bytes 10000000 | tf_op jit(solution)/shard_map/backward_first/pallas_call | solution.py:231
  140.9 8.2 %backward_rest.1 = (bf16[384,640]{1,0:T(8,128)(2,1)}, bf16[384,640]{1,0:T(8,128)(2,1)}, bf16[384,640]{1,0:T(8,128)(2,1)}) custom-call(f32[2,384,640]{2,1,0:T(8,128)} %get-tuple-element.19.by_wave, bf16[2560,640]{1,0:T(8,128)(2,1)} %wave_table.3.table_hbm.table, f32[3,1,640]{2,1,0:T(1,128)} %get-tuple-element.52.turn_cos, f32[3,1,640]{2,1,0:T(1,128)} %get-tuple-element.51.turn_sin), custom_call_target="tpu_custom_call" | custom-call | flops 3000000000 | bytes 10000000 | tf_op jit(solution)/shard_map/backward_rest/pallas_call | solution.py:261
  149.1 1.5 collective-permute-start.8
  150.6 0.4 collective-permute-start.6
  151.1 1.1 reshape.305
  152.2 0.1 bitcast_dynamic-update-slice_fusion.1
  152.3 11.1 %collective-permute-done.8.refs_2_ = bf16[384,640]{1,0:T(8,128)(2,1)S(1)} collective-permute-done((bf16[384,640]{1,0:T(8,128)(2,1)}, bf16[384,640]{1,0:T(8,128)(2,1)S(1)}, u32[]{:S(2)}, u32[]{:S(2)}) %collective-permute-start.8) | collective-permute-done | bytes 491552 | tf_op jit(solution)/shard_map/ppermute | solution.py:481
  163.4 0.8 copy-done.9
  164.2 3.0 %placed.2.refs_1_ = f32[4,384,640]{2,1,0:T(8,128)} custom-call(s32[3]{0:T(128)} %copy-done.14, bf16[384,640]{1,0:T(8,128)(2,1)} %get-tuple-element.21.refs_0_, bf16[384,640]{1,0:T(8,128)(2,1)} %copy-done.8, bf16[384,640]{1,0:T(8,128)(2,1)} %copy-done.9), custom_call_target="tpu_custom_call" | custom-call | tf_op jit(solution)/shard_map/placed/pallas_call | solution.py:288
  167.3 5.8 %collective-permute-done.6.refs_0_ = bf16[384,640]{1,0:T(8,128)(2,1)S(1)} collective-permute-done((bf16[384,640]{1,0:T(8,128)(2,1)}, bf16[384,640]{1,0:T(8,128)(2,1)S(1)}, u32[]{:S(2)}, u32[]{:S(2)}) %collective-permute-start.6) | collective-permute-done | bytes 491552 | tf_op jit(solution)/shard_map/ppermute | solution.py:481
  173.1 0.8 copy-done.7
  173.8 2.0 %placed.3 = f32[4,384,640]{2,1,0:T(8,128)} custom-call(s32[1]{0:T(128)} %bitcast.2.chosen, bf16[384,640]{1,0:T(8,128)(2,1)} %copy-done.7, f32[4,384,640]{2,1,0:T(8,128)} %placed.2.refs_1_), custom_call_target="tpu_custom_call", output_to_operand_aliasing={{}: (2, {})} | custom-call | tf_op jit(solution)/shard_map/placed/pallas_call | solution.py:288
  (50 shorter events, 0.3 us)
Async XLA Ops:
  1.3 12.3 %copy-start.14 = (s32[3]{0:T(128)}, s32[3]{0:T(128)S(1)}, u32[]{:S(2)}) copy-start(s32[3]{0:T(128)S(1)} %get-tuple-element.56.chosen) | copy-start | bytes 40
  4.9 5.3 %copy-start.17 = (bf16[384,640]{1,0:T(8,128)(2,1)S(1)}, bf16[384,640]{1,0:T(8,128)(2,1)}, u32[]{:S(2)}) copy-start(bf16[384,640]{1,0:T(8,128)(2,1)} %get-tuple-element.14) | copy-start | bytes 1474564
  4.9 5.3 %copy-start.3 = (f32[4,640]{1,0:T(4,128)S(1)}, f32[4,640]{1,0:T(4,128)}, u32[]{:S(2)}) copy-start(f32[4,640]{1,0:T(4,128)} %constant.207) | copy-start | bytes 30724
  4.9 5.9 %copy-start.2 = (f32[4,640]{1,0:T(4,128)S(1)}, f32[4,640]{1,0:T(4,128)}, u32[]{:S(2)}) copy-start(f32[4,640]{1,0:T(4,128)} %constant.208) | copy-start | bytes 30724
  4.9 7.3 %copy-start.10 = (s32[640]{0:T(1024)S(1)}, s32[640]{0:T(1024)}, u32[]{:S(2)}) copy-start(s32[640]{0:T(1024)} %param.23) | copy-start | bytes 7684
  5.0 13.4 %collective-permute-start.1 = (bf16[384,640]{1,0:T(8,128)(2,1)}, bf16[384,640]{1,0:T(8,128)(2,1)S(1)}, u32[]{:S(2)}, u32[]{:S(2)}) collective-permute-start(bf16[384,640]{1,0:T(8,128)(2,1)} %get-tuple-element.16), channel_id=1, source_target_pairs={{0,1},{1,0},{2,3},{3,2},{4,5},{5,4},{6,7},{7,6},{8,9},{9,8},{10,11... | collective-permute-start | bytes 1474568 | tf_op jit(solution)/shard_map/ppermute | solution.py:481
  7.6 14.9 %collective-permute-start.2 = (bf16[384,640]{1,0:T(8,128)(2,1)}, bf16[384,640]{1,0:T(8,128)(2,1)S(1)}, u32[]{:S(2)}, u32[]{:S(2)}) collective-permute-start(bf16[384,640]{1,0:T(8,128)(2,1)} %wind_products.3), channel_id=1, source_target_pairs={{0,2},{1,3},{2,0},{3,1},{4,6},{5,7},{6,4},{7,5},{8,10},{9,11},{10,... | collective-permute-start | bytes 1474568 | tf_op jit(solution)/shard_map/ppermute | solution.py:481
  10.2 22.2 %collective-permute-start = (bf16[384,640]{1,0:T(8,128)(2,1)S(1)}, bf16[384,640]{1,0:T(8,128)(2,1)S(1)}, u32[]{:S(2)}, u32[]{:S(2)}) collective-permute-start(bf16[384,640]{1,0:T(8,128)(2,1)S(1)} %copy-done.17), channel_id=1, source_target_pairs={{0,3},{1,2},{2,1},{3,0},{4,7},{5,6},{6,5},{7,4},{8,11},{9,10},{10,... | collective-permute-start | bytes 1474568 | tf_op jit(solution)/shard_map/ppermute | solution.py:481
  13.6 4.2 %copy-start.12 = (f32[4,1,640]{2,1,0:T(1,128)S(1)}, f32[4,1,640]{2,1,0:T(1,128)}, u32[]{:S(2)}) copy-start(f32[4,1,640]{2,1,0:T(1,128)} %constant.166.clone2.4) | copy-start | bytes 30724
  13.6 4.2 %copy-start.13 = (f32[4,1,640]{2,1,0:T(1,128)S(1)}, f32[4,1,640]{2,1,0:T(1,128)}, u32[]{:S(2)}) copy-start(f32[4,1,640]{2,1,0:T(1,128)} %constant.167.clone2.4) | copy-start | bytes 30724
  18.4 4.1 %copy-start.18 = (bf16[384,640]{1,0:T(8,128)(2,1)}, bf16[384,640]{1,0:T(8,128)(2,1)S(1)}, u32[]{:S(2)}) copy-start(bf16[384,640]{1,0:T(8,128)(2,1)S(1)} %collective-permute-done.1.refs_1_) | copy-start | bytes 1474564
  22.5 0.8 copy-start.19
  32.4 0.8 copy-start.6
  42.2 6.0 %copy-start.11 = (s32[640]{0:T(1024)S(1)}, s32[640]{0:T(1024)}, u32[]{:S(2)}) copy-start(s32[640]{0:T(1024)} %param.24) | copy-start | bytes 7684
  42.2 7.2 %copy-start.16 = (f32[4]{0:T(128)S(1)}, f32[4]{0:T(128)}, u32[]{:S(2)}) copy-start(f32[4]{0:T(128)} %param.25) | copy-start | bytes 52
  42.2 36.2 %all-to-all-start = ((bf16[32,150,128]{2,1,0:T(8,128)(2,1)}), bf16[32,150,128]{2,1,0:T(8,128)(2,1)S(1)}, u32[]{:S(2)}, u32[]{:S(2)}) async-start(bf16[32,150,128]{2,1,0:T(8,128)(2,1)} %forward.3), calls=%async_computation | async-start | bytes 2490368 | tf_op jit(solution)/shard_map/all_to_all | solution.py:532
  78.4 1.0 copy-start.1
  93.6 38.7 %all-to-all-start.1 = ((bf16[32,150,128]{2,1,0:T(8,128)(2,1)}), bf16[32,150,128]{2,1,0:T(8,128)(2,1)S(1)}, u32[]{:S(2)}, u32[]{:S(2)}) async-start(bf16[32,150,128]{2,1,0:T(8,128)(2,1)} %get-tuple-element.18), calls=%async_computation.1 | async-start | bytes 2490368 | tf_op jit(solution)/shard_map/all_to_all | solution.py:537
  102.1 4.7 %copy-start.15 = (s32[3]{0:T(128)S(1)}, s32[3]{0:T(128)}, u32[]{:S(2)}) copy-start(s32[3]{0:T(128)} %get-tuple-element.40.chosen) | copy-start | bytes 40
  102.2 6.1 %copy-start.5 = (f32[4,25,4,640]{3,2,1,0:T(4,128)S(1)}, f32[4,25,4,640]{3,2,1,0:T(4,128)}, u32[]{:S(2)}) copy-start(f32[4,25,4,640]{3,2,1,0:T(4,128)} %get-tuple-element.17) | copy-start | bytes 3072004
  108.6 9.4 %collective-permute-start.3 = (bf16[25,4,640]{2,1,0:T(4,128)(2,1)S(1)}, bf16[25,4,640]{2,1,0:T(4,128)(2,1)S(1)}, u32[]{:S(2)}, u32[]{:S(2)}) collective-permute-start(bf16[25,4,640]{2,1,0:T(4,128)(2,1)S(1)} %get-tuple-element.46), channel_id=1, source_target_pairs={{0,2},{1,3},{2,0},{3,1},{4,6},{5,7},{6,4},{7,5},{8,10},{9,11},{10,... | collective-permute-start | bytes 384008 | tf_op jit(solution)/shard_map/ppermute | solution.py:481
  110.2 12.2 %collective-permute-start.4 = (bf16[25,4,640]{2,1,0:T(4,128)(2,1)S(1)}, bf16[25,4,640]{2,1,0:T(4,128)(2,1)S(1)}, u32[]{:S(2)}, u32[]{:S(2)}) collective-permute-start(bf16[25,4,640]{2,1,0:T(4,128)(2,1)S(1)} %get-tuple-element.45), channel_id=1, source_target_pairs={{0,3},{1,2},{2,1},{3,0},{4,7},{5,6},{6,5},{7,4},{8,11},{9,10},{10,... | collective-permute-start | bytes 384008 | tf_op jit(solution)/shard_map/ppermute | solution.py:481
  110.9 40.2 %collective-permute-start.5 = (bf16[25,4,640]{2,1,0:T(4,128)(2,1)S(1)}, bf16[25,4,640]{2,1,0:T(4,128)(2,1)}, u32[]{:S(2)}, u32[]{:S(2)}) collective-permute-start(bf16[25,4,640]{2,1,0:T(4,128)(2,1)S(1)} %get-tuple-element.44), channel_id=1, source_target_pairs={{0,1},{1,0},{2,3},{3,2},{4,5},{5,4},{6,7},{7,6},{8,9},{9,8},{10,11... | collective-permute-start | bytes 384008 | tf_op jit(solution)/shard_map/ppermute | solution.py:481
  132.3 1.0 copy-start
  149.1 3.2 %collective-permute-start.7 = (bf16[384,640]{1,0:T(8,128)(2,1)}, bf16[384,640]{1,0:T(8,128)(2,1)S(1)}, u32[]{:S(2)}, u32[]{:S(2)}) collective-permute-start(bf16[384,640]{1,0:T(8,128)(2,1)} %get-tuple-element.22), channel_id=1, source_target_pairs={{0,1},{1,0},{2,3},{3,2},{4,5},{5,4},{6,7},{7,6},{8,9},{9,8},{10,11... | collective-permute-start | bytes 1474568 | tf_op jit(solution)/shard_map/ppermute | solution.py:481
  149.1 14.3 %collective-permute-start.8 = (bf16[384,640]{1,0:T(8,128)(2,1)}, bf16[384,640]{1,0:T(8,128)(2,1)S(1)}, u32[]{:S(2)}, u32[]{:S(2)}) collective-permute-start(bf16[384,640]{1,0:T(8,128)(2,1)} %get-tuple-element.23), channel_id=1, source_target_pairs={{0,2},{1,3},{2,0},{3,1},{4,6},{5,7},{6,4},{7,5},{8,10},{9,11},{10,... | collective-permute-start | bytes 1474568 | tf_op jit(solution)/shard_map/ppermute | solution.py:481
  150.6 22.4 %collective-permute-start.6 = (bf16[384,640]{1,0:T(8,128)(2,1)}, bf16[384,640]{1,0:T(8,128)(2,1)S(1)}, u32[]{:S(2)}, u32[]{:S(2)}) collective-permute-start(bf16[384,640]{1,0:T(8,128)(2,1)} %get-tuple-element.20), channel_id=1, source_target_pairs={{0,3},{1,2},{2,1},{3,0},{4,7},{5,6},{6,5},{7,4},{8,11},{9,10},{10,... | collective-permute-start | bytes 1474568 | tf_op jit(solution)/shard_map/ppermute | solution.py:481
  152.3 15.0 %copy-start.4 = (f32[100,1,2,2,640]{4,3,2,1,0:T(2,128)}, f32[100,1,2,2,640]{4,3,2,1,0:T(2,128)S(1)}, u32[]{:S(2)}) copy-start(f32[100,1,2,2,640]{4,3,2,1,0:T(2,128)S(1)} %bitcast_dynamic-update-slice_fusion) | copy-start | bytes 3072004
  152.3 11.1 %copy-start.8 = (bf16[384,640]{1,0:T(8,128)(2,1)}, bf16[384,640]{1,0:T(8,128)(2,1)S(1)}, u32[]{:S(2)}) copy-start(bf16[384,640]{1,0:T(8,128)(2,1)S(1)} %collective-permute-done.7.refs_1_) | copy-start | bytes 1474564
  163.4 0.8 copy-start.9
  173.1 0.8 copy-start.7

commit v4 on v3

--- a/solution.py
+++ b/solution.py
@@ -9,9 +9,13 @@
 from jax.experimental.pallas import tpu as pltpu
 from jax.sharding import PartitionSpec as P
 
+
 BF16 = jnp.bfloat16
 F32 = jnp.float32
-VMEM_LIMIT = 60 * 1024 * 1024
+MIB = 1024 * 1024
+VMEM_LIMIT = 24 * MIB
+LEGENDRE_LIMIT = 36 * MIB
+WHOLE_LIMIT = 60 * MIB
 STEP = 128
 LANES = 128
 DEPTH = 3
@@ -58,7 +62,7 @@
     return pl.pallas_call(
         functools.partial(table_kernel, interleaved),
         out_shape=jax.ShapeDtypeStruct(shape, BF16),
-        compiler_params=pltpu.CompilerParams(vmem_limit_bytes=VMEM_LIMIT),
+        compiler_params=pltpu.CompilerParams(vmem_limit_bytes=WHOLE_LIMIT),
         name="wave_table",
     )(
         jnp.asarray(near_cos * scaling, F32),
@@ -73,16 +77,16 @@
     return tuple(jnp.asarray(np.round(turn, 12)[:, None, :], F32) for turn in both)
 
 
-def product_kernel(count, chosen, *refs):
+def product_kernel(count, chosen, mirror, *refs):
     winds, outs = refs[: 2 * count], refs[2 * count :]
     for i in range(count):
         u, v = winds[2 * i][0], winds[2 * i + 1][0]
         lat_rows = u.shape[0]
-        outs[i][:lat_rows] = (u * v).astype(BF16)
-        outs[i][lat_rows:] = (u * u - v * v).astype(BF16)
-
-
-def wind_products(wind_u, wind_v, chosen):
+        outs[i][:lat_rows] = dot(mirror[...], (u * v).astype(BF16)).astype(BF16)
+        outs[i][lat_rows:] = dot(mirror[...], (u * u - v * v).astype(BF16)).astype(BF16)
+
+
+def wind_products(wind_u, wind_v, mirror, chosen):
     _, lat_rows, columns = wind_u.shape
     count = chosen.shape[0]
     specs = [
@@ -95,13 +99,13 @@
         grid_spec=pltpu.PrefetchScalarGridSpec(
             num_scalar_prefetch=1,
             grid=(1,),
-            in_specs=specs,
+            in_specs=[pl.BlockSpec((lat_rows, lat_rows), lambda step, chosen: (0, 0))] + specs,
             out_specs=[pl.BlockSpec((2 * lat_rows, columns), lambda step, chosen: (0, 0))] * count,
         ),
         out_shape=[jax.ShapeDtypeStruct((2 * lat_rows, columns), BF16)] * count,
-        compiler_params=pltpu.CompilerParams(vmem_limit_bytes=VMEM_LIMIT),
+        compiler_params=pltpu.CompilerParams(vmem_limit_bytes=WHOLE_LIMIT),
         name="wind_products",
-    )(chosen, *[wind_u, wind_v] * count)
+    )(chosen, mirror, *[wind_u, wind_v] * count)
 
 
 def forward_kernel(count, begun, ends, *refs):
@@ -123,7 +127,7 @@
     if not ends:
         refs[0][0], refs[0][1] = real, imag
         return
-    one_hot, mirror, out, by_wave, by_slot = refs
+    one_hot, out, by_wave, by_slot = refs
     devices, wire_rows, lanes = out.shape
     padded = one_hot.shape[0] // devices
     blocks = 2 * rows // lanes
@@ -135,12 +139,11 @@
     @pl.when(step == pl.num_programs(0) - 1)
     def _():
         for part in range(2):
-            turned = dot(mirror[...], by_wave[part]).astype(BF16)
-            by_slot[:, part * rows : (part + 1) * rows] = dot(one_hot[...], turned, NT)
+            by_slot[:, part * rows : (part + 1) * rows] = dot(one_hot[...], by_wave[part], NT)
         for device in range(devices):
             own = by_slot[device * padded : (device + 1) * padded, :]
-            out[device] = jnp.concatenate(
-                [own[:share, block * lanes : (block + 1) * lanes] for block in range(blocks)], axis=0
+            out[device] = pack_rows(
+                [own[:share, block * lanes : (block + 1) * lanes] for block in range(blocks)]
             ).astype(BF16)
 
 
@@ -159,12 +162,12 @@
     if end is None:
         out_shape, out_spec, scratch = jax.ShapeDtypeStruct((2, rows, waves), F32), sum_spec, []
     else:
-        one_hot, mirror, share = end
+        one_hot, share = end
         slots = one_hot.shape[0]
         lanes = wire_lanes(rows)
         out = (slots // round_up(share, 8), share * (2 * rows // lanes), lanes)
-        args += [one_hot, mirror]
-        in_specs += [pl.BlockSpec((slots, waves), lambda i: (0, 0)), pl.BlockSpec((rows, rows), lambda i: (0, 0))]
+        args.append(one_hot)
+        in_specs.append(pl.BlockSpec((slots, waves), lambda i: (0, 0)))
         out_shape, out_spec = jax.ShapeDtypeStruct(out, BF16), pl.BlockSpec(out, lambda i: (0, 0, 0))
         scratch = [pltpu.VMEM((2, rows, waves), BF16), pltpu.VMEM((slots, 2 * rows), F32)]
     return pl.pallas_call(
@@ -187,8 +190,9 @@
     left = []
     for i in range(count):
         cos, sin = turn_cos[i], turn_sin[i]
-        real = by_wave[0] * cos - by_wave[1] * sin
-        minus = -(by_wave[0] * sin) - by_wave[1] * cos
+        own_real, own_imag = by_wave[0].astype(F32), by_wave[1].astype(F32)
+        real = own_real * cos - own_imag * sin
+        minus = -(own_real * sin) - own_imag * cos
         left.append(jnp.concatenate([real, minus], axis=1))
     left = jnp.concatenate(left, axis=0) if count > 1 else left[0]
     high = left.astype(BF16)
@@ -202,30 +206,28 @@
 def backward_first_kernel(exact, wire, table_hbm, turn_cos, turn_sin, one_hot, mirror, out, by_wave, by_slot, table, sem):
     table_copy = pltpu.make_async_copy(table_hbm, table, sem)
     table_copy.start()
-    devices, wire_rows, lanes = wire.shape
+    devices, _, lanes = wire.shape
     rows = out.shape[0]
     waves = one_hot.shape[0]
+    lat_rows = mirror.shape[0]
     padded = by_slot.shape[0] // devices
     blocks = 2 * rows // lanes
-    share = wire_rows // blocks
     for device in range(devices):
-        own = wire[device].astype(F32)
-        for block in range(blocks):
-            piece = own[block * share : (block + 1) * share]
-            if padded > share:
-                piece = jnp.concatenate([piece, jnp.zeros((padded - share, lanes), F32)], axis=0)
+        for block, piece in enumerate(unpack_rows(wire[device].astype(F32), blocks, padded)):
             by_slot[device * padded : (device + 1) * padded, block * lanes : (block + 1) * lanes] = piece.astype(BF16)
     wave_ids = lax.broadcasted_iota(jnp.int32, (1, waves), 1)
     weight = jnp.where(wave_ids == 0, 1.0, 2.0).astype(F32)
     for part in range(2):
         ordered = dot(one_hot[...], by_slot[:, part * rows : (part + 1) * rows]).astype(BF16)
-        by_wave[part] = dot(mirror[...], ordered, NT) * weight
+        for field in range(2):
+            own = slice(field * lat_rows, (field + 1) * lat_rows)
+            by_wave[part, own, :] = (dot(mirror[...], ordered[:, own], NT) * weight).astype(BF16)
     table_copy.wait()
     out[...] = sector_lines(exact, by_wave, table, turn_cos, turn_sin)
 
 
 def backward_first(wire, table, turns, one_hot, mirror, exact):
-    rows = mirror.shape[0]
+    rows = 2 * mirror.shape[0]
     waves, slots = one_hot.shape
     vmem, hbm = pl.BlockSpec(memory_space=pltpu.VMEM), pl.BlockSpec(memory_space=pl.ANY)
     return pl.pallas_call(
@@ -234,7 +236,7 @@
         out_specs=[vmem, vmem],
         out_shape=[
             jax.ShapeDtypeStruct((rows, table.shape[1]), BF16),
-            jax.ShapeDtypeStruct((2, rows, waves), F32),
+            jax.ShapeDtypeStruct((2, rows, waves), BF16),
         ],
         scratch_shapes=[
             pltpu.VMEM((slots, 2 * rows), BF16),
@@ -264,7 +266,7 @@
         out_specs=[vmem] * count,
         out_shape=[jax.ShapeDtypeStruct((rows, table.shape[1]), BF16)] * count,
         cost_estimate=pl.CostEstimate(flops=3 * 10**9, bytes_accessed=10**7, transcendentals=0),
-        compiler_params=pltpu.CompilerParams(vmem_limit_bytes=VMEM_LIMIT),
+        compiler_params=pltpu.CompilerParams(vmem_limit_bytes=WHOLE_LIMIT),
         name="backward_rest",
     )(by_wave, table, *turns)
 
@@ -272,10 +274,13 @@
 def placing_kernel(count, chosen, *refs):
     blocks, (out, wide, sems) = refs[:count], refs[-3:]
     copies = []
+    rows, parts = wide.shape[1], sems.shape[1]
     for i in range(count):
-        wide[i] = blocks[i][...].astype(F32)
-        copies.append(pltpu.make_async_copy(wide.at[i], out.at[chosen[i]], sems.at[i]))
-        copies[-1].start()
+        for part in range(parts):
+            own = pl.ds(part * (rows // parts), rows // parts)
+            wide[i, own] = blocks[i][own].astype(F32)
+            copies.append(pltpu.make_async_copy(wide.at[i, own], out.at[chosen[i], own], sems.at[i, part]))
+            copies[-1].start()
     for copy in copies:
         copy.wait()
 
@@ -283,6 +288,7 @@
 def placed(blocks, chosen, total, earlier=None):
     count = len(blocks)
     shape = blocks[0].shape
+    parts = 4 if shape[0] % 64 == 0 else 1
     smem, vmem, hbm = (pl.BlockSpec(memory_space=space) for space in (pltpu.SMEM, pltpu.VMEM, pl.ANY))
     more = () if earlier is None else (earlier,)
     return pl.pallas_call(
@@ -290,7 +296,7 @@
         in_specs=[smem] + [vmem] * count + [hbm] * len(more),
         out_specs=hbm,
         out_shape=jax.ShapeDtypeStruct((total,) + shape, F32),
-        scratch_shapes=[pltpu.VMEM((count,) + shape, F32), pltpu.SemaphoreType.DMA((count,))],
+        scratch_shapes=[pltpu.VMEM((count,) + shape, F32), pltpu.SemaphoreType.DMA((count, parts))],
         input_output_aliases={1 + count: 0} if more else {},
         compiler_params=pltpu.CompilerParams(vmem_limit_bytes=VMEM_LIMIT),
         name="placed",
@@ -301,11 +307,33 @@
     return -(-value // unit) * unit
 
 
+def pack_rows(pieces):
+    share = pieces[0].shape[0]
+    main = share // 8 * 8
+    parts = [piece[:main] for piece in pieces] if main else []
+    parts += [piece[main:] for piece in pieces] if main < share else []
+    return jnp.concatenate(parts, axis=0) if len(parts) > 1 else parts[0]
+
+
+def unpack_rows(value, count, fill):
+    share = value.shape[0] // count
+    main = share // 8 * 8
+    rest = share - main
+    pieces = []
+    for i in range(count):
+        parts = [value[i * main : (i + 1) * main]] if main else []
+        parts += [value[count * main + i * rest : count * main + (i + 1) * rest]] if rest else []
+        parts += [jnp.zeros((fill - share, value.shape[1]), value.dtype)] if fill > share else []
+        pieces.append(jnp.concatenate(parts, axis=0) if len(parts) > 1 else parts[0])
+    return pieces
+
+
 def wire_lanes(rows):
     return LANES if 2 * rows % LANES == 0 else 2 * rows
 
 
-def legendre_kernel(sides, lat_rows, group, place, order, blocks, received, damping, basis, spectral, returned, held, buffer, sems):
+def legendre_kernel(sides, lat_rows, group, place, order, blocks, received, damping, basis, *rest):
+    spectral_out, returned_out, spectral, returned, held, buffer, sems, out_sems, spectral_sem = rest
     devices, wire_rows, lanes = received.shape
     sectors, share = spectral.shape[:2]
     slots, degrees, half_lat = basis.shape
@@ -318,6 +346,7 @@
     groups = share // group
     most = degrees // STEP
     scale = 1.0 / math.sqrt(degrees)
+    out_step = devices // out_sems.shape[0]
 
     def copies(index, count):
         ring = lax.rem(index, DEPTH)
@@ -356,11 +385,9 @@
             column += width
 
     for device in range(devices):
-        own = received[device].astype(F32)
-        for wire_block in range(wire_blocks):
-            piece = own[wire_block * share : (wire_block + 1) * share]
+        for wire_block, piece in enumerate(unpack_rows(received[device].astype(F32), wire_blocks, stride)):
             for at, width, row, block, lane in wire_pieces(device, wire_block):
-                held[block, row : row + share, lane : lane + width] = piece[:, at : at + width]
+                held[block, row : row + stride, lane : lane + width] = piece[:, at : at + width]
 
     def load_slot(slot):
         rows = pl.ds(slot, 2 * combos, stride=stride)
@@ -410,6 +437,9 @@
 
     lax.fori_loop(0, groups, loop_body, 0)
 
+    spectral_copy = pltpu.make_async_copy(spectral, spectral_out, spectral_sem)
+    spectral_copy.start()
+    out_copies = []
     for device in range(devices):
         pieces = []
         for wire_block in range(wire_blocks):
@@ -418,7 +448,15 @@
                 for _, width, row, block, lane in wire_pieces(device, wire_block)
             ]
             pieces.append(jnp.concatenate(parts, axis=1) if len(parts) > 1 else parts[0])
-        returned[device] = jnp.concatenate(pieces, axis=0).astype(BF16)
+        returned[device] = pack_rows(pieces).astype(BF16)
+        if (device + 1) % out_step == 0:
+            part = pl.ds(device + 1 - out_step, out_step)
+            out_copies.append(
+                pltpu.make_async_copy(returned.at[part], returned_out.at[part], out_sems.at[device // out_step])
+            )
+            out_copies[-1].start()
+    for copy in (*out_copies, spectral_copy):
+        copy.wait()
 
 
 def legendre(received, basis, damping, place, order, blocks, sectors, sides, lat_rows, group):
@@ -429,22 +467,26 @@
     return pl.pallas_call(
         functools.partial(legendre_kernel, sides, lat_rows, group),
         in_specs=[smem, smem, smem, vmem, vmem, hbm],
-        out_specs=[vmem, vmem],
+        out_specs=[pl.BlockSpec(memory_space=pltpu.HBM)] * 2,
         out_shape=[
             jax.ShapeDtypeStruct((sectors, share, sides, degrees), F32),
             jax.ShapeDtypeStruct(received.shape, BF16),
         ],
         scratch_shapes=[
+            pltpu.VMEM((sectors, share, sides, degrees), F32),
+            pltpu.VMEM(received.shape, BF16),
             pltpu.VMEM((half_lat // LANES, 2 * combos * round_up(share, 8), LANES), F32),
             pltpu.VMEM((DEPTH, group, degrees, half_lat), BF16),
             pltpu.SemaphoreType.DMA((DEPTH, group)),
+            pltpu.SemaphoreType.DMA((8,)),
+            pltpu.SemaphoreType.DMA,
         ],
         cost_estimate=pl.CostEstimate(
             flops=4 * share * degrees * half_lat * 2 * combos,
             bytes_accessed=2 * share * degrees * half_lat,
             transcendentals=0,
         ),
-        compiler_params=pltpu.CompilerParams(vmem_limit_bytes=VMEM_LIMIT),
+        compiler_params=pltpu.CompilerParams(vmem_limit_bytes=LEGENDRE_LIMIT),
         name="legendre",
     )(place, order, blocks, received, damping, basis)
 
@@ -471,7 +513,6 @@
     waves = wave_slots.shape[0]
     slot_total = capacity * owners
     assert levels == sectors and sectors & (sectors - 1) == 0
-    rows = 2 * lat_rows
     share = -(-capacity // sectors)
     padded = round_up(share, 8)
     length = sectors * lon_cols
@@ -484,8 +525,20 @@
         return jnp.stack([sector_index ^ mask for mask in some]).astype(jnp.int32)
 
     far, rest = masks[:1], masks[1:]
-    sent = list(wind_products(wind_u, wind_v, partners(far))) + list(wind_products(wind_u, wind_v, partners(rest)))
-    lines = {mask: across(value, mask) for mask, value in zip(masks, sent)}
+    row_ids = jnp.arange(lat_rows, dtype=jnp.int32)
+    south = owner_index >= owners // 2
+    mirror = (row_ids[:, None] == jnp.where(south, lat_rows - 1 - row_ids, row_ids)[None, :]).astype(BF16)
+
+    def exchanged(first, others):
+        arrived = {mask: across(value, mask) for mask, value in zip(far, first)}
+        made = others()
+        arrived.update({mask: across(value, mask) for mask, value in zip(rest, made)})
+        return arrived
+
+    lines = exchanged(
+        wind_products(wind_u, wind_v, mirror, partners(far)),
+        lambda: wind_products(wind_u, wind_v, mirror, partners(rest)),
+    )
 
     slot_ids = jnp.arange(slot_total, dtype=jnp.int32)
     wave_ids = jnp.arange(waves, dtype=jnp.int32)
@@ -495,10 +548,6 @@
     named = jnp.where((place_slot < share) & (in_owner < capacity), place_owner * capacity + in_owner, -1)
     one_hot = (named[:, None] == wave_slots[None, :]).astype(BF16)
     one_hot_turned = (wave_slots[:, None] == named[None, :]).astype(BF16)
-    row_ids = jnp.arange(rows, dtype=jnp.int32)
-    mirrored = row_ids // lat_rows * lat_rows + (lat_rows - 1 - row_ids % lat_rows)
-    south = owner_index >= owners // 2
-    mirror = (row_ids[:, None] == jnp.where(south, mirrored, row_ids)[None, :]).astype(BF16)
     forward_table = wave_table(lon_cols, waves, length, True)
     backward_table = wave_table(waves, lon_cols, length, False)
     turns = sector_turns(sectors, waves)
@@ -528,7 +577,7 @@
     by_arrival = list(dict.fromkeys(by_arrival))
     early, late = by_arrival[:-1], by_arrival[-1:]
     sums = forward([lines[mask] for mask in early], forward_table, turns_of(early))
-    fourier = forward([lines[mask] for mask in late], forward_table, turns_of(late), sums, (one_hot, mirror, share))
+    fourier = forward([lines[mask] for mask in late], forward_table, turns_of(late), sums, (one_hot, share))
     received = lax.all_to_all(fourier, ("lat", "lon"), split_axis=0, concat_axis=0, tiled=True)
     place = jnp.stack([first, sector_index]).astype(jnp.int32)
     spectral, returned = legendre(
@@ -543,8 +592,8 @@
 
     exact = sectors in (1, 2, 4)
     far_lines, by_wave = backward_first(regrouped, backward_table, turns_of(far), one_hot_turned, mirror, exact)
-    made = [far_lines, *backward_rest(by_wave, backward_table, turns_of(rest), exact)]
-    back = {mask: across(value, mask) for mask, value in zip(masks, made)}
+    rest_turns = turns_of(rest)
+    back = exchanged([far_lines], lambda: backward_rest(by_wave, backward_table, rest_turns, exact))
     tendency = placed([back[mask] for mask in early], partners(early), sectors)
     tendency = placed([back[mask] for mask in late], partners(late), sectors, tendency)
     return coefficients[:capacity], tendency.reshape(levels, 2, lat_rows, lon_cols)

time: 176 us -> 170 us (0.966)
  local copies, waits for them, and re-layouts: 9.93 us -> 18.4 us
  Pallas kernels: 64.3 us -> 56.7 us
  other arithmetic: 10.1 us -> 5.86 us
  starting transfers between devices: 21.7 us -> 19.8 us
    pallas_call x2, Pallas kernels: 16.7 us -> 10.5 us  [forward(): pl.pallas_call(functools.partial(forward_kernel, len(lines), earlier is n...]
    all_to_all x1, waiting for transfers between devices: 9.42 us -> 5.7 us  [body(): lax.all_to_all(returned, ('lat', 'lon'), split_axis=0, concat_axis=0, til...]
    dynamic_update_slice x4, local copies, waits for them, and re-layouts: 0.27 us -> 3.86 us  [body(): lax.dynamic_update_slice_in_dim(coefficients, own, (sector_index ^ mask)...]
    reshape x3, local copies, waits for them, and re-layouts: 1.43 us -> 4.68 us  [body(): across(spectral[mask].astype(BF16), mask).astype(F32)]
    all_to_all x1, waiting for transfers between devices: 26.4 us -> 28.9 us  [body(): lax.all_to_all(fourier, ('lat', 'lon'), split_axis=0, concat_axis=0, tile...]
    all_to_all x1, starting transfers between devices: 8.53 us -> 6.62 us  [body(): lax.all_to_all(returned, ('lat', 'lon'), split_axis=0, concat_axis=0, til...]
    pallas_call x2, Pallas kernels: 5.06 us -> 3.23 us  [placed(): pl.pallas_call(functools.partial(placing_kernel, count), in_specs=[smem]...]
    unnamed x40 -> x38, local copies, waits for them, and re-layouts: 5.27 us -> 4.28 us
  transfers between devices with their start and end apart: 11 -> 11, of which waited for: 8 -> 8; matrix products, arithmetic and copies ran while one was open for 8% -> 11% of each run, Pallas kernels for 20% -> 19%
where the time goes in v4:
time: 170 us; the launch traced here: 169 us
  waiting for transfers between devices  67.3 us (40%)
  Pallas kernels  56.7 us (33%)
  starting transfers between devices  19.8 us (12%)
  local copies, waits for them, and re-layouts  18.4 us (11%)
  other arithmetic  5.86 us (3%)
    ppermute x9, waiting for transfers between devices, across(): lax.ppermute(value, 'lon', [(i, i ^ mask) for i in range(sectors)])  32.7 us
    all_to_all x1, waiting for transfers between devices, body(): lax.all_to_all(fourier, ('lat', 'lon'), split_axis=0, concat_axis=0, tile...  28.9 us
    pallas_call x1, Pallas kernels, legendre(): pl.pallas_call(functools.partial(legendre_kernel, sides, lat_rows, group)...  14.4 us
    pallas_call x2, Pallas kernels, forward(): pl.pallas_call(functools.partial(forward_kernel, len(lines), earlier is n...  10.5 us
    pallas_call x1, Pallas kernels, backward_rest(): pl.pallas_call(functools.partial(backward_rest_kernel, exact), in_specs=[...  7.92 us
    pallas_call x1, Pallas kernels, backward_first(): pl.pallas_call(functools.partial(backward_first_kernel, exact), in_specs=...  7.4 us
    ppermute x9, starting transfers between devices, across(): lax.ppermute(value, 'lon', [(i, i ^ mask) for i in range(sectors)])  7.18 us
    pallas_call x2, Pallas kernels, wave_table(): pl.pallas_call(functools.partial(table_kernel, interleaved), out_shape=ja...  6.96 us
  transfers between devices with their start and end apart: 11, of which 8 were waited for; matrix products, arithmetic and copies ran while one was open for 11% of the time, Pallas kernels for 19%

profile of v4, /device:TPU:0, one launch (start us, length us, event | category | flops | bytes accessed | tf_op | source)
XLA Modules:
  0.0 169.1 jit_solution(5756973563599789871)
XLA Ops:
  0.7 0.7 fusion.mirror
  1.3 0.7 compare_select_fusion.2
  2.0 3.9 %wind_products.2 = (bf16[384,640]{1,0:T(8,128)(2,1)}, bf16[384,640]{1,0:T(8,128)(2,1)}, bf16[384,640]{1,0:T(8,128)(2,1)}) custom-call(s32[3]{0:T(128)} %get-tuple-element.40.chosen, bf16[192,192]{1,0:T(8,128)(2,1)} %fusion.mirror, f32[4,192,640]{2,1,0:T(8,128)} %refs_0_.3, f32[4,192,640]{2,1,0:T(8,128)} %refs_1_.3, f32[4,192,640]{2,1,0:T(8,128)} %refs_0_.3, ...), custom_call_target="tpu_custom_call" | custom-call | tf_op jit(solution)/shard_map/wind_products/pallas_call | solution.py:97
  5.9 0.6 collective-permute-start.1
  6.5 2.3 %wind_products.3 = bf16[384,640]{1,0:T(8,128)(2,1)} custom-call(s32[1]{0:T(128)} %bitcast.6.chosen, bf16[192,192]{1,0:T(8,128)(2,1)} %fusion.mirror, f32[4,192,640]{2,1,0:T(8,128)} %refs_0_.3, f32[4,192,640]{2,1,0:T(8,128)} %refs_1_.3), custom_call_target="tpu_custom_call" | custom-call | tf_op jit(solution)/shard_map/wind_products/pallas_call | solution.py:97
  8.8 2.6 %collective-permute-start.2 = (bf16[384,640]{1,0:T(8,128)(2,1)}, bf16[384,640]{1,0:T(8,128)(2,1)S(1)}, u32[]{:S(2)}, u32[]{:S(2)}) collective-permute-start(bf16[384,640]{1,0:T(8,128)(2,1)} %wind_products.3), channel_id=1, source_target_pairs={{0,2},{1,3},{2,0},{3,1},{4,6},{5,7},{6,4},{7,5},{8,10},{9,11},{10,... | collective-permute-start | bytes 1474568 | tf_op jit(solution)/shard_map/ppermute | solution.py:522
  11.4 0.0 collective-permute-start
  11.4 0.6 gather_fusion
  12.0 0.6 gather_fusion.1
  12.6 0.3 compare_convert_fusion.1.refs_5_
  12.9 0.0 copy-start.14
  12.9 0.0 copy-start.15
  12.9 0.1 broadcast_select_fusion.2
  13.0 3.5 %wave_table.2.refs_3_.refs_1_ = bf16[1280,1280]{1,0:T(8,128)(2,1)} custom-call(f32[32,640]{1,0:T(8,128)} %constant.144.clone.near_cos, f32[32,640]{1,0:T(8,128)} %constant.145.clone.near_sin, f32[20,1,640]{2,1,0:T(1,128)} %constant.146.clone.far_cos, f32[20,1,640]{2,1,0:T(1,128)} %constant.147.clone.far_sin), custom_call_target="tpu_custom_call" | custom-call | tf_op jit(solution)/shard_map/wave_table/pallas_call | solution.py:62
  16.6 7.1 %collective-permute-done.2.refs_2_ = bf16[384,640]{1,0:T(8,128)(2,1)S(1)} collective-permute-done((bf16[384,640]{1,0:T(8,128)(2,1)}, bf16[384,640]{1,0:T(8,128)(2,1)S(1)}, u32[]{:S(2)}, u32[]{:S(2)}) %collective-permute-start.2) | collective-permute-done | bytes 491552 | tf_op jit(solution)/shard_map/ppermute | solution.py:522
  23.7 1.9 %copy-done.1 = bf16[1280,1280]{1,0:T(8,128)(2,1)S(1)} copy-done((bf16[1280,1280]{1,0:T(8,128)(2,1)S(1)}, bf16[1280,1280]{1,0:T(8,128)(2,1)}, u32[]{:S(2)}) %copy-start.1) | copy-done | bytes 3276824
  25.6 5.2 %forward.2.refs_4_ = f32[2,384,640]{2,1,0:T(8,128)S(1)} custom-call(bf16[384,640]{1,0:T(8,128)(2,1)S(1)} %copy-done.7, bf16[384,640]{1,0:T(8,128)(2,1)S(1)} %collective-permute-done.1.refs_1_, bf16[384,640]{1,0:T(8,128)(2,1)S(1)} %collective-permute-done.2.refs_2_, bf16[1280,1280]{1,0:T(8,128)(2,1)S(1)} %copy-done.1, ...), custom_call_target="tpu_custom_call" | custom-call | flops 3774873600 | bytes 10000000 | tf_op jit(solution)/shard_map/forward/pallas_call | solution.py:173
  30.8 2.8 %collective-permute-done.refs_0_ = bf16[384,640]{1,0:T(8,128)(2,1)S(1)} collective-permute-done((bf16[384,640]{1,0:T(8,128)(2,1)S(1)}, bf16[384,640]{1,0:T(8,128)(2,1)S(1)}, u32[]{:S(2)}, u32[]{:S(2)}) %collective-permute-start) | collective-permute-done | bytes 491552 | tf_op jit(solution)/shard_map/ppermute | solution.py:522
  33.6 5.3 %forward.3 = bf16[32,150,128]{2,1,0:T(8,128)(2,1)} custom-call(bf16[384,640]{1,0:T(8,128)(2,1)S(1)} %collective-permute-done.refs_0_, bf16[1280,1280]{1,0:T(8,128)(2,1)S(1)} %copy-done.2, f32[1,1,640]{2,1,0:T(1,128)S(1)} %get-tuple-element.57.refs_2_, f32[1,1,640]{2,1,0:T(1,128)S(1)} %get-tuple-element.48.refs_3_, f32[2,384,640]{2,1,0:T(8,128)S(1)} %forward.2.refs_4_, ...), custom_call_target="tpu_custom_call" | custom-call | flops 1258291200 | bytes 10000000 | tf_op jit(solution)/shard_map/forward/pallas_call | solution.py:173
  39.0 6.0 %all-to-all-start = ((bf16[32,150,128]{2,1,0:T(8,128)(2,1)}), bf16[32,150,128]{2,1,0:T(8,128)(2,1)S(1)}, u32[]{:S(2)}, u32[]{:S(2)}) async-start(bf16[32,150,128]{2,1,0:T(8,128)(2,1)} %forward.3), calls=%async_computation | async-start | bytes 2490368 | tf_op jit(solution)/shard_map/all_to_all | solution.py:581
  45.0 0.2 fusion.2
  45.2 0.2 convert_reduce_fusion
  45.4 0.1 select_reduce_fusion
  45.5 0.1 slice.19
  45.6 0.1 broadcast_in_dim.104
  45.6 0.1 mul.81
  45.7 0.1 pad_add_fusion.place
  45.8 0.1 iota_compare_fusion.1
  45.9 0.1 fusion.5
  46.0 0.3 multiply_select_fusion.damping
  46.3 28.9 %all-to-all-done.received = bf16[32,150,128]{2,1,0:T(8,128)(2,1)S(1)} async-done(((bf16[32,150,128]{2,1,0:T(8,128)(2,1)}), bf16[32,150,128]{2,1,0:T(8,128)(2,1)S(1)}, u32[]{:S(2)}, u32[]{:S(2)}) %all-to-all-start) | async-done | bytes 1228832 | tf_op jit(solution)/shard_map/all_to_all | solution.py:581
  75.2 14.4 %legendre.1 = (f32[4,25,4,640]{3,2,1,0:T(4,128)S(1)}, bf16[32,150,128]{2,1,0:T(8,128)(2,1)}) custom-call(s32[2]{0:T(128)S(1)} %pad_add_fusion.place, s32[25]{0:T(128)S(1)} %get-tuple-element.38.order, s32[5]{0:T(128)S(1)} %and_select_fusion.blocks, bf16[32,150,128]{2,1,0:T(8,128)(2,1)S(1)} %all-to-all-done.received, ...), custom_call_target="tpu_custom_call" | custom-call | flops 1572864000 | bytes 24576000 | tf_op jit(solution)/shard_map/legendre/pallas_call | solution.py:467
  89.6 6.6 %all-to-all-start.1 = ((bf16[32,150,128]{2,1,0:T(8,128)(2,1)}), bf16[32,150,128]{2,1,0:T(8,128)(2,1)}, u32[]{:S(2)}, u32[]{:S(2)}) async-start(bf16[32,150,128]{2,1,0:T(8,128)(2,1)} %get-tuple-element.18), calls=%async_computation.1 | async-start | bytes 2490368 | tf_op jit(solution)/shard_map/all_to_all | solution.py:586
  96.2 3.4 %wave_table.3.table_hbm.table = bf16[2560,640]{1,0:T(8,128)(2,1)} custom-call(f32[32,640]{1,0:T(8,128)} %constant.144.clone.near_cos, f32[32,640]{1,0:T(8,128)} %constant.145.clone.near_sin, f32[20,1,640]{2,1,0:T(1,128)} %constant.146.clone.far_cos, f32[20,1,640]{2,1,0:T(1,128)} %constant.147.clone.far_sin), custom_call_target="tpu_custom_call" | custom-call | tf_op jit(solution)/shard_map/wave_table/pallas_call | solution.py:62
  99.7 0.6 gather_fusion.2
  100.2 0.6 gather_fusion.3
  100.8 1.4 compare_convert_fusion.one_hot
  102.2 0.2 convert.10
  102.4 0.9 slice_convert_fusion
  103.3 1.5 collective-permute-start.3
  104.8 0.7 broadcast_select_fusion
  105.5 0.6 collective-permute-start.5
  106.1 1.8 %reshape.290 = f32[25,1,2,2,640]{4,3,2,0,1:T(2,128)} reshape(f32[1,25,4,640]{3,2,1,0:T(4,128)} %get-tuple-element.43) | data formatting | bytes 512000 | tf_op jit(solution)/shard_map/convert_element_type | solution.py:590
  108.0 4.7 %collective-permute-done.3 = bf16[25,4,640]{2,1,0:T(4,128)(2,1)} collective-permute-done((bf16[25,4,640]{2,1,0:T(4,128)(2,1)}, bf16[25,4,640]{2,1,0:T(4,128)(2,1)}, u32[]{:S(2)}, u32[]{:S(2)}) %collective-permute-start.3) | collective-permute-done | bytes 128032 | tf_op jit(solution)/shard_map/ppermute | solution.py:522
  112.6 1.8 %reshape.285 = f32[25,1,2,2,640]{4,3,2,0,1:T(2,128)} reshape(bf16[25,4,640]{2,1,0:T(4,128)(2,1)} %collective-permute-done.3) | data formatting | bytes 384000 | tf_op jit(solution)/shard_map/reshape | solution.py:590
  114.4 1.6 collective-permute-done.4
  116.0 1.8 %reshape.287 = f32[25,1,2,2,640]{4,3,2,0,1:T(2,128)} reshape(bf16[25,4,640]{2,1,0:T(4,128)(2,1)} %collective-permute-done.4) | data formatting | bytes 384000 | tf_op jit(solution)/shard_map/reshape | solution.py:590
  117.8 1.2 broadcast_in_dim.98
  119.0 1.7 bitcast_dynamic-update-slice_fusion.3
  120.7 5.7 %all-to-all-done.1.wire = bf16[32,150,128]{2,1,0:T(8,128)(2,1)} async-done(((bf16[32,150,128]{2,1,0:T(8,128)(2,1)}), bf16[32,150,128]{2,1,0:T(8,128)(2,1)}, u32[]{:S(2)}, u32[]{:S(2)}) %all-to-all-start.1) | async-done | bytes 1228832 | tf_op jit(solution)/shard_map/all_to_all | solution.py:586
  126.4 1.3 copy-done.3
  127.7 7.4 %backward_first.1 = (bf16[384,640]{1,0:T(8,128)(2,1)}, bf16[2,384,640]{2,1,0:T(8,128)(2,1)S(1)}) custom-call(bf16[32,150,128]{2,1,0:T(8,128)(2,1)} %all-to-all-done.1.wire, bf16[2560,640]{1,0:T(8,128)(2,1)S(1)} %copy-done, f32[1,1,640]{2,1,0:T(1,128)S(1)} %get-tuple-element.58.turn_cos, f32[1,1,640]{2,1,0:T(1,128)S(1)} %get-tuple-element.47.turn_sin, ...), custom_call_target="tpu_custom_call" | custom-call | flops 1000000000 | bytes 10000000 | tf_op jit(solution)/shard_map/backward_first/pallas_call | solution.py:233
  135.2 1.0 copy-done.6
  136.1 7.9 %backward_rest.1 = (bf16[384,640]{1,0:T(8,128)(2,1)}, bf16[384,640]{1,0:T(8,128)(2,1)}, bf16[384,640]{1,0:T(8,128)(2,1)}) custom-call(bf16[2,384,640]{2,1,0:T(8,128)(2,1)} %copy-done.6, bf16[2560,640]{1,0:T(8,128)(2,1)} %wave_table.3.table_hbm.table, f32[3,1,640]{2,1,0:T(1,128)} %get-tuple-element.52.turn_cos, f32[3,1,640]{2,1,0:T(1,128)} %get-tuple-element.51.turn_sin), custom_call_target="tpu_custom_call" | custom-call | flops 3000000000 | bytes 10000000 | tf_op jit(solution)/shard_map/backward_rest/pallas_call | solution.py:263
  144.1 1.5 collective-permute-start.8
  145.5 0.4 collective-permute-start.6
  145.9 0.7 bitcast_dynamic-update-slice_fusion.2
  146.6 1.1 reshape.289
  147.7 0.7 bitcast_dynamic-update-slice_fusion.1
  148.5 0.7 bitcast_dynamic-update-slice_fusion
  149.2 9.2 %collective-permute-done.8.refs_2_ = bf16[384,640]{1,0:T(8,128)(2,1)S(1)} collective-permute-done((bf16[384,640]{1,0:T(8,128)(2,1)}, bf16[384,640]{1,0:T(8,128)(2,1)S(1)}, u32[]{:S(2)}, u32[]{:S(2)}) %collective-permute-start.8) | collective-permute-done | bytes 491552 | tf_op jit(solution)/shard_map/ppermute | solution.py:522
  158.4 2.2 %placed.2.refs_1_ = f32[4,384,640]{2,1,0:T(8,128)} custom-call(s32[3]{0:T(128)S(1)} %get-tuple-element.56.chosen, bf16[384,640]{1,0:T(8,128)(2,1)S(1)} %copy-done.5, bf16[384,640]{1,0:T(8,128)(2,1)S(1)} %collective-permute-done.7.refs_1_, bf16[384,640]{1,0:T(8,128)(2,1)S(1)} %collective-permute-done.8.refs_2_), custom_call_target="tpu_custom_call" | custom-call | tf_op jit(solution)/shard_map/placed/pallas_call | solution.py:294
  160.6 7.4 %collective-permute-done.6.refs_0_ = bf16[384,640]{1,0:T(8,128)(2,1)S(1)} collective-permute-done((bf16[384,640]{1,0:T(8,128)(2,1)}, bf16[384,640]{1,0:T(8,128)(2,1)S(1)}, u32[]{:S(2)}, u32[]{:S(2)}) %collective-permute-start.6) | collective-permute-done | bytes 491552 | tf_op jit(solution)/shard_map/ppermute | solution.py:522
  168.0 1.0 placed.3
  (48 shorter events, 0.2 us)
Async XLA Ops:
  5.9 5.5 %copy-start.18 = (bf16[384,640]{1,0:T(8,128)(2,1)S(1)}, bf16[384,640]{1,0:T(8,128)(2,1)}, u32[]{:S(2)}) copy-start(bf16[384,640]{1,0:T(8,128)(2,1)} %get-tuple-element.14) | copy-start | bytes 1474564
  5.9 5.6 %copy-start.9 = (f32[4,640]{1,0:T(4,128)S(1)}, f32[4,640]{1,0:T(4,128)}, u32[]{:S(2)}) copy-start(f32[4,640]{1,0:T(4,128)} %constant.189) | copy-start | bytes 30724
  5.9 6.1 %copy-start.8 = (f32[4,640]{1,0:T(4,128)S(1)}, f32[4,640]{1,0:T(4,128)}, u32[]{:S(2)}) copy-start(f32[4,640]{1,0:T(4,128)} %constant.190) | copy-start | bytes 30724
  5.9 6.7 %copy-start.12 = (s32[640]{0:T(1024)S(1)}, s32[640]{0:T(1024)}, u32[]{:S(2)}) copy-start(s32[640]{0:T(1024)} %param.23) | copy-start | bytes 7684
  5.9 10.7 %collective-permute-start.1 = (bf16[384,640]{1,0:T(8,128)(2,1)}, bf16[384,640]{1,0:T(8,128)(2,1)S(1)}, u32[]{:S(2)}, u32[]{:S(2)}) collective-permute-start(bf16[384,640]{1,0:T(8,128)(2,1)} %get-tuple-element.16), channel_id=1, source_target_pairs={{0,1},{1,0},{2,3},{3,2},{4,5},{5,4},{6,7},{7,6},{8,9},{9,8},{10,11... | collective-permute-start | bytes 1474568 | tf_op jit(solution)/shard_map/ppermute | solution.py:522
  8.8 14.9 %collective-permute-start.2 = (bf16[384,640]{1,0:T(8,128)(2,1)}, bf16[384,640]{1,0:T(8,128)(2,1)S(1)}, u32[]{:S(2)}, u32[]{:S(2)}) collective-permute-start(bf16[384,640]{1,0:T(8,128)(2,1)} %wind_products.3), channel_id=1, source_target_pairs={{0,2},{1,3},{2,0},{3,1},{4,6},{5,7},{6,4},{7,5},{8,10},{9,11},{10,... | collective-permute-start | bytes 1474568 | tf_op jit(solution)/shard_map/ppermute | solution.py:522
  11.4 22.2 %collective-permute-start = (bf16[384,640]{1,0:T(8,128)(2,1)S(1)}, bf16[384,640]{1,0:T(8,128)(2,1)S(1)}, u32[]{:S(2)}, u32[]{:S(2)}) collective-permute-start(bf16[384,640]{1,0:T(8,128)(2,1)S(1)} %copy-done.18), channel_id=1, source_target_pairs={{0,3},{1,2},{2,1},{3,0},{4,7},{5,6},{6,5},{7,4},{8,11},{9,10},{10,... | collective-permute-start | bytes 1474568 | tf_op jit(solution)/shard_map/ppermute | solution.py:522
  12.9 3.7 %copy-start.14 = (f32[4,1,640]{2,1,0:T(1,128)S(1)}, f32[4,1,640]{2,1,0:T(1,128)}, u32[]{:S(2)}) copy-start(f32[4,1,640]{2,1,0:T(1,128)} %constant.148.clone2.4) | copy-start | bytes 30724
  12.9 3.7 %copy-start.15 = (f32[4,1,640]{2,1,0:T(1,128)S(1)}, f32[4,1,640]{2,1,0:T(1,128)}, u32[]{:S(2)}) copy-start(f32[4,1,640]{2,1,0:T(1,128)} %constant.149.clone2.4) | copy-start | bytes 30724
  12.9 10.8 %copy-start.7 = (bf16[384,640]{1,0:T(8,128)(2,1)S(1)}, bf16[384,640]{1,0:T(8,128)(2,1)}, u32[]{:S(2)}) copy-start(bf16[384,640]{1,0:T(8,128)(2,1)} %get-tuple-element.15.refs_0_) | copy-start | bytes 1474564
  23.7 1.9 %copy-start.1 = (bf16[1280,1280]{1,0:T(8,128)(2,1)S(1)}, bf16[1280,1280]{1,0:T(8,128)(2,1)}, u32[]{:S(2)}) copy-start(bf16[1280,1280]{1,0:T(8,128)(2,1)} %wave_table.2.refs_3_.refs_1_) | copy-start | bytes 9830404
  25.6 8.0 %copy-start.2 = (bf16[1280,1280]{1,0:T(8,128)(2,1)S(1)}, bf16[1280,1280]{1,0:T(8,128)(2,1)}, u32[]{:S(2)}) copy-start(bf16[1280,1280]{1,0:T(8,128)(2,1)} %wave_table.2.refs_3_.refs_1_) | copy-start | bytes 9830404
  39.0 6.0 %copy-start.13 = (s32[640]{0:T(1024)S(1)}, s32[640]{0:T(1024)}, u32[]{:S(2)}) copy-start(s32[640]{0:T(1024)} %param.24) | copy-start | bytes 7684
  39.0 6.6 %copy-start.17 = (f32[4]{0:T(128)S(1)}, f32[4]{0:T(128)}, u32[]{:S(2)}) copy-start(f32[4]{0:T(128)} %param.25) | copy-start | bytes 52
  39.0 36.2 %all-to-all-start = ((bf16[32,150,128]{2,1,0:T(8,128)(2,1)}), bf16[32,150,128]{2,1,0:T(8,128)(2,1)S(1)}, u32[]{:S(2)}, u32[]{:S(2)}) async-start(bf16[32,150,128]{2,1,0:T(8,128)(2,1)} %forward.3), calls=%async_computation | async-start | bytes 2490368 | tf_op jit(solution)/shard_map/all_to_all | solution.py:581
  89.6 36.8 %all-to-all-start.1 = ((bf16[32,150,128]{2,1,0:T(8,128)(2,1)}), bf16[32,150,128]{2,1,0:T(8,128)(2,1)}, u32[]{:S(2)}, u32[]{:S(2)}) async-start(bf16[32,150,128]{2,1,0:T(8,128)(2,1)} %get-tuple-element.18), calls=%async_computation.1 | async-start | bytes 2490368 | tf_op jit(solution)/shard_map/all_to_all | solution.py:586
  96.2 4.6 %copy-start.16 = (s32[3]{0:T(128)S(1)}, s32[3]{0:T(128)}, u32[]{:S(2)}) copy-start(s32[3]{0:T(128)} %get-tuple-element.40.chosen) | copy-start | bytes 40
  102.4 24.0 %copy-start = (bf16[2560,640]{1,0:T(8,128)(2,1)S(1)}, bf16[2560,640]{1,0:T(8,128)(2,1)}, u32[]{:S(2)}) copy-start(bf16[2560,640]{1,0:T(8,128)(2,1)} %wave_table.3.table_hbm.table) | copy-start | bytes 9830404
  102.4 24.0 %copy-start.4 = (bf16[192,192]{1,0:T(8,128)(2,1)S(1)}, bf16[192,192]{1,0:T(8,128)(2,1)}, u32[]{:S(2)}) copy-start(bf16[192,192]{1,0:T(8,128)(2,1)} %fusion.mirror) | copy-start | bytes 221188
  103.3 9.3 %collective-permute-start.3 = (bf16[25,4,640]{2,1,0:T(4,128)(2,1)}, bf16[25,4,640]{2,1,0:T(4,128)(2,1)}, u32[]{:S(2)}, u32[]{:S(2)}) collective-permute-start(bf16[25,4,640]{2,1,0:T(4,128)(2,1)} %get-tuple-element.46), channel_id=1, source_target_pairs={{0,2},{1,3},{2,0},{3,1},{4,6},{5,7},{6,4},{7,5},{8,10},{9,11},{10,... | collective-permute-start | bytes 384008 | tf_op jit(solution)/shard_map/ppermute | solution.py:522
  104.8 11.2 %collective-permute-start.4 = (bf16[25,4,640]{2,1,0:T(4,128)(2,1)}, bf16[25,4,640]{2,1,0:T(4,128)(2,1)}, u32[]{:S(2)}, u32[]{:S(2)}) collective-permute-start(bf16[25,4,640]{2,1,0:T(4,128)(2,1)} %get-tuple-element.45), channel_id=1, source_target_pairs={{0,3},{1,2},{2,1},{3,0},{4,7},{5,6},{6,5},{7,4},{8,11},{9,10},{10,... | collective-permute-start | bytes 384008 | tf_op jit(solution)/shard_map/ppermute | solution.py:522
  105.5 41.2 %collective-permute-start.5 = (bf16[25,4,640]{2,1,0:T(4,128)(2,1)S(1)}, bf16[25,4,640]{2,1,0:T(4,128)(2,1)}, u32[]{:S(2)}, u32[]{:S(2)}) collective-permute-start(bf16[25,4,640]{2,1,0:T(4,128)(2,1)S(1)} %get-tuple-element.44), channel_id=1, source_target_pairs={{0,1},{1,0},{2,3},{3,2},{4,5},{5,4},{6,7},{7,6},{8,9},{9,8},{10,11... | collective-permute-start | bytes 384008 | tf_op jit(solution)/shard_map/ppermute | solution.py:522
  126.4 1.3 copy-start.3
  135.1 1.0 copy-start.6
  136.1 9.8 %copy-start.11 = (f32[25,1,2,2,640]{4,3,2,0,1:T(2,128)S(1)}, f32[25,1,2,2,640]{4,3,2,0,1:T(2,128)}, u32[]{:S(2)}) copy-start(f32[25,1,2,2,640]{4,3,2,0,1:T(2,128)} %reshape.287) | copy-start | bytes 768004
  136.1 12.3 %copy-start.10 = (f32[25,1,2,2,640]{4,3,2,0,1:T(2,128)S(1)}, f32[25,1,2,2,640]{4,3,2,0,1:T(2,128)}, u32[]{:S(2)}) copy-start(f32[25,1,2,2,640]{4,3,2,0,1:T(2,128)} %reshape.290) | copy-start | bytes 768004
  144.1 14.3 %copy-start.5 = (bf16[384,640]{1,0:T(8,128)(2,1)S(1)}, bf16[384,640]{1,0:T(8,128)(2,1)}, u32[]{:S(2)}) copy-start(bf16[384,640]{1,0:T(8,128)(2,1)} %get-tuple-element.21.refs_0_) | copy-start | bytes 1474564
  144.1 5.1 %collective-permute-start.7 = (bf16[384,640]{1,0:T(8,128)(2,1)}, bf16[384,640]{1,0:T(8,128)(2,1)S(1)}, u32[]{:S(2)}, u32[]{:S(2)}) collective-permute-start(bf16[384,640]{1,0:T(8,128)(2,1)} %get-tuple-element.22), channel_id=1, source_target_pairs={{0,1},{1,0},{2,3},{3,2},{4,5},{5,4},{6,7},{7,6},{8,9},{9,8},{10,11... | collective-permute-start | bytes 1474568 | tf_op jit(solution)/shard_map/ppermute | solution.py:522
  144.1 14.3 %collective-permute-start.8 = (bf16[384,640]{1,0:T(8,128)(2,1)}, bf16[384,640]{1,0:T(8,128)(2,1)S(1)}, u32[]{:S(2)}, u32[]{:S(2)}) collective-permute-start(bf16[384,640]{1,0:T(8,128)(2,1)} %get-tuple-element.23), channel_id=1, source_target_pairs={{0,2},{1,3},{2,0},{3,1},{4,6},{5,7},{6,4},{7,5},{8,10},{9,11},{10,... | collective-permute-start | bytes 1474568 | tf_op jit(solution)/shard_map/ppermute | solution.py:522
  145.5 22.4 %collective-permute-start.6 = (bf16[384,640]{1,0:T(8,128)(2,1)}, bf16[384,640]{1,0:T(8,128)(2,1)S(1)}, u32[]{:S(2)}, u32[]{:S(2)}) collective-permute-start(bf16[384,640]{1,0:T(8,128)(2,1)} %get-tuple-element.20), channel_id=1, source_target_pairs={{0,3},{1,2},{2,1},{3,0},{4,7},{5,6},{6,5},{7,4},{8,11},{9,10},{10,... | collective-permute-start | bytes 1474568 | tf_op jit(solution)/shard_map/ppermute | solution.py:522

commit v5 on v4

--- a/solution.py
+++ b/solution.py
@@ -77,35 +77,78 @@
     return tuple(jnp.asarray(np.round(turn, 12)[:, None, :], F32) for turn in both)
 
 
-def product_kernel(count, chosen, mirror, *refs):
-    winds, outs = refs[: 2 * count], refs[2 * count :]
-    for i in range(count):
-        u, v = winds[2 * i][0], winds[2 * i + 1][0]
-        lat_rows = u.shape[0]
-        outs[i][:lat_rows] = dot(mirror[...], (u * v).astype(BF16)).astype(BF16)
-        outs[i][lat_rows:] = dot(mirror[...], (u * u - v * v).astype(BF16)).astype(BF16)
-
-
-def wind_products(wind_u, wind_v, mirror, chosen):
+def chunk_widths(lat_rows):
+    main = lat_rows // LANES * LANES
+    return (main, lat_rows - main) if main and 2 * (lat_rows - main) == LANES else (lat_rows,)
+
+
+def chunk_start(widths, chunk, near):
+    if len(widths) == 1:
+        return 0
+    odd = near % 2
+    return odd * widths[1] if chunk == 0 else (1 - odd) * widths[0]
+
+
+def band_place(owner_index, owners):
+    south = owner_index >= owners // 2
+    return south, jnp.where(south, owners - 1 - owner_index, owner_index)
+
+
+def product_kernel(masks, widths, wind_u, wind_v, *refs):
+    outs, (space, sems) = refs[:-2], refs[-2:]
     _, lat_rows, columns = wind_u.shape
-    count = chosen.shape[0]
-    specs = [
-        pl.BlockSpec((1, lat_rows, columns), functools.partial(lambda i, step, chosen: (chosen[i], 0, 0), i))
-        for i in range(count)
-        for _ in range(2)
-    ]
-    return pl.pallas_call(
-        functools.partial(product_kernel, count),
-        grid_spec=pltpu.PrefetchScalarGridSpec(
-            num_scalar_prefetch=1,
-            grid=(1,),
-            in_specs=[pl.BlockSpec((lat_rows, lat_rows), lambda step, chosen: (0, 0))] + specs,
-            out_specs=[pl.BlockSpec((2 * lat_rows, columns), lambda step, chosen: (0, 0))] * count,
-        ),
-        out_shape=[jax.ShapeDtypeStruct((2 * lat_rows, columns), BF16)] * count,
+    south, near = band_place(lax.axis_index("lat"), lax.axis_size("lat"))
+    pieces = sems.shape[2]
+    size = columns // pieces
+    copies = {}
+    for i, mask in enumerate(masks):
+        level = lax.axis_index("lon") ^ mask
+        for piece in range(pieces):
+            own = pl.ds(piece * size, size)
+            for which, wind in enumerate((wind_u, wind_v)):
+                copy = pltpu.make_async_copy(
+                    wind.at[level, :, own], space.at[i, which, :, own], sems.at[i, which, piece]
+                )
+                copy.start()
+                copies[i, piece, which] = copy
+    chosen = []
+    for chunk, width in enumerate(widths):
+        start = chunk_start(widths, chunk, near)
+        ids = start + lax.broadcasted_iota(jnp.int32, (width, lat_rows), 0)
+        lats = lax.broadcasted_iota(jnp.int32, (width, lat_rows), 1)
+        chosen.append((lats == jnp.where(south, lat_rows - 1 - ids, ids)).astype(F32).astype(BF16))
+    for i in range(len(masks)):
+        for piece in range(pieces):
+            own = pl.ds(piece * size, size)
+            copies[i, piece, 0].wait()
+            copies[i, piece, 1].wait()
+            u, v = space[i, 0, :, own], space[i, 1, :, own]
+            for field, product in enumerate((u * v, u * u - v * v)):
+                product = product.astype(BF16)
+                for chunk, width in enumerate(widths):
+                    outs[i * len(widths) + chunk][field * width : (field + 1) * width, own] = dot(
+                        chosen[chunk], product
+                    ).astype(BF16)
+
+
+def wind_products(wind_u, wind_v, masks, widths):
+    _, lat_rows, columns = wind_u.shape
+    hbm, vmem = pl.BlockSpec(memory_space=pl.ANY), pl.BlockSpec(memory_space=pltpu.VMEM)
+    outs = pl.pallas_call(
+        functools.partial(product_kernel, masks, widths),
+        in_specs=[hbm, hbm],
+        out_specs=[vmem] * (len(masks) * len(widths)),
+        out_shape=[jax.ShapeDtypeStruct((2 * width, columns), BF16) for _ in masks for width in widths],
+        scratch_shapes=[
+            pltpu.VMEM((len(masks), 2, lat_rows, columns), F32),
+            pltpu.SemaphoreType.DMA((len(masks), 2, columns // LANES if columns % LANES == 0 else 1)),
+        ],
         compiler_params=pltpu.CompilerParams(vmem_limit_bytes=WHOLE_LIMIT),
         name="wind_products",
-    )(chosen, mirror, *[wind_u, wind_v] * count)
+    )(wind_u, wind_v)
+    return {
+        (chunk, mask): outs[i * len(widths) + chunk] for i, mask in enumerate(masks) for chunk in range(len(widths))
+    }
 
 
 def forward_kernel(count, begun, ends, *refs):
@@ -209,7 +252,7 @@
     devices, _, lanes = wire.shape
     rows = out.shape[0]
     waves = one_hot.shape[0]
-    lat_rows = mirror.shape[0]
+    width = mirror.shape[0]
     padded = by_slot.shape[0] // devices
     blocks = 2 * rows // lanes
     for device in range(devices):
@@ -220,7 +263,7 @@
     for part in range(2):
         ordered = dot(one_hot[...], by_slot[:, part * rows : (part + 1) * rows]).astype(BF16)
         for field in range(2):
-            own = slice(field * lat_rows, (field + 1) * lat_rows)
+            own = slice(field * width, (field + 1) * width)
             by_wave[part, own, :] = (dot(mirror[...], ordered[:, own], NT) * weight).astype(BF16)
     table_copy.wait()
     out[...] = sector_lines(exact, by_wave, table, turn_cos, turn_sin)
@@ -271,36 +314,44 @@
     )(by_wave, table, *turns)
 
 
-def placing_kernel(count, chosen, *refs):
-    blocks, (out, wide, sems) = refs[:count], refs[-3:]
+def placing_kernel(parts, widths, *refs):
+    blocks, (out, wide, sems) = refs[: len(parts)], refs[-3:]
+    _, rows, _ = out.shape
+    lat_rows = rows // 2
+    south, near = band_place(lax.axis_index("lat"), lax.axis_size("lat"))
     copies = []
-    rows, parts = wide.shape[1], sems.shape[1]
-    for i in range(count):
-        for part in range(parts):
-            own = pl.ds(part * (rows // parts), rows // parts)
+    for i, (chunk, mask) in enumerate(parts):
+        width = widths[chunk]
+        start = chunk_start(widths, chunk, near)
+        start = jnp.where(south, lat_rows - start - width, start)
+        level = lax.axis_index("lon") ^ mask
+        for field in range(2):
+            own = slice(field * width, (field + 1) * width)
             wide[i, own] = blocks[i][own].astype(F32)
-            copies.append(pltpu.make_async_copy(wide.at[i, own], out.at[chosen[i], own], sems.at[i, part]))
+            place = pl.ds(pl.multiple_of(field * lat_rows + start, math.gcd(*widths, lat_rows)), width)
+            copies.append(pltpu.make_async_copy(wide.at[i, own], out.at[level, place], sems.at[i, field]))
             copies[-1].start()
     for copy in copies:
         copy.wait()
 
 
-def placed(blocks, chosen, total, earlier=None):
-    count = len(blocks)
-    shape = blocks[0].shape
-    parts = 4 if shape[0] % 64 == 0 else 1
-    smem, vmem, hbm = (pl.BlockSpec(memory_space=space) for space in (pltpu.SMEM, pltpu.VMEM, pl.ANY))
+def placed(blocks, parts, widths, shape, earlier=None):
+    count = len(parts)
+    vmem, hbm = pl.BlockSpec(memory_space=pltpu.VMEM), pl.BlockSpec(memory_space=pl.ANY)
     more = () if earlier is None else (earlier,)
     return pl.pallas_call(
-        functools.partial(placing_kernel, count),
-        in_specs=[smem] + [vmem] * count + [hbm] * len(more),
+        functools.partial(placing_kernel, parts, widths),
+        in_specs=[vmem] * count + [hbm] * len(more),
         out_specs=hbm,
-        out_shape=jax.ShapeDtypeStruct((total,) + shape, F32),
-        scratch_shapes=[pltpu.VMEM((count,) + shape, F32), pltpu.SemaphoreType.DMA((count, parts))],
-        input_output_aliases={1 + count: 0} if more else {},
+        out_shape=jax.ShapeDtypeStruct(shape, F32),
+        scratch_shapes=[
+            pltpu.VMEM((count, 2 * max(widths[chunk] for chunk, _ in parts), shape[2]), F32),
+            pltpu.SemaphoreType.DMA((count, 2)),
+        ],
+        input_output_aliases={count: 0} if more else {},
         compiler_params=pltpu.CompilerParams(vmem_limit_bytes=VMEM_LIMIT),
         name="placed",
-    )(chosen, *blocks, *more)
+    )(*[blocks[part] for part in parts], *more)
 
 
 def round_up(value, unit):
@@ -332,9 +383,13 @@
     return LANES if 2 * rows % LANES == 0 else 2 * rows
 
 
-def legendre_kernel(sides, lat_rows, group, place, order, blocks, received, damping, basis, *rest):
-    spectral_out, returned_out, spectral, returned, held, buffer, sems, out_sems, spectral_sem = rest
-    devices, wire_rows, lanes = received.shape
+def legendre_kernel(sides, widths, group, place, order, blocks, damping, basis, *rest):
+    wires = len(widths)
+    received, rest = rest[:wires], rest[wires:]
+    spectral_out, returned_out, rest = rest[0], rest[1 : 1 + wires], rest[1 + wires :]
+    spectral, returned, (held, buffer, sems, out_sems, spectral_sem) = rest[0], rest[1 : 1 + wires], rest[1 + wires :]
+    lat_rows = sum(widths)
+    devices = received[0].shape[0]
     sectors, share = spectral.shape[:2]
     slots, degrees, half_lat = basis.shape
     sources = devices // sectors
@@ -342,11 +397,10 @@
     combos = sectors * sides
     lane_blocks = held.shape[0]
     stride = held.shape[1] // (2 * combos)
-    wire_blocks = wire_rows // share
     groups = share // group
     most = degrees // STEP
     scale = 1.0 / math.sqrt(degrees)
-    out_step = devices // out_sems.shape[0]
+    out_step = devices // out_sems.shape[1]
 
     def copies(index, count):
         ring = lax.rem(index, DEPTH)
@@ -371,23 +425,28 @@
     for index in range(min(DEPTH - 1, groups)):
         fetch(index)
 
-    def wire_pieces(device, wire_block):
+    def wire_pieces(wire, device, wire_block):
         source, sector = divmod(device, sectors)
         side, near = (0, source) if source < sources // 2 else (1, sources - 1 - source)
+        lanes, chunk_width = received[wire].shape[2], widths[wire]
+        begin = near * lat_rows + chunk_start(widths, wire, near)
         column, end = wire_block * lanes, (wire_block + 1) * lanes
         while column < end:
-            part_field, lat = divmod(column, lat_rows)
+            part_field, lat = divmod(column, chunk_width)
             part, field = divmod(part_field, fields)
             row = (side * combos + sector * sides + field * 2 + part) * stride
-            place = near * lat_rows + lat
-            width = min(end - column, lat_rows - lat, LANES - place % LANES)
-            yield column - wire_block * lanes, width, row, place // LANES, place % LANES
+            at = begin + lat
+            width = min(end - column, chunk_width - lat, LANES - at % LANES)
+            yield column - wire_block * lanes, width, row, at // LANES, at % LANES
             column += width
 
-    for device in range(devices):
-        for wire_block, piece in enumerate(unpack_rows(received[device].astype(F32), wire_blocks, stride)):
-            for at, width, row, block, lane in wire_pieces(device, wire_block):
-                held[block, row : row + stride, lane : lane + width] = piece[:, at : at + width]
+    for wire in range(wires):
+        wire_blocks = received[wire].shape[1] // share
+        for device in range(devices):
+            own_blocks = unpack_rows(received[wire][device].astype(F32), wire_blocks, stride)
+            for wire_block, piece in enumerate(own_blocks):
+                for at, width, row, block, lane in wire_pieces(wire, device, wire_block):
+                    held[block, row : row + stride, lane : lane + width] = piece[:, at : at + width]
 
     def load_slot(slot):
         rows = pl.ds(slot, 2 * combos, stride=stride)
@@ -440,45 +499,48 @@
     spectral_copy = pltpu.make_async_copy(spectral, spectral_out, spectral_sem)
     spectral_copy.start()
     out_copies = []
-    for device in range(devices):
-        pieces = []
-        for wire_block in range(wire_blocks):
-            parts = [
-                held[block, row : row + share, lane : lane + width]
-                for _, width, row, block, lane in wire_pieces(device, wire_block)
-            ]
-            pieces.append(jnp.concatenate(parts, axis=1) if len(parts) > 1 else parts[0])
-        returned[device] = pack_rows(pieces).astype(BF16)
-        if (device + 1) % out_step == 0:
-            part = pl.ds(device + 1 - out_step, out_step)
-            out_copies.append(
-                pltpu.make_async_copy(returned.at[part], returned_out.at[part], out_sems.at[device // out_step])
-            )
-            out_copies[-1].start()
+    for wire in range(wires):
+        wire_blocks = received[wire].shape[1] // share
+        for device in range(devices):
+            pieces = []
+            for wire_block in range(wire_blocks):
+                parts = [
+                    held[block, row : row + share, lane : lane + width]
+                    for _, width, row, block, lane in wire_pieces(wire, device, wire_block)
+                ]
+                pieces.append(jnp.concatenate(parts, axis=1) if len(parts) > 1 else parts[0])
+            returned[wire][device] = pack_rows(pieces).astype(BF16)
+            if (device + 1) % out_step == 0:
+                part = pl.ds(device + 1 - out_step, out_step)
+                copy = pltpu.make_async_copy(
+                    returned[wire].at[part], returned_out[wire].at[part], out_sems.at[wire, device // out_step]
+                )
+                copy.start()
+                out_copies.append(copy)
     for copy in (*out_copies, spectral_copy):
         copy.wait()
 
 
-def legendre(received, basis, damping, place, order, blocks, sectors, sides, lat_rows, group):
+def legendre(received, basis, damping, place, order, blocks, sectors, sides, widths, group):
     share = order.shape[0]
     degrees, half_lat = basis.shape[1:]
     combos = sectors * sides
     smem, vmem, hbm = (pl.BlockSpec(memory_space=space) for space in (pltpu.SMEM, pltpu.VMEM, pl.ANY))
     return pl.pallas_call(
-        functools.partial(legendre_kernel, sides, lat_rows, group),
-        in_specs=[smem, smem, smem, vmem, vmem, hbm],
-        out_specs=[pl.BlockSpec(memory_space=pltpu.HBM)] * 2,
+        functools.partial(legendre_kernel, sides, widths, group),
+        in_specs=[smem, smem, smem, vmem, hbm] + [vmem] * len(widths),
+        out_specs=[pl.BlockSpec(memory_space=pltpu.HBM)] * (1 + len(widths)),
         out_shape=[
             jax.ShapeDtypeStruct((sectors, share, sides, degrees), F32),
-            jax.ShapeDtypeStruct(received.shape, BF16),
+            *[jax.ShapeDtypeStruct(wire.shape, BF16) for wire in received],
         ],
         scratch_shapes=[
             pltpu.VMEM((sectors, share, sides, degrees), F32),
-            pltpu.VMEM(received.shape, BF16),
+            *[pltpu.VMEM(wire.shape, BF16) for wire in received],
             pltpu.VMEM((half_lat // LANES, 2 * combos * round_up(share, 8), LANES), F32),
             pltpu.VMEM((DEPTH, group, degrees, half_lat), BF16),
             pltpu.SemaphoreType.DMA((DEPTH, group)),
-            pltpu.SemaphoreType.DMA((8,)),
+            pltpu.SemaphoreType.DMA((len(widths), 8)),
             pltpu.SemaphoreType.DMA,
         ],
         cost_estimate=pl.CostEstimate(
@@ -488,7 +550,7 @@
         ),
         compiler_params=pltpu.CompilerParams(vmem_limit_bytes=LEGENDRE_LIMIT),
         name="legendre",
-    )(place, order, blocks, received, damping, basis)
+    )(place, order, blocks, damping, basis, *received)
 
 
 def degree_order(counts):
@@ -513,6 +575,7 @@
     waves = wave_slots.shape[0]
     slot_total = capacity * owners
     assert levels == sectors and sectors & (sectors - 1) == 0
+    rows = 2 * lat_rows
     share = -(-capacity // sectors)
     padded = round_up(share, 8)
     length = sectors * lon_cols
@@ -525,20 +588,19 @@
         return jnp.stack([sector_index ^ mask for mask in some]).astype(jnp.int32)
 
     far, rest = masks[:1], masks[1:]
-    row_ids = jnp.arange(lat_rows, dtype=jnp.int32)
-    south = owner_index >= owners // 2
-    mirror = (row_ids[:, None] == jnp.where(south, lat_rows - 1 - row_ids, row_ids)[None, :]).astype(BF16)
-
-    def exchanged(first, others):
-        arrived = {mask: across(value, mask) for mask, value in zip(far, first)}
-        made = others()
-        arrived.update({mask: across(value, mask) for mask, value in zip(rest, made)})
-        return arrived
-
-    lines = exchanged(
-        wind_products(wind_u, wind_v, mirror, partners(far)),
-        lambda: wind_products(wind_u, wind_v, mirror, partners(rest)),
-    )
+    widths = chunk_widths(lat_rows)
+    small_first = list(range(len(widths)))[::-1]
+
+    first_made = wind_products(wind_u, wind_v, far, widths)
+    lines = {}
+    for chunk in small_first[:1]:
+        for mask in far:
+            lines[chunk, mask] = across(first_made[chunk, mask], mask)
+    made = {**first_made, **wind_products(wind_u, wind_v, rest, widths)}
+    for chunk in small_first:
+        for mask in masks:
+            if (chunk, mask) not in lines:
+                lines[chunk, mask] = across(made[chunk, mask], mask)
 
     slot_ids = jnp.arange(slot_total, dtype=jnp.int32)
     wave_ids = jnp.arange(waves, dtype=jnp.int32)
@@ -573,29 +635,47 @@
     damping = jnp.where(kept[:, None, :], damping * (1.0 / math.sqrt(2 * half_lat)), 0.0)
     order, blocks, group = degree_order(count_here)
 
-    by_arrival = [0, *[mask for mask in reversed(masks) if mask and mask < sectors // 2], *masks]
-    by_arrival = list(dict.fromkeys(by_arrival))
+    by_arrival = list(dict.fromkeys([0, *[mask for mask in reversed(masks) if mask < sectors // 2], *masks]))
     early, late = by_arrival[:-1], by_arrival[-1:]
-    sums = forward([lines[mask] for mask in early], forward_table, turns_of(early))
-    fourier = forward([lines[mask] for mask in late], forward_table, turns_of(late), sums, (one_hot, share))
-    received = lax.all_to_all(fourier, ("lat", "lon"), split_axis=0, concat_axis=0, tiled=True)
+    received = [None] * len(widths)
+    for chunk in small_first:
+        own = {mask: lines[chunk, mask] for mask in masks}
+        if chunk == 0:
+            sums = forward([own[mask] for mask in early], forward_table, turns_of(early))
+            fourier = forward([own[mask] for mask in late], forward_table, turns_of(late), sums, (one_hot, share))
+        else:
+            fourier = forward([own[mask] for mask in by_arrival], forward_table, turns_of(by_arrival), None, (one_hot, share))
+        received[chunk] = lax.all_to_all(fourier, ("lat", "lon"), split_axis=0, concat_axis=0, tiled=True)
     place = jnp.stack([first, sector_index]).astype(jnp.int32)
-    spectral, returned = legendre(
-        received, basis, damping, place, order, blocks, sectors, sides, lat_rows, group
+    spectral, *returned = legendre(
+        received, basis, damping, place, order, blocks, sectors, sides, widths, group
     )
-    regrouped = lax.all_to_all(returned, ("lat", "lon"), split_axis=0, concat_axis=0, tiled=True)
+
+    exact = sectors in (1, 2, 4)
+    far_turns, rest_turns = turns_of(far), turns_of(rest)
+    south, _ = band_place(owner_index, owners)
+    back = {}
+    for chunk, width in enumerate(widths):
+        regrouped = lax.all_to_all(returned[chunk], ("lat", "lon"), split_axis=0, concat_axis=0, tiled=True)
+        ids = jnp.arange(width, dtype=jnp.int32)
+        mirror = (ids[:, None] == jnp.where(south, width - 1 - ids, ids)[None, :]).astype(BF16)
+        far_lines, by_wave = backward_first(regrouped, backward_table, far_turns, one_hot_turned, mirror, exact)
+        back[chunk, far[0]] = across(far_lines, far[0])
+        others = backward_rest(by_wave, backward_table, rest_turns, exact)
+        for mask, value in zip(rest, others):
+            back[chunk, mask] = across(value, mask)
 
     coefficients = jnp.zeros((sectors * share, 1, 2, 2, degrees), F32)
     for mask in masks:
         own = across(spectral[mask].astype(BF16), mask).astype(F32).reshape(share, 1, 2, 2, degrees)
         coefficients = lax.dynamic_update_slice_in_dim(coefficients, own, (sector_index ^ mask) * share, 0)
 
-    exact = sectors in (1, 2, 4)
-    far_lines, by_wave = backward_first(regrouped, backward_table, turns_of(far), one_hot_turned, mirror, exact)
-    rest_turns = turns_of(rest)
-    back = exchanged([far_lines], lambda: backward_rest(by_wave, backward_table, rest_turns, exact))
-    tendency = placed([back[mask] for mask in early], partners(early), sectors)
-    tendency = placed([back[mask] for mask in late], partners(late), sectors, tendency)
+    arrival = [(chunk, mask) for chunk in range(len(widths)) for mask in by_arrival]
+    cuts = [0, len(early), len(arrival) - 1, len(arrival)]
+    tendency = None
+    for begin, end in zip(cuts, cuts[1:]):
+        if end > begin:
+            tendency = placed(back, arrival[begin:end], widths, (sectors, rows, lon_cols), tendency)
     return coefficients[:capacity], tendency.reshape(levels, 2, lat_rows, lon_cols)
 
 

time: 170 us -> 187 us (1.10)
  waiting for transfers between devices: 67.3 us -> 44.4 us
  starting transfers between devices: 19.8 us -> 35.5 us
  local copies, waits for them, and re-layouts: 18.4 us -> 31.1 us
  Pallas kernels: 56.7 us -> 69 us
    unnamed x38 -> x62, local copies, waits for them, and re-layouts: 4.28 us -> 13.3 us
    ppermute x9 -> x15, waiting for transfers between devices: 32.7 us -> 23.9 us  [across(): lax.ppermute(value, 'lon', [(i, i ^ mask) for i in range(sectors)])]
    all_to_all x1 -> x2, waiting for transfers between devices: 28.9 us -> 20.5 us  [body(): lax.all_to_all(fourier, ('lat', 'lon'), split_axis=0, concat_axis=0, tile...]
    all_to_all x1 -> x2, starting transfers between devices: 5.97 us -> 12.8 us  [body(): lax.all_to_all(fourier, ('lat', 'lon'), split_axis=0, concat_axis=0, tile...]
    all_to_all x1 -> x2, waiting for transfers between devices: 5.7 us -> 0.01 us  [body(): lax.all_to_all(returned[chunk], ('lat', 'lon'), split_axis=0, concat_axis...]
    pallas_call x5 -> x6, Pallas kernels: 23.9 us -> 29.3 us  [the longest x1 16.6 us: legendre(): pl.pallas_call(functools.partial(legendre_kernel, sides, widths, group),...]
    ppermute x9 -> x15, starting transfers between devices: 7.18 us -> 11.9 us  [across(): lax.ppermute(value, 'lon', [(i, i ^ mask) for i in range(sectors)])]
    all_to_all x1 -> x2, starting transfers between devices: 6.62 us -> 10.7 us  [body(): lax.all_to_all(returned[chunk], ('lat', 'lon'), split_axis=0, concat_axis...]
  transfers between devices with their start and end apart: 11 -> 19, of which waited for: 8 -> 7; matrix products, arithmetic and copies ran while one was open for 11% -> 12% of each run, Pallas kernels for 19% -> 25%
where the time goes in v5:
time: 187 us; the launch traced here: 186 us
  Pallas kernels  69 us (37%)
  waiting for transfers between devices  44.4 us (24%)
  starting transfers between devices  35.5 us (19%)
  local copies, waits for them, and re-layouts  31.1 us (17%)
  other arithmetic  4.78 us (3%)
    ppermute x15, waiting for transfers between devices, across(): lax.ppermute(value, 'lon', [(i, i ^ mask) for i in range(sectors)])  23.9 us
    all_to_all x2, waiting for transfers between devices, body(): lax.all_to_all(fourier, ('lat', 'lon'), split_axis=0, concat_axis=0, tile...  20.5 us
    pallas_call x1, Pallas kernels, legendre(): pl.pallas_call(functools.partial(legendre_kernel, sides, widths, group),...  16.6 us
    unnamed x62, local copies, waits for them, and re-layouts  13.3 us
    all_to_all x2, starting transfers between devices, body(): lax.all_to_all(fourier, ('lat', 'lon'), split_axis=0, concat_axis=0, tile...  12.8 us
    pallas_call x3, Pallas kernels, forward(): pl.pallas_call(functools.partial(forward_kernel, len(lines), earlier is n...  12.8 us
    ppermute x15, starting transfers between devices, across(): lax.ppermute(value, 'lon', [(i, i ^ mask) for i in range(sectors)])  11.9 us
    pallas_call x2, Pallas kernels, backward_rest(): pl.pallas_call(functools.partial(backward_rest_kernel, exact), in_specs=[...  10.8 us
  transfers between devices with their start and end apart: 19, of which 7 were waited for; matrix products, arithmetic and copies ran while one was open for 12% of the time, Pallas kernels for 25%

profile of v5, /device:TPU:0, one launch (start us, length us, event | category | flops | bytes accessed | tf_op | source)
XLA Modules:
  0.0 186.2 jit_solution(2523455618120002110)
XLA Ops:
  0.6 5.4 %wind_products.2 = (bf16[256,640]{1,0:T(8,128)(2,1)}, bf16[128,640]{1,0:T(8,128)(2,1)}, bf16[256,640]{1,0:T(8,128)(2,1)}, bf16[128,640]{1,0:T(8,128)(2,1)}, bf16...) custom-call(f32[4,192,640]{2,1,0:T(8,128)} %wind_u.3, f32[4,192,640]{2,1,0:T(8,128)} %wind_v.3), custom_call_target="tpu_custom_call" | custom-call | tf_op jit(solution)/shard_map/wind_products/pallas_call | solution.py:137
  6.1 2.5 %collective-permute-start = (bf16[256,640]{1,0:T(8,128)(2,1)}, bf16[256,640]{1,0:T(8,128)(2,1)}, u32[]{:S(2)}, u32[]{:S(2)}) collective-permute-start(bf16[256,640]{1,0:T(8,128)(2,1)} %get-tuple-element.26), channel_id=1, source_target_pairs={{0,3},{1,2},{2,1},{3,0},{4,7},{5,6},{6,5},{7,4},{8,11},{9,10},{10,... | collective-permute-start | bytes 983048 | tf_op jit(solution)/shard_map/ppermute | solution.py:585
  8.6 0.7 collective-permute-start.1
  9.3 2.9 %wind_products.3 = (bf16[256,640]{1,0:T(8,128)(2,1)}, bf16[128,640]{1,0:T(8,128)(2,1)}) custom-call(f32[4,192,640]{2,1,0:T(8,128)} %wind_u.3, f32[4,192,640]{2,1,0:T(8,128)} %wind_v.3), custom_call_target="tpu_custom_call" | custom-call | tf_op jit(solution)/shard_map/wind_products/pallas_call | solution.py:137
  12.8 1.4 collective-permute-start.5
  14.3 0.6 gather_fusion.3
  14.8 0.6 gather_fusion.2
  15.9 3.8 %wave_table.2.refs_3_.refs_1_.refs_4_ = bf16[1280,1280]{1,0:T(8,128)(2,1)} custom-call(f32[32,640]{1,0:T(8,128)} %constant.155.clone.near_cos, f32[32,640]{1,0:T(8,128)} %constant.156.clone.near_sin, f32[20,1,640]{2,1,0:T(1,128)} %constant.157.clone.far_cos, f32[20,1,640]{2,1,0:T(1,128)} %constant.158.clone.far_sin), custom_call_target="tpu_custom_call" | custom-call | tf_op jit(solution)/shard_map/wave_table/pallas_call | solution.py:62
  20.1 1.3 collective-permute-done.4.refs_2_
  21.4 2.5 %collective-permute-done.5.refs_3_ = bf16[128,640]{1,0:T(8,128)(2,1)S(1)} collective-permute-done((bf16[128,640]{1,0:T(8,128)(2,1)S(1)}, bf16[128,640]{1,0:T(8,128)(2,1)S(1)}, u32[]{:S(2)}, u32[]{:S(2)}) %collective-permute-start.5) | collective-permute-done | bytes 163872 | tf_op jit(solution)/shard_map/ppermute | solution.py:585
  23.9 1.9 %copy-done.2 = bf16[1280,1280]{1,0:T(8,128)(2,1)S(1)} copy-done((bf16[1280,1280]{1,0:T(8,128)(2,1)S(1)}, bf16[1280,1280]{1,0:T(8,128)(2,1)}, u32[]{:S(2)}) %copy-start.2) | copy-done | bytes 3276824
  25.9 3.7 %forward.5 = bf16[32,50,128]{2,1,0:T(8,128)(2,1)S(1)} custom-call(bf16[128,640]{1,0:T(8,128)(2,1)S(1)} %copy-done.21, bf16[128,640]{1,0:T(8,128)(2,1)S(1)} %collective-permute-done.3.refs_1_, bf16[128,640]{1,0:T(8,128)(2,1)S(1)} %collective-permute-done.4.refs_2_, bf16[128,640]{1,0:T(8,128)(2,1)S(1)} %collective-permute-done.5.refs_3_, ...), custom_call_target="tpu_custom_call" | custom-call | flops 1677721600 | bytes 10000000 | tf_op jit(solution)/shard_map/forward/pallas_call | solution.py:216
  29.6 0.8 copy-done.12
  30.4 6.9 %all-to-all-start.1 = ((bf16[32,50,128]{2,1,0:T(8,128)(2,1)}), bf16[32,50,128]{2,1,0:T(8,128)(2,1)}, u32[]{:S(2)}, u32[]{:S(2)}) async-start(bf16[32,50,128]{2,1,0:T(8,128)(2,1)} %copy-done.12), calls=%async_computation.1 | async-start | bytes 917504 | tf_op jit(solution)/shard_map/all_to_all | solution.py:648
  37.3 0.6 gather_fusion.1
  37.9 0.6 gather_fusion
  38.5 3.4 %wave_table.3.table_hbm.table = bf16[2560,640]{1,0:T(8,128)(2,1)} custom-call(f32[32,640]{1,0:T(8,128)} %constant.155.clone.near_cos, f32[32,640]{1,0:T(8,128)} %constant.156.clone.near_sin, f32[20,1,640]{2,1,0:T(1,128)} %constant.157.clone.far_cos, f32[20,1,640]{2,1,0:T(1,128)} %constant.158.clone.far_sin), custom_call_target="tpu_custom_call" | custom-call | tf_op jit(solution)/shard_map/wave_table/pallas_call | solution.py:62
  41.8 0.6 gather_fusion.5
  42.4 0.6 gather_fusion.4
  43.2 1.0 copy-done.17
  44.1 4.9 %forward.3.refs_4_ = f32[2,256,640]{2,1,0:T(8,128)S(1)} custom-call(bf16[256,640]{1,0:T(8,128)(2,1)S(1)} %copy-done.17, bf16[256,640]{1,0:T(8,128)(2,1)} %collective-permute-done.1.refs_1_, bf16[256,640]{1,0:T(8,128)(2,1)} %collective-permute-done.2.refs_2_, bf16[1280,1280]{1,0:T(8,128)(2,1)S(1)} %copy-done.3, f32[3,1,640]{2,1,0:T(1,128)S(1)} %get-tuple-element.81.refs_4_, ...), custom_call_target="tpu_custom_call" | custom-call | flops 2516582400 | bytes 10000000 | tf_op jit(solution)/shard_map/forward/pallas_call | solution.py:216
  49.1 4.1 %forward.4 = bf16[32,100,128]{2,1,0:T(8,128)(2,1)S(1)} custom-call(bf16[256,640]{1,0:T(8,128)(2,1)} %collective-permute-done.refs_0_, bf16[1280,1280]{1,0:T(8,128)(2,1)S(1)} %copy-done.3, f32[1,1,640]{2,1,0:T(1,128)S(1)} %get-tuple-element.84.refs_2_, f32[1,1,640]{2,1,0:T(1,128)S(1)} %get-tuple-element.73.refs_3_, f32[2,256,640]{2,1,0:T(8,128)S(1)} %forward.3.refs_4_, ...), custom_call_target="tpu_custom_call" | custom-call | flops 838860800 | bytes 10000000 | tf_op jit(solution)/shard_map/forward/pallas_call | solution.py:216
  53.2 0.9 copy-done.8
  54.1 5.9 %all-to-all-start = ((bf16[32,100,128]{2,1,0:T(8,128)(2,1)}), bf16[32,100,128]{2,1,0:T(8,128)(2,1)S(1)}, u32[]{:S(2)}, u32[]{:S(2)}) async-start(bf16[32,100,128]{2,1,0:T(8,128)(2,1)} %copy-done.8), calls=%async_computation | async-start | bytes 1703936 | tf_op jit(solution)/shard_map/all_to_all | solution.py:648
  61.4 20.5 %all-to-all-done.rest_0_ = bf16[32,100,128]{2,1,0:T(8,128)(2,1)S(1)} async-done(((bf16[32,100,128]{2,1,0:T(8,128)(2,1)}), bf16[32,100,128]{2,1,0:T(8,128)(2,1)S(1)}, u32[]{:S(2)}, u32[]{:S(2)}) %all-to-all-start) | async-done | bytes 819232 | tf_op jit(solution)/shard_map/all_to_all | solution.py:648
  81.9 0.9 copy-done.9
  82.8 1.2 copy-done.10
  83.9 16.6 %legendre.1 = (f32[4,25,4,640]{3,2,1,0:T(4,128)S(1)}, bf16[32,100,128]{2,1,0:T(8,128)(2,1)S(1)}, bf16[32,50,128]{2,1,0:T(8,128)(2,1)S(1)}) custom-call(s32[2]{0:T(128)S(1)} %pad_add_fusion.place, s32[25]{0:T(128)S(1)} %get-tuple-element.61.order, s32[5]{0:T(128)S(1)} %and_select_fusion.blocks, f32[25,16,640]{2,1,0:T(8,128)S(1)} %multiply_select_fusion.damping, ...), custom_call_target="tpu_custom_call" | custom-call | flops 1572864000 | bytes 24576000 | tf_op jit(solution)/shard_map/legendre/pallas_call | solution.py:529
  100.6 0.9 copy-done.11
  101.5 0.8 copy-done.13
  102.3 6.4 %all-to-all-start.3 = ((bf16[32,100,128]{2,1,0:T(8,128)(2,1)}), bf16[32,100,128]{2,1,0:T(8,128)(2,1)}, u32[]{:S(2)}, u32[]{:S(2)}) async-start(bf16[32,100,128]{2,1,0:T(8,128)(2,1)} %copy-done.11), calls=%async_computation.3 | async-start | bytes 1703936 | tf_op jit(solution)/shard_map/all_to_all | solution.py:659
  108.7 1.3 compare_convert_fusion.one_hot
  110.3 0.9 slice_convert_fusion
  111.2 1.7 collective-permute-start.6
  113.3 0.7 broadcast_select_fusion.2
  114.0 1.8 reshape.326
  115.8 5.7 %collective-permute-done.6 = bf16[25,4,640]{2,1,0:T(4,128)(2,1)} collective-permute-done((bf16[25,4,640]{2,1,0:T(4,128)(2,1)}, bf16[25,4,640]{2,1,0:T(4,128)(2,1)}, u32[]{:S(2)}, u32[]{:S(2)}) %collective-permute-start.6) | collective-permute-done | bytes 128032 | tf_op jit(solution)/shard_map/ppermute | solution.py:585
  121.5 1.8 reshape.321
  123.3 1.9 %collective-permute-done.7 = bf16[25,4,640]{2,1,0:T(4,128)(2,1)} collective-permute-done((bf16[25,4,640]{2,1,0:T(4,128)(2,1)}, bf16[25,4,640]{2,1,0:T(4,128)(2,1)}, u32[]{:S(2)}, u32[]{:S(2)}) %collective-permute-start.7) | collective-permute-done | bytes 128032 | tf_op jit(solution)/shard_map/ppermute | solution.py:585
  125.2 1.8 reshape.323
  127.0 1.8 reshape.325
  128.8 1.2 broadcast_in_dim.109
  130.0 1.7 bitcast_dynamic-update-slice_fusion.3
  131.7 4.3 %all-to-all-start.2 = ((bf16[32,50,128]{2,1,0:T(8,128)(2,1)}), bf16[32,50,128]{2,1,0:T(8,128)(2,1)}, u32[]{:S(2)}, u32[]{:S(2)}) async-start(bf16[32,50,128]{2,1,0:T(8,128)(2,1)} %copy-done.13), calls=%async_computation.2 | async-start | bytes 917504 | tf_op jit(solution)/shard_map/all_to_all | solution.py:659
  136.0 1.7 bitcast_dynamic-update-slice_fusion.2
  137.7 1.7 bitcast_dynamic-update-slice_fusion.1
  139.3 1.3 copy-done.4
  140.7 4.8 %backward_first.3 = (bf16[256,640]{1,0:T(8,128)(2,1)S(1)}, bf16[2,256,640]{2,1,0:T(8,128)(2,1)S(1)}) custom-call(bf16[32,100,128]{2,1,0:T(8,128)(2,1)} %all-to-all-done.3.wire, bf16[2560,640]{1,0:T(8,128)(2,1)S(1)} %copy-done, f32[1,1,640]{2,1,0:T(1,128)S(1)} %get-tuple-element.85.turn_cos, f32[1,1,640]{2,1,0:T(1,128)S(1)} %get-tuple-element.72.turn_sin, ...), custom_call_target="tpu_custom_call" | custom-call | flops 1000000000 | bytes 10000000 | tf_op jit(solution)/shard_map/backward_first/pallas_call | solution.py:276
  145.5 0.8 copy-done.16
  146.4 0.7 copy-done.18
  147.1 6.3 %backward_rest.3 = (bf16[256,640]{1,0:T(8,128)(2,1)}, bf16[256,640]{1,0:T(8,128)(2,1)}, bf16[256,640]{1,0:T(8,128)(2,1)}) custom-call(bf16[2,256,640]{2,1,0:T(8,128)(2,1)} %copy-done.16, bf16[2560,640]{1,0:T(8,128)(2,1)} %wave_table.3.table_hbm.table, f32[3,1,640]{2,1,0:T(1,128)} %get-tuple-element.77.turn_cos, f32[3,1,640]{2,1,0:T(1,128)} %get-tuple-element.76.turn_sin), custom_call_target="tpu_custom_call" | custom-call | flops 3000000000 | bytes 10000000 | tf_op jit(solution)/shard_map/backward_rest/pallas_call | solution.py:306
  153.4 1.3 copy-done.5
  154.7 4.2 %backward_first.2 = (bf16[128,640]{1,0:T(8,128)(2,1)S(1)}, bf16[2,128,640]{2,1,0:T(8,128)(2,1)S(1)}) custom-call(bf16[32,50,128]{2,1,0:T(8,128)(2,1)} %all-to-all-done.2.wire, bf16[2560,640]{1,0:T(8,128)(2,1)S(1)} %copy-done.1, f32[1,1,640]{2,1,0:T(1,128)S(1)} %get-tuple-element.85.turn_cos, f32[1,1,640]{2,1,0:T(1,128)S(1)} %get-tuple-element.72.turn_sin, ...), custom_call_target="tpu_custom_call" | custom-call | flops 1000000000 | bytes 10000000 | tf_op jit(solution)/shard_map/backward_first/pallas_call | solution.py:276
  159.0 0.7 copy-done.20
  159.7 1.6 collective-permute-start.10
  161.8 4.4 %backward_rest.2 = (bf16[128,640]{1,0:T(8,128)(2,1)}, bf16[128,640]{1,0:T(8,128)(2,1)}, bf16[128,640]{1,0:T(8,128)(2,1)}) custom-call(bf16[2,128,640]{2,1,0:T(8,128)(2,1)} %copy-done.20, bf16[2560,640]{1,0:T(8,128)(2,1)} %wave_table.3.table_hbm.table, f32[3,1,640]{2,1,0:T(1,128)} %get-tuple-element.77.turn_cos, f32[3,1,640]{2,1,0:T(1,128)} %get-tuple-element.76.turn_sin), custom_call_target="tpu_custom_call" | custom-call | flops 3000000000 | bytes 10000000 | tf_op jit(solution)/shard_map/backward_rest/pallas_call | solution.py:306
  166.3 0.9 collective-permute-start.9
  167.2 0.7 collective-permute-start.11
  168.4 0.7 bitcast_dynamic-update-slice_fusion
  169.2 8.5 %collective-permute-done.14.refs_2_ = bf16[256,640]{1,0:T(8,128)(2,1)S(1)} collective-permute-done((bf16[256,640]{1,0:T(8,128)(2,1)S(1)}, bf16[256,640]{1,0:T(8,128)(2,1)S(1)}, u32[]{:S(2)}, u32[]{:S(2)}) %collective-permute-start.14) | collective-permute-done | bytes 327712 | tf_op jit(solution)/shard_map/ppermute | solution.py:585
  177.6 2.3 %placed.3.refs_4_ = f32[4,384,640]{2,1,0:T(8,128)} custom-call(bf16[256,640]{1,0:T(8,128)(2,1)S(1)} %copy-done.14, bf16[256,640]{1,0:T(8,128)(2,1)} %collective-permute-done.13.refs_1_, bf16[256,640]{1,0:T(8,128)(2,1)S(1)} %collective-permute-done.14.refs_2_), custom_call_target="tpu_custom_call" | custom-call | tf_op jit(solution)/shard_map/placed/pallas_call | solution.py:342
  179.9 4.0 %collective-permute-done.12.refs_3_ = bf16[128,640]{1,0:T(8,128)(2,1)S(1)} collective-permute-done((bf16[128,640]{1,0:T(8,128)(2,1)S(1)}, bf16[128,640]{1,0:T(8,128)(2,1)S(1)}, u32[]{:S(2)}, u32[]{:S(2)}) %collective-permute-start.12) | collective-permute-done | bytes 163872 | tf_op jit(solution)/shard_map/ppermute | solution.py:585
  184.0 1.2 placed.4.refs_1_
  185.2 0.8 placed.5
  (97 shorter events, 4.8 us)
Async XLA Ops:
  6.0 6.7 %copy-start.30 = (bf16[128,640]{1,0:T(8,128)(2,1)S(1)}, bf16[128,640]{1,0:T(8,128)(2,1)}, u32[]{:S(2)}) copy-start(bf16[128,640]{1,0:T(8,128)(2,1)} %get-tuple-element.33) | copy-start | bytes 491524
  6.0 8.2 %copy-start.23 = (f32[4,640]{1,0:T(4,128)S(1)}, f32[4,640]{1,0:T(4,128)}, u32[]{:S(2)}) copy-start(f32[4,640]{1,0:T(4,128)} %constant.203) | copy-start | bytes 30724
  6.1 8.8 %copy-start.22 = (f32[4,640]{1,0:T(4,128)S(1)}, f32[4,640]{1,0:T(4,128)}, u32[]{:S(2)}) copy-start(f32[4,640]{1,0:T(4,128)} %constant.202) | copy-start | bytes 30724
  6.1 9.3 %copy-start.25 = (s32[640]{0:T(1024)S(1)}, s32[640]{0:T(1024)}, u32[]{:S(2)}) copy-start(s32[640]{0:T(1024)} %param.25) | copy-start | bytes 7684
  6.1 43.0 %collective-permute-start = (bf16[256,640]{1,0:T(8,128)(2,1)}, bf16[256,640]{1,0:T(8,128)(2,1)}, u32[]{:S(2)}, u32[]{:S(2)}) collective-permute-start(bf16[256,640]{1,0:T(8,128)(2,1)} %get-tuple-element.26), channel_id=1, source_target_pairs={{0,3},{1,2},{2,1},{3,0},{4,7},{5,6},{6,5},{7,4},{8,11},{9,10},{10,... | collective-permute-start | bytes 983048 | tf_op jit(solution)/shard_map/ppermute | solution.py:585
  8.6 34.5 %collective-permute-start.1 = (bf16[256,640]{1,0:T(8,128)(2,1)}, bf16[256,640]{1,0:T(8,128)(2,1)}, u32[]{:S(2)}, u32[]{:S(2)}) collective-permute-start(bf16[256,640]{1,0:T(8,128)(2,1)} %get-tuple-element.28), channel_id=1, source_target_pairs={{0,1},{1,0},{2,3},{3,2},{4,5},{5,4},{6,7},{7,6},{8,9},{9,8},{10,11... | collective-permute-start | bytes 983048 | tf_op jit(solution)/shard_map/ppermute | solution.py:585
  9.3 10.4 %collective-permute-start.3 = (bf16[128,640]{1,0:T(8,128)(2,1)}, bf16[128,640]{1,0:T(8,128)(2,1)S(1)}, u32[]{:S(2)}, u32[]{:S(2)}) collective-permute-start(bf16[128,640]{1,0:T(8,128)(2,1)} %get-tuple-element.31), channel_id=1, source_target_pairs={{0,1},{1,0},{2,3},{3,2},{4,5},{5,4},{6,7},{7,6},{8,9},{9,8},{10,11... | collective-permute-start | bytes 491528 | tf_op jit(solution)/shard_map/ppermute | solution.py:585
  12.2 11.7 %copy-start.21 = (bf16[128,640]{1,0:T(8,128)(2,1)S(1)}, bf16[128,640]{1,0:T(8,128)(2,1)}, u32[]{:S(2)}) copy-start(bf16[128,640]{1,0:T(8,128)(2,1)} %get-tuple-element.30.refs_0_) | copy-start | bytes 491524
  12.2 9.2 %collective-permute-start.4 = (bf16[128,640]{1,0:T(8,128)(2,1)}, bf16[128,640]{1,0:T(8,128)(2,1)S(1)}, u32[]{:S(2)}, u32[]{:S(2)}) collective-permute-start(bf16[128,640]{1,0:T(8,128)(2,1)} %get-tuple-element.32), channel_id=1, source_target_pairs={{0,2},{1,3},{2,0},{3,1},{4,6},{5,7},{6,4},{7,5},{8,10},{9,11},{10,... | collective-permute-start | bytes 491528 | tf_op jit(solution)/shard_map/ppermute | solution.py:585
  12.8 11.2 %collective-permute-start.5 = (bf16[128,640]{1,0:T(8,128)(2,1)S(1)}, bf16[128,640]{1,0:T(8,128)(2,1)S(1)}, u32[]{:S(2)}, u32[]{:S(2)}) collective-permute-start(bf16[128,640]{1,0:T(8,128)(2,1)S(1)} %copy-done.30), channel_id=1, source_target_pairs={{0,3},{1,2},{2,1},{3,0},{4,7},{5,6},{6,5},{7,4},{8,11},{9,10},{10,... | collective-permute-start | bytes 491528 | tf_op jit(solution)/shard_map/ppermute | solution.py:585
  15.7 8.2 %copy-start.6 = (bf16[1024,640]{1,0:T(8,128)(2,1)}, bf16[1024,640]{1,0:T(8,128)(2,1)S(1)}, u32[]{:S(2)}) copy-start(bf16[1024,640]{1,0:T(8,128)(2,1)S(1)} %compare_convert_fusion.1.refs_5_.refs_7_) | copy-start | bytes 3932164
  19.7 23.5 %collective-permute-start.2 = (bf16[256,640]{1,0:T(8,128)(2,1)}, bf16[256,640]{1,0:T(8,128)(2,1)}, u32[]{:S(2)}, u32[]{:S(2)}) collective-permute-start(bf16[256,640]{1,0:T(8,128)(2,1)} %get-tuple-element.29), channel_id=1, source_target_pairs={{0,2},{1,3},{2,0},{3,1},{4,6},{5,7},{6,4},{7,5},{8,10},{9,11},{10,... | collective-permute-start | bytes 983048 | tf_op jit(solution)/shard_map/ppermute | solution.py:585
  23.9 1.9 %copy-start.2 = (bf16[1280,1280]{1,0:T(8,128)(2,1)S(1)}, bf16[1280,1280]{1,0:T(8,128)(2,1)}, u32[]{:S(2)}) copy-start(bf16[1280,1280]{1,0:T(8,128)(2,1)} %wave_table.2.refs_3_.refs_1_.refs_4_) | copy-start | bytes 9830404
  29.6 0.8 copy-start.12
  30.4 12.6 %copy-start.27 = (f32[4,1,640]{2,1,0:T(1,128)S(1)}, f32[4,1,640]{2,1,0:T(1,128)}, u32[]{:S(2)}) copy-start(f32[4,1,640]{2,1,0:T(1,128)} %constant.160.clone2.5) | copy-start | bytes 30724
  30.4 12.6 %copy-start.28 = (f32[4,1,640]{2,1,0:T(1,128)S(1)}, f32[4,1,640]{2,1,0:T(1,128)}, u32[]{:S(2)}) copy-start(f32[4,1,640]{2,1,0:T(1,128)} %constant.159.clone2.5) | copy-start | bytes 30724
  30.4 12.8 %copy-start.3 = (bf16[1280,1280]{1,0:T(8,128)(2,1)S(1)}, bf16[1280,1280]{1,0:T(8,128)(2,1)}, u32[]{:S(2)}) copy-start(bf16[1280,1280]{1,0:T(8,128)(2,1)} %wave_table.2.refs_3_.refs_1_.refs_4_) | copy-start | bytes 9830404
  30.4 23.7 %all-to-all-start.1 = ((bf16[32,50,128]{2,1,0:T(8,128)(2,1)}), bf16[32,50,128]{2,1,0:T(8,128)(2,1)}, u32[]{:S(2)}, u32[]{:S(2)}) async-start(bf16[32,50,128]{2,1,0:T(8,128)(2,1)} %copy-done.12), calls=%async_computation.1 | async-start | bytes 917504 | tf_op jit(solution)/shard_map/all_to_all | solution.py:648
  43.2 1.0 copy-start.17
  44.1 5.0 %copy-start.7 = (bf16[1024,640]{1,0:T(8,128)(2,1)S(1)}, bf16[1024,640]{1,0:T(8,128)(2,1)}, u32[]{:S(2)}) copy-start(bf16[1024,640]{1,0:T(8,128)(2,1)} %copy-done.6) | copy-start | bytes 3932164
  49.1 11.0 %copy-start.26 = (s32[640]{0:T(1024)S(1)}, s32[640]{0:T(1024)}, u32[]{:S(2)}) copy-start(s32[640]{0:T(1024)} %param.26) | copy-start | bytes 7684
  49.1 11.6 %copy-start.29 = (f32[4]{0:T(128)S(1)}, f32[4]{0:T(128)}, u32[]{:S(2)}) copy-start(f32[4]{0:T(128)} %param.27) | copy-start | bytes 52
  53.2 0.9 copy-start.8
  54.1 27.8 %all-to-all-start = ((bf16[32,100,128]{2,1,0:T(8,128)(2,1)}), bf16[32,100,128]{2,1,0:T(8,128)(2,1)S(1)}, u32[]{:S(2)}, u32[]{:S(2)}) async-start(bf16[32,100,128]{2,1,0:T(8,128)(2,1)} %copy-done.8), calls=%async_computation | async-start | bytes 1703936 | tf_op jit(solution)/shard_map/all_to_all | solution.py:648
  81.9 0.9 copy-start.9
  82.8 1.2 copy-start.10
  100.6 0.9 copy-start.11
  101.5 0.8 copy-start.13
  102.3 29.4 %all-to-all-start.3 = ((bf16[32,100,128]{2,1,0:T(8,128)(2,1)}), bf16[32,100,128]{2,1,0:T(8,128)(2,1)}, u32[]{:S(2)}, u32[]{:S(2)}) async-start(bf16[32,100,128]{2,1,0:T(8,128)(2,1)} %copy-done.11), calls=%async_computation.3 | async-start | bytes 1703936 | tf_op jit(solution)/shard_map/all_to_all | solution.py:659
  111.1 28.2 %copy-start = (bf16[2560,640]{1,0:T(8,128)(2,1)S(1)}, bf16[2560,640]{1,0:T(8,128)(2,1)}, u32[]{:S(2)}) copy-start(bf16[2560,640]{1,0:T(8,128)(2,1)} %wave_table.3.table_hbm.table) | copy-start | bytes 9830404
  111.2 10.4 %collective-permute-start.6 = (bf16[25,4,640]{2,1,0:T(4,128)(2,1)}, bf16[25,4,640]{2,1,0:T(4,128)(2,1)}, u32[]{:S(2)}, u32[]{:S(2)}) collective-permute-start(bf16[25,4,640]{2,1,0:T(4,128)(2,1)} %get-tuple-element.71), channel_id=1, source_target_pairs={{0,2},{1,3},{2,0},{3,1},{4,6},{5,7},{6,4},{7,5},{8,10},{9,11},{10,... | collective-permute-start | bytes 384008 | tf_op jit(solution)/shard_map/ppermute | solution.py:585
  112.9 12.4 %collective-permute-start.7 = (bf16[25,4,640]{2,1,0:T(4,128)(2,1)}, bf16[25,4,640]{2,1,0:T(4,128)(2,1)}, u32[]{:S(2)}, u32[]{:S(2)}) collective-permute-start(bf16[25,4,640]{2,1,0:T(4,128)(2,1)} %get-tuple-element.70), channel_id=1, source_target_pairs={{0,3},{1,2},{2,1},{3,0},{4,7},{5,6},{6,5},{7,4},{8,11},{9,10},{10,... | collective-permute-start | bytes 384008 | tf_op jit(solution)/shard_map/ppermute | solution.py:585
  112.9 14.1 %collective-permute-start.8 = (bf16[25,4,640]{2,1,0:T(4,128)(2,1)S(1)}, bf16[25,4,640]{2,1,0:T(4,128)(2,1)}, u32[]{:S(2)}, u32[]{:S(2)}) collective-permute-start(bf16[25,4,640]{2,1,0:T(4,128)(2,1)S(1)} %get-tuple-element.69), channel_id=1, source_target_pairs={{0,1},{1,0},{2,3},{3,2},{4,5},{5,4},{6,7},{7,6},{8,9},{9,8},{10,11... | collective-permute-start | bytes 384008 | tf_op jit(solution)/shard_map/ppermute | solution.py:585
  131.7 21.7 %all-to-all-start.2 = ((bf16[32,50,128]{2,1,0:T(8,128)(2,1)}), bf16[32,50,128]{2,1,0:T(8,128)(2,1)}, u32[]{:S(2)}, u32[]{:S(2)}) async-start(bf16[32,50,128]{2,1,0:T(8,128)(2,1)} %copy-done.13), calls=%async_computation.2 | async-start | bytes 917504 | tf_op jit(solution)/shard_map/all_to_all | solution.py:659
  139.3 1.3 copy-start.4
  145.5 0.8 copy-start.16
  146.4 0.7 copy-start.18
  147.1 6.3 %copy-start.1 = (bf16[2560,640]{1,0:T(8,128)(2,1)S(1)}, bf16[2560,640]{1,0:T(8,128)(2,1)}, u32[]{:S(2)}) copy-start(bf16[2560,640]{1,0:T(8,128)(2,1)} %wave_table.3.table_hbm.table) | copy-start | bytes 9830404
  153.4 14.5 %collective-permute-start.13 = (bf16[256,640]{1,0:T(8,128)(2,1)}, bf16[256,640]{1,0:T(8,128)(2,1)}, u32[]{:S(2)}, u32[]{:S(2)}) collective-permute-start(bf16[256,640]{1,0:T(8,128)(2,1)} %get-tuple-element.45), channel_id=1, source_target_pairs={{0,1},{1,0},{2,3},{3,2},{4,5},{5,4},{6,7},{7,6},{8,9},{9,8},{10,11... | collective-permute-start | bytes 983048 | tf_op jit(solution)/shard_map/ppermute | solution.py:585
  153.4 1.3 copy-start.5
  154.7 6.5 %copy-start.19 = (bf16[256,640]{1,0:T(8,128)(2,1)S(1)}, bf16[256,640]{1,0:T(8,128)(2,1)}, u32[]{:S(2)}) copy-start(bf16[256,640]{1,0:T(8,128)(2,1)} %copy-done.18) | copy-start | bytes 983044
  159.0 0.7 copy-start.20
  159.7 24.3 %collective-permute-start.10 = (bf16[256,640]{1,0:T(8,128)(2,1)}, bf16[256,640]{1,0:T(8,128)(2,1)S(1)}, u32[]{:S(2)}, u32[]{:S(2)}) collective-permute-start(bf16[256,640]{1,0:T(8,128)(2,1)} %get-tuple-element.40), channel_id=1, source_target_pairs={{0,3},{1,2},{2,1},{3,0},{4,7},{5,6},{6,5},{7,4},{8,11},{9,10},{10,... | collective-permute-start | bytes 983048 | tf_op jit(solution)/shard_map/ppermute | solution.py:585
  161.3 16.3 %collective-permute-start.14 = (bf16[256,640]{1,0:T(8,128)(2,1)S(1)}, bf16[256,640]{1,0:T(8,128)(2,1)S(1)}, u32[]{:S(2)}, u32[]{:S(2)}) collective-permute-start(bf16[256,640]{1,0:T(8,128)(2,1)S(1)} %copy-done.19), channel_id=1, source_target_pairs={{0,2},{1,3},{2,0},{3,1},{4,6},{5,7},{6,4},{7,5},{8,10},{9,11},{10,... | collective-permute-start | bytes 983048 | tf_op jit(solution)/shard_map/ppermute | solution.py:585
  161.8 6.6 %copy-start.24 = (f32[25,1,2,2,640]{4,3,2,0,1:T(2,128)S(1)}, f32[25,1,2,2,640]{4,3,2,0,1:T(2,128)}, u32[]{:S(2)}) copy-start(f32[25,1,2,2,640]{4,3,2,0,1:T(2,128)} %reshape.326) | copy-start | bytes 768004
  161.8 15.8 %copy-start.14 = (bf16[256,640]{1,0:T(8,128)(2,1)S(1)}, bf16[256,640]{1,0:T(8,128)(2,1)}, u32[]{:S(2)}) copy-start(bf16[256,640]{1,0:T(8,128)(2,1)} %get-tuple-element.44.refs_0_) | copy-start | bytes 983044
  166.3 18.9 %collective-permute-start.9 = (bf16[128,640]{1,0:T(8,128)(2,1)}, bf16[128,640]{1,0:T(8,128)(2,1)S(1)}, u32[]{:S(2)}, u32[]{:S(2)}) collective-permute-start(bf16[128,640]{1,0:T(8,128)(2,1)} %get-tuple-element.37), channel_id=1, source_target_pairs={{0,3},{1,2},{2,1},{3,0},{4,7},{5,6},{6,5},{7,4},{8,11},{9,10},{10,... | collective-permute-start | bytes 491528 | tf_op jit(solution)/shard_map/ppermute | solution.py:585
  167.2 12.7 %collective-permute-start.11 = (bf16[128,640]{1,0:T(8,128)(2,1)}, bf16[128,640]{1,0:T(8,128)(2,1)S(1)}, u32[]{:S(2)}, u32[]{:S(2)}) collective-permute-start(bf16[128,640]{1,0:T(8,128)(2,1)} %get-tuple-element.42), channel_id=1, source_target_pairs={{0,1},{1,0},{2,3},{3,2},{4,5},{5,4},{6,7},{7,6},{8,9},{9,8},{10,11... | collective-permute-start | bytes 491528 | tf_op jit(solution)/shard_map/ppermute | solution.py:585
  167.9 16.1 %copy-start.15 = (bf16[128,640]{1,0:T(8,128)(2,1)S(1)}, bf16[128,640]{1,0:T(8,128)(2,1)}, u32[]{:S(2)}) copy-start(bf16[128,640]{1,0:T(8,128)(2,1)} %get-tuple-element.41.refs_1_) | copy-start | bytes 491524
  167.9 16.1 %collective-permute-start.12 = (bf16[128,640]{1,0:T(8,128)(2,1)S(1)}, bf16[128,640]{1,0:T(8,128)(2,1)S(1)}, u32[]{:S(2)}, u32[]{:S(2)}) collective-permute-start(bf16[128,640]{1,0:T(8,128)(2,1)S(1)} %get-tuple-element.43), channel_id=1, source_target_pairs={{0,2},{1,3},{2,0},{3,1},{4,6},{5,7},{6,4},{7,5},{8,10},{9,11},{10,... | collective-permute-start | bytes 491528 | tf_op jit(solution)/shard_map/ppermute | solution.py:585

commit v6 on v5

--- a/solution.py
+++ b/solution.py
@@ -13,7 +13,7 @@
 BF16 = jnp.bfloat16
 F32 = jnp.float32
 MIB = 1024 * 1024
-VMEM_LIMIT = 24 * MIB
+VMEM_LIMIT = 20 * MIB
 LEGENDRE_LIMIT = 36 * MIB
 WHOLE_LIMIT = 60 * MIB
 STEP = 128
@@ -32,11 +32,19 @@
     return np.cos(turns), np.sin(turns)
 
 
-def table_kernel(interleaved, near_cos, near_sin, far_cos, far_sin, out):
+def table_kernel(interleaved, near_cos, near_sin, far_cos, far_sin, named, wave_slots, out, hot_out, space, hot, sems):
     near, lanes = near_cos.shape
-    count = far_cos.shape[0] * near
+    steps = far_cos.shape[0]
+    count = steps * near
     size = min(LANES, lanes)
-    for step in range(far_cos.shape[0]):
+    if interleaved:
+        hot[...] = (named[...] == wave_slots[...]).astype(F32).astype(BF16)
+    else:
+        slots_down = jnp.broadcast_to(wave_slots[...].astype(F32), (8, wave_slots.shape[1])).T[:, :1]
+        hot[...] = (slots_down == named[...].astype(F32)).astype(F32).astype(BF16)
+    copies = [pltpu.make_async_copy(hot, hot_out, sems.at[0])]
+    copies[0].start()
+    for step in range(steps):
         cos = far_cos[step] * near_cos[...] - far_sin[step] * near_sin[...]
         sin = far_sin[step] * near_cos[...] + far_cos[step] * near_sin[...]
         high = (cos.astype(BF16), sin.astype(BF16))
@@ -47,21 +55,29 @@
                     row = term * count + step * near
                     for block in range(lanes // size):
                         lane = (2 * block + which) * size
-                        out[row : row + near, lane : lane + size] = value[:, block * size : (block + 1) * size]
+                        space[row : row + near, lane : lane + size] = value[:, block * size : (block + 1) * size]
                 else:
                     row = (2 * term + which) * count + step * near
-                    out[row : row + near, :] = value
-
-
-def wave_table(rows, columns, length, interleaved):
+                    space[row : row + near, :] = value
+    copies.append(pltpu.make_async_copy(space, out, sems.at[1]))
+    copies[1].start()
+    for copy in copies:
+        copy.wait()
+
+
+def wave_table(rows, columns, length, interleaved, named, wave_slots):
     near = 32
     near_cos, near_sin = phases(np.arange(near), np.arange(columns), length)
     far_cos, far_sin = phases(np.arange(rows // near) * near, np.arange(columns), length)
     scaling = 1.0 / math.sqrt(length)
     shape = (2 * rows, 2 * columns) if interleaved else (4 * rows, columns)
+    waves, slots = wave_slots.shape[0], named.shape[0]
+    hot_shape = (slots, waves) if interleaved else (waves, slots)
     return pl.pallas_call(
         functools.partial(table_kernel, interleaved),
-        out_shape=jax.ShapeDtypeStruct(shape, BF16),
+        out_specs=[pl.BlockSpec(memory_space=pltpu.HBM)] * 2,
+        out_shape=[jax.ShapeDtypeStruct(shape, BF16), jax.ShapeDtypeStruct(hot_shape, BF16)],
+        scratch_shapes=[pltpu.VMEM(shape, BF16), pltpu.VMEM(hot_shape, BF16), pltpu.SemaphoreType.DMA((2,))],
         compiler_params=pltpu.CompilerParams(vmem_limit_bytes=WHOLE_LIMIT),
         name="wave_table",
     )(
@@ -69,6 +85,8 @@
         jnp.asarray(near_sin * scaling, F32),
         jnp.asarray(far_cos[:, None, :], F32),
         jnp.asarray(far_sin[:, None, :], F32),
+        named[:, None] if interleaved else named[None, :],
+        wave_slots[None, :],
     )
 
 
@@ -170,7 +188,7 @@
     if not ends:
         refs[0][0], refs[0][1] = real, imag
         return
-    one_hot, out, by_wave, by_slot = refs
+    one_hot, out, by_wave, by_slot, wire, sems = refs
     devices, wire_rows, lanes = out.shape
     padded = one_hot.shape[0] // devices
     blocks = 2 * rows // lanes
@@ -183,11 +201,18 @@
     def _():
         for part in range(2):
             by_slot[:, part * rows : (part + 1) * rows] = dot(one_hot[...], by_wave[part], NT)
+        copies, out_step = [], devices // sems.shape[0]
         for device in range(devices):
             own = by_slot[device * padded : (device + 1) * padded, :]
-            out[device] = pack_rows(
+            wire[device] = pack_rows(
                 [own[:share, block * lanes : (block + 1) * lanes] for block in range(blocks)]
             ).astype(BF16)
+            if (device + 1) % out_step == 0:
+                piece = pl.ds(device + 1 - out_step, out_step)
+                copies.append(pltpu.make_async_copy(wire.at[piece], out.at[piece], sems.at[device // out_step]))
+                copies[-1].start()
+        for copy in copies:
+            copy.wait()
 
 
 def forward(lines, table, turns, earlier=None, end=None):
@@ -211,8 +236,9 @@
         out = (slots // round_up(share, 8), share * (2 * rows // lanes), lanes)
         args.append(one_hot)
         in_specs.append(pl.BlockSpec((slots, waves), lambda i: (0, 0)))
-        out_shape, out_spec = jax.ShapeDtypeStruct(out, BF16), pl.BlockSpec(out, lambda i: (0, 0, 0))
+        out_shape, out_spec = jax.ShapeDtypeStruct(out, BF16), pl.BlockSpec(memory_space=pltpu.HBM)
         scratch = [pltpu.VMEM((2, rows, waves), BF16), pltpu.VMEM((slots, 2 * rows), F32)]
+        scratch += [pltpu.VMEM(out, BF16), pltpu.SemaphoreType.DMA((4,))]
     return pl.pallas_call(
         functools.partial(forward_kernel, len(lines), earlier is not None, end is not None),
         grid=(waves // size,),
@@ -246,8 +272,13 @@
     return total.astype(BF16)
 
 
-def backward_first_kernel(exact, wire, table_hbm, turn_cos, turn_sin, one_hot, mirror, out, by_wave, by_slot, table, sem):
-    table_copy = pltpu.make_async_copy(table_hbm, table, sem)
+def backward_first_kernel(
+    exact, wire, table_hbm, turn_cos, turn_sin, one_hot_hbm, mirror, out, by_wave_out, by_slot, table, one_hot, by_wave, sems
+):
+    one_hot_copy = pltpu.make_async_copy(one_hot_hbm, one_hot, sems.at[0])
+    table_copy = pltpu.make_async_copy(table_hbm, table, sems.at[1])
+    by_wave_copy = pltpu.make_async_copy(by_wave, by_wave_out, sems.at[2])
+    one_hot_copy.start()
     table_copy.start()
     devices, _, lanes = wire.shape
     rows = out.shape[0]
@@ -258,6 +289,7 @@
     for device in range(devices):
         for block, piece in enumerate(unpack_rows(wire[device].astype(F32), blocks, padded)):
             by_slot[device * padded : (device + 1) * padded, block * lanes : (block + 1) * lanes] = piece.astype(BF16)
+    one_hot_copy.wait()
     wave_ids = lax.broadcasted_iota(jnp.int32, (1, waves), 1)
     weight = jnp.where(wave_ids == 0, 1.0, 2.0).astype(F32)
     for part in range(2):
@@ -265,8 +297,10 @@
         for field in range(2):
             own = slice(field * width, (field + 1) * width)
             by_wave[part, own, :] = (dot(mirror[...], ordered[:, own], NT) * weight).astype(BF16)
+    by_wave_copy.start()
     table_copy.wait()
     out[...] = sector_lines(exact, by_wave, table, turn_cos, turn_sin)
+    by_wave_copy.wait()
 
 
 def backward_first(wire, table, turns, one_hot, mirror, exact):
@@ -275,8 +309,8 @@
     vmem, hbm = pl.BlockSpec(memory_space=pltpu.VMEM), pl.BlockSpec(memory_space=pl.ANY)
     return pl.pallas_call(
         functools.partial(backward_first_kernel, exact),
-        in_specs=[vmem, hbm, vmem, vmem, vmem, vmem],
-        out_specs=[vmem, vmem],
+        in_specs=[vmem, hbm, vmem, vmem, hbm, vmem],
+        out_specs=[vmem, pl.BlockSpec(memory_space=pltpu.HBM)],
         out_shape=[
             jax.ShapeDtypeStruct((rows, table.shape[1]), BF16),
             jax.ShapeDtypeStruct((2, rows, waves), BF16),
@@ -284,7 +318,9 @@
         scratch_shapes=[
             pltpu.VMEM((slots, 2 * rows), BF16),
             pltpu.VMEM(table.shape, BF16),
-            pltpu.SemaphoreType.DMA,
+            pltpu.VMEM(one_hot.shape, BF16),
+            pltpu.VMEM((2, rows, waves), BF16),
+            pltpu.SemaphoreType.DMA((3,)),
         ],
         cost_estimate=pl.CostEstimate(flops=10**9, bytes_accessed=10**7, transcendentals=0),
         compiler_params=pltpu.CompilerParams(vmem_limit_bytes=VMEM_LIMIT),
@@ -573,7 +609,6 @@
     levels, lat_rows, lon_cols = wind_u.shape
     capacity, degrees, half_lat = basis.shape
     waves = wave_slots.shape[0]
-    slot_total = capacity * owners
     assert levels == sectors and sectors & (sectors - 1) == 0
     rows = 2 * lat_rows
     share = -(-capacity // sectors)
@@ -602,16 +637,17 @@
             if (chunk, mask) not in lines:
                 lines[chunk, mask] = across(made[chunk, mask], mask)
 
-    slot_ids = jnp.arange(slot_total, dtype=jnp.int32)
     wave_ids = jnp.arange(waves, dtype=jnp.int32)
     places = jnp.arange(owners * sectors * padded, dtype=jnp.int32)
     place_owner, place_sector, place_slot = places // (sectors * padded), places // padded % sectors, places % padded
     in_owner = place_sector * share + place_slot
     named = jnp.where((place_slot < share) & (in_owner < capacity), place_owner * capacity + in_owner, -1)
-    one_hot = (named[:, None] == wave_slots[None, :]).astype(BF16)
-    one_hot_turned = (wave_slots[:, None] == named[None, :]).astype(BF16)
-    forward_table = wave_table(lon_cols, waves, length, True)
-    backward_table = wave_table(waves, lon_cols, length, False)
+    forward_table, one_hot = wave_table(lon_cols, waves, length, True, named, wave_slots)
+    backward_table, one_hot_turned = wave_table(waves, lon_cols, length, False, named, wave_slots)
+    forward_table, one_hot, backward_table, one_hot_turned = (
+        pltpu.with_memory_space_constraint(value, pltpu.HBM)
+        for value in (forward_table, one_hot, backward_table, one_hot_turned)
+    )
     turns = sector_turns(sectors, waves)
 
     def turns_of(some):
@@ -654,13 +690,17 @@
     exact = sectors in (1, 2, 4)
     far_turns, rest_turns = turns_of(far), turns_of(rest)
     south, _ = band_place(owner_index, owners)
-    back = {}
+    back, regrouped = {}, []
+    for chunk, wire in enumerate(returned):
+        if chunk:
+            wire, regrouped[-1] = lax.optimization_barrier((wire, regrouped[-1]))
+        regrouped.append(lax.all_to_all(wire, ("lat", "lon"), split_axis=0, concat_axis=0, tiled=True))
     for chunk, width in enumerate(widths):
-        regrouped = lax.all_to_all(returned[chunk], ("lat", "lon"), split_axis=0, concat_axis=0, tiled=True)
         ids = jnp.arange(width, dtype=jnp.int32)
         mirror = (ids[:, None] == jnp.where(south, width - 1 - ids, ids)[None, :]).astype(BF16)
-        far_lines, by_wave = backward_first(regrouped, backward_table, far_turns, one_hot_turned, mirror, exact)
+        far_lines, by_wave = backward_first(regrouped[chunk], backward_table, far_turns, one_hot_turned, mirror, exact)
         back[chunk, far[0]] = across(far_lines, far[0])
+        by_wave = pltpu.with_memory_space_constraint(by_wave, pltpu.HBM)
         others = backward_rest(by_wave, backward_table, rest_turns, exact)
         for mask, value in zip(rest, others):
             back[chunk, mask] = across(value, mask)

time: 187 us -> 165 us (0.88)
  local copies, waits for them, and re-layouts: 31.1 us -> 8.91 us
  Pallas kernels: 69 us -> 74 us
  starting transfers between devices: 35.5 us -> 33.6 us
    unnamed x62 -> x30, local copies, waits for them, and re-layouts: 13.3 us -> 3.42 us
    ppermute x15, waiting for transfers between devices: 23.9 us -> 17 us  [across(): lax.ppermute(value, 'lon', [(i, i ^ mask) for i in range(sectors)])]
    pallas_call x3, Pallas kernels: 12.8 us -> 18.9 us  [forward(): pl.pallas_call(functools.partial(forward_kernel, len(lines), earlier is n...]
    dynamic_update_slice x4, local copies, waits for them, and re-layouts: 5.76 us -> 0.27 us  [body(): lax.dynamic_update_slice_in_dim(coefficients, own, (sector_index ^ mask)...]
    reshape x3, local copies, waits for them, and re-layouts: 5.35 us -> 0.53 us  [body(): across(spectral[mask].astype(BF16), mask).astype(F32)]
    all_to_all x2, waiting for transfers between devices: 0.01 us -> 4.1 us  [body(): lax.all_to_all(wire, ('lat', 'lon'), split_axis=0, concat_axis=0, tiled=T...]
  transfers between devices with their start and end apart: 19 -> 19, of which waited for: 7 -> 9; matrix products, arithmetic and copies ran while one was open for 12% -> 6% of each run, Pallas kernels for 25% -> 33%
where the time goes in v6:
time: 165 us
  Pallas kernels  74 us (45%)
  waiting for transfers between devices  42.7 us (26%)
  starting transfers between devices  33.6 us (20%)
  local copies, waits for them, and re-layouts  8.91 us (5%)
  other arithmetic  4.08 us (2%)
    all_to_all x2, waiting for transfers between devices, body(): lax.all_to_all(fourier, ('lat', 'lon'), split_axis=0, concat_axis=0, tile...  21.5 us
    pallas_call x3, Pallas kernels, forward(): pl.pallas_call(functools.partial(forward_kernel, len(lines), earlier is n...  18.9 us
    ppermute x15, waiting for transfers between devices, across(): lax.ppermute(value, 'lon', [(i, i ^ mask) for i in range(sectors)])  17 us
    pallas_call x1, Pallas kernels, legendre(): pl.pallas_call(functools.partial(legendre_kernel, sides, widths, group),...  15.6 us
    ppermute x15, starting transfers between devices, across(): lax.ppermute(value, 'lon', [(i, i ^ mask) for i in range(sectors)])  12 us
    all_to_all x2, starting transfers between devices, body(): lax.all_to_all(fourier, ('lat', 'lon'), split_axis=0, concat_axis=0, tile...  11.4 us
    pallas_call x2, Pallas kernels, backward_rest(): pl.pallas_call(functools.partial(backward_rest_kernel, exact), in_specs=[...  10.5 us
    all_to_all x2, starting transfers between devices, body(): lax.all_to_all(wire, ('lat', 'lon'), split_axis=0, concat_axis=0, tiled=T...  10.1 us
  transfers between devices with their start and end apart: 19, of which 9 were waited for; matrix products, arithmetic and copies ran while one was open for 6% of the time, Pallas kernels for 33%

profile of v6, /device:TPU:0, one launch (start us, length us, event | category | flops | bytes accessed | tf_op | source)
XLA Modules:
  0.0 164.6 jit_solution(17197809199303570453)
XLA Ops:
  0.7 2.9 %wind_products.3 = (bf16[256,640]{1,0:T(8,128)(2,1)}, bf16[128,640]{1,0:T(8,128)(2,1)}) custom-call(f32[4,192,640]{2,1,0:T(8,128)} %wind_u.3, f32[4,192,640]{2,1,0:T(8,128)} %wind_v.3), custom_call_target="tpu_custom_call" | custom-call | tf_op jit(solution)/shard_map/wind_products/pallas_call | solution.py:155
  3.6 3.1 %collective-permute-start.4 = (bf16[128,640]{1,0:T(8,128)(2,1)}, bf16[128,640]{1,0:T(8,128)(2,1)S(1)}, u32[]{:S(2)}, u32[]{:S(2)}) collective-permute-start(bf16[128,640]{1,0:T(8,128)(2,1)} %get-tuple-element.40), channel_id=1, source_target_pairs={{0,2},{1,3},{2,0},{3,1},{4,6},{5,7},{6,4},{7,5},{8,10},{9,11},{10,... | collective-permute-start | bytes 491528 | tf_op jit(solution)/shard_map/ppermute | solution.py:620
  6.7 5.4 %wind_products.2 = (bf16[256,640]{1,0:T(8,128)(2,1)}, bf16[128,640]{1,0:T(8,128)(2,1)}, bf16[256,640]{1,0:T(8,128)(2,1)}, bf16[128,640]{1,0:T(8,128)(2,1)}, bf16...) custom-call(f32[4,192,640]{2,1,0:T(8,128)} %wind_u.3, f32[4,192,640]{2,1,0:T(8,128)} %wind_v.3), custom_call_target="tpu_custom_call" | custom-call | tf_op jit(solution)/shard_map/wind_products/pallas_call | solution.py:155
  12.2 2.0 %collective-permute-start.5 = (bf16[128,640]{1,0:T(8,128)(2,1)}, bf16[128,640]{1,0:T(8,128)(2,1)S(1)}, u32[]{:S(2)}, u32[]{:S(2)}) collective-permute-start(bf16[128,640]{1,0:T(8,128)(2,1)} %get-tuple-element.41), channel_id=1, source_target_pairs={{0,3},{1,2},{2,1},{3,0},{4,7},{5,6},{6,5},{7,4},{8,11},{9,10},{10,... | collective-permute-start | bytes 491528 | tf_op jit(solution)/shard_map/ppermute | solution.py:620
  14.4 0.6 gather_fusion.3
  15.0 0.6 gather_fusion.2
  15.6 1.0 fusion.11.named
  16.7 0.6 broadcast_in_dim.119.wave_slots
  17.3 4.3 %wave_table.2 = (bf16[1280,1280]{1,0:T(8,128)(2,1)}, bf16[1024,640]{1,0:T(8,128)(2,1)}) custom-call(f32[32,640]{1,0:T(8,128)} %constant.155.clone.near_cos, f32[32,640]{1,0:T(8,128)} %constant.156.clone.near_sin, f32[20,1,640]{2,1,0:T(1,128)} %constant.157.clone.far_cos, f32[20,1,640]{2,1,0:T(1,128)} %constant.158.clone.far_sin, s32[1024,1]{1,0:T(8,128)} %fusion.11.named, ...), custom_call_target="tpu_custom_call" | custom-call | tf_op jit(solution)/shard_map/wave_table/pallas_call | solution.py:76
  21.7 0.2 collective-permute-start.1
  21.9 0.2 collective-permute-done.5.refs_3_
  22.1 0.9 copy-done.6
  23.0 6.9 %forward.5 = bf16[32,50,128]{2,1,0:T(8,128)(2,1)} custom-call(bf16[128,640]{1,0:T(8,128)(2,1)S(1)} %copy-done.6, bf16[128,640]{1,0:T(8,128)(2,1)S(1)} %collective-permute-done.3.refs_1_, bf16[128,640]{1,0:T(8,128)(2,1)S(1)} %collective-permute-done.4.refs_2_, bf16[128,640]{1,0:T(8,128)(2,1)S(1)} %collective-permute-done.5.refs_3_, ...), custom_call_target="tpu_custom_call" | custom-call | flops 1677721600 | bytes 10000000 | tf_op jit(solution)/shard_map/forward/pallas_call | solution.py:242
  29.9 6.4 %all-to-all-start.1 = ((bf16[32,50,128]{2,1,0:T(8,128)(2,1)}), bf16[32,50,128]{2,1,0:T(8,128)(2,1)S(1)}, u32[]{:S(2)}, u32[]{:S(2)}) async-start(bf16[32,50,128]{2,1,0:T(8,128)(2,1)} %forward.5), calls=%async_computation.1 | async-start | bytes 917504 | tf_op jit(solution)/shard_map/all_to_all | solution.py:684
  36.4 0.6 gather_fusion.1
  37.0 0.6 gather_fusion
  37.8 5.4 %forward.3.refs_4_ = f32[2,256,640]{2,1,0:T(8,128)S(1)} custom-call(bf16[256,640]{1,0:T(8,128)(2,1)S(1)} %copy-done.4, bf16[256,640]{1,0:T(8,128)(2,1)S(1)} %collective-permute-done.1.refs_1_, bf16[256,640]{1,0:T(8,128)(2,1)S(1)} %collective-permute-done.2.refs_2_, bf16[1280,1280]{1,0:T(8,128)(2,1)} %get-tuple-element.33.refs_3_.refs_1_.refs_4_, ...), custom_call_target="tpu_custom_call" | custom-call | flops 2516582400 | bytes 10000000 | tf_op jit(solution)/shard_map/forward/pallas_call | solution.py:242
  43.2 6.6 %forward.4 = bf16[32,100,128]{2,1,0:T(8,128)(2,1)} custom-call(bf16[256,640]{1,0:T(8,128)(2,1)S(1)} %collective-permute-done.refs_0_, bf16[1280,1280]{1,0:T(8,128)(2,1)} %get-tuple-element.33.refs_3_.refs_1_.refs_4_, f32[1,1,640]{2,1,0:T(1,128)S(1)} %get-tuple-element.96.refs_2_, f32[1,1,640]{2,1,0:T(1,128)S(1)} %get-tuple-element.85.refs_3_, ...), custom_call_target="tpu_custom_call" | custom-call | flops 838860800 | bytes 10000000 | tf_op jit(solution)/shard_map/forward/pallas_call | solution.py:242
  49.8 1.0 all-to-all-done.1.rest_1_
  50.8 5.0 %all-to-all-start = ((bf16[32,100,128]{2,1,0:T(8,128)(2,1)}), bf16[32,100,128]{2,1,0:T(8,128)(2,1)S(1)}, u32[]{:S(2)}, u32[]{:S(2)}) async-start(bf16[32,100,128]{2,1,0:T(8,128)(2,1)} %forward.4), calls=%async_computation | async-start | bytes 1703936 | tf_op jit(solution)/shard_map/all_to_all | solution.py:684
  55.8 0.2 fusion.18
  56.0 0.2 convert_reduce_fusion
  56.8 0.3 multiply_select_fusion.damping
  57.1 20.5 %all-to-all-done.rest_0_ = bf16[32,100,128]{2,1,0:T(8,128)(2,1)S(1)} async-done(((bf16[32,100,128]{2,1,0:T(8,128)(2,1)}), bf16[32,100,128]{2,1,0:T(8,128)(2,1)S(1)}, u32[]{:S(2)}, u32[]{:S(2)}) %all-to-all-start) | async-done | bytes 819232 | tf_op jit(solution)/shard_map/all_to_all | solution.py:684
  77.6 15.6 %legendre.1 = (f32[4,25,4,640]{3,2,1,0:T(4,128)S(1)}, bf16[32,100,128]{2,1,0:T(8,128)(2,1)S(1)}, bf16[32,50,128]{2,1,0:T(8,128)(2,1)}) custom-call(s32[2]{0:T(128)S(1)} %pad_add_fusion.place, s32[25]{0:T(128)S(1)} %get-tuple-element.73.order, s32[5]{0:T(128)S(1)} %and_select_fusion.5.blocks, f32[25,16,640]{2,1,0:T(8,128)S(1)} %multiply_select_fusion.damping, ...), custom_call_target="tpu_custom_call" | custom-call | flops 1572864000 | bytes 24576000 | tf_op jit(solution)/shard_map/legendre/pallas_call | solution.py:565
  93.3 0.9 copy-done
  94.2 6.3 %all-to-all-start.2 = ((bf16[32,100,128]{2,1,0:T(8,128)(2,1)}), bf16[32,100,128]{2,1,0:T(8,128)(2,1)S(1)}, u32[]{:S(2)}, u32[]{:S(2)}) async-start(bf16[32,100,128]{2,1,0:T(8,128)(2,1)} %copy-done), calls=%async_computation.2 | async-start | bytes 1703936 | tf_op jit(solution)/shard_map/all_to_all | solution.py:697
  100.5 0.6 gather_fusion.5
  101.0 0.6 gather_fusion.4
  101.6 0.6 and_select_fusion.1.named
  102.2 4.1 %wave_table.3 = (bf16[2560,640]{1,0:T(8,128)(2,1)}, bf16[640,1024]{1,0:T(8,128)(2,1)}) custom-call(f32[32,640]{1,0:T(8,128)} %constant.155.clone.near_cos, f32[32,640]{1,0:T(8,128)} %constant.156.clone.near_sin, f32[20,1,640]{2,1,0:T(1,128)} %constant.157.clone.far_cos, f32[20,1,640]{2,1,0:T(1,128)} %constant.158.clone.far_sin, ...), custom_call_target="tpu_custom_call" | custom-call | tf_op jit(solution)/shard_map/wave_table/pallas_call | solution.py:76
  106.4 0.2 convert.10
  106.6 0.2 slice_convert_fusion
  106.7 0.3 collective-permute-start.8
  107.0 1.6 collective-permute-start.7
  108.7 0.3 collective-permute-start.6
  108.9 0.7 broadcast_select_fusion.2
  109.6 0.2 reshape.491
  109.8 0.2 reshape.490
  110.0 4.6 %collective-permute-done.7 = bf16[25,4,640]{2,1,0:T(4,128)(2,1)S(1)} collective-permute-done((bf16[25,4,640]{2,1,0:T(4,128)(2,1)S(1)}, bf16[25,4,640]{2,1,0:T(4,128)(2,1)S(1)}, u32[]{:S(2)}, u32[]{:S(2)}) %collective-permute-start.7) | collective-permute-done | bytes 128032 | tf_op jit(solution)/shard_map/ppermute | solution.py:620
  114.7 0.2 reshape.488
  114.8 3.2 %collective-permute-done.6 = bf16[25,4,640]{2,1,0:T(4,128)(2,1)S(1)} collective-permute-done((bf16[25,4,640]{2,1,0:T(4,128)(2,1)S(1)}, bf16[25,4,640]{2,1,0:T(4,128)(2,1)S(1)}, u32[]{:S(2)}, u32[]{:S(2)}) %collective-permute-start.6) | collective-permute-done | bytes 128032 | tf_op jit(solution)/shard_map/ppermute | solution.py:620
  118.0 0.2 reshape.486
  118.2 0.3 broadcast_in_dim.111
  118.5 3.9 %all-to-all-done.2.wire = bf16[32,100,128]{2,1,0:T(8,128)(2,1)S(1)} async-done(((bf16[32,100,128]{2,1,0:T(8,128)(2,1)}), bf16[32,100,128]{2,1,0:T(8,128)(2,1)S(1)}, u32[]{:S(2)}, u32[]{:S(2)}) %all-to-all-start.2) | async-done | bytes 819232 | tf_op jit(solution)/shard_map/all_to_all | solution.py:697
  122.4 3.8 %all-to-all-start.3 = ((bf16[32,50,128]{2,1,0:T(8,128)(2,1)}), bf16[32,50,128]{2,1,0:T(8,128)(2,1)S(1)}, u32[]{:S(2)}, u32[]{:S(2)}) async-start(bf16[32,50,128]{2,1,0:T(8,128)(2,1)} %get-tuple-element.45), calls=%async_computation.3 | async-start | bytes 917504 | tf_op jit(solution)/shard_map/all_to_all | solution.py:697
  126.4 4.8 %backward_first.3 = (bf16[256,640]{1,0:T(8,128)(2,1)S(1)}, bf16[2,256,640]{2,1,0:T(8,128)(2,1)S(1)}) custom-call(bf16[32,100,128]{2,1,0:T(8,128)(2,1)S(1)} %all-to-all-done.2.wire, bf16[2560,640]{1,0:T(8,128)(2,1)} %get-tuple-element.46.table_hbm.table, f32[1,1,640]{2,1,0:T(1,128)S(1)} %get-tuple-element.97.turn_cos, ...), custom_call_target="tpu_custom_call" | custom-call | flops 1000000000 | bytes 10000000 | tf_op jit(solution)/shard_map/backward_first/pallas_call | solution.py:310
  131.2 0.8 copy-done.3
  132.1 6.1 %backward_rest.3 = (bf16[256,640]{1,0:T(8,128)(2,1)}, bf16[256,640]{1,0:T(8,128)(2,1)}, bf16[256,640]{1,0:T(8,128)(2,1)}) custom-call(bf16[2,256,640]{2,1,0:T(8,128)(2,1)} %copy-done.3, bf16[2560,640]{1,0:T(8,128)(2,1)} %get-tuple-element.46.table_hbm.table, f32[3,1,640]{2,1,0:T(1,128)} %get-tuple-element.89.turn_cos, f32[3,1,640]{2,1,0:T(1,128)} %get-tuple-element.88.turn_sin), custom_call_target="tpu_custom_call" | custom-call | flops 3000000000 | bytes 10000000 | tf_op jit(solution)/shard_map/backward_rest/pallas_call | solution.py:342
  138.2 1.3 collective-permute-start.10
  139.4 0.4 collective-permute-start.13
  139.8 0.5 collective-permute-start.14
  140.3 0.2 all-to-all-done.3.wire
  140.5 4.1 %backward_first.2 = (bf16[128,640]{1,0:T(8,128)(2,1)S(1)}, bf16[2,128,640]{2,1,0:T(8,128)(2,1)S(1)}) custom-call(bf16[32,50,128]{2,1,0:T(8,128)(2,1)S(1)} %all-to-all-done.3.wire, bf16[2560,640]{1,0:T(8,128)(2,1)} %get-tuple-element.46.table_hbm.table, f32[1,1,640]{2,1,0:T(1,128)S(1)} %get-tuple-element.97.turn_cos, ...), custom_call_target="tpu_custom_call" | custom-call | flops 1000000000 | bytes 10000000 | tf_op jit(solution)/shard_map/backward_first/pallas_call | solution.py:310
  144.7 0.7 copy-done.5
  145.4 4.4 %backward_rest.2 = (bf16[128,640]{1,0:T(8,128)(2,1)}, bf16[128,640]{1,0:T(8,128)(2,1)}, bf16[128,640]{1,0:T(8,128)(2,1)}) custom-call(bf16[2,128,640]{2,1,0:T(8,128)(2,1)} %copy-done.5, bf16[2560,640]{1,0:T(8,128)(2,1)} %get-tuple-element.46.table_hbm.table, f32[3,1,640]{2,1,0:T(1,128)} %get-tuple-element.89.turn_cos, f32[3,1,640]{2,1,0:T(1,128)} %get-tuple-element.88.turn_sin), custom_call_target="tpu_custom_call" | custom-call | flops 3000000000 | bytes 10000000 | tf_op jit(solution)/shard_map/backward_rest/pallas_call | solution.py:342
  149.8 0.8 collective-permute-start.9
  150.6 0.7 collective-permute-start.11
  151.3 0.7 collective-permute-start.12
  152.0 3.6 %collective-permute-done.14.refs_2_ = bf16[256,640]{1,0:T(8,128)(2,1)S(1)} collective-permute-done((bf16[256,640]{1,0:T(8,128)(2,1)S(1)}, bf16[256,640]{1,0:T(8,128)(2,1)S(1)}, u32[]{:S(2)}, u32[]{:S(2)}) %collective-permute-start.14) | collective-permute-done | bytes 327712 | tf_op jit(solution)/shard_map/ppermute | solution.py:620
  155.6 1.3 placed.3.refs_4_
  157.0 5.4 %collective-permute-done.12.refs_3_ = bf16[128,640]{1,0:T(8,128)(2,1)S(1)} collective-permute-done((bf16[128,640]{1,0:T(8,128)(2,1)S(1)}, bf16[128,640]{1,0:T(8,128)(2,1)S(1)}, u32[]{:S(2)}, u32[]{:S(2)}) %collective-permute-start.12) | collective-permute-done | bytes 163872 | tf_op jit(solution)/shard_map/ppermute | solution.py:620
  162.4 1.2 placed.4.refs_1_
  163.7 0.8 placed.5
  (65 shorter events, 1.6 us)
Async XLA Ops:
  0.6 13.8 %copy-start.8 = (f32[4,640]{1,0:T(4,128)S(1)}, f32[4,640]{1,0:T(4,128)}, u32[]{:S(2)}) copy-start(f32[4,640]{1,0:T(4,128)} %constant.203) | copy-start | bytes 30724
  0.6 14.3 %copy-start.7 = (f32[4,640]{1,0:T(4,128)S(1)}, f32[4,640]{1,0:T(4,128)}, u32[]{:S(2)}) copy-start(f32[4,640]{1,0:T(4,128)} %constant.202) | copy-start | bytes 30724
  3.6 13.1 %copy-start.10 = (s32[640]{0:T(1024)S(1)}, s32[640]{0:T(1024)}, u32[]{:S(2)}) copy-start(s32[640]{0:T(1024)} %param.25) | copy-start | bytes 7684
  3.6 18.1 %collective-permute-start.4 = (bf16[128,640]{1,0:T(8,128)(2,1)}, bf16[128,640]{1,0:T(8,128)(2,1)S(1)}, u32[]{:S(2)}, u32[]{:S(2)}) collective-permute-start(bf16[128,640]{1,0:T(8,128)(2,1)} %get-tuple-element.40), channel_id=1, source_target_pairs={{0,2},{1,3},{2,0},{3,1},{4,6},{5,7},{6,4},{7,5},{8,10},{9,11},{10,... | collective-permute-start | bytes 491528 | tf_op jit(solution)/shard_map/ppermute | solution.py:620
  6.7 31.1 %collective-permute-start.2 = (bf16[256,640]{1,0:T(8,128)(2,1)}, bf16[256,640]{1,0:T(8,128)(2,1)S(1)}, u32[]{:S(2)}, u32[]{:S(2)}) collective-permute-start(bf16[256,640]{1,0:T(8,128)(2,1)} %get-tuple-element.36), channel_id=1, source_target_pairs={{0,2},{1,3},{2,0},{3,1},{4,6},{5,7},{6,4},{7,5},{8,10},{9,11},{10,... | collective-permute-start | bytes 983048 | tf_op jit(solution)/shard_map/ppermute | solution.py:620
  12.1 9.8 %collective-permute-start.3 = (bf16[128,640]{1,0:T(8,128)(2,1)}, bf16[128,640]{1,0:T(8,128)(2,1)S(1)}, u32[]{:S(2)}, u32[]{:S(2)}) collective-permute-start(bf16[128,640]{1,0:T(8,128)(2,1)} %get-tuple-element.39), channel_id=1, source_target_pairs={{0,1},{1,0},{2,3},{3,2},{4,5},{5,4},{6,7},{7,6},{8,9},{9,8},{10,11... | collective-permute-start | bytes 491528 | tf_op jit(solution)/shard_map/ppermute | solution.py:620
  12.2 9.9 %collective-permute-start.5 = (bf16[128,640]{1,0:T(8,128)(2,1)}, bf16[128,640]{1,0:T(8,128)(2,1)S(1)}, u32[]{:S(2)}, u32[]{:S(2)}) collective-permute-start(bf16[128,640]{1,0:T(8,128)(2,1)} %get-tuple-element.41), channel_id=1, source_target_pairs={{0,3},{1,2},{2,1},{3,0},{4,7},{5,6},{6,5},{7,4},{8,11},{9,10},{10,... | collective-permute-start | bytes 491528 | tf_op jit(solution)/shard_map/ppermute | solution.py:620
  14.3 28.9 %collective-permute-start = (bf16[256,640]{1,0:T(8,128)(2,1)}, bf16[256,640]{1,0:T(8,128)(2,1)S(1)}, u32[]{:S(2)}, u32[]{:S(2)}) collective-permute-start(bf16[256,640]{1,0:T(8,128)(2,1)} %get-tuple-element.32), channel_id=1, source_target_pairs={{0,3},{1,2},{2,1},{3,0},{4,7},{5,6},{6,5},{7,4},{8,11},{9,10},{10,... | collective-permute-start | bytes 983048 | tf_op jit(solution)/shard_map/ppermute | solution.py:620
  21.7 16.1 %collective-permute-start.1 = (bf16[256,640]{1,0:T(8,128)(2,1)}, bf16[256,640]{1,0:T(8,128)(2,1)S(1)}, u32[]{:S(2)}, u32[]{:S(2)}) collective-permute-start(bf16[256,640]{1,0:T(8,128)(2,1)} %get-tuple-element.35), channel_id=1, source_target_pairs={{0,1},{1,0},{2,3},{3,2},{4,5},{5,4},{6,7},{7,6},{8,9},{9,8},{10,11... | collective-permute-start | bytes 983048 | tf_op jit(solution)/shard_map/ppermute | solution.py:620
  22.1 0.9 copy-start.6
  23.0 14.6 %copy-start.12 = (f32[4,1,640]{2,1,0:T(1,128)S(1)}, f32[4,1,640]{2,1,0:T(1,128)}, u32[]{:S(2)}) copy-start(f32[4,1,640]{2,1,0:T(1,128)} %constant.160.clone2.5) | copy-start | bytes 30724
  23.0 14.6 %copy-start.13 = (f32[4,1,640]{2,1,0:T(1,128)S(1)}, f32[4,1,640]{2,1,0:T(1,128)}, u32[]{:S(2)}) copy-start(f32[4,1,640]{2,1,0:T(1,128)} %constant.159.clone2.5) | copy-start | bytes 30724
  23.0 14.7 %copy-start.4 = (bf16[256,640]{1,0:T(8,128)(2,1)S(1)}, bf16[256,640]{1,0:T(8,128)(2,1)}, u32[]{:S(2)}) copy-start(bf16[256,640]{1,0:T(8,128)(2,1)} %get-tuple-element.34.refs_0_) | copy-start | bytes 983044
  29.9 20.9 %all-to-all-start.1 = ((bf16[32,50,128]{2,1,0:T(8,128)(2,1)}), bf16[32,50,128]{2,1,0:T(8,128)(2,1)S(1)}, u32[]{:S(2)}, u32[]{:S(2)}) async-start(bf16[32,50,128]{2,1,0:T(8,128)(2,1)} %forward.5), calls=%async_computation.1 | async-start | bytes 917504 | tf_op jit(solution)/shard_map/all_to_all | solution.py:684
  43.2 12.6 %copy-start.11 = (s32[640]{0:T(1024)S(1)}, s32[640]{0:T(1024)}, u32[]{:S(2)}) copy-start(s32[640]{0:T(1024)} %param.26) | copy-start | bytes 7684
  43.2 13.2 %copy-start.14 = (f32[4]{0:T(128)S(1)}, f32[4]{0:T(128)}, u32[]{:S(2)}) copy-start(f32[4]{0:T(128)} %param.27) | copy-start | bytes 52
  50.8 26.8 %all-to-all-start = ((bf16[32,100,128]{2,1,0:T(8,128)(2,1)}), bf16[32,100,128]{2,1,0:T(8,128)(2,1)S(1)}, u32[]{:S(2)}, u32[]{:S(2)}) async-start(bf16[32,100,128]{2,1,0:T(8,128)(2,1)} %forward.4), calls=%async_computation | async-start | bytes 1703936 | tf_op jit(solution)/shard_map/all_to_all | solution.py:684
  93.3 0.9 copy-start
  94.2 28.3 %all-to-all-start.2 = ((bf16[32,100,128]{2,1,0:T(8,128)(2,1)}), bf16[32,100,128]{2,1,0:T(8,128)(2,1)S(1)}, u32[]{:S(2)}, u32[]{:S(2)}) async-start(bf16[32,100,128]{2,1,0:T(8,128)(2,1)} %copy-done), calls=%async_computation.2 | async-start | bytes 1703936 | tf_op jit(solution)/shard_map/all_to_all | solution.py:697
  106.7 3.1 %collective-permute-start.8 = (bf16[25,4,640]{2,1,0:T(4,128)(2,1)S(1)}, bf16[25,4,640]{2,1,0:T(4,128)(2,1)S(1)}, u32[]{:S(2)}, u32[]{:S(2)}) collective-permute-start(bf16[25,4,640]{2,1,0:T(4,128)(2,1)S(1)} %get-tuple-element.81), channel_id=1, source_target_pairs={{0,1},{1,0},{2,3},{3,2},{4,5},{5,4},{6,7},{7,6},{8,9},{9,8},{10,11... | collective-permute-start | bytes 384008 | tf_op jit(solution)/shard_map/ppermute | solution.py:620
  107.0 7.6 %collective-permute-start.7 = (bf16[25,4,640]{2,1,0:T(4,128)(2,1)S(1)}, bf16[25,4,640]{2,1,0:T(4,128)(2,1)S(1)}, u32[]{:S(2)}, u32[]{:S(2)}) collective-permute-start(bf16[25,4,640]{2,1,0:T(4,128)(2,1)S(1)} %get-tuple-element.82), channel_id=1, source_target_pairs={{0,3},{1,2},{2,1},{3,0},{4,7},{5,6},{6,5},{7,4},{8,11},{9,10},{10,... | collective-permute-start | bytes 384008 | tf_op jit(solution)/shard_map/ppermute | solution.py:620
  108.7 9.3 %collective-permute-start.6 = (bf16[25,4,640]{2,1,0:T(4,128)(2,1)S(1)}, bf16[25,4,640]{2,1,0:T(4,128)(2,1)S(1)}, u32[]{:S(2)}, u32[]{:S(2)}) collective-permute-start(bf16[25,4,640]{2,1,0:T(4,128)(2,1)S(1)} %get-tuple-element.83), channel_id=1, source_target_pairs={{0,2},{1,3},{2,0},{3,1},{4,6},{5,7},{6,4},{7,5},{8,10},{9,11},{10,... | collective-permute-start | bytes 384008 | tf_op jit(solution)/shard_map/ppermute | solution.py:620
  122.4 18.1 %all-to-all-start.3 = ((bf16[32,50,128]{2,1,0:T(8,128)(2,1)}), bf16[32,50,128]{2,1,0:T(8,128)(2,1)S(1)}, u32[]{:S(2)}, u32[]{:S(2)}) async-start(bf16[32,50,128]{2,1,0:T(8,128)(2,1)} %get-tuple-element.45), calls=%async_computation.3 | async-start | bytes 917504 | tf_op jit(solution)/shard_map/all_to_all | solution.py:697
  131.2 0.8 copy-start.3
  138.2 18.8 %collective-permute-start.10 = (bf16[256,640]{1,0:T(8,128)(2,1)}, bf16[256,640]{1,0:T(8,128)(2,1)S(1)}, u32[]{:S(2)}, u32[]{:S(2)}) collective-permute-start(bf16[256,640]{1,0:T(8,128)(2,1)} %get-tuple-element.52), channel_id=1, source_target_pairs={{0,3},{1,2},{2,1},{3,0},{4,7},{5,6},{6,5},{7,4},{8,11},{9,10},{10,... | collective-permute-start | bytes 983048 | tf_op jit(solution)/shard_map/ppermute | solution.py:620
  139.4 11.9 %collective-permute-start.13 = (bf16[256,640]{1,0:T(8,128)(2,1)}, bf16[256,640]{1,0:T(8,128)(2,1)S(1)}, u32[]{:S(2)}, u32[]{:S(2)}) collective-permute-start(bf16[256,640]{1,0:T(8,128)(2,1)} %get-tuple-element.57), channel_id=1, source_target_pairs={{0,1},{1,0},{2,3},{3,2},{4,5},{5,4},{6,7},{7,6},{8,9},{9,8},{10,11... | collective-permute-start | bytes 983048 | tf_op jit(solution)/shard_map/ppermute | solution.py:620
  139.8 15.8 %collective-permute-start.14 = (bf16[256,640]{1,0:T(8,128)(2,1)S(1)}, bf16[256,640]{1,0:T(8,128)(2,1)S(1)}, u32[]{:S(2)}, u32[]{:S(2)}) collective-permute-start(bf16[256,640]{1,0:T(8,128)(2,1)S(1)} %get-tuple-element.58), channel_id=1, source_target_pairs={{0,2},{1,3},{2,0},{3,1},{4,6},{5,7},{6,4},{7,5},{8,10},{9,11},{10,... | collective-permute-start | bytes 983048 | tf_op jit(solution)/shard_map/ppermute | solution.py:620
  144.6 0.7 copy-start.5
  145.4 10.3 %copy-start.1 = (bf16[256,640]{1,0:T(8,128)(2,1)S(1)}, bf16[256,640]{1,0:T(8,128)(2,1)}, u32[]{:S(2)}) copy-start(bf16[256,640]{1,0:T(8,128)(2,1)} %get-tuple-element.56.refs_0_) | copy-start | bytes 983044
  149.8 12.6 %copy-start.2 = (bf16[128,640]{1,0:T(8,128)(2,1)S(1)}, bf16[128,640]{1,0:T(8,128)(2,1)}, u32[]{:S(2)}) copy-start(bf16[128,640]{1,0:T(8,128)(2,1)} %get-tuple-element.53.refs_1_) | copy-start | bytes 491524
  149.8 13.9 %collective-permute-start.9 = (bf16[128,640]{1,0:T(8,128)(2,1)}, bf16[128,640]{1,0:T(8,128)(2,1)S(1)}, u32[]{:S(2)}, u32[]{:S(2)}) collective-permute-start(bf16[128,640]{1,0:T(8,128)(2,1)} %get-tuple-element.49), channel_id=1, source_target_pairs={{0,3},{1,2},{2,1},{3,0},{4,7},{5,6},{6,5},{7,4},{8,11},{9,10},{10,... | collective-permute-start | bytes 491528 | tf_op jit(solution)/shard_map/ppermute | solution.py:620
  150.6 6.4 %collective-permute-start.11 = (bf16[128,640]{1,0:T(8,128)(2,1)}, bf16[128,640]{1,0:T(8,128)(2,1)S(1)}, u32[]{:S(2)}, u32[]{:S(2)}) collective-permute-start(bf16[128,640]{1,0:T(8,128)(2,1)} %get-tuple-element.54), channel_id=1, source_target_pairs={{0,1},{1,0},{2,3},{3,2},{4,5},{5,4},{6,7},{7,6},{8,9},{9,8},{10,11... | collective-permute-start | bytes 491528 | tf_op jit(solution)/shard_map/ppermute | solution.py:620
  151.3 11.1 %collective-permute-start.12 = (bf16[128,640]{1,0:T(8,128)(2,1)S(1)}, bf16[128,640]{1,0:T(8,128)(2,1)S(1)}, u32[]{:S(2)}, u32[]{:S(2)}) collective-permute-start(bf16[128,640]{1,0:T(8,128)(2,1)S(1)} %get-tuple-element.55), channel_id=1, source_target_pairs={{0,2},{1,3},{2,0},{3,1},{4,6},{5,7},{6,4},{7,5},{8,10},{9,11},{10,... | collective-permute-start | bytes 491528 | tf_op jit(solution)/shard_map/ppermute | solution.py:620
  152.0 11.7 %copy-start.9 = (f32[100,1,2,2,640]{4,3,2,1,0:T(2,128)}, f32[100,1,2,2,640]{4,3,2,1,0:T(2,128)S(1)}, u32[]{:S(2)}) copy-start(f32[100,1,2,2,640]{4,3,2,1,0:T(2,128)S(1)} %bitcast_dynamic-update-slice_fusion) | copy-start | bytes 3072004

commit v7 on v6

--- a/solution.py
+++ b/solution.py
@@ -13,7 +13,7 @@
 BF16 = jnp.bfloat16
 F32 = jnp.float32
 MIB = 1024 * 1024
-VMEM_LIMIT = 20 * MIB
+VMEM_LIMIT = 24 * MIB
 LEGENDRE_LIMIT = 36 * MIB
 WHOLE_LIMIT = 60 * MIB
 STEP = 128
@@ -159,7 +159,7 @@
         out_shape=[jax.ShapeDtypeStruct((2 * width, columns), BF16) for _ in masks for width in widths],
         scratch_shapes=[
             pltpu.VMEM((len(masks), 2, lat_rows, columns), F32),
-            pltpu.SemaphoreType.DMA((len(masks), 2, columns // LANES if columns % LANES == 0 else 1)),
+            pltpu.SemaphoreType.DMA((len(masks), 2, 1)),
         ],
         compiler_params=pltpu.CompilerParams(vmem_limit_bytes=WHOLE_LIMIT),
         name="wind_products",
@@ -345,7 +345,7 @@
         out_specs=[vmem] * count,
         out_shape=[jax.ShapeDtypeStruct((rows, table.shape[1]), BF16)] * count,
         cost_estimate=pl.CostEstimate(flops=3 * 10**9, bytes_accessed=10**7, transcendentals=0),
-        compiler_params=pltpu.CompilerParams(vmem_limit_bytes=WHOLE_LIMIT),
+        compiler_params=pltpu.CompilerParams(vmem_limit_bytes=VMEM_LIMIT),
         name="backward_rest",
     )(by_wave, table, *turns)
 
@@ -419,9 +419,9 @@
     return LANES if 2 * rows % LANES == 0 else 2 * rows
 
 
-def legendre_kernel(sides, widths, group, place, order, blocks, damping, basis, *rest):
+def legendre_kernel(sides, widths_in, widths, group, place, order, blocks, damping, basis, *rest):
     wires = len(widths)
-    received, rest = rest[:wires], rest[wires:]
+    received, rest = rest[: len(widths_in)], rest[len(widths_in) :]
     spectral_out, returned_out, rest = rest[0], rest[1 : 1 + wires], rest[1 + wires :]
     spectral, returned, (held, buffer, sems, out_sems, spectral_sem) = rest[0], rest[1 : 1 + wires], rest[1 + wires :]
     lat_rows = sum(widths)
@@ -461,11 +461,12 @@
     for index in range(min(DEPTH - 1, groups)):
         fetch(index)
 
-    def wire_pieces(wire, device, wire_block):
+    def wire_pieces(kinds, wire, device, wire_block):
         source, sector = divmod(device, sectors)
         side, near = (0, source) if source < sources // 2 else (1, sources - 1 - source)
-        lanes, chunk_width = received[wire].shape[2], widths[wire]
-        begin = near * lat_rows + chunk_start(widths, wire, near)
+        chunk_width = kinds[wire]
+        lanes = wire_lanes(fields * chunk_width)
+        begin = near * lat_rows + chunk_start(kinds, wire, near)
         column, end = wire_block * lanes, (wire_block + 1) * lanes
         while column < end:
             part_field, lat = divmod(column, chunk_width)
@@ -476,12 +477,12 @@
             yield column - wire_block * lanes, width, row, at // LANES, at % LANES
             column += width
 
-    for wire in range(wires):
+    for wire in range(len(widths_in)):
         wire_blocks = received[wire].shape[1] // share
         for device in range(devices):
             own_blocks = unpack_rows(received[wire][device].astype(F32), wire_blocks, stride)
             for wire_block, piece in enumerate(own_blocks):
-                for at, width, row, block, lane in wire_pieces(wire, device, wire_block):
+                for at, width, row, block, lane in wire_pieces(widths_in, wire, device, wire_block):
                     held[block, row : row + stride, lane : lane + width] = piece[:, at : at + width]
 
     def load_slot(slot):
@@ -536,13 +537,13 @@
     spectral_copy.start()
     out_copies = []
     for wire in range(wires):
-        wire_blocks = received[wire].shape[1] // share
+        wire_blocks = returned[wire].shape[1] // share
         for device in range(devices):
             pieces = []
             for wire_block in range(wire_blocks):
                 parts = [
                     held[block, row : row + share, lane : lane + width]
-                    for _, width, row, block, lane in wire_pieces(wire, device, wire_block)
+                    for _, width, row, block, lane in wire_pieces(widths, wire, device, wire_block)
                 ]
                 pieces.append(jnp.concatenate(parts, axis=1) if len(parts) > 1 else parts[0])
             returned[wire][device] = pack_rows(pieces).astype(BF16)
@@ -557,22 +558,27 @@
         copy.wait()
 
 
-def legendre(received, basis, damping, place, order, blocks, sectors, sides, widths, group):
+def legendre(received, basis, damping, place, order, blocks, sectors, sides, widths_in, widths, group):
     share = order.shape[0]
+    devices = received[0].shape[0]
+    returned = []
+    for width in widths:
+        lanes = wire_lanes(2 * width)
+        returned.append((devices, share * (4 * width // lanes), lanes))
     degrees, half_lat = basis.shape[1:]
     combos = sectors * sides
     smem, vmem, hbm = (pl.BlockSpec(memory_space=space) for space in (pltpu.SMEM, pltpu.VMEM, pl.ANY))
     return pl.pallas_call(
-        functools.partial(legendre_kernel, sides, widths, group),
-        in_specs=[smem, smem, smem, vmem, hbm] + [vmem] * len(widths),
+        functools.partial(legendre_kernel, sides, widths_in, widths, group),
+        in_specs=[smem, smem, smem, vmem, hbm] + [vmem] * len(widths_in),
         out_specs=[pl.BlockSpec(memory_space=pltpu.HBM)] * (1 + len(widths)),
         out_shape=[
             jax.ShapeDtypeStruct((sectors, share, sides, degrees), F32),
-            *[jax.ShapeDtypeStruct(wire.shape, BF16) for wire in received],
+            *[jax.ShapeDtypeStruct(wire, BF16) for wire in returned],
         ],
         scratch_shapes=[
             pltpu.VMEM((sectors, share, sides, degrees), F32),
-            *[pltpu.VMEM(wire.shape, BF16) for wire in received],
+            *[pltpu.VMEM(wire, BF16) for wire in returned],
             pltpu.VMEM((half_lat // LANES, 2 * combos * round_up(share, 8), LANES), F32),
             pltpu.VMEM((DEPTH, group, degrees, half_lat), BF16),
             pltpu.SemaphoreType.DMA((DEPTH, group)),
@@ -623,15 +629,15 @@
         return jnp.stack([sector_index ^ mask for mask in some]).astype(jnp.int32)
 
     far, rest = masks[:1], masks[1:]
-    widths = chunk_widths(lat_rows)
-    small_first = list(range(len(widths)))[::-1]
-
-    first_made = wind_products(wind_u, wind_v, far, widths)
+    whole, widths = (lat_rows,), chunk_widths(lat_rows)
+    small_first = [0]
+
+    first_made = wind_products(wind_u, wind_v, far, whole)
     lines = {}
     for chunk in small_first[:1]:
         for mask in far:
             lines[chunk, mask] = across(first_made[chunk, mask], mask)
-    made = {**first_made, **wind_products(wind_u, wind_v, rest, widths)}
+    made = {**first_made, **wind_products(wind_u, wind_v, rest, whole)}
     for chunk in small_first:
         for mask in masks:
             if (chunk, mask) not in lines:
@@ -644,9 +650,8 @@
     named = jnp.where((place_slot < share) & (in_owner < capacity), place_owner * capacity + in_owner, -1)
     forward_table, one_hot = wave_table(lon_cols, waves, length, True, named, wave_slots)
     backward_table, one_hot_turned = wave_table(waves, lon_cols, length, False, named, wave_slots)
-    forward_table, one_hot, backward_table, one_hot_turned = (
-        pltpu.with_memory_space_constraint(value, pltpu.HBM)
-        for value in (forward_table, one_hot, backward_table, one_hot_turned)
+    backward_table, one_hot_turned = (
+        pltpu.with_memory_space_constraint(value, pltpu.HBM) for value in (backward_table, one_hot_turned)
     )
     turns = sector_turns(sectors, waves)
 
@@ -673,7 +678,7 @@
 
     by_arrival = list(dict.fromkeys([0, *[mask for mask in reversed(masks) if mask < sectors // 2], *masks]))
     early, late = by_arrival[:-1], by_arrival[-1:]
-    received = [None] * len(widths)
+    received = [None]
     for chunk in small_first:
         own = {mask: lines[chunk, mask] for mask in masks}
         if chunk == 0:
@@ -684,7 +689,7 @@
         received[chunk] = lax.all_to_all(fourier, ("lat", "lon"), split_axis=0, concat_axis=0, tiled=True)
     place = jnp.stack([first, sector_index]).astype(jnp.int32)
     spectral, *returned = legendre(
-        received, basis, damping, place, order, blocks, sectors, sides, widths, group
+        received, basis, damping, place, order, blocks, sectors, sides, whole, widths, group
     )
 
     exact = sectors in (1, 2, 4)
@@ -700,7 +705,6 @@
         mirror = (ids[:, None] == jnp.where(south, width - 1 - ids, ids)[None, :]).astype(BF16)
         far_lines, by_wave = backward_first(regrouped[chunk], backward_table, far_turns, one_hot_turned, mirror, exact)
         back[chunk, far[0]] = across(far_lines, far[0])
-        by_wave = pltpu.with_memory_space_constraint(by_wave, pltpu.HBM)
         others = backward_rest(by_wave, backward_table, rest_turns, exact)
         for mask, value in zip(rest, others):
             back[chunk, mask] = across(value, mask)

time: 165 us -> 165 us (level)
  waiting for transfers between devices: 42.7 us -> 63.2 us
  Pallas kernels: 74 us -> 61.8 us
  starting transfers between devices: 33.6 us -> 26.6 us
    ppermute x15 -> x12, waiting for transfers between devices: 17 us -> 29 us  [across(): lax.ppermute(value, 'lon', [(i, i ^ mask) for i in range(sectors)])]
    pallas_call x3 -> x2, Pallas kernels: 18.9 us -> 10.4 us  [forward(): pl.pallas_call(functools.partial(forward_kernel, len(lines), earlier is n...]
    all_to_all x2 -> x1, waiting for transfers between devices: 21.5 us -> 28.9 us  [body(): lax.all_to_all(fourier, ('lat', 'lon'), split_axis=0, concat_axis=0, tile...]
    all_to_all x2 -> x1, starting transfers between devices: 11.4 us -> 6.82 us  [body(): lax.all_to_all(fourier, ('lat', 'lon'), split_axis=0, concat_axis=0, tile...]
    pallas_call x2, Pallas kernels: 8.31 us -> 5.35 us  [wind_products(): pl.pallas_call(functools.partial(product_kernel, masks, widths), in_specs...]
    ppermute x15 -> x12, starting transfers between devices: 12 us -> 9.88 us  [across(): lax.ppermute(value, 'lon', [(i, i ^ mask) for i in range(sectors)])]
    gather x6 -> x4, local copies, waits for them, and re-layouts: 3.38 us -> 2.25 us  [turns_of(): return tuple((jnp.take(turn, at, axis=0) for turn in turns))]
    unnamed x30 -> x26, local copies, waits for them, and re-layouts: 3.42 us -> 2.87 us
  transfers between devices with their start and end apart: 19 -> 15, of which waited for: 9 -> 8; matrix products, arithmetic and copies ran while one was open for 6% -> 5% of each run, Pallas kernels for 33% -> 23%
where the time goes in v7:
time: 165 us; the launch traced here: 164 us
  waiting for transfers between devices  63.2 us (38%)
  Pallas kernels  61.8 us (37%)
  starting transfers between devices  26.6 us (16%)
  local copies, waits for them, and re-layouts  7.9 us (5%)
  other arithmetic  3.3 us (2%)
    ppermute x12, waiting for transfers between devices, across(): lax.ppermute(value, 'lon', [(i, i ^ mask) for i in range(sectors)])  29 us
    all_to_all x1, waiting for transfers between devices, body(): lax.all_to_all(fourier, ('lat', 'lon'), split_axis=0, concat_axis=0, tile...  28.9 us
    pallas_call x1, Pallas kernels, legendre(): pl.pallas_call(functools.partial(legendre_kernel, sides, widths_in, width...  15.6 us
    pallas_call x2, Pallas kernels, forward(): pl.pallas_call(functools.partial(forward_kernel, len(lines), earlier is n...  10.4 us
    all_to_all x2, starting transfers between devices, body(): lax.all_to_all(wire, ('lat', 'lon'), split_axis=0, concat_axis=0, tiled=T...  9.89 us
    ppermute x12, starting transfers between devices, across(): lax.ppermute(value, 'lon', [(i, i ^ mask) for i in range(sectors)])  9.88 us
    pallas_call x2, Pallas kernels, backward_rest(): pl.pallas_call(functools.partial(backward_rest_kernel, exact), in_specs=[...  9.45 us
    pallas_call x2, Pallas kernels, backward_first(): pl.pallas_call(functools.partial(backward_first_kernel, exact), in_specs=...  9.26 us
  transfers between devices with their start and end apart: 15, of which 8 were waited for; matrix products, arithmetic and copies ran while one was open for 5% of the time, Pallas kernels for 23%

profile of v7, /device:TPU:0, one launch (start us, length us, event | category | flops | bytes accessed | tf_op | source)
XLA Modules:
  0.0 164.1 jit_solution(3696981861712481205)
XLA Ops:
  0.6 3.0 %wind_products.2 = (bf16[384,640]{1,0:T(8,128)(2,1)}, bf16[384,640]{1,0:T(8,128)(2,1)}, bf16[384,640]{1,0:T(8,128)(2,1)}) custom-call(f32[4,192,640]{2,1,0:T(8,128)} %wind_u.3, f32[4,192,640]{2,1,0:T(8,128)} %wind_v.3), custom_call_target="tpu_custom_call" | custom-call | tf_op jit(solution)/shard_map/wind_products/pallas_call | solution.py:155
  3.7 2.5 %collective-permute-start = (bf16[384,640]{1,0:T(8,128)(2,1)}, bf16[384,640]{1,0:T(8,128)(2,1)S(1)}, u32[]{:S(2)}, u32[]{:S(2)}) collective-permute-start(bf16[384,640]{1,0:T(8,128)(2,1)} %get-tuple-element.26), channel_id=1, source_target_pairs={{0,3},{1,2},{2,1},{3,0},{4,7},{5,6},{6,5},{7,4},{8,11},{9,10},{10,... | collective-permute-start | bytes 1474568 | tf_op jit(solution)/shard_map/ppermute | solution.py:626
  6.2 0.7 collective-permute-start.1
  6.9 2.3 %wind_products.3 = bf16[384,640]{1,0:T(8,128)(2,1)} custom-call(f32[4,192,640]{2,1,0:T(8,128)} %wind_u.3, f32[4,192,640]{2,1,0:T(8,128)} %wind_v.3), custom_call_target="tpu_custom_call" | custom-call | tf_op jit(solution)/shard_map/wind_products/pallas_call | solution.py:155
  9.3 0.1 collective-permute-start.2
  9.4 0.1 compare_and_fusion
  9.5 0.6 gather_fusion.1
  10.0 0.6 gather_fusion
  10.6 0.1 broadcast_select_fusion.2
  10.7 1.0 fusion.11.named
  11.7 0.6 broadcast_in_dim.110.wave_slots
  12.3 4.3 %wave_table.2 = (bf16[1280,1280]{1,0:T(8,128)(2,1)}, bf16[1024,640]{1,0:T(8,128)(2,1)}) custom-call(f32[32,640]{1,0:T(8,128)} %constant.145.clone.near_cos, f32[32,640]{1,0:T(8,128)} %constant.146.clone.near_sin, f32[20,1,640]{2,1,0:T(1,128)} %constant.147.clone.far_cos, f32[20,1,640]{2,1,0:T(1,128)} %constant.148.clone.far_sin, s32[1024,1]{1,0:T(8,128)} %fusion.11.named, ...), custom_call_target="tpu_custom_call" | custom-call | tf_op jit(solution)/shard_map/wave_table/pallas_call | solution.py:76
  16.7 12.0 %collective-permute-done.2.refs_2_ = bf16[384,640]{1,0:T(8,128)(2,1)S(1)} collective-permute-done((bf16[384,640]{1,0:T(8,128)(2,1)}, bf16[384,640]{1,0:T(8,128)(2,1)S(1)}, u32[]{:S(2)}, u32[]{:S(2)}) %collective-permute-start.2) | collective-permute-done | bytes 491552 | tf_op jit(solution)/shard_map/ppermute | solution.py:626
  28.7 1.9 %copy-done = bf16[1280,1280]{1,0:T(8,128)(2,1)S(1)} copy-done((bf16[1280,1280]{1,0:T(8,128)(2,1)S(1)}, bf16[1280,1280]{1,0:T(8,128)(2,1)}, u32[]{:S(2)}) %copy-start) | copy-done | bytes 3276824
  30.6 5.1 %forward.2.refs_4_ = f32[2,384,640]{2,1,0:T(8,128)S(1)} custom-call(bf16[384,640]{1,0:T(8,128)(2,1)S(1)} %copy-done.4, bf16[384,640]{1,0:T(8,128)(2,1)S(1)} %collective-permute-done.1.refs_1_, bf16[384,640]{1,0:T(8,128)(2,1)S(1)} %collective-permute-done.2.refs_2_, bf16[1280,1280]{1,0:T(8,128)(2,1)S(1)} %copy-done, ...), custom_call_target="tpu_custom_call" | custom-call | flops 3774873600 | bytes 10000000 | tf_op jit(solution)/shard_map/forward/pallas_call | solution.py:242
  35.8 5.2 %forward.3 = bf16[32,150,128]{2,1,0:T(8,128)(2,1)} custom-call(bf16[384,640]{1,0:T(8,128)(2,1)S(1)} %collective-permute-done.refs_0_, bf16[1280,1280]{1,0:T(8,128)(2,1)S(1)} %copy-done.1, f32[1,1,640]{2,1,0:T(1,128)S(1)} %get-tuple-element.81.refs_2_, f32[1,1,640]{2,1,0:T(1,128)S(1)} %get-tuple-element.72.refs_3_, f32[2,384,640]{2,1,0:T(8,128)S(1)} %forward.2.refs_4_, ...), custom_call_target="tpu_custom_call" | custom-call | flops 1258291200 | bytes 10000000 | tf_op jit(solution)/shard_map/forward/pallas_call | solution.py:242
  41.1 6.8 %all-to-all-start = ((bf16[32,150,128]{2,1,0:T(8,128)(2,1)}), bf16[32,150,128]{2,1,0:T(8,128)(2,1)S(1)}, u32[]{:S(2)}, u32[]{:S(2)}) async-start(bf16[32,150,128]{2,1,0:T(8,128)(2,1)} %forward.3), calls=%async_computation | async-start | bytes 2490368 | tf_op jit(solution)/shard_map/all_to_all | solution.py:689
  47.9 0.2 fusion.18
  48.2 0.2 convert_reduce_fusion
  48.3 0.1 select_reduce_fusion
  48.4 0.1 slice.19
  48.6 0.1 mul.91
  48.7 0.1 pad_add_fusion.place
  48.8 0.1 iota_compare_fusion
  48.9 0.1 fusion.21
  49.0 0.3 multiply_select_fusion.damping
  49.2 28.9 %all-to-all-done.rest_0_ = bf16[32,150,128]{2,1,0:T(8,128)(2,1)S(1)} async-done(((bf16[32,150,128]{2,1,0:T(8,128)(2,1)}), bf16[32,150,128]{2,1,0:T(8,128)(2,1)S(1)}, u32[]{:S(2)}, u32[]{:S(2)}) %all-to-all-start) | async-done | bytes 1228832 | tf_op jit(solution)/shard_map/all_to_all | solution.py:689
  78.1 15.6 %legendre.1 = (f32[4,25,4,640]{3,2,1,0:T(4,128)S(1)}, bf16[32,100,128]{2,1,0:T(8,128)(2,1)S(1)}, bf16[32,50,128]{2,1,0:T(8,128)(2,1)}) custom-call(s32[2]{0:T(128)S(1)} %pad_add_fusion.place, s32[25]{0:T(128)S(1)} %get-tuple-element.62.order, s32[5]{0:T(128)S(1)} %and_select_fusion.5.blocks, f32[25,16,640]{2,1,0:T(8,128)S(1)} %multiply_select_fusion.damping, ...), custom_call_target="tpu_custom_call" | custom-call | flops 1572864000 | bytes 24576000 | tf_op jit(solution)/shard_map/legendre/pallas_call | solution.py:571
  93.8 0.9 copy-done.3
  94.6 6.3 %all-to-all-start.1 = ((bf16[32,100,128]{2,1,0:T(8,128)(2,1)}), bf16[32,100,128]{2,1,0:T(8,128)(2,1)S(1)}, u32[]{:S(2)}, u32[]{:S(2)}) async-start(bf16[32,100,128]{2,1,0:T(8,128)(2,1)} %copy-done.3), calls=%async_computation.1 | async-start | bytes 1703936 | tf_op jit(solution)/shard_map/all_to_all | solution.py:702
  100.9 0.6 gather_fusion.3
  101.5 0.6 gather_fusion.2
  102.1 0.6 and_select_fusion.1.named
  102.7 4.1 %wave_table.3 = (bf16[2560,640]{1,0:T(8,128)(2,1)}, bf16[640,1024]{1,0:T(8,128)(2,1)}) custom-call(f32[32,640]{1,0:T(8,128)} %constant.145.clone.near_cos, f32[32,640]{1,0:T(8,128)} %constant.146.clone.near_sin, f32[20,1,640]{2,1,0:T(1,128)} %constant.147.clone.far_cos, f32[20,1,640]{2,1,0:T(1,128)} %constant.148.clone.far_sin, ...), custom_call_target="tpu_custom_call" | custom-call | tf_op jit(solution)/shard_map/wave_table/pallas_call | solution.py:76
  106.8 0.2 convert.10
  107.0 0.2 slice_convert_fusion
  107.2 1.8 %collective-permute-start.3 = (bf16[25,4,640]{2,1,0:T(4,128)(2,1)S(1)}, bf16[25,4,640]{2,1,0:T(4,128)(2,1)S(1)}, u32[]{:S(2)}, u32[]{:S(2)}) collective-permute-start(bf16[25,4,640]{2,1,0:T(4,128)(2,1)S(1)} %get-tuple-element.70), channel_id=1, source_target_pairs={{0,2},{1,3},{2,0},{3,1},{4,6},{5,7},{6,4},{7,5},{8,10},{9,11},{10,... | collective-permute-start | bytes 384008 | tf_op jit(solution)/shard_map/ppermute | solution.py:626
  109.0 0.4 collective-permute-start.5
  109.4 0.1 broadcast_select_fusion
  109.5 0.2 reshape.461
  109.7 5.5 %collective-permute-done.3 = bf16[25,4,640]{2,1,0:T(4,128)(2,1)S(1)} collective-permute-done((bf16[25,4,640]{2,1,0:T(4,128)(2,1)S(1)}, bf16[25,4,640]{2,1,0:T(4,128)(2,1)S(1)}, u32[]{:S(2)}, u32[]{:S(2)}) %collective-permute-start.3) | collective-permute-done | bytes 128032 | tf_op jit(solution)/shard_map/ppermute | solution.py:626
  115.2 0.2 reshape.456
  115.4 2.6 %collective-permute-done.4 = bf16[25,4,640]{2,1,0:T(4,128)(2,1)S(1)} collective-permute-done((bf16[25,4,640]{2,1,0:T(4,128)(2,1)S(1)}, bf16[25,4,640]{2,1,0:T(4,128)(2,1)S(1)}, u32[]{:S(2)}, u32[]{:S(2)}) %collective-permute-start.4) | collective-permute-done | bytes 128032 | tf_op jit(solution)/shard_map/ppermute | solution.py:626
  118.1 0.2 reshape.458
  118.3 0.2 reshape.460
  118.4 0.3 broadcast_in_dim.102
  118.8 4.1 %all-to-all-done.1.wire = bf16[32,100,128]{2,1,0:T(8,128)(2,1)S(1)} async-done(((bf16[32,100,128]{2,1,0:T(8,128)(2,1)}), bf16[32,100,128]{2,1,0:T(8,128)(2,1)S(1)}, u32[]{:S(2)}, u32[]{:S(2)}) %all-to-all-start.1) | async-done | bytes 819232 | tf_op jit(solution)/shard_map/all_to_all | solution.py:702
  122.9 3.6 %all-to-all-start.2 = ((bf16[32,50,128]{2,1,0:T(8,128)(2,1)}), bf16[32,50,128]{2,1,0:T(8,128)(2,1)S(1)}, u32[]{:S(2)}, u32[]{:S(2)}) async-start(bf16[32,50,128]{2,1,0:T(8,128)(2,1)} %get-tuple-element.34), calls=%async_computation.2 | async-start | bytes 917504 | tf_op jit(solution)/shard_map/all_to_all | solution.py:702
  126.7 5.1 %backward_first.3 = (bf16[256,640]{1,0:T(8,128)(2,1)S(1)}, bf16[2,256,640]{2,1,0:T(8,128)(2,1)S(1)}) custom-call(bf16[32,100,128]{2,1,0:T(8,128)(2,1)S(1)} %all-to-all-done.1.wire, bf16[2560,640]{1,0:T(8,128)(2,1)} %get-tuple-element.35.table_hbm.table, f32[1,1,640]{2,1,0:T(1,128)S(1)} %get-tuple-element.82.turn_cos, ...), custom_call_target="tpu_custom_call" | custom-call | flops 1000000000 | bytes 10000000 | tf_op jit(solution)/shard_map/backward_first/pallas_call | solution.py:310
  131.8 5.8 %backward_rest.3 = (bf16[256,640]{1,0:T(8,128)(2,1)S(1)}, bf16[256,640]{1,0:T(8,128)(2,1)}, bf16[256,640]{1,0:T(8,128)(2,1)S(1)}) custom-call(bf16[2,256,640]{2,1,0:T(8,128)(2,1)S(1)} %get-tuple-element.40.by_wave, bf16[2560,640]{1,0:T(8,128)(2,1)} %get-tuple-element.35.table_hbm.table, f32[3,1,640]{2,1,0:T(1,128)S(1)} %get-tuple-element.76.turn_cos, ...), custom_call_target="tpu_custom_call" | custom-call | flops 3000000000 | bytes 10000000 | tf_op jit(solution)/shard_map/backward_rest/pallas_call | solution.py:342
  137.7 1.5 collective-permute-start.7
  139.1 0.4 collective-permute-start.10
  139.5 0.3 collective-permute-start.11
  139.8 1.2 all-to-all-done.2.wire
  141.0 4.1 %backward_first.2 = (bf16[128,640]{1,0:T(8,128)(2,1)S(1)}, bf16[2,128,640]{2,1,0:T(8,128)(2,1)S(1)}) custom-call(bf16[32,50,128]{2,1,0:T(8,128)(2,1)S(1)} %all-to-all-done.2.wire, bf16[2560,640]{1,0:T(8,128)(2,1)} %get-tuple-element.35.table_hbm.table, f32[1,1,640]{2,1,0:T(1,128)S(1)} %get-tuple-element.82.turn_cos, ...), custom_call_target="tpu_custom_call" | custom-call | flops 1000000000 | bytes 10000000 | tf_op jit(solution)/shard_map/backward_first/pallas_call | solution.py:310
  145.1 3.6 %backward_rest.2 = (bf16[128,640]{1,0:T(8,128)(2,1)S(1)}, bf16[128,640]{1,0:T(8,128)(2,1)S(1)}, bf16[128,640]{1,0:T(8,128)(2,1)S(1)}) custom-call(bf16[2,128,640]{2,1,0:T(8,128)(2,1)S(1)} %get-tuple-element.37.by_wave, bf16[2560,640]{1,0:T(8,128)(2,1)} %get-tuple-element.35.table_hbm.table, f32[3,1,640]{2,1,0:T(1,128)S(1)} %get-tuple-element.76.turn_cos, ...), custom_call_target="tpu_custom_call" | custom-call | flops 3000000000 | bytes 10000000 | tf_op jit(solution)/shard_map/backward_rest/pallas_call | solution.py:342
  148.8 0.7 collective-permute-start.6
  149.6 1.4 collective-permute-start.9
  151.0 0.7 bitcast_dynamic-update-slice_fusion
  151.7 3.4 %collective-permute-done.11.refs_2_ = bf16[256,640]{1,0:T(8,128)(2,1)S(1)} collective-permute-done((bf16[256,640]{1,0:T(8,128)(2,1)S(1)}, bf16[256,640]{1,0:T(8,128)(2,1)S(1)}, u32[]{:S(2)}, u32[]{:S(2)}) %collective-permute-start.11) | collective-permute-done | bytes 327712 | tf_op jit(solution)/shard_map/ppermute | solution.py:626
  155.1 1.3 placed.3.refs_4_
  156.5 5.4 %collective-permute-done.9.refs_3_ = bf16[128,640]{1,0:T(8,128)(2,1)S(1)} collective-permute-done((bf16[128,640]{1,0:T(8,128)(2,1)S(1)}, bf16[128,640]{1,0:T(8,128)(2,1)S(1)}, u32[]{:S(2)}, u32[]{:S(2)}) %collective-permute-start.9) | collective-permute-done | bytes 163872 | tf_op jit(solution)/shard_map/ppermute | solution.py:626
  161.9 1.2 placed.4.refs_1_
  163.1 0.8 placed.5
  (47 shorter events, 0.5 us)
Async XLA Ops:
  3.7 32.1 %collective-permute-start = (bf16[384,640]{1,0:T(8,128)(2,1)}, bf16[384,640]{1,0:T(8,128)(2,1)S(1)}, u32[]{:S(2)}, u32[]{:S(2)}) collective-permute-start(bf16[384,640]{1,0:T(8,128)(2,1)} %get-tuple-element.26), channel_id=1, source_target_pairs={{0,3},{1,2},{2,1},{3,0},{4,7},{5,6},{6,5},{7,4},{8,11},{9,10},{10,... | collective-permute-start | bytes 1474568 | tf_op jit(solution)/shard_map/ppermute | solution.py:626
  6.2 3.3 %copy-start.6 = (f32[4,640]{1,0:T(4,128)S(1)}, f32[4,640]{1,0:T(4,128)}, u32[]{:S(2)}) copy-start(f32[4,640]{1,0:T(4,128)} %constant.191) | copy-start | bytes 30724
  6.2 3.8 %copy-start.5 = (f32[4,640]{1,0:T(4,128)S(1)}, f32[4,640]{1,0:T(4,128)}, u32[]{:S(2)}) copy-start(f32[4,640]{1,0:T(4,128)} %constant.190) | copy-start | bytes 30724
  6.2 5.5 %copy-start.8 = (s32[640]{0:T(1024)S(1)}, s32[640]{0:T(1024)}, u32[]{:S(2)}) copy-start(s32[640]{0:T(1024)} %param.23) | copy-start | bytes 7684
  6.2 10.5 %copy-start.10 = (f32[4,1,640]{2,1,0:T(1,128)S(1)}, f32[4,1,640]{2,1,0:T(1,128)}, u32[]{:S(2)}) copy-start(f32[4,1,640]{2,1,0:T(1,128)} %constant.150.clone2.4) | copy-start | bytes 30724
  6.2 10.5 %copy-start.11 = (f32[4,1,640]{2,1,0:T(1,128)S(1)}, f32[4,1,640]{2,1,0:T(1,128)}, u32[]{:S(2)}) copy-start(f32[4,1,640]{2,1,0:T(1,128)} %constant.149.clone2.4) | copy-start | bytes 30724
  6.2 22.5 %copy-start.4 = (bf16[384,640]{1,0:T(8,128)(2,1)S(1)}, bf16[384,640]{1,0:T(8,128)(2,1)}, u32[]{:S(2)}) copy-start(bf16[384,640]{1,0:T(8,128)(2,1)} %get-tuple-element.28.refs_0_) | copy-start | bytes 1474564
  6.2 10.5 %collective-permute-start.1 = (bf16[384,640]{1,0:T(8,128)(2,1)}, bf16[384,640]{1,0:T(8,128)(2,1)S(1)}, u32[]{:S(2)}, u32[]{:S(2)}) collective-permute-start(bf16[384,640]{1,0:T(8,128)(2,1)} %get-tuple-element.29), channel_id=1, source_target_pairs={{0,1},{1,0},{2,3},{3,2},{4,5},{5,4},{6,7},{7,6},{8,9},{9,8},{10,11... | collective-permute-start | bytes 1474568 | tf_op jit(solution)/shard_map/ppermute | solution.py:626
  9.3 19.4 %collective-permute-start.2 = (bf16[384,640]{1,0:T(8,128)(2,1)}, bf16[384,640]{1,0:T(8,128)(2,1)S(1)}, u32[]{:S(2)}, u32[]{:S(2)}) collective-permute-start(bf16[384,640]{1,0:T(8,128)(2,1)} %wind_products.3), channel_id=1, source_target_pairs={{0,2},{1,3},{2,0},{3,1},{4,6},{5,7},{6,4},{7,5},{8,10},{9,11},{10,... | collective-permute-start | bytes 1474568 | tf_op jit(solution)/shard_map/ppermute | solution.py:626
  28.7 1.9 %copy-start = (bf16[1280,1280]{1,0:T(8,128)(2,1)S(1)}, bf16[1280,1280]{1,0:T(8,128)(2,1)}, u32[]{:S(2)}) copy-start(bf16[1280,1280]{1,0:T(8,128)(2,1)} %get-tuple-element.27.refs_3_.refs_1_) | copy-start | bytes 9830404
  30.6 5.2 %copy-start.1 = (bf16[1280,1280]{1,0:T(8,128)(2,1)S(1)}, bf16[1280,1280]{1,0:T(8,128)(2,1)}, u32[]{:S(2)}) copy-start(bf16[1280,1280]{1,0:T(8,128)(2,1)} %get-tuple-element.27.refs_3_.refs_1_) | copy-start | bytes 9830404
  30.6 5.2 %copy-start.2 = (bf16[1024,640]{1,0:T(8,128)(2,1)S(1)}, bf16[1024,640]{1,0:T(8,128)(2,1)}, u32[]{:S(2)}) copy-start(bf16[1024,640]{1,0:T(8,128)(2,1)} %get-tuple-element.30.refs_5_) | copy-start | bytes 3932164
  41.0 6.9 %copy-start.9 = (s32[640]{0:T(1024)S(1)}, s32[640]{0:T(1024)}, u32[]{:S(2)}) copy-start(s32[640]{0:T(1024)} %param.24) | copy-start | bytes 7684
  41.1 7.5 %copy-start.12 = (f32[4]{0:T(128)S(1)}, f32[4]{0:T(128)}, u32[]{:S(2)}) copy-start(f32[4]{0:T(128)} %param.25) | copy-start | bytes 52
  41.1 37.1 %all-to-all-start = ((bf16[32,150,128]{2,1,0:T(8,128)(2,1)}), bf16[32,150,128]{2,1,0:T(8,128)(2,1)S(1)}, u32[]{:S(2)}, u32[]{:S(2)}) async-start(bf16[32,150,128]{2,1,0:T(8,128)(2,1)} %forward.3), calls=%async_computation | async-start | bytes 2490368 | tf_op jit(solution)/shard_map/all_to_all | solution.py:689
  93.7 0.9 copy-start.3
  94.6 28.3 %all-to-all-start.1 = ((bf16[32,100,128]{2,1,0:T(8,128)(2,1)}), bf16[32,100,128]{2,1,0:T(8,128)(2,1)S(1)}, u32[]{:S(2)}, u32[]{:S(2)}) async-start(bf16[32,100,128]{2,1,0:T(8,128)(2,1)} %copy-done.3), calls=%async_computation.1 | async-start | bytes 1703936 | tf_op jit(solution)/shard_map/all_to_all | solution.py:702
  107.2 8.0 %collective-permute-start.3 = (bf16[25,4,640]{2,1,0:T(4,128)(2,1)S(1)}, bf16[25,4,640]{2,1,0:T(4,128)(2,1)S(1)}, u32[]{:S(2)}, u32[]{:S(2)}) collective-permute-start(bf16[25,4,640]{2,1,0:T(4,128)(2,1)S(1)} %get-tuple-element.70), channel_id=1, source_target_pairs={{0,2},{1,3},{2,0},{3,1},{4,6},{5,7},{6,4},{7,5},{8,10},{9,11},{10,... | collective-permute-start | bytes 384008 | tf_op jit(solution)/shard_map/ppermute | solution.py:626
  109.0 9.0 %collective-permute-start.4 = (bf16[25,4,640]{2,1,0:T(4,128)(2,1)S(1)}, bf16[25,4,640]{2,1,0:T(4,128)(2,1)S(1)}, u32[]{:S(2)}, u32[]{:S(2)}) collective-permute-start(bf16[25,4,640]{2,1,0:T(4,128)(2,1)S(1)} %get-tuple-element.69), channel_id=1, source_target_pairs={{0,3},{1,2},{2,1},{3,0},{4,7},{5,6},{6,5},{7,4},{8,11},{9,10},{10,... | collective-permute-start | bytes 384008 | tf_op jit(solution)/shard_map/ppermute | solution.py:626
  109.0 9.2 %collective-permute-start.5 = (bf16[25,4,640]{2,1,0:T(4,128)(2,1)S(1)}, bf16[25,4,640]{2,1,0:T(4,128)(2,1)S(1)}, u32[]{:S(2)}, u32[]{:S(2)}) collective-permute-start(bf16[25,4,640]{2,1,0:T(4,128)(2,1)S(1)} %get-tuple-element.68), channel_id=1, source_target_pairs={{0,1},{1,0},{2,3},{3,2},{4,5},{5,4},{6,7},{7,6},{8,9},{9,8},{10,11... | collective-permute-start | bytes 384008 | tf_op jit(solution)/shard_map/ppermute | solution.py:626
  122.9 18.1 %all-to-all-start.2 = ((bf16[32,50,128]{2,1,0:T(8,128)(2,1)}), bf16[32,50,128]{2,1,0:T(8,128)(2,1)S(1)}, u32[]{:S(2)}, u32[]{:S(2)}) async-start(bf16[32,50,128]{2,1,0:T(8,128)(2,1)} %get-tuple-element.34), calls=%async_computation.2 | async-start | bytes 917504 | tf_op jit(solution)/shard_map/all_to_all | solution.py:702
  126.7 11.0 %copy-start.7 = (f32[100,1,2,2,640]{4,3,2,1,0:T(2,128)}, f32[100,1,2,2,640]{4,3,2,1,0:T(2,128)S(1)}, u32[]{:S(2)}) copy-start(f32[100,1,2,2,640]{4,3,2,1,0:T(2,128)S(1)} %bitcast_dynamic-update-slice_fusion.1) | copy-start | bytes 3072004
  137.7 18.8 %collective-permute-start.7 = (bf16[256,640]{1,0:T(8,128)(2,1)S(1)}, bf16[256,640]{1,0:T(8,128)(2,1)S(1)}, u32[]{:S(2)}, u32[]{:S(2)}) collective-permute-start(bf16[256,640]{1,0:T(8,128)(2,1)S(1)} %get-tuple-element.41), channel_id=1, source_target_pairs={{0,3},{1,2},{2,1},{3,0},{4,7},{5,6},{6,5},{7,4},{8,11},{9,10},{10,... | collective-permute-start | bytes 983048 | tf_op jit(solution)/shard_map/ppermute | solution.py:626
  139.1 10.4 %collective-permute-start.10 = (bf16[256,640]{1,0:T(8,128)(2,1)}, bf16[256,640]{1,0:T(8,128)(2,1)S(1)}, u32[]{:S(2)}, u32[]{:S(2)}) collective-permute-start(bf16[256,640]{1,0:T(8,128)(2,1)} %get-tuple-element.46), channel_id=1, source_target_pairs={{0,1},{1,0},{2,3},{3,2},{4,5},{5,4},{6,7},{7,6},{8,9},{9,8},{10,11... | collective-permute-start | bytes 983048 | tf_op jit(solution)/shard_map/ppermute | solution.py:626
  139.5 15.6 %collective-permute-start.11 = (bf16[256,640]{1,0:T(8,128)(2,1)S(1)}, bf16[256,640]{1,0:T(8,128)(2,1)S(1)}, u32[]{:S(2)}, u32[]{:S(2)}) collective-permute-start(bf16[256,640]{1,0:T(8,128)(2,1)S(1)} %get-tuple-element.47), channel_id=1, source_target_pairs={{0,2},{1,3},{2,0},{3,1},{4,6},{5,7},{6,4},{7,5},{8,10},{9,11},{10,... | collective-permute-start | bytes 983048 | tf_op jit(solution)/shard_map/ppermute | solution.py:626
  148.8 14.4 %collective-permute-start.6 = (bf16[128,640]{1,0:T(8,128)(2,1)S(1)}, bf16[128,640]{1,0:T(8,128)(2,1)S(1)}, u32[]{:S(2)}, u32[]{:S(2)}) collective-permute-start(bf16[128,640]{1,0:T(8,128)(2,1)S(1)} %get-tuple-element.38), channel_id=1, source_target_pairs={{0,3},{1,2},{2,1},{3,0},{4,7},{5,6},{6,5},{7,4},{8,11},{9,10},{10,... | collective-permute-start | bytes 491528 | tf_op jit(solution)/shard_map/ppermute | solution.py:626
  149.5 7.0 %collective-permute-start.8 = (bf16[128,640]{1,0:T(8,128)(2,1)S(1)}, bf16[128,640]{1,0:T(8,128)(2,1)S(1)}, u32[]{:S(2)}, u32[]{:S(2)}) collective-permute-start(bf16[128,640]{1,0:T(8,128)(2,1)S(1)} %get-tuple-element.43), channel_id=1, source_target_pairs={{0,1},{1,0},{2,3},{3,2},{4,5},{5,4},{6,7},{7,6},{8,9},{9,8},{10,11... | collective-permute-start | bytes 491528 | tf_op jit(solution)/shard_map/ppermute | solution.py:626
  149.6 12.3 %collective-permute-start.9 = (bf16[128,640]{1,0:T(8,128)(2,1)S(1)}, bf16[128,640]{1,0:T(8,128)(2,1)S(1)}, u32[]{:S(2)}, u32[]{:S(2)}) collective-permute-start(bf16[128,640]{1,0:T(8,128)(2,1)S(1)} %get-tuple-element.44), channel_id=1, source_target_pairs={{0,2},{1,3},{2,0},{3,1},{4,6},{5,7},{6,4},{7,5},{8,10},{9,11},{10,... | collective-permute-start | bytes 491528 | tf_op jit(solution)/shard_map/ppermute | solution.py:626

commit v8 on v7

--- a/solution.py
+++ b/solution.py
@@ -194,13 +194,12 @@
     blocks = 2 * rows // lanes
     share = wire_rows // blocks
     place = pl.ds(pl.multiple_of(step * size, size), size)
-    by_wave[0, :, place] = real.astype(BF16)
-    by_wave[1, :, place] = (-imag).astype(BF16)
+    by_wave[:rows, place] = real.astype(BF16)
+    by_wave[rows:, place] = (-imag).astype(BF16)
 
     @pl.when(step == pl.num_programs(0) - 1)
     def _():
-        for part in range(2):
-            by_slot[:, part * rows : (part + 1) * rows] = dot(one_hot[...], by_wave[part], NT)
+        by_slot[...] = dot(one_hot[...], by_wave[...], NT)
         copies, out_step = [], devices // sems.shape[0]
         for device in range(devices):
             own = by_slot[device * padded : (device + 1) * padded, :]
@@ -237,7 +236,7 @@
         args.append(one_hot)
         in_specs.append(pl.BlockSpec((slots, waves), lambda i: (0, 0)))
         out_shape, out_spec = jax.ShapeDtypeStruct(out, BF16), pl.BlockSpec(memory_space=pltpu.HBM)
-        scratch = [pltpu.VMEM((2, rows, waves), BF16), pltpu.VMEM((slots, 2 * rows), F32)]
+        scratch = [pltpu.VMEM((2 * rows, waves), BF16), pltpu.VMEM((slots, 2 * rows), F32)]
         scratch += [pltpu.VMEM(out, BF16), pltpu.SemaphoreType.DMA((4,))]
     return pl.pallas_call(
         functools.partial(forward_kernel, len(lines), earlier is not None, end is not None),
@@ -292,11 +291,12 @@
     one_hot_copy.wait()
     wave_ids = lax.broadcasted_iota(jnp.int32, (1, waves), 1)
     weight = jnp.where(wave_ids == 0, 1.0, 2.0).astype(F32)
+    ordered = dot(one_hot[...], by_slot[...]).astype(BF16)
     for part in range(2):
-        ordered = dot(one_hot[...], by_slot[:, part * rows : (part + 1) * rows]).astype(BF16)
         for field in range(2):
             own = slice(field * width, (field + 1) * width)
-            by_wave[part, own, :] = (dot(mirror[...], ordered[:, own], NT) * weight).astype(BF16)
+            lanes_here = slice(part * rows + field * width, part * rows + (field + 1) * width)
+            by_wave[part, own, :] = (dot(mirror[...], ordered[:, lanes_here], NT) * weight).astype(BF16)
     by_wave_copy.start()
     table_copy.wait()
     out[...] = sector_lines(exact, by_wave, table, turn_cos, turn_sin)

time: 165 us -> 164 us (level)
  Pallas kernels: 61.8 us -> 60 us
  transfers between devices with their start and end apart: 15 -> 15, of which waited for: 8 -> 8; matrix products, arithmetic and copies ran while one was open for 5% -> 5% of each run, Pallas kernels for 23% -> 22%
where the time goes in v8:
time: 164 us; the launch traced here: 163 us
  waiting for transfers between devices  63.9 us (39%)
  Pallas kernels  60 us (37%)
  starting transfers between devices  26.6 us (16%)
  local copies, waits for them, and re-layouts  7.9 us (5%)
  other arithmetic  3.3 us (2%)
    ppermute x12, waiting for transfers between devices, across(): lax.ppermute(value, 'lon', [(i, i ^ mask) for i in range(sectors)])  28.9 us
    all_to_all x1, waiting for transfers between devices, body(): lax.all_to_all(fourier, ('lat', 'lon'), split_axis=0, concat_axis=0, tile...  28.9 us
    pallas_call x1, Pallas kernels, legendre(): pl.pallas_call(functools.partial(legendre_kernel, sides, widths_in, width...  15.6 us
    pallas_call x2, Pallas kernels, forward(): pl.pallas_call(functools.partial(forward_kernel, len(lines), earlier is n...  10 us
    all_to_all x2, starting transfers between devices, body(): lax.all_to_all(wire, ('lat', 'lon'), split_axis=0, concat_axis=0, tiled=T...  9.89 us
    ppermute x12, starting transfers between devices, across(): lax.ppermute(value, 'lon', [(i, i ^ mask) for i in range(sectors)])  9.88 us
    pallas_call x2, Pallas kernels, backward_rest(): pl.pallas_call(functools.partial(backward_rest_kernel, exact), in_specs=[...  9.44 us
    pallas_call x2, Pallas kernels, wave_table(): pl.pallas_call(functools.partial(table_kernel, interleaved), out_specs=[p...  8.41 us
  transfers between devices with their start and end apart: 15, of which 8 were waited for; matrix products, arithmetic and copies ran while one was open for 5% of the time, Pallas kernels for 22%

profile of v8, /device:TPU:0, one launch (start us, length us, event | category | flops | bytes accessed | tf_op | source)
XLA Modules:
  0.0 163.0 jit_solution(8967760549321078869)
XLA Ops:
  0.6 3.0 %wind_products.2 = (bf16[384,640]{1,0:T(8,128)(2,1)}, bf16[384,640]{1,0:T(8,128)(2,1)}, bf16[384,640]{1,0:T(8,128)(2,1)}) custom-call(f32[4,192,640]{2,1,0:T(8,128)} %wind_u.3, f32[4,192,640]{2,1,0:T(8,128)} %wind_v.3), custom_call_target="tpu_custom_call" | custom-call | tf_op jit(solution)/shard_map/wind_products/pallas_call | solution.py:155
  3.7 2.5 %collective-permute-start = (bf16[384,640]{1,0:T(8,128)(2,1)}, bf16[384,640]{1,0:T(8,128)(2,1)S(1)}, u32[]{:S(2)}, u32[]{:S(2)}) collective-permute-start(bf16[384,640]{1,0:T(8,128)(2,1)} %get-tuple-element.26), channel_id=1, source_target_pairs={{0,3},{1,2},{2,1},{3,0},{4,7},{5,6},{6,5},{7,4},{8,11},{9,10},{10,... | collective-permute-start | bytes 1474568 | tf_op jit(solution)/shard_map/ppermute | solution.py:626
  6.2 0.7 collective-permute-start.1
  6.9 2.3 %wind_products.3 = bf16[384,640]{1,0:T(8,128)(2,1)} custom-call(f32[4,192,640]{2,1,0:T(8,128)} %wind_u.3, f32[4,192,640]{2,1,0:T(8,128)} %wind_v.3), custom_call_target="tpu_custom_call" | custom-call | tf_op jit(solution)/shard_map/wind_products/pallas_call | solution.py:155
  9.3 0.1 collective-permute-start.2
  9.4 0.1 compare_and_fusion
  9.5 0.6 gather_fusion.1
  10.0 0.6 gather_fusion
  10.6 0.1 broadcast_select_fusion.2
  10.7 1.0 fusion.11.named
  11.7 0.6 broadcast_in_dim.110.wave_slots
  12.3 4.3 %wave_table.2 = (bf16[1280,1280]{1,0:T(8,128)(2,1)}, bf16[1024,640]{1,0:T(8,128)(2,1)}) custom-call(f32[32,640]{1,0:T(8,128)} %constant.145.clone.near_cos, f32[32,640]{1,0:T(8,128)} %constant.146.clone.near_sin, f32[20,1,640]{2,1,0:T(1,128)} %constant.147.clone.far_cos, f32[20,1,640]{2,1,0:T(1,128)} %constant.148.clone.far_sin, s32[1024,1]{1,0:T(8,128)} %fusion.11.named, ...), custom_call_target="tpu_custom_call" | custom-call | tf_op jit(solution)/shard_map/wave_table/pallas_call | solution.py:76
  16.7 12.0 %collective-permute-done.2.refs_2_ = bf16[384,640]{1,0:T(8,128)(2,1)S(1)} collective-permute-done((bf16[384,640]{1,0:T(8,128)(2,1)}, bf16[384,640]{1,0:T(8,128)(2,1)S(1)}, u32[]{:S(2)}, u32[]{:S(2)}) %collective-permute-start.2) | collective-permute-done | bytes 491552 | tf_op jit(solution)/shard_map/ppermute | solution.py:626
  28.7 1.9 %copy-done = bf16[1280,1280]{1,0:T(8,128)(2,1)S(1)} copy-done((bf16[1280,1280]{1,0:T(8,128)(2,1)S(1)}, bf16[1280,1280]{1,0:T(8,128)(2,1)}, u32[]{:S(2)}) %copy-start) | copy-done | bytes 3276824
  30.6 5.1 %forward.2.refs_4_ = f32[2,384,640]{2,1,0:T(8,128)S(1)} custom-call(bf16[384,640]{1,0:T(8,128)(2,1)S(1)} %copy-done.4, bf16[384,640]{1,0:T(8,128)(2,1)S(1)} %collective-permute-done.1.refs_1_, bf16[384,640]{1,0:T(8,128)(2,1)S(1)} %collective-permute-done.2.refs_2_, bf16[1280,1280]{1,0:T(8,128)(2,1)S(1)} %copy-done, ...), custom_call_target="tpu_custom_call" | custom-call | flops 3774873600 | bytes 10000000 | tf_op jit(solution)/shard_map/forward/pallas_call | solution.py:241
  35.8 4.9 %forward.3 = bf16[32,150,128]{2,1,0:T(8,128)(2,1)} custom-call(bf16[384,640]{1,0:T(8,128)(2,1)S(1)} %collective-permute-done.refs_0_, bf16[1280,1280]{1,0:T(8,128)(2,1)S(1)} %copy-done.1, f32[1,1,640]{2,1,0:T(1,128)S(1)} %get-tuple-element.81.refs_2_, f32[1,1,640]{2,1,0:T(1,128)S(1)} %get-tuple-element.72.refs_3_, f32[2,384,640]{2,1,0:T(8,128)S(1)} %forward.2.refs_4_, ...), custom_call_target="tpu_custom_call" | custom-call | flops 1258291200 | bytes 10000000 | tf_op jit(solution)/shard_map/forward/pallas_call | solution.py:241
  40.7 6.8 %all-to-all-start = ((bf16[32,150,128]{2,1,0:T(8,128)(2,1)}), bf16[32,150,128]{2,1,0:T(8,128)(2,1)S(1)}, u32[]{:S(2)}, u32[]{:S(2)}) async-start(bf16[32,150,128]{2,1,0:T(8,128)(2,1)} %forward.3), calls=%async_computation | async-start | bytes 2490368 | tf_op jit(solution)/shard_map/all_to_all | solution.py:689
  47.6 0.2 fusion.18
  47.8 0.2 convert_reduce_fusion
  48.0 0.1 select_reduce_fusion
  48.1 0.1 slice.19
  48.3 0.1 mul.91
  48.4 0.1 iota_compare_fusion
  48.5 0.1 fusion.21
  48.6 0.3 multiply_select_fusion.damping
  48.9 28.9 %all-to-all-done.rest_0_ = bf16[32,150,128]{2,1,0:T(8,128)(2,1)S(1)} async-done(((bf16[32,150,128]{2,1,0:T(8,128)(2,1)}), bf16[32,150,128]{2,1,0:T(8,128)(2,1)S(1)}, u32[]{:S(2)}, u32[]{:S(2)}) %all-to-all-start) | async-done | bytes 1228832 | tf_op jit(solution)/shard_map/all_to_all | solution.py:689
  77.8 15.6 %legendre.1 = (f32[4,25,4,640]{3,2,1,0:T(4,128)S(1)}, bf16[32,100,128]{2,1,0:T(8,128)(2,1)S(1)}, bf16[32,50,128]{2,1,0:T(8,128)(2,1)}) custom-call(s32[2]{0:T(128)S(1)} %pad_add_fusion.place, s32[25]{0:T(128)S(1)} %get-tuple-element.62.order, s32[5]{0:T(128)S(1)} %and_select_fusion.5.blocks, f32[25,16,640]{2,1,0:T(8,128)S(1)} %multiply_select_fusion.damping, ...), custom_call_target="tpu_custom_call" | custom-call | flops 1572864000 | bytes 24576000 | tf_op jit(solution)/shard_map/legendre/pallas_call | solution.py:571
  93.4 0.9 copy-done.3
  94.3 6.3 %all-to-all-start.1 = ((bf16[32,100,128]{2,1,0:T(8,128)(2,1)}), bf16[32,100,128]{2,1,0:T(8,128)(2,1)S(1)}, u32[]{:S(2)}, u32[]{:S(2)}) async-start(bf16[32,100,128]{2,1,0:T(8,128)(2,1)} %copy-done.3), calls=%async_computation.1 | async-start | bytes 1703936 | tf_op jit(solution)/shard_map/all_to_all | solution.py:702
  100.6 0.6 gather_fusion.3
  101.2 0.6 gather_fusion.2
  101.7 0.6 and_select_fusion.1.named
  102.3 4.1 %wave_table.3 = (bf16[2560,640]{1,0:T(8,128)(2,1)}, bf16[640,1024]{1,0:T(8,128)(2,1)}) custom-call(f32[32,640]{1,0:T(8,128)} %constant.145.clone.near_cos, f32[32,640]{1,0:T(8,128)} %constant.146.clone.near_sin, f32[20,1,640]{2,1,0:T(1,128)} %constant.147.clone.far_cos, f32[20,1,640]{2,1,0:T(1,128)} %constant.148.clone.far_sin, ...), custom_call_target="tpu_custom_call" | custom-call | tf_op jit(solution)/shard_map/wave_table/pallas_call | solution.py:76
  106.5 0.2 convert.10
  106.7 0.2 slice_convert_fusion
  106.9 1.8 %collective-permute-start.3 = (bf16[25,4,640]{2,1,0:T(4,128)(2,1)S(1)}, bf16[25,4,640]{2,1,0:T(4,128)(2,1)S(1)}, u32[]{:S(2)}, u32[]{:S(2)}) collective-permute-start(bf16[25,4,640]{2,1,0:T(4,128)(2,1)S(1)} %get-tuple-element.70), channel_id=1, source_target_pairs={{0,2},{1,3},{2,0},{3,1},{4,6},{5,7},{6,4},{7,5},{8,10},{9,11},{10,... | collective-permute-start | bytes 384008 | tf_op jit(solution)/shard_map/ppermute | solution.py:626
  108.7 0.4 collective-permute-start.5
  109.1 0.1 broadcast_select_fusion
  109.2 0.2 reshape.461
  109.4 5.5 %collective-permute-done.3 = bf16[25,4,640]{2,1,0:T(4,128)(2,1)S(1)} collective-permute-done((bf16[25,4,640]{2,1,0:T(4,128)(2,1)S(1)}, bf16[25,4,640]{2,1,0:T(4,128)(2,1)S(1)}, u32[]{:S(2)}, u32[]{:S(2)}) %collective-permute-start.3) | collective-permute-done | bytes 128032 | tf_op jit(solution)/shard_map/ppermute | solution.py:626
  114.9 0.2 reshape.456
  115.1 2.6 %collective-permute-done.4 = bf16[25,4,640]{2,1,0:T(4,128)(2,1)S(1)} collective-permute-done((bf16[25,4,640]{2,1,0:T(4,128)(2,1)S(1)}, bf16[25,4,640]{2,1,0:T(4,128)(2,1)S(1)}, u32[]{:S(2)}, u32[]{:S(2)}) %collective-permute-start.4) | collective-permute-done | bytes 128032 | tf_op jit(solution)/shard_map/ppermute | solution.py:626
  117.7 0.2 reshape.458
  117.9 0.2 reshape.460
  118.1 0.3 broadcast_in_dim.102
  118.4 4.1 %all-to-all-done.1.wire = bf16[32,100,128]{2,1,0:T(8,128)(2,1)S(1)} async-done(((bf16[32,100,128]{2,1,0:T(8,128)(2,1)}), bf16[32,100,128]{2,1,0:T(8,128)(2,1)S(1)}, u32[]{:S(2)}, u32[]{:S(2)}) %all-to-all-start.1) | async-done | bytes 819232 | tf_op jit(solution)/shard_map/all_to_all | solution.py:702
  122.6 3.6 %all-to-all-start.2 = ((bf16[32,50,128]{2,1,0:T(8,128)(2,1)}), bf16[32,50,128]{2,1,0:T(8,128)(2,1)S(1)}, u32[]{:S(2)}, u32[]{:S(2)}) async-start(bf16[32,50,128]{2,1,0:T(8,128)(2,1)} %get-tuple-element.34), calls=%async_computation.2 | async-start | bytes 917504 | tf_op jit(solution)/shard_map/all_to_all | solution.py:702
  126.4 4.3 %backward_first.3 = (bf16[256,640]{1,0:T(8,128)(2,1)S(1)}, bf16[2,256,640]{2,1,0:T(8,128)(2,1)S(1)}) custom-call(bf16[32,100,128]{2,1,0:T(8,128)(2,1)S(1)} %all-to-all-done.1.wire, bf16[2560,640]{1,0:T(8,128)(2,1)} %get-tuple-element.35.table_hbm.table, f32[1,1,640]{2,1,0:T(1,128)S(1)} %get-tuple-element.82.turn_cos, ...), custom_call_target="tpu_custom_call" | custom-call | flops 1000000000 | bytes 10000000 | tf_op jit(solution)/shard_map/backward_first/pallas_call | solution.py:310
  130.6 5.8 %backward_rest.3 = (bf16[256,640]{1,0:T(8,128)(2,1)S(1)}, bf16[256,640]{1,0:T(8,128)(2,1)}, bf16[256,640]{1,0:T(8,128)(2,1)S(1)}) custom-call(bf16[2,256,640]{2,1,0:T(8,128)(2,1)S(1)} %get-tuple-element.40.by_wave, bf16[2560,640]{1,0:T(8,128)(2,1)} %get-tuple-element.35.table_hbm.table, f32[3,1,640]{2,1,0:T(1,128)S(1)} %get-tuple-element.76.turn_cos, ...), custom_call_target="tpu_custom_call" | custom-call | flops 3000000000 | bytes 10000000 | tf_op jit(solution)/shard_map/backward_rest/pallas_call | solution.py:342
  136.5 1.5 collective-permute-start.7
  137.9 0.4 collective-permute-start.10
  138.4 0.2 collective-permute-start.11
  138.6 2.0 %all-to-all-done.2.wire = bf16[32,50,128]{2,1,0:T(8,128)(2,1)S(1)} async-done(((bf16[32,50,128]{2,1,0:T(8,128)(2,1)}), bf16[32,50,128]{2,1,0:T(8,128)(2,1)S(1)}, u32[]{:S(2)}, u32[]{:S(2)}) %all-to-all-start.2) | async-done | bytes 409632 | tf_op jit(solution)/shard_map/all_to_all | solution.py:702
  140.6 3.5 %backward_first.2 = (bf16[128,640]{1,0:T(8,128)(2,1)S(1)}, bf16[2,128,640]{2,1,0:T(8,128)(2,1)S(1)}) custom-call(bf16[32,50,128]{2,1,0:T(8,128)(2,1)S(1)} %all-to-all-done.2.wire, bf16[2560,640]{1,0:T(8,128)(2,1)} %get-tuple-element.35.table_hbm.table, f32[1,1,640]{2,1,0:T(1,128)S(1)} %get-tuple-element.82.turn_cos, ...), custom_call_target="tpu_custom_call" | custom-call | flops 1000000000 | bytes 10000000 | tf_op jit(solution)/shard_map/backward_first/pallas_call | solution.py:310
  144.2 3.6 %backward_rest.2 = (bf16[128,640]{1,0:T(8,128)(2,1)S(1)}, bf16[128,640]{1,0:T(8,128)(2,1)S(1)}, bf16[128,640]{1,0:T(8,128)(2,1)S(1)}) custom-call(bf16[2,128,640]{2,1,0:T(8,128)(2,1)S(1)} %get-tuple-element.37.by_wave, bf16[2560,640]{1,0:T(8,128)(2,1)} %get-tuple-element.35.table_hbm.table, f32[3,1,640]{2,1,0:T(1,128)S(1)} %get-tuple-element.76.turn_cos, ...), custom_call_target="tpu_custom_call" | custom-call | flops 3000000000 | bytes 10000000 | tf_op jit(solution)/shard_map/backward_rest/pallas_call | solution.py:342
  147.8 0.7 collective-permute-start.6
  148.5 0.1 collective-permute-start.8
  148.6 1.4 collective-permute-start.9
  150.0 0.7 bitcast_dynamic-update-slice_fusion
  150.8 3.4 %collective-permute-done.11.refs_2_ = bf16[256,640]{1,0:T(8,128)(2,1)S(1)} collective-permute-done((bf16[256,640]{1,0:T(8,128)(2,1)S(1)}, bf16[256,640]{1,0:T(8,128)(2,1)S(1)}, u32[]{:S(2)}, u32[]{:S(2)}) %collective-permute-start.11) | collective-permute-done | bytes 327712 | tf_op jit(solution)/shard_map/ppermute | solution.py:626
  154.2 1.3 placed.3.refs_4_
  155.6 5.3 %collective-permute-done.9.refs_3_ = bf16[128,640]{1,0:T(8,128)(2,1)S(1)} collective-permute-done((bf16[128,640]{1,0:T(8,128)(2,1)S(1)}, bf16[128,640]{1,0:T(8,128)(2,1)S(1)}, u32[]{:S(2)}, u32[]{:S(2)}) %collective-permute-start.9) | collective-permute-done | bytes 163872 | tf_op jit(solution)/shard_map/ppermute | solution.py:626
  160.8 1.2 placed.4.refs_1_
  162.1 0.8 placed.5
  (47 shorter events, 0.5 us)
Async XLA Ops:
  3.7 32.1 %collective-permute-start = (bf16[384,640]{1,0:T(8,128)(2,1)}, bf16[384,640]{1,0:T(8,128)(2,1)S(1)}, u32[]{:S(2)}, u32[]{:S(2)}) collective-permute-start(bf16[384,640]{1,0:T(8,128)(2,1)} %get-tuple-element.26), channel_id=1, source_target_pairs={{0,3},{1,2},{2,1},{3,0},{4,7},{5,6},{6,5},{7,4},{8,11},{9,10},{10,... | collective-permute-start | bytes 1474568 | tf_op jit(solution)/shard_map/ppermute | solution.py:626
  6.2 3.3 %copy-start.6 = (f32[4,640]{1,0:T(4,128)S(1)}, f32[4,640]{1,0:T(4,128)}, u32[]{:S(2)}) copy-start(f32[4,640]{1,0:T(4,128)} %constant.191) | copy-start | bytes 30724
  6.2 3.8 %copy-start.5 = (f32[4,640]{1,0:T(4,128)S(1)}, f32[4,640]{1,0:T(4,128)}, u32[]{:S(2)}) copy-start(f32[4,640]{1,0:T(4,128)} %constant.190) | copy-start | bytes 30724
  6.2 5.5 %copy-start.8 = (s32[640]{0:T(1024)S(1)}, s32[640]{0:T(1024)}, u32[]{:S(2)}) copy-start(s32[640]{0:T(1024)} %param.23) | copy-start | bytes 7684
  6.2 10.5 %copy-start.10 = (f32[4,1,640]{2,1,0:T(1,128)S(1)}, f32[4,1,640]{2,1,0:T(1,128)}, u32[]{:S(2)}) copy-start(f32[4,1,640]{2,1,0:T(1,128)} %constant.150.clone2.4) | copy-start | bytes 30724
  6.2 10.5 %copy-start.11 = (f32[4,1,640]{2,1,0:T(1,128)S(1)}, f32[4,1,640]{2,1,0:T(1,128)}, u32[]{:S(2)}) copy-start(f32[4,1,640]{2,1,0:T(1,128)} %constant.149.clone2.4) | copy-start | bytes 30724
  6.2 22.5 %copy-start.4 = (bf16[384,640]{1,0:T(8,128)(2,1)S(1)}, bf16[384,640]{1,0:T(8,128)(2,1)}, u32[]{:S(2)}) copy-start(bf16[384,640]{1,0:T(8,128)(2,1)} %get-tuple-element.28.refs_0_) | copy-start | bytes 1474564
  6.2 10.5 %collective-permute-start.1 = (bf16[384,640]{1,0:T(8,128)(2,1)}, bf16[384,640]{1,0:T(8,128)(2,1)S(1)}, u32[]{:S(2)}, u32[]{:S(2)}) collective-permute-start(bf16[384,640]{1,0:T(8,128)(2,1)} %get-tuple-element.29), channel_id=1, source_target_pairs={{0,1},{1,0},{2,3},{3,2},{4,5},{5,4},{6,7},{7,6},{8,9},{9,8},{10,11... | collective-permute-start | bytes 1474568 | tf_op jit(solution)/shard_map/ppermute | solution.py:626
  9.3 19.4 %collective-permute-start.2 = (bf16[384,640]{1,0:T(8,128)(2,1)}, bf16[384,640]{1,0:T(8,128)(2,1)S(1)}, u32[]{:S(2)}, u32[]{:S(2)}) collective-permute-start(bf16[384,640]{1,0:T(8,128)(2,1)} %wind_products.3), channel_id=1, source_target_pairs={{0,2},{1,3},{2,0},{3,1},{4,6},{5,7},{6,4},{7,5},{8,10},{9,11},{10,... | collective-permute-start | bytes 1474568 | tf_op jit(solution)/shard_map/ppermute | solution.py:626
  28.7 1.9 %copy-start = (bf16[1280,1280]{1,0:T(8,128)(2,1)S(1)}, bf16[1280,1280]{1,0:T(8,128)(2,1)}, u32[]{:S(2)}) copy-start(bf16[1280,1280]{1,0:T(8,128)(2,1)} %get-tuple-element.27.refs_3_.refs_1_) | copy-start | bytes 9830404
  30.6 5.2 %copy-start.1 = (bf16[1280,1280]{1,0:T(8,128)(2,1)S(1)}, bf16[1280,1280]{1,0:T(8,128)(2,1)}, u32[]{:S(2)}) copy-start(bf16[1280,1280]{1,0:T(8,128)(2,1)} %get-tuple-element.27.refs_3_.refs_1_) | copy-start | bytes 9830404
  30.6 5.2 %copy-start.2 = (bf16[1024,640]{1,0:T(8,128)(2,1)S(1)}, bf16[1024,640]{1,0:T(8,128)(2,1)}, u32[]{:S(2)}) copy-start(bf16[1024,640]{1,0:T(8,128)(2,1)} %get-tuple-element.30.refs_5_) | copy-start | bytes 3932164
  40.7 6.9 %copy-start.9 = (s32[640]{0:T(1024)S(1)}, s32[640]{0:T(1024)}, u32[]{:S(2)}) copy-start(s32[640]{0:T(1024)} %param.24) | copy-start | bytes 7684
  40.7 7.5 %copy-start.12 = (f32[4]{0:T(128)S(1)}, f32[4]{0:T(128)}, u32[]{:S(2)}) copy-start(f32[4]{0:T(128)} %param.25) | copy-start | bytes 52
  40.7 37.1 %all-to-all-start = ((bf16[32,150,128]{2,1,0:T(8,128)(2,1)}), bf16[32,150,128]{2,1,0:T(8,128)(2,1)S(1)}, u32[]{:S(2)}, u32[]{:S(2)}) async-start(bf16[32,150,128]{2,1,0:T(8,128)(2,1)} %forward.3), calls=%async_computation | async-start | bytes 2490368 | tf_op jit(solution)/shard_map/all_to_all | solution.py:689
  93.4 0.9 copy-start.3
  94.3 28.3 %all-to-all-start.1 = ((bf16[32,100,128]{2,1,0:T(8,128)(2,1)}), bf16[32,100,128]{2,1,0:T(8,128)(2,1)S(1)}, u32[]{:S(2)}, u32[]{:S(2)}) async-start(bf16[32,100,128]{2,1,0:T(8,128)(2,1)} %copy-done.3), calls=%async_computation.1 | async-start | bytes 1703936 | tf_op jit(solution)/shard_map/all_to_all | solution.py:702
  106.9 8.0 %collective-permute-start.3 = (bf16[25,4,640]{2,1,0:T(4,128)(2,1)S(1)}, bf16[25,4,640]{2,1,0:T(4,128)(2,1)S(1)}, u32[]{:S(2)}, u32[]{:S(2)}) collective-permute-start(bf16[25,4,640]{2,1,0:T(4,128)(2,1)S(1)} %get-tuple-element.70), channel_id=1, source_target_pairs={{0,2},{1,3},{2,0},{3,1},{4,6},{5,7},{6,4},{7,5},{8,10},{9,11},{10,... | collective-permute-start | bytes 384008 | tf_op jit(solution)/shard_map/ppermute | solution.py:626
  108.7 9.0 %collective-permute-start.4 = (bf16[25,4,640]{2,1,0:T(4,128)(2,1)S(1)}, bf16[25,4,640]{2,1,0:T(4,128)(2,1)S(1)}, u32[]{:S(2)}, u32[]{:S(2)}) collective-permute-start(bf16[25,4,640]{2,1,0:T(4,128)(2,1)S(1)} %get-tuple-element.69), channel_id=1, source_target_pairs={{0,3},{1,2},{2,1},{3,0},{4,7},{5,6},{6,5},{7,4},{8,11},{9,10},{10,... | collective-permute-start | bytes 384008 | tf_op jit(solution)/shard_map/ppermute | solution.py:626
  108.7 9.2 %collective-permute-start.5 = (bf16[25,4,640]{2,1,0:T(4,128)(2,1)S(1)}, bf16[25,4,640]{2,1,0:T(4,128)(2,1)S(1)}, u32[]{:S(2)}, u32[]{:S(2)}) collective-permute-start(bf16[25,4,640]{2,1,0:T(4,128)(2,1)S(1)} %get-tuple-element.68), channel_id=1, source_target_pairs={{0,1},{1,0},{2,3},{3,2},{4,5},{5,4},{6,7},{7,6},{8,9},{9,8},{10,11... | collective-permute-start | bytes 384008 | tf_op jit(solution)/shard_map/ppermute | solution.py:626
  122.6 18.1 %all-to-all-start.2 = ((bf16[32,50,128]{2,1,0:T(8,128)(2,1)}), bf16[32,50,128]{2,1,0:T(8,128)(2,1)S(1)}, u32[]{:S(2)}, u32[]{:S(2)}) async-start(bf16[32,50,128]{2,1,0:T(8,128)(2,1)} %get-tuple-element.34), calls=%async_computation.2 | async-start | bytes 917504 | tf_op jit(solution)/shard_map/all_to_all | solution.py:702
  126.3 10.1 %copy-start.7 = (f32[100,1,2,2,640]{4,3,2,1,0:T(2,128)}, f32[100,1,2,2,640]{4,3,2,1,0:T(2,128)S(1)}, u32[]{:S(2)}) copy-start(f32[100,1,2,2,640]{4,3,2,1,0:T(2,128)S(1)} %bitcast_dynamic-update-slice_fusion.1) | copy-start | bytes 3072004
  136.5 19.1 %collective-permute-start.7 = (bf16[256,640]{1,0:T(8,128)(2,1)S(1)}, bf16[256,640]{1,0:T(8,128)(2,1)S(1)}, u32[]{:S(2)}, u32[]{:S(2)}) collective-permute-start(bf16[256,640]{1,0:T(8,128)(2,1)S(1)} %get-tuple-element.41), channel_id=1, source_target_pairs={{0,3},{1,2},{2,1},{3,0},{4,7},{5,6},{6,5},{7,4},{8,11},{9,10},{10,... | collective-permute-start | bytes 983048 | tf_op jit(solution)/shard_map/ppermute | solution.py:626
  137.9 10.7 %collective-permute-start.10 = (bf16[256,640]{1,0:T(8,128)(2,1)}, bf16[256,640]{1,0:T(8,128)(2,1)S(1)}, u32[]{:S(2)}, u32[]{:S(2)}) collective-permute-start(bf16[256,640]{1,0:T(8,128)(2,1)} %get-tuple-element.46), channel_id=1, source_target_pairs={{0,1},{1,0},{2,3},{3,2},{4,5},{5,4},{6,7},{7,6},{8,9},{9,8},{10,11... | collective-permute-start | bytes 983048 | tf_op jit(solution)/shard_map/ppermute | solution.py:626
  138.4 15.9 %collective-permute-start.11 = (bf16[256,640]{1,0:T(8,128)(2,1)S(1)}, bf16[256,640]{1,0:T(8,128)(2,1)S(1)}, u32[]{:S(2)}, u32[]{:S(2)}) collective-permute-start(bf16[256,640]{1,0:T(8,128)(2,1)S(1)} %get-tuple-element.47), channel_id=1, source_target_pairs={{0,2},{1,3},{2,0},{3,1},{4,6},{5,7},{6,4},{7,5},{8,10},{9,11},{10,... | collective-permute-start | bytes 983048 | tf_op jit(solution)/shard_map/ppermute | solution.py:626
  147.8 14.2 %collective-permute-start.6 = (bf16[128,640]{1,0:T(8,128)(2,1)S(1)}, bf16[128,640]{1,0:T(8,128)(2,1)S(1)}, u32[]{:S(2)}, u32[]{:S(2)}) collective-permute-start(bf16[128,640]{1,0:T(8,128)(2,1)S(1)} %get-tuple-element.38), channel_id=1, source_target_pairs={{0,3},{1,2},{2,1},{3,0},{4,7},{5,6},{6,5},{7,4},{8,11},{9,10},{10,... | collective-permute-start | bytes 491528 | tf_op jit(solution)/shard_map/ppermute | solution.py:626
  148.5 7.0 %collective-permute-start.8 = (bf16[128,640]{1,0:T(8,128)(2,1)S(1)}, bf16[128,640]{1,0:T(8,128)(2,1)S(1)}, u32[]{:S(2)}, u32[]{:S(2)}) collective-permute-start(bf16[128,640]{1,0:T(8,128)(2,1)S(1)} %get-tuple-element.43), channel_id=1, source_target_pairs={{0,1},{1,0},{2,3},{3,2},{4,5},{5,4},{6,7},{7,6},{8,9},{9,8},{10,11... | collective-permute-start | bytes 491528 | tf_op jit(solution)/shard_map/ppermute | solution.py:626
  148.6 12.2 %collective-permute-start.9 = (bf16[128,640]{1,0:T(8,128)(2,1)S(1)}, bf16[128,640]{1,0:T(8,128)(2,1)S(1)}, u32[]{:S(2)}, u32[]{:S(2)}) collective-permute-start(bf16[128,640]{1,0:T(8,128)(2,1)S(1)} %get-tuple-element.44), channel_id=1, source_target_pairs={{0,2},{1,3},{2,0},{3,1},{4,6},{5,7},{6,4},{7,5},{8,10},{9,11},{10,... | collective-permute-start | bytes 491528 | tf_op jit(solution)/shard_map/ppermute | solution.py:626

commit v9 on v8

--- a/solution.py
+++ b/solution.py
@@ -32,7 +32,8 @@
     return np.cos(turns), np.sin(turns)
 
 
-def table_kernel(interleaved, near_cos, near_sin, far_cos, far_sin, named, wave_slots, out, hot_out, space, hot, sems):
+def table_kernel(interleaved, near_cos, near_sin, far_cos, far_sin, named, wave_slots, out, hot_out, *rest):
+    space, hot, sems = rest[-3:]
     near, lanes = near_cos.shape
     steps = far_cos.shape[0]
     count = steps * near
@@ -65,7 +66,7 @@
         copy.wait()
 
 
-def wave_table(rows, columns, length, interleaved, named, wave_slots):
+def wave_table(rows, columns, length, interleaved, named, wave_slots, *spares):
     near = 32
     near_cos, near_sin = phases(np.arange(near), np.arange(columns), length)
     far_cos, far_sin = phases(np.arange(rows // near) * near, np.arange(columns), length)
@@ -75,8 +76,8 @@
     hot_shape = (slots, waves) if interleaved else (waves, slots)
     return pl.pallas_call(
         functools.partial(table_kernel, interleaved),
-        out_specs=[pl.BlockSpec(memory_space=pltpu.HBM)] * 2,
-        out_shape=[jax.ShapeDtypeStruct(shape, BF16), jax.ShapeDtypeStruct(hot_shape, BF16)],
+        out_specs=[pl.BlockSpec(memory_space=pltpu.HBM)] * (2 + len(spares)),
+        out_shape=[jax.ShapeDtypeStruct(one, BF16) for one in (shape, hot_shape, *spares)],
         scratch_shapes=[pltpu.VMEM(shape, BF16), pltpu.VMEM(hot_shape, BF16), pltpu.SemaphoreType.DMA((2,))],
         compiler_params=pltpu.CompilerParams(vmem_limit_bytes=WHOLE_LIMIT),
         name="wave_table",
@@ -421,7 +422,7 @@
 
 def legendre_kernel(sides, widths_in, widths, group, place, order, blocks, damping, basis, *rest):
     wires = len(widths)
-    received, rest = rest[: len(widths_in)], rest[len(widths_in) :]
+    received, rest = rest[: len(widths_in)], rest[len(widths_in) + 1 :]
     spectral_out, returned_out, rest = rest[0], rest[1 : 1 + wires], rest[1 + wires :]
     spectral, returned, (held, buffer, sems, out_sems, spectral_sem) = rest[0], rest[1 : 1 + wires], rest[1 + wires :]
     lat_rows = sum(widths)
@@ -558,19 +559,22 @@
         copy.wait()
 
 
-def legendre(received, basis, damping, place, order, blocks, sectors, sides, widths_in, widths, group):
+def wire_shape(devices, share, width):
+    lanes = wire_lanes(2 * width)
+    return devices, share * (4 * width // lanes), lanes
+
+
+def legendre(received, spare, basis, damping, place, order, blocks, sectors, sides, widths_in, widths, group):
     share = order.shape[0]
     devices = received[0].shape[0]
-    returned = []
-    for width in widths:
-        lanes = wire_lanes(2 * width)
-        returned.append((devices, share * (4 * width // lanes), lanes))
+    returned = [wire_shape(devices, share, width) for width in widths]
     degrees, half_lat = basis.shape[1:]
     combos = sectors * sides
+    spare = pltpu.with_memory_space_constraint(spare, pltpu.HBM)
     smem, vmem, hbm = (pl.BlockSpec(memory_space=space) for space in (pltpu.SMEM, pltpu.VMEM, pl.ANY))
     return pl.pallas_call(
         functools.partial(legendre_kernel, sides, widths_in, widths, group),
-        in_specs=[smem, smem, smem, vmem, hbm] + [vmem] * len(widths_in),
+        in_specs=[smem, smem, smem, vmem, hbm] + [vmem] * len(widths_in) + [hbm],
         out_specs=[pl.BlockSpec(memory_space=pltpu.HBM)] * (1 + len(widths)),
         out_shape=[
             jax.ShapeDtypeStruct((sectors, share, sides, degrees), F32),
@@ -585,6 +589,7 @@
             pltpu.SemaphoreType.DMA((len(widths), 8)),
             pltpu.SemaphoreType.DMA,
         ],
+        input_output_aliases={5 + len(widths_in): 1},
         cost_estimate=pl.CostEstimate(
             flops=4 * share * degrees * half_lat * 2 * combos,
             bytes_accessed=2 * share * degrees * half_lat,
@@ -592,7 +597,7 @@
         ),
         compiler_params=pltpu.CompilerParams(vmem_limit_bytes=LEGENDRE_LIMIT),
         name="legendre",
-    )(place, order, blocks, damping, basis, *received)
+    )(place, order, blocks, damping, basis, *received, spare)
 
 
 def degree_order(counts):
@@ -648,7 +653,9 @@
     place_owner, place_sector, place_slot = places // (sectors * padded), places // padded % sectors, places % padded
     in_owner = place_sector * share + place_slot
     named = jnp.where((place_slot < share) & (in_owner < capacity), place_owner * capacity + in_owner, -1)
-    forward_table, one_hot = wave_table(lon_cols, waves, length, True, named, wave_slots)
+    forward_table, one_hot, spare = wave_table(
+        lon_cols, waves, length, True, named, wave_slots, wire_shape(owners * sectors, share, widths[0])
+    )
     backward_table, one_hot_turned = wave_table(waves, lon_cols, length, False, named, wave_slots)
     backward_table, one_hot_turned = (
         pltpu.with_memory_space_constraint(value, pltpu.HBM) for value in (backward_table, one_hot_turned)
@@ -689,7 +696,7 @@
         received[chunk] = lax.all_to_all(fourier, ("lat", "lon"), split_axis=0, concat_axis=0, tiled=True)
     place = jnp.stack([first, sector_index]).astype(jnp.int32)
     spectral, *returned = legendre(
-        received, basis, damping, place, order, blocks, sectors, sides, whole, widths, group
+        received, spare, basis, damping, place, order, blocks, sectors, sides, whole, widths, group
     )
 
     exact = sectors in (1, 2, 4)

time: 164 us -> 155 us (0.945)
  waiting for transfers between devices: 63.9 us -> 57.9 us
  Pallas kernels: 60 us -> 57.7 us
    ppermute x12, waiting for transfers between devices: 28.9 us -> 22.8 us  [across(): lax.ppermute(value, 'lon', [(i, i ^ mask) for i in range(sectors)])]
  transfers between devices with their start and end apart: 15 -> 15, of which waited for: 8 -> 10; matrix products, arithmetic and copies ran while one was open for 5% -> 6% of each run, Pallas kernels for 22% -> 22%
where the time goes in v9:
time: 155 us; the launch traced here: 154 us
  waiting for transfers between devices  57.9 us (37%)
  Pallas kernels  57.7 us (37%)
  starting transfers between devices  25.5 us (16%)
  local copies, waits for them, and re-layouts  8.65 us (6%)
  other arithmetic  3.34 us (2%)
    all_to_all x1, waiting for transfers between devices, body(): lax.all_to_all(fourier, ('lat', 'lon'), split_axis=0, concat_axis=0, tile...  28.9 us
    ppermute x12, waiting for transfers between devices, across(): lax.ppermute(value, 'lon', [(i, i ^ mask) for i in range(sectors)])  22.8 us
    pallas_call x1, Pallas kernels, legendre(): pl.pallas_call(functools.partial(legendre_kernel, sides, widths_in, width...  14.4 us
    all_to_all x2, starting transfers between devices, body(): lax.all_to_all(wire, ('lat', 'lon'), split_axis=0, concat_axis=0, tiled=T...  10.1 us
    pallas_call x2, Pallas kernels, forward(): pl.pallas_call(functools.partial(forward_kernel, len(lines), earlier is n...  9.99 us
    ppermute x12, starting transfers between devices, across(): lax.ppermute(value, 'lon', [(i, i ^ mask) for i in range(sectors)])  9.37 us
    pallas_call x2, Pallas kernels, backward_rest(): pl.pallas_call(functools.partial(backward_rest_kernel, exact), in_specs=[...  8.79 us
    pallas_call x2, Pallas kernels, wave_table(): pl.pallas_call(functools.partial(table_kernel, interleaved), out_specs=[p...  8.41 us
  transfers between devices with their start and end apart: 15, of which 10 were waited for; matrix products, arithmetic and copies ran while one was open for 6% of the time, Pallas kernels for 22%

profile of v9, /device:TPU:0, one launch (start us, length us, event | category | flops | bytes accessed | tf_op | source)
XLA Modules:
  0.0 154.5 jit_solution(16937935343590548949)
XLA Ops:
  0.6 3.0 %wind_products.2 = (bf16[384,640]{1,0:T(8,128)(2,1)}, bf16[384,640]{1,0:T(8,128)(2,1)}, bf16[384,640]{1,0:T(8,128)(2,1)}) custom-call(f32[4,192,640]{2,1,0:T(8,128)} %wind_u.3, f32[4,192,640]{2,1,0:T(8,128)} %wind_v.3), custom_call_target="tpu_custom_call" | custom-call | tf_op jit(solution)/shard_map/wind_products/pallas_call | solution.py:156
  3.8 0.6 collective-permute-start.1
  4.3 2.3 %wind_products.3 = bf16[384,640]{1,0:T(8,128)(2,1)} custom-call(f32[4,192,640]{2,1,0:T(8,128)} %wind_u.3, f32[4,192,640]{2,1,0:T(8,128)} %wind_v.3), custom_call_target="tpu_custom_call" | custom-call | tf_op jit(solution)/shard_map/wind_products/pallas_call | solution.py:156
  6.7 2.7 %collective-permute-start.2 = (bf16[384,640]{1,0:T(8,128)(2,1)}, bf16[384,640]{1,0:T(8,128)(2,1)S(1)}, u32[]{:S(2)}, u32[]{:S(2)}) collective-permute-start(bf16[384,640]{1,0:T(8,128)(2,1)} %wind_products.3), channel_id=1, source_target_pairs={{0,2},{1,3},{2,0},{3,1},{4,6},{5,7},{6,4},{7,5},{8,10},{9,11},{10,... | collective-permute-start | bytes 1474568 | tf_op jit(solution)/shard_map/ppermute | solution.py:631
  9.4 0.1 compare_and_fusion
  9.5 0.6 gather_fusion
  10.1 0.6 gather_fusion.1
  10.7 0.1 broadcast_select_fusion.2
  10.8 1.1 fusion.11.named
  11.8 0.6 broadcast_in_dim.110.wave_slots
  12.4 4.3 %wave_table.2 = (bf16[1280,1280]{1,0:T(8,128)(2,1)}, bf16[1024,640]{1,0:T(8,128)(2,1)}, bf16[32,100,128]{2,1,0:T(8,128)(2,1)}) custom-call(f32[32,640]{1,0:T(8,128)} %constant.145.clone.near_cos, f32[32,640]{1,0:T(8,128)} %constant.146.clone.near_sin, f32[20,1,640]{2,1,0:T(1,128)} %constant.147.clone.far_cos, f32[20,1,640]{2,1,0:T(1,128)} %constant.148.clone.far_sin, ...), custom_call_target="tpu_custom_call" | custom-call | tf_op jit(solution)/shard_map/wave_table/pallas_call | solution.py:77
  16.8 4.9 %collective-permute-done.2.refs_2_ = bf16[384,640]{1,0:T(8,128)(2,1)S(1)} collective-permute-done((bf16[384,640]{1,0:T(8,128)(2,1)}, bf16[384,640]{1,0:T(8,128)(2,1)S(1)}, u32[]{:S(2)}, u32[]{:S(2)}) %collective-permute-start.2) | collective-permute-done | bytes 491552 | tf_op jit(solution)/shard_map/ppermute | solution.py:631
  21.7 1.9 %copy-done = bf16[1280,1280]{1,0:T(8,128)(2,1)S(1)} copy-done((bf16[1280,1280]{1,0:T(8,128)(2,1)S(1)}, bf16[1280,1280]{1,0:T(8,128)(2,1)}, u32[]{:S(2)}) %copy-start) | copy-done | bytes 3276824
  23.6 5.1 %forward.2.refs_4_ = f32[2,384,640]{2,1,0:T(8,128)S(1)} custom-call(bf16[384,640]{1,0:T(8,128)(2,1)S(1)} %copy-done.3, bf16[384,640]{1,0:T(8,128)(2,1)S(1)} %collective-permute-done.1.refs_1_, bf16[384,640]{1,0:T(8,128)(2,1)S(1)} %collective-permute-done.2.refs_2_, bf16[1280,1280]{1,0:T(8,128)(2,1)S(1)} %copy-done, ...), custom_call_target="tpu_custom_call" | custom-call | flops 3774873600 | bytes 10000000 | tf_op jit(solution)/shard_map/forward/pallas_call | solution.py:242
  28.8 2.8 %collective-permute-done.refs_0_ = bf16[384,640]{1,0:T(8,128)(2,1)S(1)} collective-permute-done((bf16[384,640]{1,0:T(8,128)(2,1)S(1)}, bf16[384,640]{1,0:T(8,128)(2,1)S(1)}, u32[]{:S(2)}, u32[]{:S(2)}) %collective-permute-start) | collective-permute-done | bytes 491552 | tf_op jit(solution)/shard_map/ppermute | solution.py:631
  31.5 4.9 %forward.3 = bf16[32,150,128]{2,1,0:T(8,128)(2,1)} custom-call(bf16[384,640]{1,0:T(8,128)(2,1)S(1)} %collective-permute-done.refs_0_, bf16[1280,1280]{1,0:T(8,128)(2,1)S(1)} %copy-done.1, f32[1,1,640]{2,1,0:T(1,128)S(1)} %get-tuple-element.83.refs_2_, f32[1,1,640]{2,1,0:T(1,128)S(1)} %get-tuple-element.74.refs_3_, f32[2,384,640]{2,1,0:T(8,128)S(1)} %forward.2.refs_4_, ...), custom_call_target="tpu_custom_call" | custom-call | flops 1258291200 | bytes 10000000 | tf_op jit(solution)/shard_map/forward/pallas_call | solution.py:242
  36.4 6.0 %all-to-all-start = ((bf16[32,150,128]{2,1,0:T(8,128)(2,1)}), bf16[32,150,128]{2,1,0:T(8,128)(2,1)S(1)}, u32[]{:S(2)}, u32[]{:S(2)}) async-start(bf16[32,150,128]{2,1,0:T(8,128)(2,1)} %forward.3), calls=%async_computation | async-start | bytes 2490368 | tf_op jit(solution)/shard_map/all_to_all | solution.py:696
  42.5 0.2 fusion.18
  42.7 0.2 convert_reduce_fusion
  42.9 0.1 select_reduce_fusion
  43.0 0.1 slice.19
  43.1 0.1 mul.91
  43.3 0.1 iota_compare_fusion
  43.4 0.1 fusion.21
  43.5 0.3 multiply_select_fusion.damping
  43.8 28.9 %all-to-all-done.rest_0_ = bf16[32,150,128]{2,1,0:T(8,128)(2,1)S(1)} async-done(((bf16[32,150,128]{2,1,0:T(8,128)(2,1)}), bf16[32,150,128]{2,1,0:T(8,128)(2,1)S(1)}, u32[]{:S(2)}, u32[]{:S(2)}) %all-to-all-start) | async-done | bytes 1228832 | tf_op jit(solution)/shard_map/all_to_all | solution.py:696
  72.7 14.4 %legendre.1 = (f32[4,25,4,640]{3,2,1,0:T(4,128)S(1)}, bf16[32,100,128]{2,1,0:T(8,128)(2,1)}, bf16[32,50,128]{2,1,0:T(8,128)(2,1)}) custom-call(s32[2]{0:T(128)S(1)} %pad_add_fusion.place, s32[25]{0:T(128)S(1)} %get-tuple-element.64.order, s32[5]{0:T(128)S(1)} %and_select_fusion.5.blocks, ...), custom_call_target="tpu_custom_call", output_to_operand_aliasing={{1}: (6, {})} | custom-call | flops 1572864000 | bytes 24576000 | tf_op jit(solution)/shard_map/legendre/pallas_call | solution.py:575
  87.1 6.3 %all-to-all-start.1 = ((bf16[32,100,128]{2,1,0:T(8,128)(2,1)}), bf16[32,100,128]{2,1,0:T(8,128)(2,1)S(1)}, u32[]{:S(2)}, u32[]{:S(2)}) async-start(bf16[32,100,128]{2,1,0:T(8,128)(2,1)} %get-tuple-element.35), calls=%async_computation.1 | async-start | bytes 1703936 | tf_op jit(solution)/shard_map/all_to_all | solution.py:709
  93.4 0.6 gather_fusion.2
  94.0 0.6 gather_fusion.3
  94.6 0.6 and_select_fusion.1.named
  95.2 4.1 %wave_table.3 = (bf16[2560,640]{1,0:T(8,128)(2,1)}, bf16[640,1024]{1,0:T(8,128)(2,1)}) custom-call(f32[32,640]{1,0:T(8,128)} %constant.145.clone.near_cos, f32[32,640]{1,0:T(8,128)} %constant.146.clone.near_sin, f32[20,1,640]{2,1,0:T(1,128)} %constant.147.clone.far_cos, f32[20,1,640]{2,1,0:T(1,128)} %constant.148.clone.far_sin, ...), custom_call_target="tpu_custom_call" | custom-call | tf_op jit(solution)/shard_map/wave_table/pallas_call | solution.py:77
  99.4 0.2 convert.10
  99.5 0.2 slice_convert_fusion
  99.7 1.8 %collective-permute-start.3 = (bf16[25,4,640]{2,1,0:T(4,128)(2,1)S(1)}, bf16[25,4,640]{2,1,0:T(4,128)(2,1)S(1)}, u32[]{:S(2)}, u32[]{:S(2)}) collective-permute-start(bf16[25,4,640]{2,1,0:T(4,128)(2,1)S(1)} %get-tuple-element.72), channel_id=1, source_target_pairs={{0,2},{1,3},{2,0},{3,1},{4,6},{5,7},{6,4},{7,5},{8,10},{9,11},{10,... | collective-permute-start | bytes 384008 | tf_op jit(solution)/shard_map/ppermute | solution.py:631
  101.6 0.4 collective-permute-start.5
  101.9 0.1 broadcast_select_fusion
  102.0 0.9 reshape.461
  102.9 4.8 %collective-permute-done.3 = bf16[25,4,640]{2,1,0:T(4,128)(2,1)S(1)} collective-permute-done((bf16[25,4,640]{2,1,0:T(4,128)(2,1)S(1)}, bf16[25,4,640]{2,1,0:T(4,128)(2,1)S(1)}, u32[]{:S(2)}, u32[]{:S(2)}) %collective-permute-start.3) | collective-permute-done | bytes 128032 | tf_op jit(solution)/shard_map/ppermute | solution.py:631
  107.7 0.2 reshape.456
  107.9 2.7 %collective-permute-done.4 = bf16[25,4,640]{2,1,0:T(4,128)(2,1)S(1)} collective-permute-done((bf16[25,4,640]{2,1,0:T(4,128)(2,1)S(1)}, bf16[25,4,640]{2,1,0:T(4,128)(2,1)S(1)}, u32[]{:S(2)}, u32[]{:S(2)}) %collective-permute-start.4) | collective-permute-done | bytes 128032 | tf_op jit(solution)/shard_map/ppermute | solution.py:631
  110.6 0.2 reshape.458
  110.8 0.2 reshape.460
  111.0 0.3 broadcast_in_dim.102
  111.3 4.1 %all-to-all-done.1.wire = bf16[32,100,128]{2,1,0:T(8,128)(2,1)S(1)} async-done(((bf16[32,100,128]{2,1,0:T(8,128)(2,1)}), bf16[32,100,128]{2,1,0:T(8,128)(2,1)S(1)}, u32[]{:S(2)}, u32[]{:S(2)}) %all-to-all-start.1) | async-done | bytes 819232 | tf_op jit(solution)/shard_map/all_to_all | solution.py:709
  115.4 3.8 %all-to-all-start.2 = ((bf16[32,50,128]{2,1,0:T(8,128)(2,1)}), bf16[32,50,128]{2,1,0:T(8,128)(2,1)S(1)}, u32[]{:S(2)}, u32[]{:S(2)}) async-start(bf16[32,50,128]{2,1,0:T(8,128)(2,1)} %get-tuple-element.36), calls=%async_computation.2 | async-start | bytes 917504 | tf_op jit(solution)/shard_map/all_to_all | solution.py:709
  119.4 0.9 copy-done.6
  120.4 3.9 %backward_first.3 = (bf16[256,640]{1,0:T(8,128)(2,1)S(1)}, bf16[2,256,640]{2,1,0:T(8,128)(2,1)S(1)}) custom-call(bf16[32,100,128]{2,1,0:T(8,128)(2,1)S(1)} %all-to-all-done.1.wire, bf16[2560,640]{1,0:T(8,128)(2,1)} %get-tuple-element.37.table_hbm.table, f32[1,1,640]{2,1,0:T(1,128)S(1)} %get-tuple-element.84.turn_cos, ...), custom_call_target="tpu_custom_call" | custom-call | flops 1000000000 | bytes 10000000 | tf_op jit(solution)/shard_map/backward_first/pallas_call | solution.py:311
  124.3 5.1 %backward_rest.3 = (bf16[256,640]{1,0:T(8,128)(2,1)S(1)}, bf16[256,640]{1,0:T(8,128)(2,1)S(1)}, bf16[256,640]{1,0:T(8,128)(2,1)S(1)}) custom-call(bf16[2,256,640]{2,1,0:T(8,128)(2,1)S(1)} %get-tuple-element.42.by_wave, bf16[2560,640]{1,0:T(8,128)(2,1)} %get-tuple-element.37.table_hbm.table, f32[3,1,640]{2,1,0:T(1,128)S(1)} %get-tuple-element.78.turn_cos, ...), custom_call_target="tpu_custom_call" | custom-call | flops 3000000000 | bytes 10000000 | tf_op jit(solution)/shard_map/backward_rest/pallas_call | solution.py:343
  129.4 0.1 collective-permute-start.10
  129.5 1.6 %collective-permute-start.11 = (bf16[256,640]{1,0:T(8,128)(2,1)S(1)}, bf16[256,640]{1,0:T(8,128)(2,1)S(1)}, u32[]{:S(2)}, u32[]{:S(2)}) collective-permute-start(bf16[256,640]{1,0:T(8,128)(2,1)S(1)} %get-tuple-element.49), channel_id=1, source_target_pairs={{0,2},{1,3},{2,0},{3,1},{4,6},{5,7},{6,4},{7,5},{8,10},{9,11},{10,... | collective-permute-start | bytes 983048 | tf_op jit(solution)/shard_map/ppermute | solution.py:631
  131.1 0.2 collective-permute-start.7
  131.3 2.1 %all-to-all-done.2.wire = bf16[32,50,128]{2,1,0:T(8,128)(2,1)S(1)} async-done(((bf16[32,50,128]{2,1,0:T(8,128)(2,1)}), bf16[32,50,128]{2,1,0:T(8,128)(2,1)S(1)}, u32[]{:S(2)}, u32[]{:S(2)}) %all-to-all-start.2) | async-done | bytes 409632 | tf_op jit(solution)/shard_map/all_to_all | solution.py:709
  133.5 3.5 %backward_first.2 = (bf16[128,640]{1,0:T(8,128)(2,1)S(1)}, bf16[2,128,640]{2,1,0:T(8,128)(2,1)S(1)}) custom-call(bf16[32,50,128]{2,1,0:T(8,128)(2,1)S(1)} %all-to-all-done.2.wire, bf16[2560,640]{1,0:T(8,128)(2,1)} %get-tuple-element.37.table_hbm.table, f32[1,1,640]{2,1,0:T(1,128)S(1)} %get-tuple-element.84.turn_cos, ...), custom_call_target="tpu_custom_call" | custom-call | flops 1000000000 | bytes 10000000 | tf_op jit(solution)/shard_map/backward_first/pallas_call | solution.py:311
  137.0 3.7 %backward_rest.2 = (bf16[128,640]{1,0:T(8,128)(2,1)S(1)}, bf16[128,640]{1,0:T(8,128)(2,1)S(1)}, bf16[128,640]{1,0:T(8,128)(2,1)S(1)}) custom-call(bf16[2,128,640]{2,1,0:T(8,128)(2,1)S(1)} %get-tuple-element.39.by_wave, bf16[2560,640]{1,0:T(8,128)(2,1)} %get-tuple-element.37.table_hbm.table, f32[3,1,640]{2,1,0:T(1,128)S(1)} %get-tuple-element.78.turn_cos, ...), custom_call_target="tpu_custom_call" | custom-call | flops 3000000000 | bytes 10000000 | tf_op jit(solution)/shard_map/backward_rest/pallas_call | solution.py:343
  140.8 1.0 collective-permute-start.9
  141.8 0.8 collective-permute-start.6
  142.6 0.7 bitcast_dynamic-update-slice_fusion
  143.3 1.3 placed.3.refs_4_
  144.7 1.9 %collective-permute-done.7.refs_0_ = bf16[256,640]{1,0:T(8,128)(2,1)S(1)} collective-permute-done((bf16[256,640]{1,0:T(8,128)(2,1)S(1)}, bf16[256,640]{1,0:T(8,128)(2,1)S(1)}, u32[]{:S(2)}, u32[]{:S(2)}) %collective-permute-start.7) | collective-permute-done | bytes 327712 | tf_op jit(solution)/shard_map/ppermute | solution.py:631
  146.5 4.3 %collective-permute-done.9.refs_3_ = bf16[128,640]{1,0:T(8,128)(2,1)S(1)} collective-permute-done((bf16[128,640]{1,0:T(8,128)(2,1)S(1)}, bf16[128,640]{1,0:T(8,128)(2,1)S(1)}, u32[]{:S(2)}, u32[]{:S(2)}) %collective-permute-start.9) | collective-permute-done | bytes 163872 | tf_op jit(solution)/shard_map/ppermute | solution.py:631
  150.8 1.2 placed.4.refs_1_
  152.1 1.5 collective-permute-done.6.refs_0_
  153.6 0.8 placed.5
  (49 shorter events, 0.6 us)
Async XLA Ops:
  3.7 5.7 %copy-start.13 = (bf16[384,640]{1,0:T(8,128)(2,1)S(1)}, bf16[384,640]{1,0:T(8,128)(2,1)}, u32[]{:S(2)}) copy-start(bf16[384,640]{1,0:T(8,128)(2,1)} %get-tuple-element.27) | copy-start | bytes 1474564
  3.7 5.8 %copy-start.5 = (f32[4,640]{1,0:T(4,128)S(1)}, f32[4,640]{1,0:T(4,128)}, u32[]{:S(2)}) copy-start(f32[4,640]{1,0:T(4,128)} %constant.190) | copy-start | bytes 30724
  3.7 6.4 %copy-start.4 = (f32[4,640]{1,0:T(4,128)S(1)}, f32[4,640]{1,0:T(4,128)}, u32[]{:S(2)}) copy-start(f32[4,640]{1,0:T(4,128)} %constant.191) | copy-start | bytes 30724
  3.7 8.1 %copy-start.8 = (s32[640]{0:T(1024)S(1)}, s32[640]{0:T(1024)}, u32[]{:S(2)}) copy-start(s32[640]{0:T(1024)} %param.23) | copy-start | bytes 7684
  3.7 13.0 %copy-start.10 = (f32[4,1,640]{2,1,0:T(1,128)S(1)}, f32[4,1,640]{2,1,0:T(1,128)}, u32[]{:S(2)}) copy-start(f32[4,1,640]{2,1,0:T(1,128)} %constant.149.clone2.4) | copy-start | bytes 30724
  3.7 13.0 %copy-start.11 = (f32[4,1,640]{2,1,0:T(1,128)S(1)}, f32[4,1,640]{2,1,0:T(1,128)}, u32[]{:S(2)}) copy-start(f32[4,1,640]{2,1,0:T(1,128)} %constant.150.clone2.4) | copy-start | bytes 30724
  3.7 17.9 %copy-start.3 = (bf16[384,640]{1,0:T(8,128)(2,1)S(1)}, bf16[384,640]{1,0:T(8,128)(2,1)}, u32[]{:S(2)}) copy-start(bf16[384,640]{1,0:T(8,128)(2,1)} %get-tuple-element.29.refs_0_) | copy-start | bytes 1474564
  3.8 13.0 %collective-permute-start.1 = (bf16[384,640]{1,0:T(8,128)(2,1)}, bf16[384,640]{1,0:T(8,128)(2,1)S(1)}, u32[]{:S(2)}, u32[]{:S(2)}) collective-permute-start(bf16[384,640]{1,0:T(8,128)(2,1)} %get-tuple-element.30), channel_id=1, source_target_pairs={{0,1},{1,0},{2,3},{3,2},{4,5},{5,4},{6,7},{7,6},{8,9},{9,8},{10,11... | collective-permute-start | bytes 1474568 | tf_op jit(solution)/shard_map/ppermute | solution.py:631
  6.7 15.0 %collective-permute-start.2 = (bf16[384,640]{1,0:T(8,128)(2,1)}, bf16[384,640]{1,0:T(8,128)(2,1)S(1)}, u32[]{:S(2)}, u32[]{:S(2)}) collective-permute-start(bf16[384,640]{1,0:T(8,128)(2,1)} %wind_products.3), channel_id=1, source_target_pairs={{0,2},{1,3},{2,0},{3,1},{4,6},{5,7},{6,4},{7,5},{8,10},{9,11},{10,... | collective-permute-start | bytes 1474568 | tf_op jit(solution)/shard_map/ppermute | solution.py:631
  9.4 22.1 %collective-permute-start = (bf16[384,640]{1,0:T(8,128)(2,1)S(1)}, bf16[384,640]{1,0:T(8,128)(2,1)S(1)}, u32[]{:S(2)}, u32[]{:S(2)}) collective-permute-start(bf16[384,640]{1,0:T(8,128)(2,1)S(1)} %copy-done.13), channel_id=1, source_target_pairs={{0,3},{1,2},{2,1},{3,0},{4,7},{5,6},{6,5},{7,4},{8,11},{9,10},{10,... | collective-permute-start | bytes 1474568 | tf_op jit(solution)/shard_map/ppermute | solution.py:631
  21.7 1.9 %copy-start = (bf16[1280,1280]{1,0:T(8,128)(2,1)S(1)}, bf16[1280,1280]{1,0:T(8,128)(2,1)}, u32[]{:S(2)}) copy-start(bf16[1280,1280]{1,0:T(8,128)(2,1)} %get-tuple-element.28.refs_3_.refs_1_) | copy-start | bytes 9830404
  23.6 7.9 %copy-start.1 = (bf16[1280,1280]{1,0:T(8,128)(2,1)S(1)}, bf16[1280,1280]{1,0:T(8,128)(2,1)}, u32[]{:S(2)}) copy-start(bf16[1280,1280]{1,0:T(8,128)(2,1)} %get-tuple-element.28.refs_3_.refs_1_) | copy-start | bytes 9830404
  23.6 7.9 %copy-start.2 = (bf16[1024,640]{1,0:T(8,128)(2,1)S(1)}, bf16[1024,640]{1,0:T(8,128)(2,1)}, u32[]{:S(2)}) copy-start(bf16[1024,640]{1,0:T(8,128)(2,1)} %get-tuple-element.31.refs_5_) | copy-start | bytes 3932164
  36.4 6.1 %copy-start.9 = (s32[640]{0:T(1024)S(1)}, s32[640]{0:T(1024)}, u32[]{:S(2)}) copy-start(s32[640]{0:T(1024)} %param.24) | copy-start | bytes 7684
  36.4 6.7 %copy-start.12 = (f32[4]{0:T(128)S(1)}, f32[4]{0:T(128)}, u32[]{:S(2)}) copy-start(f32[4]{0:T(128)} %param.25) | copy-start | bytes 52
  36.4 36.3 %all-to-all-start = ((bf16[32,150,128]{2,1,0:T(8,128)(2,1)}), bf16[32,150,128]{2,1,0:T(8,128)(2,1)S(1)}, u32[]{:S(2)}, u32[]{:S(2)}) async-start(bf16[32,150,128]{2,1,0:T(8,128)(2,1)} %forward.3), calls=%async_computation | async-start | bytes 2490368 | tf_op jit(solution)/shard_map/all_to_all | solution.py:696
  87.1 28.3 %all-to-all-start.1 = ((bf16[32,100,128]{2,1,0:T(8,128)(2,1)}), bf16[32,100,128]{2,1,0:T(8,128)(2,1)S(1)}, u32[]{:S(2)}, u32[]{:S(2)}) async-start(bf16[32,100,128]{2,1,0:T(8,128)(2,1)} %get-tuple-element.35), calls=%async_computation.1 | async-start | bytes 1703936 | tf_op jit(solution)/shard_map/all_to_all | solution.py:709
  99.7 8.0 %collective-permute-start.3 = (bf16[25,4,640]{2,1,0:T(4,128)(2,1)S(1)}, bf16[25,4,640]{2,1,0:T(4,128)(2,1)S(1)}, u32[]{:S(2)}, u32[]{:S(2)}) collective-permute-start(bf16[25,4,640]{2,1,0:T(4,128)(2,1)S(1)} %get-tuple-element.72), channel_id=1, source_target_pairs={{0,2},{1,3},{2,0},{3,1},{4,6},{5,7},{6,4},{7,5},{8,10},{9,11},{10,... | collective-permute-start | bytes 384008 | tf_op jit(solution)/shard_map/ppermute | solution.py:631
  101.6 9.0 %collective-permute-start.4 = (bf16[25,4,640]{2,1,0:T(4,128)(2,1)S(1)}, bf16[25,4,640]{2,1,0:T(4,128)(2,1)S(1)}, u32[]{:S(2)}, u32[]{:S(2)}) collective-permute-start(bf16[25,4,640]{2,1,0:T(4,128)(2,1)S(1)} %get-tuple-element.71), channel_id=1, source_target_pairs={{0,3},{1,2},{2,1},{3,0},{4,7},{5,6},{6,5},{7,4},{8,11},{9,10},{10,... | collective-permute-start | bytes 384008 | tf_op jit(solution)/shard_map/ppermute | solution.py:631
  101.6 9.2 %collective-permute-start.5 = (bf16[25,4,640]{2,1,0:T(4,128)(2,1)S(1)}, bf16[25,4,640]{2,1,0:T(4,128)(2,1)S(1)}, u32[]{:S(2)}, u32[]{:S(2)}) collective-permute-start(bf16[25,4,640]{2,1,0:T(4,128)(2,1)S(1)} %get-tuple-element.70), channel_id=1, source_target_pairs={{0,1},{1,0},{2,3},{3,2},{4,5},{5,4},{6,7},{7,6},{8,9},{9,8},{10,11... | collective-permute-start | bytes 384008 | tf_op jit(solution)/shard_map/ppermute | solution.py:631
  115.4 18.1 %all-to-all-start.2 = ((bf16[32,50,128]{2,1,0:T(8,128)(2,1)}), bf16[32,50,128]{2,1,0:T(8,128)(2,1)S(1)}, u32[]{:S(2)}, u32[]{:S(2)}) async-start(bf16[32,50,128]{2,1,0:T(8,128)(2,1)} %get-tuple-element.36), calls=%async_computation.2 | async-start | bytes 917504 | tf_op jit(solution)/shard_map/all_to_all | solution.py:709
  119.4 1.0 copy-start.6
  129.4 12.4 %collective-permute-start.10 = (bf16[256,640]{1,0:T(8,128)(2,1)S(1)}, bf16[256,640]{1,0:T(8,128)(2,1)S(1)}, u32[]{:S(2)}, u32[]{:S(2)}) collective-permute-start(bf16[256,640]{1,0:T(8,128)(2,1)S(1)} %get-tuple-element.48), channel_id=1, source_target_pairs={{0,1},{1,0},{2,3},{3,2},{4,5},{5,4},{6,7},{7,6},{8,9},{9,8},{10,11... | collective-permute-start | bytes 983048 | tf_op jit(solution)/shard_map/ppermute | solution.py:631
  129.5 13.8 %collective-permute-start.11 = (bf16[256,640]{1,0:T(8,128)(2,1)S(1)}, bf16[256,640]{1,0:T(8,128)(2,1)S(1)}, u32[]{:S(2)}, u32[]{:S(2)}) collective-permute-start(bf16[256,640]{1,0:T(8,128)(2,1)S(1)} %get-tuple-element.49), channel_id=1, source_target_pairs={{0,2},{1,3},{2,0},{3,1},{4,6},{5,7},{6,4},{7,5},{8,10},{9,11},{10,... | collective-permute-start | bytes 983048 | tf_op jit(solution)/shard_map/ppermute | solution.py:631
  131.1 15.4 %collective-permute-start.7 = (bf16[256,640]{1,0:T(8,128)(2,1)S(1)}, bf16[256,640]{1,0:T(8,128)(2,1)S(1)}, u32[]{:S(2)}, u32[]{:S(2)}) collective-permute-start(bf16[256,640]{1,0:T(8,128)(2,1)S(1)} %get-tuple-element.43), channel_id=1, source_target_pairs={{0,3},{1,2},{2,1},{3,0},{4,7},{5,6},{6,5},{7,4},{8,11},{9,10},{10,... | collective-permute-start | bytes 983048 | tf_op jit(solution)/shard_map/ppermute | solution.py:631
  137.0 5.6 %copy-start.7 = (f32[25,1,2,2,640]{4,3,2,0,1:T(2,128)S(1)}, f32[25,1,2,2,640]{4,3,2,0,1:T(2,128)}, u32[]{:S(2)}) copy-start(f32[25,1,2,2,640]{4,3,2,0,1:T(2,128)} %reshape.461) | copy-start | bytes 768004
  140.7 5.9 %collective-permute-start.8 = (bf16[128,640]{1,0:T(8,128)(2,1)S(1)}, bf16[128,640]{1,0:T(8,128)(2,1)S(1)}, u32[]{:S(2)}, u32[]{:S(2)}) collective-permute-start(bf16[128,640]{1,0:T(8,128)(2,1)S(1)} %get-tuple-element.45), channel_id=1, source_target_pairs={{0,1},{1,0},{2,3},{3,2},{4,5},{5,4},{6,7},{7,6},{8,9},{9,8},{10,11... | collective-permute-start | bytes 491528 | tf_op jit(solution)/shard_map/ppermute | solution.py:631
  140.8 10.1 %collective-permute-start.9 = (bf16[128,640]{1,0:T(8,128)(2,1)S(1)}, bf16[128,640]{1,0:T(8,128)(2,1)S(1)}, u32[]{:S(2)}, u32[]{:S(2)}) collective-permute-start(bf16[128,640]{1,0:T(8,128)(2,1)S(1)} %get-tuple-element.46), channel_id=1, source_target_pairs={{0,2},{1,3},{2,0},{3,1},{4,6},{5,7},{6,4},{7,5},{8,10},{9,11},{10,... | collective-permute-start | bytes 491528 | tf_op jit(solution)/shard_map/ppermute | solution.py:631
  141.8 11.8 %collective-permute-start.6 = (bf16[128,640]{1,0:T(8,128)(2,1)S(1)}, bf16[128,640]{1,0:T(8,128)(2,1)S(1)}, u32[]{:S(2)}, u32[]{:S(2)}) collective-permute-start(bf16[128,640]{1,0:T(8,128)(2,1)S(1)} %get-tuple-element.40), channel_id=1, source_target_pairs={{0,3},{1,2},{2,1},{3,0},{4,7},{5,6},{6,5},{7,4},{8,11},{9,10},{10,... | collective-permute-start | bytes 491528 | tf_op jit(solution)/shard_map/ppermute | solution.py:631
